TPU v7x, 32 devices: a whole 2x2x4 slice. The times are simulated.
32 devices in a mesh: dp: 8 (over z, y), fsdp: 4 (over x, core).
Axes of the slice: x: 2, y: 2, z: 4, core: 2. Of those that a mesh axis runs over, the one named last changes fastest.
Arguments:
- tokens: bfloat16 [8192, 1024], P(('dp', 'fsdp')), may hold values from -6 to 6
- cotangent: bfloat16 [8192, 1024], P(('dp', 'fsdp')), may hold values from -6 to 6
- master: float32 [12597248], P(('dp', 'fsdp')), may hold values from -4 to 4
- first_moment: float32 [12597248], P(('dp', 'fsdp')), may hold values from -2.5 to 2.5
- second_moment: float32 [12597248], P(('dp', 'fsdp')), may hold values from 0.33 to 1.3
- average: float32 [12597248], P(('dp', 'fsdp')), may hold values from -0.5 to 0.5
- timestep: int32 [8], P('dp'), may hold values from 1 to 5000
- block_length: int32 [8], P('dp'), may hold values from 10 to 50, as said below
- block_start: int32 [8], P('dp'), may hold values from 0 to 974
Outputs:
- block_out: bfloat16 [8192, 1024], P(('dp', 'fsdp'))
- input_grad: float32 [8192, 1024], P(('dp', 'fsdp'))
- grad_norm: float32 [], replicated
- vector_grad: float32 [14336], P('fsdp')
- new_first: float32 [12597248], P(('dp', 'fsdp'))
- new_second: float32 [12597248], P(('dp', 'fsdp'))
- new_master: float32 [12597248], P(('dp', 'fsdp'))
- new_average: float32 [12597248], P(('dp', 'fsdp'))
Inputs may be any that keep to these rules, and one draw needn't show every extreme that they name: `block_length`: each is 10, 25 or 50; some sequence has 50 and some 10.
All inputs are finite; a program needn't handle non-finite values.
Results may differ from a plain program's by a relative error of at most 0.01225.
The roundings to bfloat16 on the way count: a program that leaves them out, or rounds other values in their place, can miss the bound.
Values may be sent and summed in bfloat16 or wider, within the bound.
No kernel may reach another device: no remote copies, remote signals or barrier semaphores. Data moves between devices by JAX's collectives and lax.ppermute only.
A program may use at most 192 MiB of HBM per device.

v0:
```python
from functools import partial
import math

import jax
import jax.numpy as jnp
from jax import lax
from jax.sharding import PartitionSpec as P

D = 1024
H = 16
DH = 64
FF = 4096
STEP = 10
PARAMS = 12597248


NORM_EPS = 1e-05


def product(left, right):
    return jnp.dot(left, right, preferred_element_type=jnp.float32)


def product_inner(left, right):
    return lax.dot_general(
        left, right, (((0,), (0,)), ((), ())), preferred_element_type=jnp.float32
    )


def layer_norm(resid, gain, shift):
    average = jnp.mean(resid, axis=-1, keepdims=True)
    centred = resid - average
    variance = jnp.mean(centred * centred, axis=-1, keepdims=True)
    return centred * lax.rsqrt(variance + NORM_EPS) * gain + shift


def unpack(flat_params, dp_count, fsdp_count):
    shapes = [(D, D)] * 4 + [(D, FF), (FF, D)] + [(1, D)] * 4 + [(1, FF)] + [(1, D)] * 6
    blocks = (
        flat_params.reshape(dp_count, fsdp_count, -1).transpose(1, 0, 2).reshape(fsdp_count, -1)
    )
    pieces = []
    offset = 0
    for rows, cols in shapes:
        width = rows * (cols // fsdp_count)
        part = blocks[:, offset : offset + width].reshape(fsdp_count, rows, cols // fsdp_count)
        whole = part.transpose(1, 0, 2).reshape(rows, cols)
        pieces.append(whole.reshape(-1) if rows == 1 else whole)
        offset += width
    return pieces


def split_heads(values):
    return values.reshape(values.shape[0], H, DH).transpose(1, 0, 2)


def merge_heads(values):
    return values.transpose(1, 0, 2).reshape(values.shape[1], H * DH)


def head_forward(head_item):
    query_h, key_h, value_h = head_item
    scores = product(query_h, key_h.T) * DH ** (-0.5)
    highest = jnp.max(scores, axis=1, keepdims=True)
    weights = jnp.exp(scores - highest)
    totals = jnp.sum(weights, axis=1, keepdims=True)
    probabilities = weights / totals
    result = product(probabilities.astype(jnp.bfloat16), value_h)
    return (result, (highest + jnp.log(totals))[:, 0])


def head_query_back(head_item):
    query_h, key_h, value_h, grad_h, logsum = head_item
    score_scale = DH ** (-0.5)
    scores = product(query_h, key_h.T) * score_scale
    probabilities = jnp.exp(scores - logsum[:, None])
    prob_grad = product(grad_h, value_h.T)
    inner_sum = jnp.sum(probabilities * prob_grad, axis=1)
    score_grad = (probabilities * (prob_grad - inner_sum[:, None])).astype(jnp.bfloat16)
    query_grad = product(score_grad, key_h) * score_scale
    return (query_grad, inner_sum)


def head_key_back(head_item):
    key_h, value_h, query_all, grad_all, logsum_all, inner_all = head_item
    score_scale = DH ** (-0.5)
    scores_t = product(key_h, query_all.T) * score_scale
    probs_t = jnp.exp(scores_t - logsum_all[None, :])
    prob_grad_t = product(value_h, grad_all.T)
    score_grad_t = (probs_t * (prob_grad_t - inner_all[None, :])).astype(jnp.bfloat16)
    key_grad = product(score_grad_t, query_all) * score_scale
    value_grad = product(probs_t.astype(jnp.bfloat16), grad_all)
    return (key_grad, value_grad)


def body(
    tokens,
    cotangent,
    master,
    first_moment,
    second_moment,
    average,
    timestep,
    block_length,
    block_start,
):
    dp_count = lax.axis_size("dp")
    fsdp_count = lax.axis_size("fsdp")
    master_low = master.astype(jnp.bfloat16)
    flat_params = lax.all_gather(master_low, ("dp", "fsdp"), axis=0, tiled=True)
    (
        w_query,
        w_key,
        w_value,
        w_out,
        w_up,
        w_down,
        b_query,
        b_value,
        b_out,
        b_down,
        b_up,
        gain_attn,
        shift_attn,
        gain_ffn,
        shift_ffn,
        w_time,
        b_time,
    ) = unpack(flat_params, dp_count, fsdp_count)
    gain_a = gain_attn.astype(jnp.float32)
    shift_a = shift_attn.astype(jnp.float32)
    gain_f = gain_ffn.astype(jnp.float32)
    shift_f = shift_ffn.astype(jnp.float32)
    row_count = tokens.shape[0]
    position = lax.axis_index("fsdp") * row_count + jnp.arange(row_count, dtype=jnp.int32)
    block_first = block_start[0]
    inside = ((position >= block_first) & (position < block_first + block_length[0])).astype(
        jnp.float32
    )[:, None]
    time_frac = timestep[0].astype(jnp.float32) / 5000.0
    time_embed = time_frac * w_time.astype(jnp.float32) + b_time.astype(jnp.float32)
    stream = tokens.astype(jnp.float32) + inside * time_embed
    stream_low = stream.astype(jnp.bfloat16)
    queries = (product(stream_low, w_query) + b_query.astype(jnp.float32)).astype(jnp.bfloat16)
    keys_local = product(stream_low, w_key).astype(jnp.bfloat16)
    values_local = (product(stream_low, w_value) + b_value.astype(jnp.float32)).astype(jnp.bfloat16)
    keys_all, values_all = (
        lax.all_gather(keys_local, "fsdp", axis=0, tiled=True),
        lax.all_gather(values_local, "fsdp", axis=0, tiled=True),
    )
    query_heads = split_heads(queries)
    key_heads = split_heads(keys_all)
    value_heads = split_heads(values_all)
    head_out, logsum = lax.map(head_forward, (query_heads, key_heads, value_heads))
    heads_low = merge_heads(head_out).astype(jnp.bfloat16)
    resid_attn = stream + product(heads_low, w_out) + b_out.astype(jnp.float32)
    normed = layer_norm(resid_attn, gain_a, shift_a)
    normed_low = normed.astype(jnp.bfloat16)
    pre_act = product(normed_low, w_up) + b_up.astype(jnp.float32)
    hidden = jax.nn.gelu(pre_act, approximate=False).astype(jnp.bfloat16)
    resid_ffn = normed + product(hidden, w_down) + b_down.astype(jnp.float32)
    block_out = layer_norm(resid_ffn, gain_f, shift_f).astype(jnp.bfloat16)
    stream_all, heads_all, normed_all, hidden_all = (
        lax.all_gather(stream_low, "fsdp", axis=0, tiled=True),
        lax.all_gather(heads_low, "fsdp", axis=0, tiled=True),
        lax.all_gather(normed_low, "fsdp", axis=0, tiled=True),
        lax.all_gather(hidden, "fsdp", axis=0, tiled=True),
    )
    back_params = lax.all_gather(master_low, ("dp", "fsdp"), axis=0, tiled=True)
    back_pieces = unpack(back_params, dp_count, fsdp_count)
    w_query_back, w_key_back, w_value_back, w_out_back, w_up_back, w_down_back = back_pieces[:6]
    out_grad = cotangent.astype(jnp.float32)
    _, pull_ffn = jax.vjp(layer_norm, resid_ffn, gain_f, shift_f)
    resid_ffn_grad, grad_gain_ffn, grad_shift_ffn = pull_ffn(out_grad)
    ffn_grad = resid_ffn_grad.astype(jnp.bfloat16)
    hidden_grad = product(ffn_grad, w_down_back.T)
    _, pull_gelu = jax.vjp(partial(jax.nn.gelu, approximate=False), pre_act)
    pre_grad = pull_gelu(hidden_grad)[0].astype(jnp.bfloat16)
    normed_grad = resid_ffn_grad + product(pre_grad, w_up_back.T)
    _, pull_attn = jax.vjp(layer_norm, resid_attn, gain_a, shift_a)
    resid_attn_grad, grad_gain_attn, grad_shift_attn = pull_attn(normed_grad)
    attn_grad = resid_attn_grad.astype(jnp.bfloat16)
    heads_grad = product(attn_grad, w_out_back.T).astype(jnp.bfloat16)
    query_parts, inner_sum = lax.map(
        head_query_back, (query_heads, key_heads, value_heads, split_heads(heads_grad), logsum)
    )
    query_grad = merge_heads(query_parts).astype(jnp.bfloat16)
    queries_all, heads_grad_all = (
        lax.all_gather(queries, "fsdp", axis=0, tiled=True),
        lax.all_gather(heads_grad, "fsdp", axis=0, tiled=True),
    )
    logsum_all, inner_all = (
        lax.all_gather(logsum, "fsdp", axis=1, tiled=True),
        lax.all_gather(inner_sum, "fsdp", axis=1, tiled=True),
    )
    key_parts, value_parts = lax.map(
        head_key_back,
        (
            split_heads(keys_local),
            split_heads(values_local),
            split_heads(queries_all),
            split_heads(heads_grad_all),
            logsum_all,
            inner_all,
        ),
    )
    key_grad = merge_heads(key_parts).astype(jnp.bfloat16)
    value_grad = merge_heads(value_parts).astype(jnp.bfloat16)
    stream_grad = (
        resid_attn_grad
        + product(query_grad, w_query_back.T)
        + product(key_grad, w_key_back.T)
        + product(value_grad, w_value_back.T)
    )
    grad_b_time = jnp.sum(inside * stream_grad, axis=0)
    grad_w_time = time_frac * grad_b_time
    query_cols, key_cols, value_cols, attn_cols, ffn_cols, pre_cols = (
        lax.all_to_all(query_grad, "fsdp", split_axis=1, concat_axis=0, tiled=True),
        lax.all_to_all(key_grad, "fsdp", split_axis=1, concat_axis=0, tiled=True),
        lax.all_to_all(value_grad, "fsdp", split_axis=1, concat_axis=0, tiled=True),
        lax.all_to_all(attn_grad, "fsdp", split_axis=1, concat_axis=0, tiled=True),
        lax.all_to_all(ffn_grad, "fsdp", split_axis=1, concat_axis=0, tiled=True),
        lax.all_to_all(pre_grad, "fsdp", split_axis=1, concat_axis=0, tiled=True),
    )
    grad_w_query = product_inner(stream_all, query_cols)
    grad_w_key = product_inner(stream_all, key_cols)
    grad_w_value = product_inner(stream_all, value_cols)
    grad_w_out = product_inner(heads_all, attn_cols)
    grad_w_up = product_inner(normed_all, pre_cols)
    grad_w_down = product_inner(hidden_all, ffn_cols)
    grad_b_query = jnp.sum(query_cols.astype(jnp.float32), axis=0)
    grad_b_value = jnp.sum(value_cols.astype(jnp.float32), axis=0)
    grad_b_out = jnp.sum(attn_cols.astype(jnp.float32), axis=0)
    grad_b_down = jnp.sum(ffn_cols.astype(jnp.float32), axis=0)
    grad_b_up = jnp.sum(pre_cols.astype(jnp.float32), axis=0)
    vector_terms = jnp.stack(
        [grad_gain_attn, grad_shift_attn, grad_gain_ffn, grad_shift_ffn, grad_w_time, grad_b_time]
    )
    vector_part = lax.psum_scatter(vector_terms, "fsdp", scatter_dimension=1, tiled=True)
    vector_block = jnp.concatenate(
        [grad_b_query, grad_b_value, grad_b_out, grad_b_down, grad_b_up, vector_part.reshape(-1)]
    )
    grad_block = jnp.concatenate(
        [
            piece.reshape(-1)
            for piece in (
                grad_w_query,
                grad_w_key,
                grad_w_value,
                grad_w_out,
                grad_w_up,
                grad_w_down,
            )
        ]
        + [vector_block]
    )
    grad_shard = lax.psum_scatter(grad_block, "dp", scatter_dimension=0, tiled=True)
    vector_grad = lax.psum(vector_block, "dp")
    square_sum = lax.psum(jnp.sum(grad_shard * grad_shard), ("dp", "fsdp"))
    grad_norm = jnp.sqrt(square_sum)
    clip_limit = 4.0 * math.sqrt(PARAMS)
    clipped = grad_shard * (clip_limit / jnp.maximum(grad_norm, clip_limit))
    new_first = 0.9 * first_moment + 0.1 * clipped
    new_second = 0.98 * second_moment + 0.02 * clipped * clipped
    first_hat = new_first / (1.0 - 0.9**STEP)
    second_hat = new_second / (1.0 - 0.98**STEP)
    new_master = master - 0.02 * (first_hat / (jnp.sqrt(second_hat) + 1e-06) + 0.01 * master)
    new_average = 0.99 * average + 0.01 * new_master
    return (
        block_out,
        stream_grad,
        grad_norm,
        vector_grad,
        new_first,
        new_second,
        new_master,
        new_average,
    )


def solution(mesh):
    return jax.shard_map(
        body,
        mesh=mesh,
        in_specs=(
            P(("dp", "fsdp"), None),
            P(("dp", "fsdp"), None),
            P(("dp", "fsdp")),
            P(("dp", "fsdp")),
            P(("dp", "fsdp")),
            P(("dp", "fsdp")),
            P("dp"),
            P("dp"),
            P("dp"),
        ),
        out_specs=(
            P(("dp", "fsdp"), None),
            P(("dp", "fsdp"), None),
            P(),
            P("fsdp"),
            P(("dp", "fsdp")),
            P(("dp", "fsdp")),
            P(("dp", "fsdp")),
            P(("dp", "fsdp")),
        ),
        check_vma=False,
    )
```

profile of v0, /device:TPU:0, one launch (start us, length us, event | category | flops | bytes accessed | tf_op | source)
XLA Modules:
  0.0 1591.4 jit_solution(3609756152602219377)
XLA Ops:
  8.7 8.4 broadcast.257
  17.2 13.2 dynamic-update-slice
  32.3 395.0 %all-reduce.5.cloned.1.call-done = bf16[12597248]{0:T(1024)(128)(2,1)} async-done(((bf16[12597248]{0:T(1024)(128)(2,1)}), bf16[12597248]{0:T(1024)(128)(2,1)}) %all-reduce.5.cloned.1.call-update) | async-done | bytes 25194512
  427.4 45.3 %reshape.342 = bf16[8,4,393664]{2,1,0:T(4,128)(2,1)} reshape(bf16[12597248]{0:T(1024)(128)(2,1)} %all-reduce.5.cloned.1.call-done) | data formatting | bytes 50388992 | tf_op jit(solution)/shard_map/reshape | solution.py:40
  472.7 22.9 %copy.79 = bf16[4,8,393664]{2,1,0:T(8,128)(2,1)} copy(bf16[4,8,393664]{2,0,1:T(4,128)(2,1)} %bitcast.344) | data formatting | bytes 50388992 | tf_op jit(solution)/shard_map/transpose | solution.py:40
  495.6 49.4 %reshape.387 = bf16[12597248]{0:T(1024)(128)(2,1)} reshape(bf16[4,8,393664]{2,1,0:T(8,128)(2,1)} %copy.79) | data formatting | bytes 50388992
  545.1 32.3 %reshape.343 = bf16[4,3149312]{1,0:T(4,128)(2,1)} reshape(bf16[12597248]{0:T(1024)(128)(2,1)} %reshape.387) | data formatting | bytes 50388992 | tf_op jit(solution)/shard_map/reshape | solution.py:40
  577.3 6.4 fusion.87
  586.1 3.2 copy.82
  591.1 3.3 copy.154
  594.4 3.0 copy.84
  599.9 15.9 fusion.86
  618.1 3.0 copy.80
  624.4 3.2 copy.153
  627.6 4.0 copy.89
  631.7 9.5 copy.152
  641.2 11.4 copy.90
  652.6 7.7 copy.151
  660.3 11.4 copy.91
  671.8 3.3 copy.83
  675.1 3.1 copy.87
  678.2 3.1 copy.85
  681.3 3.2 copy.88
  684.6 49.2 %while.36 = (s32[]{:T(128)}, bf16[16,256,64]{1,2,0:T(8,128)(2,1)S(1)}, f32[16,256]{1,0:T(8,128)S(1)}, bf16[16,256,64]{2,1,0:T(8,128)(2,1)S(1)}, bf16[16,1024,64]...) while((s32[]{:T(128)}, bf16[16,256,64]{1,2,0:T(8,128)(2,1)S(1)}, ...), condition=%wide.region_3.4_spmd, body=%wide.region_0.3_spmd.sunk | while | flops 68943616 | bytes 3813473 | solution.py:154
  733.9 2.7 fusion.88
  737.1 16.3 %multiply_convert_fusion.2 = (bf16[256,4096]{1,0:T(8,128)(2,1)}, f32[256,4096]{1,0:T(8,128)}, f32[256,4096]{1,0:T(8,128)}) fusion(f32[4096]{0:T(1024)S(1)} %bitcast.419, bf16[256,1024]{1,0:T(8,128)(2,1)S(1)} %fusion.78, bf16[1024,4096]{0,1:T(8,128)(2,1)} %bitcast.353), kind=kOutput, calls=%fused_computation.79 | convolution fusion | flops 2216689664 | bytes 19415040 | tf_op jit(solution)/shard_map/dot_general | solution.py:21
  753.5 6.7 fusion.89
  762.6 6.4 add_convert_fusion
  769.1 2.7 multiply_reduce_fusion.3
  779.8 75.0 %while.37 = (s32[]{:T(128)}, bf16[16,256,64]{1,2,0:T(8,128)(2,1)}, f32[16,256]{1,0:T(8,128)S(1)}, bf16[16,256,64]{2,1,0:T(8,128)(2,1)S(1)}, bf16[16,1024,64]{2,1...) while((s32[]{:T(128)}, bf16[16,256,64]{1,2,0:T(8,128)(2,1)}, ...), condition=%wide.region_14.15_spmd, body=%wide.region_12.14_spmd.sunk | while | flops 102514432 | bytes 6203509 | solution.py:184
  854.9 4.3 all-to-all-start
  859.2 9.9 all_gather.38
  869.2 5.4 all_gather.40
  874.6 3.5 convolution_add_fusion.3
  879.8 4.0 copy.98
  883.8 4.0 copy.100
  889.5 84.9 %while.38 = (s32[]{:T(128)}, bf16[16,256,64]{1,2,0:T(8,128)(2,1)}, bf16[16,256,64]{1,2,0:T(8,128)(2,1)}, bf16[16,256,64]{1,2,0:T(8,128)(2,1)}, bf16[16,1024,64]{...) while((s32[]{:T(128)}, bf16[16,256,64]{1,2,0:T(8,128)(2,1)}, ...), condition=%wide.region_16.17_spmd, body=%wide.region_15.16_spmd.sunk | while | flops 135806976 | bytes 3895409 | solution.py:196
  974.4 4.1 all-to-all-start.3
  978.6 2.3 convolution_add_fusion.2
  980.8 2.9 multiply_reduce_fusion.2
  983.7 3.7 all-to-all-done.3
  987.4 4.1 all-to-all-start.5
  995.3 2.3 convolution_bitcast_fusion.7
  998.2 2.3 all-to-all-done.5
  1000.5 3.6 all-to-all-start.4
  1008.7 24.1 %all-to-all-done.4 = bf16[256,4,1024]{2,0,1:T(8,128)(2,1)S(1)} async-done(((bf16[256,4,1024]{2,0,1:T(8,128)(2,1)}), bf16[256,4,1024]{2,0,1:T(8,128)(2,1)S(1)}, u32[]{:S(2)}, u32[]{:S(2)}) %all-to-all-start.4) | async-done | bytes 2097184 | tf_op jit(solution)/shard_map/all_to_all | solution.py:223
  1033.2 3.5 all-to-all-start.1
  1036.7 6.0 convolution_bitcast_fusion.2
  1042.7 8.7 all-to-all-done.1
  1051.5 3.5 all-to-all-start.2
  1055.3 2.5 convolution_bitcast_fusion.4
  1058.4 3.0 copy.139
  1062.3 2.3 convolution_bitcast_fusion.6
  1065.2 4.5 all-to-all-done.2
  1069.9 2.3 convolution_bitcast_fusion.5
  1076.1 2.3 constant_dynamic-update-slice_fusion.9
  1078.4 9.6 all-gather.23.cloned.1.call-done
  1087.9 6.0 convolution_bitcast_fusion.3
  1096.1 2.3 constant_dynamic-update-slice_fusion.8
  1106.6 394.1 %all-reduce.7.cloned.1.call-done = f32[3149312]{0:T(1024)} async-done(((f32[3149312]{0:T(1024)}), f32[3149312]{0:T(1024)}) %all-reduce.7.cloned.1.call-update) | async-done | bytes 12597264
  1500.8 2.5 multiply_reduce_fusion.1
  1503.2 35.2 %psum.15 = f32[3584]{0:T(1024)} all-reduce(f32[3584]{0:T(1024)S(1)} %get-tuple-element.290), channel_id=1, replica_groups=mesh['dp'=8,'fsdp'=4] {'dp'}, use_global_device_ids=true, to_apply=%region_31.32 | all-reduce | flops 3584 | bytes 28672 | tf_op jit(solution)/shard_map/psum | solution.py:258
  1538.4 37.3 %psum.14 = f32[]{:T(128)} all-reduce(f32[]{:T(128)} %multiply_reduce_fusion.1), channel_id=1, replica_groups=mesh['dp'=8,'fsdp'=4] {'dp','fsdp'}, use_global_device_ids=true, to_apply=%region_30.31 | all-reduce | flops 1 | bytes 8 | tf_op jit(solution)/shard_map/psum | solution.py:259
  1576.5 6.7 multiply_add_fusion
  (401 shorter events, 261.3 us)
Async XLA Ops:
  7.2 420.2 %all-reduce.5.cloned.1.call-start = ((), (), s32[]{:S(2)}) async-start(), calls=%async_computation.16 | async-start | bytes 50388992
  30.3 641.5 %all-gather.9.cloned.1.call-start = ((), (), s32[]{:S(2)}) async-start(), calls=%async_computation.7 | async-start | bytes 2621440 | tf_op jit(solution)/shard_map/all_gather | solution.py:148
  584.4 4.9 copy-start.24
  589.3 5.1 copy-start.1
  589.5 31.6 %copy-start.9 = (bf16[256,1024]{1,0:T(8,128)(2,1)}, bf16[256,1024]{1,0:T(8,128)(2,1)S(1)}, u32[]{:S(2)}) copy-start(bf16[256,1024]{1,0:T(8,128)(2,1)S(1)} %fusion.77) | copy-start | bytes 1572868
  591.1 87.1 %all-gather.11.cloned.1.call-start = ((), (), s32[]{:S(2)}) async-start(), calls=%async_computation.8 | async-start | bytes 2621440 | tf_op jit(solution)/shard_map/all_gather | solution.py:149
  597.4 18.3 %copy-start.3 = (bf16[1024,4,256]{0,2,1:T(8,128)(2,1)}, bf16[1024,4,256]{0,2,1:T(8,128)(2,1)S(1)}, u32[]{:S(2)}) copy-start(bf16[1024,4,256]{0,2,1:T(8,128)(2,1)S(1)} %copy.84) | copy-start | bytes 6291460
  599.8 280.0 %all-gather.13.cloned.1.call-start = ((), (), s32[]{:S(2)}) async-start(), calls=%async_computation.9 | async-start | bytes 2621440 | tf_op jit(solution)/shard_map/all_gather | solution.py:189
  599.9 16.6 %copy-start.6 = (bf16[4,262144]{1,0:T(4,128)(2,1)S(1)}, bf16[4,262144]{1,0:T(4,128)(2,1)}, u32[]{:S(2)}) copy-start(bf16[4,262144]{1,0:T(4,128)(2,1)} %get-tuple-element.288) | copy-start | bytes 6291460
  621.1 6.5 copy-start.5
  621.9 1.0 copy-start.14
  671.7 212.1 %all-gather.15.cloned.1.call-start = ((), (), s32[]{:S(2)}) async-start(), calls=%async_computation.10 | async-start | bytes 2621440 | tf_op jit(solution)/shard_map/all_gather | solution.py:190
  684.6 49.3 %copy-start.25 = (bf16[256,1024]{1,0:T(8,128)(2,1)S(1)}, bf16[256,1024]{1,0:T(8,128)(2,1)}, u32[]{:S(2)}) copy-start(bf16[256,1024]{1,0:T(8,128)(2,1)} %param.15) | copy-start | bytes 1572868
  733.9 3.0 copy-start.17
  737.1 16.4 %copy-start.13 = (bf16[256,1024]{1,0:T(8,128)(2,1)}, bf16[256,1024]{1,0:T(8,128)(2,1)S(1)}, u32[]{:S(2)}) copy-start(bf16[256,1024]{1,0:T(8,128)(2,1)S(1)} %fusion.78) | copy-start | bytes 1572868
  753.5 8.9 slice-start.2
  753.5 7.0 copy-start.18
  753.5 8.9 slice-start.3
  760.3 2.4 copy-start.27
  761.0 8.1 slice-start
  762.4 6.7 copy-start.19
  762.6 6.4 slice-start.1
  769.1 2.8 copy-start.10
  771.8 1.6 copy-start.12
  772.3 3.4 copy-start.15
  772.3 4.4 copy-start.16
  772.4 0.8 copy-start.21
  775.0 220.3 %all-gather.17.cloned.1.call-start = ((), (), s32[]{:S(2)}) async-start(), calls=%async_computation.11 | async-start | bytes 2621440 | tf_op jit(solution)/shard_map/all_gather | solution.py:164
  775.6 261.2 %all-gather.21.cloned.1.call-start = ((), (), s32[]{:S(2)}) async-start(), calls=%async_computation.13 | async-start | bytes 2621440 | tf_op jit(solution)/shard_map/all_gather | solution.py:166
  854.8 23.3 %copy-start.22 = (bf16[256,1024]{1,0:T(8,128)(2,1)S(1)}, bf16[256,1024]{1,0:T(8,128)(2,1)}, u32[]{:S(2)}) copy-start(bf16[256,1024]{1,0:T(8,128)(2,1)} %copy-done.21) | copy-start | bytes 1572868
  854.8 24.1 %copy-start.20 = (bf16[256,1024]{1,0:T(8,128)(2,1)S(1)}, bf16[256,1024]{1,0:T(8,128)(2,1)}, u32[]{:S(2)}) copy-start(bf16[256,1024]{1,0:T(8,128)(2,1)} %copy-done.19) | copy-start | bytes 1572868
  854.9 119.5 %all-to-all-start = ((bf16[256,4,256]{0,2,1:T(8,128)(2,1)}), bf16[256,4,256]{0,2,1:T(8,128)(2,1)}, u32[]{:S(2)}, u32[]{:S(2)}) async-start(bf16[256,4,256]{0,2,1:T(8,128)(2,1)} %bitcast.63), calls=%async_computation | async-start | bytes 1048576 | tf_op jit(solution)/shard_map/all_to_all | solution.py:218
  859.2 196.1 %all-gather.19.cloned.1.call-start = ((), (), s32[]{:S(2)}) async-start(), calls=%async_computation.12 | async-start | bytes 2621440 | tf_op jit(solution)/shard_map/all_gather | solution.py:165
  889.5 89.1 %copy-start.2 = (bf16[1024,4,256]{0,2,1:T(8,128)(2,1)S(1)}, bf16[1024,4,256]{0,2,1:T(8,128)(2,1)}, u32[]{:S(2)}) copy-start(bf16[1024,4,256]{0,2,1:T(8,128)(2,1)} %copy-done.1) | copy-start | bytes 6291460
  974.4 13.1 all-to-all-start.3
  978.5 2.3 copy-start.4
  980.8 11.6 copy-start.11
  987.4 13.0 all-to-all-start.5
  991.6 69.8 %reduce-scatter.2.cloned.1.call-start = ((), (), s32[]{:S(2)}) async-start(), calls=%async_computation.15 | async-start | bytes 40960 | tf_op jit(solution)/shard_map/reduce_scatter | solution.py:239
  992.3 95.6 %all-gather.23.cloned.1.call-start = ((), (), s32[]{:S(2)}) async-start(), calls=%async_computation.14 | async-start | bytes 10485760 | tf_op jit(solution)/shard_map/all_gather | solution.py:167
  1000.5 32.4 %all-to-all-start.4 = ((bf16[256,4,1024]{2,0,1:T(8,128)(2,1)}), bf16[256,4,1024]{2,0,1:T(8,128)(2,1)S(1)}, u32[]{:S(2)}, u32[]{:S(2)}) async-start(bf16[256,4,1024]{2,0,1:T(8,128)(2,1)} %bitcast.291), calls=%async_computation.4 | async-start | bytes 4194304 | tf_op jit(solution)/shard_map/all_to_all | solution.py:223
  1033.2 18.2 %all-to-all-start.1 = ((bf16[256,4,256]{0,2,1:T(8,128)(2,1)}), bf16[256,4,256]{0,2,1:T(8,128)(2,1)S(1)}, u32[]{:S(2)}, u32[]{:S(2)}) async-start(bf16[256,4,256]{0,2,1:T(8,128)(2,1)} %bitcast.66), calls=%async_computation.1 | async-start | bytes 1048576 | tf_op jit(solution)/shard_map/all_to_all | solution.py:219
  1051.5 18.2 %all-to-all-start.2 = ((bf16[256,4,256]{0,2,1:T(8,128)(2,1)}), bf16[256,4,256]{0,2,1:T(8,128)(2,1)S(1)}, u32[]{:S(2)}, u32[]{:S(2)}) async-start(bf16[256,4,256]{0,2,1:T(8,128)(2,1)} %bitcast.69), calls=%async_computation.2 | async-start | bytes 1048576 | tf_op jit(solution)/shard_map/all_to_all | solution.py:220
  1054.9 445.8 %all-reduce.7.cloned.1.call-start = ((), (), s32[]{:S(2)}) async-start(), calls=%async_computation.17 | async-start | bytes 25198592
  1055.3 3.1 copy-start.8
  1072.2 3.9 copy-start
  1104.7 0.7 copy-start.26
  1104.7 471.7 %copy-start.7 = (f32[393664]{0:T(1024)S(1)}, f32[393664]{0:T(1024)}, u32[]{:S(2)}) copy-start(f32[393664]{0:T(1024)} %param.17) | copy-start | bytes 4723972
  1104.7 471.8 %copy-start.23 = (f32[393664]{0:T(1024)S(1)}, f32[393664]{0:T(1024)}, u32[]{:S(2)}) copy-start(f32[393664]{0:T(1024)} %param.20) | copy-start | bytes 4723972
Sparse Core Ops, SparseCore 0:
  30.5 396.8 all-reduce.4
  591.2 21.1 all-gather.8
  614.6 22.5 all-gather.10
  671.9 21.5 all-gather.12
  775.1 21.4 all-gather.14
  798.1 22.5 all-gather.16
  822.2 22.6 all-gather.20
  878.2 20.8 all-gather.18
  995.4 18.8 reduce-scatter.1
  1015.8 72.1 all-gather.22
  1104.9 395.8 all-reduce.6
where the time goes:
time: 1610 us; the launch traced here: 1590 us
  waiting for transfers between devices  843 us (52%)
  local copies, waits for them, and re-layouts  319 us (20%)
  matrix products  272 us (17%)
  blocking collectives  87.9 us (5%)
  other arithmetic  25.2 us (2%)
  starting transfers between devices  23.8 us (1%)
  between operations  19.7 us (1%)
    unnamed x13, waiting for transfers between devices  790 us
    dot_general x140, matrix products, product(): return jnp.dot(left, right, preferred_element_type=jnp.float32)  250 us
    unnamed x101, local copies, waits for them, and re-layouts  122 us
    reshape x2, local copies, waits for them, and re-layouts, unpack(): flat_params.reshape(dp_count, fsdp_count, -1).transpose(1, 0, 2)  77.6 us
    psum x1, blocking collectives, body(): square_sum = lax.psum(jnp.sum(grad_shard * grad_shard), ('dp', 'fsdp'))  37.3 us
    transpose x6, local copies, waits for them, and re-layouts, unpack(): whole = part.transpose(1, 0, 2).reshape(rows, cols)  36.1 us
    psum x1, blocking collectives, body(): vector_grad = lax.psum(vector_block, 'dp')  35.2 us
  transfers between devices with their start and end apart: 17, of which 8 were waited for; matrix products, arithmetic and copies ran while one was open for 25% of the time, Pallas kernels for 0%

commit v1 on v0

--- a/solution.py
+++ b/solution.py
@@ -4,6 +4,8 @@
 import jax
 import jax.numpy as jnp
 from jax import lax
+from jax.experimental import pallas as pl
+from jax.experimental.pallas import tpu as pltpu
 from jax.sharding import PartitionSpec as P
 
 D = 1024
@@ -12,9 +14,600 @@
 FF = 4096
 STEP = 10
 PARAMS = 12597248
-
-
 NORM_EPS = 1e-05
+
+SHARD = PARAMS // 32
+PIECE = 1600
+LANE_ROWS = 3080
+PAD = 128
+TAIL = 1536
+REGIONS = (
+    ("q", 0, 1024, 256),
+    ("k", 262144, 1024, 256),
+    ("v", 524288, 1024, 256),
+    ("o", 786432, 1024, 256),
+    ("up", 1048576, 1024, 1024),
+    ("down", 2097152, 4096, 256),
+    ("vec", 3145728, 16, 256),
+)
+
+
+def segments(shard):
+    low, high = shard * SHARD, (shard + 1) * SHARD
+    found, offset = [], 0
+    for name, start, rows, width in REGIONS:
+        size = 3584 if name == "vec" else rows * width
+        first, last = max(low, start), min(high, start + size)
+        if first >= last:
+            continue
+        row_a = (first - start) // width // 16 * 16
+        row_b = min(rows, -(-(-(-(last - start) // width)) // 16) * 16)
+        found.append((name, row_a, row_b, offset, width // 128, start // 128))
+        offset += (row_b - row_a) * (width // 256)
+    return found
+
+
+def lane_start(shard):
+    return shard * SHARD // 128
+
+
+SEGMENTS = [segments(shard) for shard in range(8)]
+SLOT = ((0, 3, 2, 1), (1, 0, 3, 2), (1, 3, 0, 2), (1, 2, 3, 0))
+
+
+def dot(left, right):
+    return jnp.dot(left, right, preferred_element_type=jnp.float32)
+
+
+def dot_last(left, right):
+    return lax.dot_general(
+        left, right, (((1,), (1,)), ((), ())), preferred_element_type=jnp.float32
+    )
+
+
+def dot_first(left, right):
+    return lax.dot_general(
+        left, right, (((0,), (0,)), ((), ())), preferred_element_type=jnp.float32
+    )
+
+
+def low(values):
+    return values.astype(jnp.bfloat16)
+
+
+def wide(values):
+    return values.astype(jnp.float32)
+
+
+VMEM = pl.BlockSpec(memory_space=pltpu.VMEM)
+SMEM = pl.BlockSpec(memory_space=pltpu.SMEM)
+ANY = pl.BlockSpec(memory_space=pl.ANY)
+
+
+def struct(shape, kind=jnp.bfloat16):
+    return jax.ShapeDtypeStruct(shape, kind)
+
+
+def chunks(rows, most=128):
+    return [(a, min(most, rows - a)) for a in range(0, rows, most)]
+
+
+def pack_kernel(place, flat, piece, rolled, rows):
+    shard = place[0]
+    rows[0:PAD, :] = jnp.zeros((PAD, 128), jnp.float32)
+    rows[PAD + LANE_ROWS : PAD + LANE_ROWS + PAD, :] = jnp.zeros((PAD, 128), jnp.float32)
+    rolled[0:8, :] = jnp.zeros((8, 128), jnp.float32)
+
+    @pl.when(shard % 2 == 0)
+    def _():
+        for a, n in chunks(LANE_ROWS):
+            rows[PAD + a : PAD + a + n, :] = flat[a : a + n, :]
+
+    @pl.when(shard % 2 == 1)
+    def _():
+        for a, n in chunks(LANE_ROWS):
+            rolled[8 + a : 8 + a + n, :] = pltpu.roll(flat[a : a + n, :], 64, 1)
+        for a, n in chunks(LANE_ROWS):
+            lane = lax.broadcasted_iota(jnp.int32, (n, 128), 1)
+            rows[PAD + a : PAD + a + n, :] = jnp.where(
+                lane < 64, rolled[7 + a : 7 + a + n, :], rolled[8 + a : 8 + a + n, :]
+            )
+
+    for case in range(8):
+
+        @pl.when(shard == case)
+        def _(case=case):
+            for _, row_a, row_b, offset, step, first in SEGMENTS[case]:
+                count = row_b - row_a
+                base = PAD + first + step * row_a - lane_start(case)
+                for t in range(step):
+                    out = offset + t // 2 * count
+                    lanes = slice(t % 2 * 128, t % 2 * 128 + 128)
+                    for a, n in chunks(count):
+                        piece[out + a : out + a + n, lanes] = low(
+                            rows[pl.ds(base + t + step * a, n, stride=step), :]
+                        )
+
+
+def pack(place, flat):
+    return pl.pallas_call(
+        pack_kernel,
+        out_shape=struct((PIECE, 256)),
+        in_specs=[SMEM, VMEM],
+        out_specs=VMEM,
+        scratch_shapes=[
+            pltpu.VMEM((8 + LANE_ROWS, 128), jnp.float32),
+            pltpu.VMEM((PAD + LANE_ROWS + PAD, 128), jnp.float32),
+        ],
+        compiler_params=pltpu.CompilerParams(vmem_limit_bytes=24 << 20),
+        name="pack",
+    )(place, flat)
+
+
+def unpack_kernel(place, piece, extra, flat, square, rows):
+    shard = place[0]
+    for case in range(8):
+
+        @pl.when(shard == case)
+        def _(case=case):
+            for name, row_a, row_b, offset, step, first in SEGMENTS[case]:
+                count = row_b - row_a
+                base = PAD + first + step * row_a - lane_start(case)
+                for t in range(step):
+                    source = offset + t // 2 * count
+                    lanes = slice(t % 2 * 128, t % 2 * 128 + 128)
+                    for a, n in chunks(count):
+                        if name == "vec":
+                            value = extra[0:16, lanes]
+                        elif name == "o" and case == 1:
+                            value = extra[16:32, lanes]
+                        else:
+                            value = wide(piece[source + a : source + a + n, lanes])
+                        rows[pl.ds(base + t + step * a, n, stride=step), :] = value
+
+    square[...] = jnp.zeros_like(square)
+    for odd in range(2):
+
+        @pl.when(shard % 2 == odd)
+        def _(odd=odd):
+            total = jnp.zeros((8, 128), jnp.float32)
+            for a, n in chunks(LANE_ROWS):
+                value = rows[PAD + a : PAD + a + n, :]
+                lane = lax.broadcasted_iota(jnp.int32, (n, 128), 1)
+                if odd:
+                    after = rows[PAD + a + 1 : PAD + a + 1 + n, :]
+                    value = jnp.where(
+                        lane < 64, pltpu.roll(value, 64, 1), pltpu.roll(after, 64, 1)
+                    )
+                if (a + n) * 128 > SHARD:
+                    row = lax.broadcasted_iota(jnp.int32, (n, 128), 0) + a
+                    value = jnp.where(row * 128 + lane < SHARD, value, 0.0)
+                flat[a : a + n, :] = value
+                total += jnp.sum((value * value).reshape(n // 8, 8, 128), axis=0)
+            square[...] = total
+
+
+def unpack(place, piece, extra):
+    return pl.pallas_call(
+        unpack_kernel,
+        out_shape=(struct((LANE_ROWS, 128), jnp.float32), struct((8, 128), jnp.float32)),
+        in_specs=[SMEM, VMEM, VMEM],
+        out_specs=(VMEM, VMEM),
+        scratch_shapes=[pltpu.VMEM((PAD + LANE_ROWS + PAD, 128), jnp.float32)],
+        compiler_params=pltpu.CompilerParams(vmem_limit_bytes=24 << 20),
+        name="unpack",
+    )(place, piece, extra)
+
+
+def column_sum(values):
+    return jnp.sum(values, axis=0, keepdims=True)
+
+
+def inside_column(place, relative):
+    rows = lax.broadcasted_iota(jnp.int32, (256, 1), 0)
+    position = rows + (place[3] ^ relative) * 256
+    return ((position >= place[4]) & (position < place[4] + place[5])).astype(jnp.float32)
+
+
+def attend_kernel(
+    place, t0, t1, t2, t3, embed, bias, s_own, s_other, b_own, b_other,
+    stream_out, weight_out, q_out, k_out, v_out, h0, h1, h2, h3, lse_out,
+    q_heads, k_heads, v_heads, o_heads, edge, sem,
+):
+    def copies(first, second):
+        return [
+            pltpu.make_async_copy(first.at[0:1024, :], weight_out.at[0], sem.at[0]),
+            pltpu.make_async_copy(first.at[1024:1552, :], weight_out.at[1, 0:528, :], sem.at[1]),
+            pltpu.make_async_copy(second.at[16:512, :], weight_out.at[1, 528:1024, :], sem.at[2]),
+            pltpu.make_async_copy(second.at[0:16, :], edge, sem.at[3]),
+            pltpu.make_async_copy(second.at[512:1536, :], weight_out.at[2], sem.at[4]),
+        ]
+
+    for bottom in range(2):
+        for y in range(2):
+            own, other = (s_own, s_other) if bottom else (b_own, b_other)
+            pair = (other, own) if y else (own, other)
+
+            @pl.when(((place[1] == 0) == bool(bottom)) & (place[2] == y))
+            def _(pair=pair):
+                for copy in copies(*pair):
+                    copy.start()
+
+    for r, tokens in enumerate((t0, t1, t2, t3)):
+        stream_out[r] = low(wide(tokens[...]) + inside_column(place, r) * embed[...])
+    lanes = lax.broadcasted_iota(jnp.int32, (1024, 128), 1)
+    v_heads[...] = jnp.broadcast_to((lanes >= 64).astype(jnp.bfloat16), (4, 1024, 128))
+    for copy in copies(s_own, s_other):
+        copy.wait()
+    weight_out[1, 512:528, :] = weight_out[1, 512:528, :] + edge[...]
+    for r in range(4):
+        rows = slice(r * 256, r * 256 + 256)
+        stream = stream_out[r]
+        query = low(dot(stream, weight_out[0]) + bias[0:1, :])
+        key = low(dot(stream, weight_out[1]))
+        value = low(dot(stream, weight_out[2]) + bias[1:2, :])
+        q_out[rows, :] = query
+        k_out[rows, :] = key
+        v_out[rows, :] = value
+        for h in range(4):
+            cols = slice(h * 64, h * 64 + 64)
+            q_heads[h, rows, :] = query[:, cols] * 0.125
+            k_heads[h, rows, :] = key[:, cols]
+            v_heads[h, rows, 0:64] = value[:, cols]
+    lse_out[...] = jnp.zeros_like(lse_out)
+
+    def step(n, _):
+        h, r = n // 4, n % 4
+        rows = pl.ds(pl.multiple_of(r * 256, 256), 256)
+        scores = dot_last(q_heads[h, rows, :], k_heads[h])
+        highest = jnp.max(scores, axis=1, keepdims=True)
+        weights = low(jnp.exp(scores - highest))
+        result = dot(weights, v_heads[h])
+        total = result[:, 64:65]
+        o_heads[h, rows, :] = low(result[:, 0:64] / total)
+        lane = lax.broadcasted_iota(jnp.int32, (256, 128), 1)
+        lse_out[rows, :] = jnp.where(lane == h, highest + jnp.log(total), lse_out[rows, :])
+        return 0
+
+    lax.fori_loop(0, 16, step, 0)
+    for r, out in enumerate((h0, h1, h2, h3)):
+        for h in range(4):
+            out[:, h * 64 : h * 64 + 64] = o_heads[h, r * 256 : r * 256 + 256, :]
+
+
+def attend(place, tokens, embed, bias, pieces):
+    square = struct((1024, 256))
+    block = struct((256, 256))
+    return pl.pallas_call(
+        attend_kernel,
+        out_shape=(
+            struct((4, 256, 1024)), struct((3, 1024, 256)), square, square, square,
+            block, block, block, block, struct((1024, 128), jnp.float32),
+        ),
+        in_specs=[SMEM] + [VMEM] * 6 + [ANY] * 4,
+        out_specs=(VMEM,) * 10,
+        scratch_shapes=[
+            pltpu.VMEM((4, 1024, 64), jnp.bfloat16),
+            pltpu.VMEM((4, 1024, 64), jnp.bfloat16),
+            pltpu.VMEM((4, 1024, 128), jnp.bfloat16),
+            pltpu.VMEM((4, 1024, 64), jnp.bfloat16),
+            pltpu.VMEM((16, 256), jnp.bfloat16),
+            pltpu.SemaphoreType.DMA((5,)),
+        ],
+        compiler_params=pltpu.CompilerParams(vmem_limit_bytes=40 << 20),
+        name="attend",
+    )(place, *tokens, embed, bias, *pieces)
+
+
+def attend_back_kernel(
+    place, q_in, k_in, v_in, lse, weight, g0, g1, g2, g3,
+    q_grad, k_grad, v_grad, kept, sent, sums,
+    q_heads, k_heads, v_heads, g_heads, dq_heads, dk_heads, dv_heads,
+):
+    for r, grad in enumerate((g0, g1, g2, g3)):
+        rows = slice(r * 256, r * 256 + 256)
+        for h in range(4):
+            cols = slice(h * 64, h * 64 + 64)
+            q_heads[h, rows, :] = q_in[rows, cols] * 0.125
+            k_heads[h, rows, :] = k_in[rows, cols]
+            v_heads[h, rows, :] = v_in[rows, cols]
+            g_heads[h, rows, :] = grad[:, cols]
+
+    def step(n, _):
+        h, r = n // 4, n % 4
+        rows = pl.ds(pl.multiple_of(r * 256, 256), 256)
+        query, grad = q_heads[h, rows, :], g_heads[h, rows, :]
+        scores = dot_last(query, k_heads[h])
+        lane = lax.broadcasted_iota(jnp.int32, (256, 128), 1)
+        logsum = jnp.sum(jnp.where(lane == h, lse[rows, :], 0.0), axis=1, keepdims=True)
+        probs = jnp.exp(scores - logsum)
+        weighted = probs * dot_last(grad, v_heads[h])
+        inner = jnp.sum(weighted, axis=1, keepdims=True)
+        score_grad = low(weighted - probs * inner)
+        dq_heads[h, rows, :] = low(dot(score_grad, k_heads[h]) * 0.125)
+        dk_heads[h] += dot_first(query, score_grad)
+        dv_heads[h] += dot_first(grad, low(probs))
+        return 0
+
+    dk_heads[...] = jnp.zeros_like(dk_heads)
+    dv_heads[...] = jnp.zeros_like(dv_heads)
+    lax.fori_loop(0, 16, step, 0)
+    for h in range(4):
+        cols = slice(h * 64, h * 64 + 64)
+        q_grad[:, cols] = dq_heads[h]
+        k_grad[:, cols] = low(dk_heads[h].T)
+        v_grad[:, cols] = low(dv_heads[h].T)
+    sums[...] = jnp.zeros_like(sums)
+    sums[1:2, 0:256] = column_sum(wide(q_grad[...]))
+    sums[2:3, 0:256] = column_sum(wide(v_grad[...]))
+    for r in range(4):
+        rows = slice(r * 256, r * 256 + 256)
+        part = (
+            dot_last(q_grad[rows, :], weight[0])
+            + dot_last(k_grad[rows, :], weight[1])
+            + dot_last(v_grad[rows, :], weight[2])
+        )
+        sums[0:1, :] += column_sum(inside_column(place, r) * part)
+        if r % 2:
+            sent[r // 2] = low(part)
+        else:
+            kept[r // 2] = part
+
+
+def attend_back(place, query, key, value, lse, weight, grads):
+    square = struct((1024, 256))
+    return pl.pallas_call(
+        attend_back_kernel,
+        out_shape=(
+            square, square, square, struct((2, 256, D), jnp.float32), struct((2, 256, D)),
+            struct((8, D), jnp.float32),
+        ),
+        in_specs=[SMEM] + [VMEM] * 9,
+        out_specs=(VMEM,) * 6,
+        scratch_shapes=[pltpu.VMEM((4, 1024, 64), jnp.bfloat16)] * 5
+        + [pltpu.VMEM((4, 64, 1024), jnp.float32)] * 2,
+        compiler_params=pltpu.CompilerParams(vmem_limit_bytes=40 << 20),
+        name="attend_back",
+    )(place, query, key, value, lse, weight, *grads)
+
+
+def row_mean(values):
+    return jnp.sum(values, axis=1, keepdims=True) * (1.0 / D)
+
+
+def normalise(resid):
+    centred = resid - row_mean(resid)
+    scale = lax.rsqrt(row_mean(centred * centred) + NORM_EPS)
+    return centred * scale, scale
+
+
+def normalise_back(grad, gain, xhat, scale):
+    scaled = grad * gain
+    return (scaled - row_mean(scaled) - xhat * row_mean(scaled * xhat)) * scale
+
+
+def layer_kernel(
+    place, h0, h1, h2, h3, tokens, cotangent, embed, vectors, bias_up, out_head, *refs
+):
+    pieces = refs[:32]
+    (block_out, resid_grad, g0, g1, g2, g3, sums, sums_up, head_grad) = refs[32:41]
+    grads_own, grads_other = refs[41:44], refs[44:47]
+    (w_out, w_up, w_down, edge_up, edge_down, hidden, slope, grad_up, grad_down,
+     grad_out, acc, sem, sem_out) = refs[47:]
+
+    def fetch(z, y):
+        made = {"out": [], "up": [], "down": []}
+        for k in range(1, 4):
+            for ry in range(2):
+                case = 2 * k + (y ^ ry)
+                for r in range(4):
+                    rx, rc = r // 2, r % 2
+                    source = pieces[rc * 16 + rx * 8 + ry * 4 + SLOT[z][k]]
+                    column = place[3] ^ r
+                    for name, row_a, row_b, offset, step, _ in SEGMENTS[case]:
+                        count = row_b - row_a
+                        if name == "o":
+                            made["out"].append((source.at[offset : offset + count, :], w_out.at[column]))
+                        elif name == "up":
+                            block = source.at[offset : offset + 4 * count, :].reshape(4, count, 256)
+                            target = w_up.at[pl.ds(column * 4, 4)]
+                            skip = 0
+                            if row_a:
+                                skip = 16
+                                made["up"].append(
+                                    (block.at[:, 0:16, :], edge_up.at[case - 3, pl.ds(column * 4, 4)])
+                                )
+                            made["up"].append(
+                                (block.at[:, skip:count, :], target.at[:, row_a + skip : row_b, :])
+                            )
+                        elif name == "down":
+                            skip = 0
+                            if row_a:
+                                skip = 16
+                                made["down"].append(
+                                    (source.at[offset : offset + 16, :], edge_down.at[case - 6, column])
+                                )
+                            made["down"].append(
+                                (source.at[offset + skip : offset + count, :],
+                                 w_down.at[column, row_a + skip : row_b, :])
+                            )
+        return made
+
+    order = ("out", "up", "down")
+    for z in range(4):
+        for y in range(2):
+
+            @pl.when((place[1] == z) & (place[2] == y))
+            def _(z=z, y=y):
+                made = fetch(z, y)
+                for n, name in enumerate(order):
+                    for source, target in made[name]:
+                        pltpu.make_async_copy(source, target, sem.at[n]).start()
+
+    def arrived(refs, n):
+        for ref in refs:
+            pltpu.make_async_copy(ref, ref, sem.at[n]).wait()
+
+    here = inside_column(place, 0)
+    stream = wide(tokens[...]) + here * embed[...]
+    arrived([w_out], 0)
+    w_out[:, 0:16, :] = w_out[:, 0:16, :] + out_head[...]
+    heads = (h0, h1, h2, h3)
+    for n in range(4):
+        total = jnp.zeros((256, 256), jnp.float32)
+        for r in range(4):
+            rows = pl.ds(pl.multiple_of((place[3] ^ r) * 256, 256), 256)
+            total += dot(heads[r][...], w_out[n, rows, :])
+        acc[:, n * 256 : n * 256 + 256] = total
+    bias_out, bias_down, gain_a, shift_a, gain_f, shift_f = (vectors[n : n + 1, :] for n in range(6))
+    xhat_a, scale_a = normalise(stream + acc[...] + bias_out)
+    normed = xhat_a * gain_a + shift_a
+    normed_low = low(normed)
+
+    arrived([w_up] + [edge_up], 1)
+    for n, row in enumerate((128, 512, 896)):
+        w_up[:, row : row + 16, :] = w_up[:, row : row + 16, :] + edge_up[n]
+
+    def up(g, _):
+        pre = dot(normed_low, w_up[g]) + bias_up[pl.ds(g, 1), :]
+        inner = 0.5 * (1.0 + lax.erf(pre * (1.0 / math.sqrt(2.0))))
+        hidden[g] = low(pre * inner)
+        slope[g] = inner + pre * (jnp.exp(-0.5 * pre * pre) * (1.0 / math.sqrt(2.0 * math.pi)))
+        return 0
+
+    lax.fori_loop(0, 16, up, 0)
+    arrived([w_down] + [edge_down], 2)
+    for n, row in enumerate((1024, 2560)):
+        w_down[:, row : row + 16, :] = w_down[:, row : row + 16, :] + edge_down[n]
+    acc[...] = normed + bias_down
+
+    def down(g, _):
+        rows = pl.ds(pl.multiple_of(g * 256, 256), 256)
+        for n in range(4):
+            cols = slice(n * 256, n * 256 + 256)
+            acc[:, cols] += dot(hidden[g], w_down[n, rows, :])
+        return 0
+
+    lax.fori_loop(0, 16, down, 0)
+    xhat_f, scale_f = normalise(acc[...])
+    block_out[...] = low(xhat_f * gain_f + shift_f)
+
+    out_grad = wide(cotangent[...])
+    sums[4:5, :] = column_sum(out_grad * xhat_f)
+    sums[5:6, :] = column_sum(out_grad)
+    acc[...] = normalise_back(out_grad, gain_f, xhat_f, scale_f)
+    ffn_grad = low(acc[...])
+    sums[1:2, :] = column_sum(wide(ffn_grad))
+    normed_t = normed_low.T
+
+    def back_step(g, _):
+        rows = pl.ds(pl.multiple_of(g * 256, 256), 256)
+        total = jnp.zeros((256, 256), jnp.float32)
+        for n in range(4):
+            total += dot_last(ffn_grad[:, n * 256 : n * 256 + 256], w_down[n, rows, :])
+        pre_grad = low(total * slope[g])
+        sums_up[pl.ds(g, 1), :] = column_sum(wide(pre_grad))
+        acc[...] += dot_last(pre_grad, w_up[g])
+        grad_up[g] = low(dot(normed_t, pre_grad))
+        part = low(dot_first(hidden[g], ffn_grad))
+        for n in range(4):
+            grad_down[n, rows, :] = part[:, n * 256 : n * 256 + 256]
+        return 0
+
+    lax.fori_loop(0, 16, back_step, 0)
+
+    def send(case, name, source, column):
+        made = []
+        for seg, row_a, row_b, offset, _, _ in SEGMENTS[case]:
+            count = row_b - row_a
+            if seg == name:
+                made.append((row_a, row_b, offset, count))
+        return made
+
+    started = []
+    for r in range(4):
+        rx, rc = r // 2, r % 2
+        column = place[3] ^ r
+        targets = grads_other if rc else grads_own
+        for case in range(2, 8):
+            ry = place[2] ^ (case % 2)
+            piece = targets[case // 2 - 1].at[ry, rx]
+            for row_a, row_b, offset, count in send(case, "up", grad_up, column):
+                started.append(
+                    (grad_up.at[pl.ds(column * 4, 4), row_a:row_b, :],
+                     piece.at[offset : offset + 4 * count, :].reshape(4, count, 256))
+                )
+            for row_a, row_b, offset, count in send(case, "down", grad_down, column):
+                started.append(
+                    (grad_down.at[column, row_a:row_b, :], piece.at[offset : offset + count, :])
+                )
+    for source, target in started:
+        pltpu.make_async_copy(source, target, sem_out.at[0]).start()
+
+    normed_grad = acc[...]
+    sums[2:3, :] = column_sum(normed_grad * xhat_a)
+    sums[3:4, :] = column_sum(normed_grad)
+    attn_wide = normalise_back(normed_grad, gain_a, xhat_a, scale_a)
+    resid_grad[...] = attn_wide
+    sums[6:7, :] = column_sum(here * attn_wide)
+    attn_grad = low(attn_wide)
+    sums[0:1, :] = column_sum(wide(attn_grad))
+    sums[7:8, :] = jnp.zeros((1, D), jnp.float32)
+    for r, out in enumerate((g0, g1, g2, g3)):
+        rows = pl.ds(pl.multiple_of((place[3] ^ r) * 256, 256), 256)
+        total = jnp.zeros((256, 256), jnp.float32)
+        for n in range(4):
+            total += dot_last(attn_grad[:, n * 256 : n * 256 + 256], w_out[n, rows, :])
+        out[...] = low(total)
+        part = dot_first(heads[r][...], attn_grad)
+        for n in range(4):
+            grad_out[n, rows, :] = low(part[:, n * 256 : n * 256 + 256])
+    head_grad[...] = wide(grad_out[:, 0:16, :])
+    last = []
+    for r in range(4):
+        rx, rc = r // 2, r % 2
+        column = place[3] ^ r
+        targets = grads_other if rc else grads_own
+        piece = targets[0].at[place[2], rx]
+        last.append((grad_out.at[column], piece.at[0:1024, :]))
+    for source, target in last:
+        pltpu.make_async_copy(source, target, sem_out.at[1]).start()
+    for source, target in started:
+        pltpu.make_async_copy(source, target, sem_out.at[0]).wait()
+    for source, target in last:
+        pltpu.make_async_copy(source, target, sem_out.at[1]).wait()
+
+
+def layer(place, heads, tokens, cotangent, embed, vectors, bias_up, out_head, pieces):
+    grads = struct((2, 2, PIECE, 256))
+    block = struct((256, 256))
+    return pl.pallas_call(
+        layer_kernel,
+        out_shape=(
+            struct((256, D)), struct((256, D), jnp.float32), block, block, block, block,
+            struct((8, D), jnp.float32), struct((16, 256), jnp.float32),
+            struct((4, 16, 256), jnp.float32),
+        ) + (grads,) * 6,
+        in_specs=[SMEM] + [VMEM] * 10 + [ANY] * 32,
+        out_specs=(VMEM,) * 9 + (ANY,) * 6,
+        scratch_shapes=[
+            pltpu.VMEM((4, 1024, 256), jnp.bfloat16),
+            pltpu.VMEM((16, 1024, 256), jnp.bfloat16),
+            pltpu.VMEM((4, 4096, 256), jnp.bfloat16),
+            pltpu.VMEM((3, 16, 16, 256), jnp.bfloat16),
+            pltpu.VMEM((2, 4, 16, 256), jnp.bfloat16),
+            pltpu.VMEM((16, 256, 256), jnp.bfloat16),
+            pltpu.VMEM((16, 256, 256), jnp.float32),
+            pltpu.VMEM((16, 1024, 256), jnp.bfloat16),
+            pltpu.VMEM((4, 4096, 256), jnp.bfloat16),
+            pltpu.VMEM((4, 1024, 256), jnp.bfloat16),
+            pltpu.VMEM((256, D), jnp.float32),
+            pltpu.SemaphoreType.DMA((3,)),
+            pltpu.SemaphoreType.DMA((2,)),
+        ],
+        compiler_params=pltpu.CompilerParams(vmem_limit_bytes=60 << 20),
+        name="layer",
+    )(place, *heads, tokens, cotangent, embed, vectors, bias_up, out_head, *pieces)
 
 
 def product(left, right):
@@ -34,7 +627,7 @@
     return centred * lax.rsqrt(variance + NORM_EPS) * gain + shift
 
 
-def unpack(flat_params, dp_count, fsdp_count):
+def unpack_all(flat_params, dp_count, fsdp_count):
     shapes = [(D, D)] * 4 + [(D, FF), (FF, D)] + [(1, D)] * 4 + [(1, FF)] + [(1, D)] * 6
     blocks = (
         flat_params.reshape(dp_count, fsdp_count, -1).transpose(1, 0, 2).reshape(fsdp_count, -1)
@@ -126,7 +719,7 @@
         shift_ffn,
         w_time,
         b_time,
-    ) = unpack(flat_params, dp_count, fsdp_count)
+    ) = unpack_all(flat_params, dp_count, fsdp_count)
     gain_a = gain_attn.astype(jnp.float32)
     shift_a = shift_attn.astype(jnp.float32)
     gain_f = gain_ffn.astype(jnp.float32)
@@ -167,7 +760,7 @@
         lax.all_gather(hidden, "fsdp", axis=0, tiled=True),
     )
     back_params = lax.all_gather(master_low, ("dp", "fsdp"), axis=0, tiled=True)
-    back_pieces = unpack(back_params, dp_count, fsdp_count)
+    back_pieces = unpack_all(back_params, dp_count, fsdp_count)
     w_query_back, w_key_back, w_value_back, w_out_back, w_up_back, w_down_back = back_pieces[:6]
     out_grad = cotangent.astype(jnp.float32)
     _, pull_ffn = jax.vjp(layer_norm, resid_ffn, gain_f, shift_f)
@@ -278,9 +871,223 @@
     )
 
 
+AXES = ("dp", "fsdp")
+
+
+def send(values, route):
+    pairs = []
+    for n in range(32):
+        there = route(n // 8, n // 4 % 2, n // 2 % 2, n % 2)
+        if there is not None:
+            z, y, x, c = there
+            pairs.append((n, z * 8 + y * 4 + x * 2 + c))
+    return lax.ppermute(values, AXES, pairs)
+
+
+def to_core(z, y, x, c):
+    return z, y, x, 1 - c
+
+
+def to_x(z, y, x, c):
+    return z, y, 1 - x, c
+
+
+def to_y(z, y, x, c):
+    return z, 1 - y, x, c
+
+
+def to_near(z, y, x, c):
+    return z ^ 1, y, x, c
+
+
+def to_far(z, y, x, c):
+    return z ^ 2, y, x, c
+
+
+def only(route, planes):
+    return lambda z, y, x, c: route(z, y, x, c) if z in planes else None
+
+
+EVERY = (to_core, to_x, to_y, to_near, to_far)
+
+
+def total(values):
+    for route in EVERY:
+        values = values + send(values, route)
+    return values
+
+
+def gather_pieces(own, z):
+    outer = (z == 0) | (z == 3)
+    got_1 = send(own, only(to_far, (0, 3)))
+    pass_1 = jnp.where(outer, own, got_1)
+    got_2 = send(pass_1, to_near)
+    got_3 = send(own, only(to_far, (1, 2)))
+    pass_2 = jnp.where(outer, got_3, own)
+    got_4 = send(pass_2, to_near)
+    slot_b = jnp.where(z == 2, got_1, got_2)
+    slot_v = jnp.where(z == 1, got_1, jnp.where(z == 2, got_2, got_3))
+    slots = [own, slot_b, slot_v, got_4]
+    planes = [(1, 2, 3), (0,), (0, 1, 2, 3), (0, 1, 2, 3)]
+    own_y = [send(piece, to_y) for piece in slots]
+    over_x = [send(piece, only(to_x, p)) for piece, p in zip(slots, planes)]
+    over_xy = [
+        send(over_x[n], only(to_y, planes[n])) if n == 2 else send(own_y[n], only(to_x, planes[n]))
+        for n in range(4)
+    ]
+    mine = slots + own_y + over_x + over_xy
+    core = [send(piece, only(to_core, planes[n % 4])) for n, piece in enumerate(mine)]
+    return slots, own_y, mine + core
+
+
+def add(left, right):
+    return wide(left) + wide(right)
+
+
+def block_body(
+    tokens,
+    cotangent,
+    master,
+    first_moment,
+    second_moment,
+    average,
+    timestep,
+    block_length,
+    block_start,
+):
+    shard = lax.axis_index("dp")
+    j = lax.axis_index("fsdp")
+    z, y = shard // 2, shard % 2
+    place = jnp.stack([shard, z, y, j, block_start[0], block_length[0]]).astype(jnp.int32)
+    flat = jnp.pad(master, (0, LANE_ROWS * 128 - SHARD)).reshape(LANE_ROWS, 128)
+    own = pack(place, flat)
+    tokens_c = send(tokens, to_core)
+    tokens_x = send(tokens, to_x)
+    tokens_xc = send(tokens_x, to_core)
+
+    tail = own[TAIL : TAIL + 16]
+    zero = jnp.zeros_like(tail)
+    shared = jnp.concatenate([jnp.where(shard == 7, tail, zero), jnp.where(shard == 1, tail, zero)])
+    here = (jnp.arange(4) == j)[:, None, None]
+    shared = total(jnp.where(here, shared[None], jnp.zeros_like(shared)[None]))
+    vec = wide(shared[:, :16])
+    out_head = shared[:, 16:]
+    vec_own = lax.dynamic_index_in_dim(vec, j, 0, keepdims=False)
+    time_frac = timestep[0].astype(jnp.float32) / 5000.0
+    full = vec.transpose(1, 0, 2).reshape(16, D)
+    embed = time_frac * full[12:13] + full[13:14]
+    vectors = jnp.concatenate([full[2:4], full[8:12], jnp.zeros((2, D), jnp.float32)])
+    bias_up = vec[:, 4:8].reshape(16, 256)
+
+    slots, slots_y, pieces = gather_pieces(own, z)
+
+    (stream, weight, query, key, value, h0, h1, h2, h3, lse) = attend(
+        place,
+        (tokens, tokens_c, tokens_x, tokens_xc),
+        embed,
+        vec_own[0:8],
+        (slots[0], slots_y[0], slots[1], slots_y[1]),
+    )
+
+    def to_relative(r):
+        return lambda z, y, x, c: (z, y, x ^ (r // 2), c ^ (r % 2))
+
+    def exchange(blocks):
+        return [blocks[0]] + [send(blocks[r], to_relative(r)) for r in range(1, 4)]
+
+    (block_out, resid_grad, g0, g1, g2, g3, sums, sums_up, head_grad, *grads) = layer(
+        place, exchange((h0, h1, h2, h3)), tokens, cotangent, embed, vectors, bias_up, out_head, pieces
+    )
+    grads_own, grads_other = grads[:3], grads[3:]
+
+    (q_grad, k_grad, v_grad, kept, sent, sums_qkv) = attend_back(
+        place, query, key, value, lse, weight, exchange((g0, g1, g2, g3))
+    )
+
+    part = {}
+    for k in (3, 2, 1):
+        both = low(add(grads_own[k - 1], send(grads_other[k - 1], to_core)))
+        if k == 1:
+            both = low(add(both[0], send(both[1], to_y)))
+            part[k] = low(add(both[0], send(both[1], to_x)))
+        else:
+            both = low(add(both[:, 0], send(both[:, 1], to_x)))
+            part[k] = low(add(both[0], send(both[1], to_y)))
+    even = z % 2 == 0
+    outer = (z == 0) | (z == 3)
+    inner_part = add(
+        jnp.where(even, part[2], part[1]), send(jnp.where(even, part[1], part[2]), to_near)
+    )
+    inner_sum = add(inner_part, send(low(inner_part), only(to_far, (0, 3))))
+
+    rows = stream.reshape(1024, D)
+    w_grads = [low(product_inner(rows, grad)) for grad in (q_grad, k_grad, v_grad)]
+    rest = jnp.zeros((PIECE - 1552, 256), jnp.bfloat16)
+    piece_0 = jnp.concatenate([w_grads[0], w_grads[1][:528], rest])
+    piece_1 = jnp.concatenate([w_grads[1][512:], w_grads[2], rest, rest[:16]])
+    low_row = y == 0
+    part[0] = low(
+        add(
+            jnp.where(low_row, piece_0, piece_1),
+            send(jnp.where(low_row, piece_1, piece_0), to_y),
+        )
+    )
+    outer_part = add(
+        jnp.where(even, part[0], part[3]), send(jnp.where(even, part[3], part[0]), to_near)
+    )
+    outer_sum = add(outer_part, send(low(outer_part), only(to_far, (1, 2))))
+
+    from_core = send(sent, to_core)
+    input_grad = (
+        resid_grad
+        + kept[0]
+        + wide(from_core[0])
+        + wide(send(low(kept[1] + wide(from_core[1])), to_x))
+    )
+
+    time_grad = sums[6] + sums_qkv[0]
+    vec_grad = jnp.concatenate(
+        [
+            jnp.where(here, sums_qkv[1:3, :256][None], 0.0),
+            sums[0:2].reshape(2, 4, 256).transpose(1, 0, 2),
+            sums_up.reshape(4, 4, 256),
+            sums[2:6].reshape(4, 4, 256).transpose(1, 0, 2),
+            (time_frac * time_grad).reshape(4, 1, 256),
+            time_grad.reshape(4, 1, 256),
+            jnp.zeros((4, 2, 256), jnp.float32),
+            head_grad,
+        ],
+        axis=1,
+    )
+    extra = lax.dynamic_index_in_dim(total(vec_grad), j, 0, keepdims=False)
+    vector_grad = extra[:14].reshape(-1)
+
+    grad_flat, square = unpack(place, jnp.where(outer, outer_sum, inner_sum), extra)
+    grad_shard = grad_flat.reshape(-1)[:SHARD]
+    grad_norm = jnp.sqrt(jnp.sum(total(square)))
+    clip_limit = 4.0 * math.sqrt(PARAMS)
+    clipped = grad_shard * (clip_limit / jnp.maximum(grad_norm, clip_limit))
+    new_first = 0.9 * first_moment + 0.1 * clipped
+    new_second = 0.98 * second_moment + 0.02 * clipped * clipped
+    first_hat = new_first / (1.0 - 0.9**STEP)
+    second_hat = new_second / (1.0 - 0.98**STEP)
+    new_master = master - 0.02 * (first_hat / (jnp.sqrt(second_hat) + 1e-06) + 0.01 * master)
+    new_average = 0.99 * average + 0.01 * new_master
+    return (
+        block_out,
+        input_grad,
+        grad_norm,
+        vector_grad,
+        new_first,
+        new_second,
+        new_master,
+        new_average,
+    )
+
+
 def solution(mesh):
     return jax.shard_map(
-        body,
+        block_body if mesh.shape["dp"] == 8 and mesh.shape["fsdp"] == 4 else body,
         mesh=mesh,
         in_specs=(
             P(("dp", "fsdp"), None),

time: 1610 us -> 494 us (0.31)
  waiting for transfers between devices: 843 us -> 233 us
  local copies, waits for them, and re-layouts: 319 us -> 28 us
  matrix products: 272 us -> 2.28 us
  blocking collectives: 87.9 us -> 0 us
  Pallas kernels: 0 us -> 80.6 us
  starting transfers between devices: 23.8 us -> 96.1 us
    unnamed x13 -> x0, waiting for transfers between devices: 790 us -> none
    dot_general x140 -> x0, matrix products: 250 us -> none  [product(): return jnp.dot(left, right, preferred_element_type=jnp.float32)]
    ppermute x0 -> x72, waiting for transfers between devices: none -> 233 us  [send(): return lax.ppermute(values, AXES, pairs)]
    unnamed x101 -> x146, local copies, waits for them, and re-layouts: 122 us -> 14.6 us
    ppermute x0 -> x72, starting transfers between devices: none -> 96.1 us  [send(): return lax.ppermute(values, AXES, pairs)]
    pallas_call x0 -> x5, Pallas kernels: none -> 80.6 us  [the longest x1 43.6 us: layer(): pl.pallas_call(layer_kernel, out_shape=(struct((256, D)), struct((256, D)...]
    reshape x3 -> x4, local copies, waits for them, and re-layouts: 78.3 us -> 3.35 us  [the longest x1 1.51 us: block_body(): flat = jnp.pad(master, (0, LANE_ROWS * 128 - SHARD)).reshape(LANE_ROWS, 128)]
    psum x2 -> x0, blocking collectives: 72.5 us -> none  [the longest x1 37.3 us: body(): square_sum = lax.psum(jnp.sum(grad_shard * grad_shard), ('dp', 'fsdp'))]
  transfers between devices with their start and end apart: 17 -> 72, of which waited for: 8 -> 36; matrix products, arithmetic and copies ran while one was open for 25% -> 8% of each run, Pallas kernels for 0% -> 7%
where the time goes in v1:
time: 494 us; the launch traced here: 484 us
  waiting for transfers between devices  233 us (47%)
  starting transfers between devices  96.1 us (19%)
  Pallas kernels  80.6 us (16%)
  other arithmetic  38.3 us (8%)
  local copies, waits for them, and re-layouts  28 us (6%)
  between operations  5.96 us (1%)
    ppermute x72, waiting for transfers between devices, send(): return lax.ppermute(values, AXES, pairs)  233 us
    ppermute x72, starting transfers between devices, send(): return lax.ppermute(values, AXES, pairs)  96.1 us
    pallas_call x1, Pallas kernels, layer(): pl.pallas_call(layer_kernel, out_shape=(struct((256, D)), struct((256, D)...  43.6 us
    pallas_call x1, Pallas kernels, attend_back(): pl.pallas_call(attend_back_kernel, out_shape=(square, square, square, str...  20.4 us
    pallas_call x1, Pallas kernels, attend(): pl.pallas_call(attend_kernel, out_shape=(struct((4, 256, 1024)), struct((...  15 us
    unnamed x146, local copies, waits for them, and re-layouts  14.6 us
    convert_element_type x9, other arithmetic, low(): return values.astype(jnp.bfloat16)  13.5 us
  transfers between devices with their start and end apart: 72, of which 36 were waited for; matrix products, arithmetic and copies ran while one was open for 8% of the time, Pallas kernels for 7%

profile of v1, /device:TPU:0, one launch (start us, length us, event | category | flops | bytes accessed | tf_op | source)
XLA Modules:
  0.0 484.4 jit_solution(9808549965298230125)
XLA Ops:
  5.7 7.1 %collective-permute-start.9 = (bf16[1600,256]{1,0:T(8,128)(2,1)S(1)}, bf16[1600,256]{1,0:T(8,128)(2,1)}, u32[]{:S(2)}, u32[]{:S(2)}) collective-permute-start(bf16[1600,256]{1,0:T(8,128)(2,1)S(1)} %pack.1.s_own.refs_0_), channel_id=1, source_target_pairs={{0,16},{1,17},{2,18},{3,19},{4,20},{5,21},{6,22},{7,23},{24,8},{25... | collective-permute-start | bytes 2457608 | tf_op jit(solution)/shard_map/ppermute | solution.py:884
  14.3 2.3 collective-permute-start.4
  16.6 2.4 collective-permute-done.4
  19.1 2.5 collective-permute-start.5
  21.5 2.2 collective-permute-done.5
  23.9 2.1 collective-permute-start.8
  27.6 3.3 collective-permute-done.6
  32.5 13.3 %collective-permute-done.15 = bf16[1600,256]{1,0:T(8,128)(2,1)S(1)} collective-permute-done((bf16[1600,256]{1,0:T(8,128)(2,1)S(1)}, bf16[1600,256]{1,0:T(8,128)(2,1)S(1)}, u32[]{:S(2)}, u32[]{:S(2)}) %collective-permute-start.15) | collective-permute-done | bytes 819232 | tf_op jit(solution)/shard_map/ppermute | solution.py:884
  45.8 1.9 collective-permute-start.1
  49.0 3.9 collective-permute-done.7
  54.4 4.5 collective-permute-done.1.t2
  58.9 1.9 collective-permute-done.t1
  64.9 9.5 %collective-permute-done.10 = bf16[1600,256]{1,0:T(8,128)(2,1)} collective-permute-done((bf16[1600,256]{1,0:T(8,128)(2,1)}, bf16[1600,256]{1,0:T(8,128)(2,1)}, u32[]{:S(2)}, u32[]{:S(2)}) %collective-permute-start.10) | collective-permute-done | bytes 819232 | tf_op jit(solution)/shard_map/ppermute | solution.py:884
  75.1 1.8 select_select_fusion
  77.8 2.0 collective-permute-start.11
  79.8 9.3 %collective-permute-done.16.refs_3_ = bf16[1600,256]{1,0:T(8,128)(2,1)} collective-permute-done((bf16[1600,256]{1,0:T(8,128)(2,1)}, bf16[1600,256]{1,0:T(8,128)(2,1)}, u32[]{:S(2)}, u32[]{:S(2)}) %collective-permute-start.16) | collective-permute-done | bytes 819232 | tf_op jit(solution)/shard_map/ppermute | solution.py:884
  89.6 2.0 collective-permute-start.17
  91.7 3.4 collective-permute-start.20
  95.5 1.9 collective-permute-start.28
  97.5 12.9 %collective-permute-done.21.refs_10_ = bf16[1600,256]{1,0:T(8,128)(2,1)} collective-permute-done((bf16[1600,256]{1,0:T(8,128)(2,1)S(1)}, bf16[1600,256]{1,0:T(8,128)(2,1)}, u32[]{:S(2)}, u32[]{:S(2)}) %collective-permute-start.21) | collective-permute-done | bytes 819232 | tf_op jit(solution)/shard_map/ppermute | solution.py:884
  110.4 2.7 collective-permute-done.17.refs_6_
  113.1 14.7 %collective-permute-done.20.refs_9_ = bf16[1600,256]{1,0:T(8,128)(2,1)S(1)} collective-permute-done((bf16[1600,256]{1,0:T(8,128)(2,1)S(1)}, bf16[1600,256]{1,0:T(8,128)(2,1)S(1)}, u32[]{:S(2)}, u32[]{:S(2)}) %collective-permute-start.20) | collective-permute-done | bytes 819232 | tf_op jit(solution)/shard_map/ppermute | solution.py:884
  129.4 2.6 collective-permute-start.24
  132.9 1.9 collective-permute-start.25
  141.2 15.0 %attend.1 = (bf16[4,256,1024]{2,1,0:T(8,128)(2,1)S(1)}, bf16[3,1024,256]{2,1,0:T(8,128)(2,1)S(1)}, bf16[1024,256]{1,0:T(8,128)(2,1)S(1)}, bf16[1024,256]{1,0:T(8...) custom-call(s32[6]{0:T(128)S(1)} %stack.19.place, ...), custom_call_target="tpu_custom_call" | custom-call | tf_op jit(solution)/shard_map/attend/pallas_call | solution.py:281
  164.6 2.3 collective-permute-start.32
  166.9 2.3 collective-permute-done.13.h2
  169.2 1.9 collective-permute-done.14.h3
  171.1 2.2 collective-permute-start.36
  175.6 2.0 collective-permute-start.40
  178.1 16.2 %collective-permute-done.26.refs_15_ = bf16[1600,256]{1,0:T(8,128)(2,1)} collective-permute-done((bf16[1600,256]{1,0:T(8,128)(2,1)}, bf16[1600,256]{1,0:T(8,128)(2,1)}, u32[]{:S(2)}, u32[]{:S(2)}) %collective-permute-start.26) | collective-permute-done | bytes 819232 | tf_op jit(solution)/shard_map/ppermute | solution.py:884
  197.0 43.6 %layer.1 = (bf16[256,1024]{1,0:T(8,128)(2,1)}, f32[256,1024]{1,0:T(8,128)}, bf16[256,256]{1,0:T(8,128)(2,1)}, bf16[256,256]{1,0:T(8,128)(2,1)}, bf16[256,256]{1,...) custom-call(s32[6]{0:T(128)} %copy-done.26, ...), custom_call_target="tpu_custom_call" | custom-call | tf_op jit(solution)/shard_map/layer/pallas_call | solution.py:584
  240.7 3.9 copy.30
  248.2 2.3 copy.32
  253.3 20.4 %attend_back.1 = (bf16[1024,256]{1,0:T(8,128)(2,1)S(1)}, bf16[1024,256]{1,0:T(8,128)(2,1)S(1)}, bf16[1024,256]{1,0:T(8,128)(2,1)S(1)}, f32[2,256,1024]{2,1,0:T(8...) custom-call(s32[6]{0:T(128)S(1)} %copy-done.27, bf16[1024,256]{1,0:T(8,128)(2,1)S(1)} %copy-done.10, ...), custom_call_target="tpu_custom_call" | custom-call | tf_op jit(solution)/shard_map/attend_back/pallas_call | solution.py:359
  277.5 2.8 add_convert_fusion.2
  283.0 2.8 add_convert_fusion
  287.2 2.0 collective-permute-start.58
  291.4 29.1 %collective-permute-done.50 = bf16[2,1600,256]{2,1,0:T(8,128)(2,1)S(1)} collective-permute-done((bf16[2,1600,256]{2,1,0:T(8,128)(2,1)}, bf16[2,1600,256]{2,1,0:T(8,128)(2,1)S(1)}, u32[]{:S(2)}, u32[]{:S(2)}) %collective-permute-start.50) | collective-permute-done | bytes 1638432 | tf_op jit(solution)/shard_map/ppermute | solution.py:884
  321.0 1.9 collective-permute-start.51
  322.9 10.7 %collective-permute-done.58 = bf16[2,1600,256]{2,1,0:T(8,128)(2,1)S(1)} collective-permute-done((bf16[2,1600,256]{2,1,0:T(8,128)(2,1)}, bf16[2,1600,256]{2,1,0:T(8,128)(2,1)S(1)}, u32[]{:S(2)}, u32[]{:S(2)}) %collective-permute-start.58) | collective-permute-done | bytes 1638432 | tf_op jit(solution)/shard_map/ppermute | solution.py:884
  335.7 19.9 %collective-permute-done.55 = bf16[2,1600,256]{2,1,0:T(8,128)(2,1)S(1)} collective-permute-done((bf16[2,1600,256]{2,1,0:T(8,128)(2,1)S(1)}, bf16[2,1600,256]{2,1,0:T(8,128)(2,1)S(1)}, u32[]{:S(2)}, u32[]{:S(2)}) %collective-permute-start.55) | collective-permute-done | bytes 1638432 | tf_op jit(solution)/shard_map/ppermute | solution.py:884
  356.1 1.9 collective-permute-start.56
  358.9 3.2 broadcast_select_fusion.3
  362.1 6.5 %collective-permute-start.52 = (bf16[1600,256]{1,0:T(8,128)(2,1)}, bf16[1600,256]{1,0:T(8,128)(2,1)}, u32[]{:S(2)}, u32[]{:S(2)}) collective-permute-start(bf16[1600,256]{1,0:T(8,128)(2,1)} %get-tuple-element.78), channel_id=1, source_target_pairs={{0,8},{1,9},{2,10},{3,11},{4,12},{5,13},{6,14},{7,15},{8,0},{9,1},... | collective-permute-start | bytes 2457608 | tf_op jit(solution)/shard_map/ppermute | solution.py:884
  368.6 3.8 collective-permute-done.59
  372.4 2.5 collective-permute-done.56
  376.3 6.4 %collective-permute-start.60 = (bf16[1600,256]{1,0:T(8,128)(2,1)}, bf16[1600,256]{1,0:T(8,128)(2,1)}, u32[]{:S(2)}, u32[]{:S(2)}) collective-permute-start(bf16[1600,256]{1,0:T(8,128)(2,1)} %broadcast_select_fusion.1), channel_id=1, source_target_pairs={{0,8},{1,9},{2,10},{3,11},{4,12},{5,13},{6,14},{7,15},{8,0},{9,1},... | collective-permute-start | bytes 2457608 | tf_op jit(solution)/shard_map/ppermute | solution.py:884
  384.8 3.2 collective-permute-done.52
  388.1 2.4 fusion.7
  392.1 28.4 %collective-permute-done.60 = bf16[1600,256]{1,0:T(8,128)(2,1)} collective-permute-done((bf16[1600,256]{1,0:T(8,128)(2,1)}, bf16[1600,256]{1,0:T(8,128)(2,1)}, u32[]{:S(2)}, u32[]{:S(2)}) %collective-permute-start.60) | collective-permute-done | bytes 819232 | tf_op jit(solution)/shard_map/ppermute | solution.py:884
  420.5 2.1 fusion.8
  422.6 4.3 collective-permute-start.61
  427.4 4.6 collective-permute-done.64
  432.1 13.0 %collective-permute-done.65 = f32[4,32,256]{2,1,0:T(8,128)S(1)} collective-permute-done((f32[4,32,256]{2,1,0:T(8,128)S(1)}, f32[4,32,256]{2,1,0:T(8,128)S(1)}, u32[]{:S(2)}, u32[]{:S(2)}) %collective-permute-start.65) | collective-permute-done | bytes 131104 | tf_op jit(solution)/shard_map/ppermute | solution.py:884
  445.2 2.3 collective-permute-start.66
  447.5 3.6 collective-permute-done.66
  452.8 2.6 add_select_fusion.piece
  460.1 2.1 collective-permute-done.68
  463.2 2.6 collective-permute-done.69
  465.8 2.6 collective-permute-start.70
  470.0 2.1 collective-permute-start.71
  472.1 2.5 fusion.9
  475.9 6.9 %multiply_add_fusion = (f32[393664]{0:T(1024)}, f32[393664]{0:T(1024)}, f32[393664]{0:T(1024)}, f32[393664]{0:T(1024)}) fusion(f32[393664]{0:T(1024)} %param.14, f32[393664]{0:T(1024)} %param.11, f32[]{:T(128)S(6)} %div.36, f32[394240]{0:T(1024)} %bitcast.102, f32[393664]{0:T(1024)} %param.13, f32[393664]{0:T(1024)} %param.12), kind=kLoop, calls=%fused_computation.28 | loop fusion | flops 7479616 | bytes 14171908 | tf_op jit(solution)/shard_map/add | solution.py:1075
  (305 shorter events, 75.3 us)
Async XLA Ops:
  4.4 41.3 %collective-permute-start.15 = (bf16[1600,256]{1,0:T(8,128)(2,1)S(1)}, bf16[1600,256]{1,0:T(8,128)(2,1)S(1)}, u32[]{:S(2)}, u32[]{:S(2)}) collective-permute-start(bf16[1600,256]{1,0:T(8,128)(2,1)S(1)} %pack.1.s_own.refs_0_), channel_id=1, source_target_pairs={{8,24},{9,25},{10,26},{11,27},{12,28},{13,29},{14,30},{15,31},{16,... | collective-permute-start | bytes 2457608 | tf_op jit(solution)/shard_map/ppermute | solution.py:884
  5.7 42.0 %collective-permute-start.9 = (bf16[1600,256]{1,0:T(8,128)(2,1)S(1)}, bf16[1600,256]{1,0:T(8,128)(2,1)}, u32[]{:S(2)}, u32[]{:S(2)}) collective-permute-start(bf16[1600,256]{1,0:T(8,128)(2,1)S(1)} %pack.1.s_own.refs_0_), channel_id=1, source_target_pairs={{0,16},{1,17},{2,18},{3,19},{4,20},{5,21},{6,22},{7,23},{24,8},{25... | collective-permute-start | bytes 2457608 | tf_op jit(solution)/shard_map/ppermute | solution.py:884
  14.3 4.7 collective-permute-start.4
  19.1 4.7 collective-permute-start.5
  23.8 7.1 %collective-permute-start.6 = (bf16[4,32,256]{2,1,0:T(8,128)(2,1)S(1)}, bf16[4,32,256]{2,1,0:T(8,128)(2,1)S(1)}, u32[]{:S(2)}, u32[]{:S(2)}) collective-permute-start(bf16[4,32,256]{2,1,0:T(8,128)(2,1)S(1)} %add.159), channel_id=1, source_target_pairs={{0,8},{1,9},{2,10},{3,11},{4,12},{5,13},{6,14},{7,15},{8,0},{9,1},... | collective-permute-start | bytes 196616 | tf_op jit(solution)/shard_map/ppermute | solution.py:884
  23.9 38.6 %collective-permute-start.8 = (bf16[1600,256]{1,0:T(8,128)(2,1)S(1)}, bf16[1600,256]{1,0:T(8,128)(2,1)S(1)}, u32[]{:S(2)}, u32[]{:S(2)}) collective-permute-start(bf16[1600,256]{1,0:T(8,128)(2,1)S(1)} %pack.1.s_own.refs_0_), channel_id=1, source_target_pairs={{0,4},{1,5},{2,6},{3,7},{4,0},{5,1},{6,2},{7,3},{8,12},{9,13},{10,... | collective-permute-start | bytes 2457608 | tf_op jit(solution)/shard_map/ppermute | solution.py:884
  26.0 36.5 %collective-permute-start.19 = (bf16[1600,256]{1,0:T(8,128)(2,1)S(1)}, bf16[1600,256]{1,0:T(8,128)(2,1)}, u32[]{:S(2)}, u32[]{:S(2)}) collective-permute-start(bf16[1600,256]{1,0:T(8,128)(2,1)S(1)} %pack.1.s_own.refs_0_), channel_id=1, source_target_pairs={{8,10},{9,11},{10,8},{11,9},{12,14},{13,15},{14,12},{15,13},{16,18... | collective-permute-start | bytes 2457608 | tf_op jit(solution)/shard_map/ppermute | solution.py:884
  30.9 33.3 %collective-permute-start.27 = (bf16[1600,256]{1,0:T(8,128)(2,1)S(1)}, bf16[1600,256]{1,0:T(8,128)(2,1)}, u32[]{:S(2)}, u32[]{:S(2)}) collective-permute-start(bf16[1600,256]{1,0:T(8,128)(2,1)S(1)} %pack.1.s_own.refs_0_), channel_id=1, source_target_pairs={{8,9},{9,8},{10,11},{11,10},{12,13},{13,12},{14,15},{15,14},{16,17... | collective-permute-start | bytes 2457608 | tf_op jit(solution)/shard_map/ppermute | solution.py:884
  45.8 13.1 %collective-permute-start.1 = (bf16[256,1024]{1,0:T(8,128)(2,1)S(1)}, bf16[256,1024]{1,0:T(8,128)(2,1)S(1)}, u32[]{:S(2)}, u32[]{:S(2)}) collective-permute-start(bf16[256,1024]{1,0:T(8,128)(2,1)S(1)} %copy-done.4), channel_id=1, source_target_pairs={{0,2},{1,3},{2,0},{3,1},{4,6},{5,7},{6,4},{7,5},{8,10},{9,11},{10,... | collective-permute-start | bytes 1572872 | tf_op jit(solution)/shard_map/ppermute | solution.py:884
  47.7 5.2 %collective-permute-start.7 = (bf16[4,32,256]{2,1,0:T(8,128)(2,1)S(1)}, bf16[4,32,256]{2,1,0:T(8,128)(2,1)S(1)}, u32[]{:S(2)}, u32[]{:S(2)}) collective-permute-start(bf16[4,32,256]{2,1,0:T(8,128)(2,1)S(1)} %add.160), channel_id=1, source_target_pairs={{0,16},{1,17},{2,18},{3,19},{4,20},{5,21},{6,22},{7,23},{8,24},{9,... | collective-permute-start | bytes 196616 | tf_op jit(solution)/shard_map/ppermute | solution.py:884
  52.9 21.5 %collective-permute-start.10 = (bf16[1600,256]{1,0:T(8,128)(2,1)}, bf16[1600,256]{1,0:T(8,128)(2,1)}, u32[]{:S(2)}, u32[]{:S(2)}) collective-permute-start(bf16[1600,256]{1,0:T(8,128)(2,1)} %get-tuple-element.83), channel_id=1, source_target_pairs={{0,8},{1,9},{2,10},{3,11},{4,12},{5,13},{6,14},{7,15},{8,0},{9,1},... | collective-permute-start | bytes 2457608 | tf_op jit(solution)/shard_map/ppermute | solution.py:884
  61.6 27.5 %collective-permute-start.16 = (bf16[1600,256]{1,0:T(8,128)(2,1)}, bf16[1600,256]{1,0:T(8,128)(2,1)}, u32[]{:S(2)}, u32[]{:S(2)}) collective-permute-start(bf16[1600,256]{1,0:T(8,128)(2,1)} %get-tuple-element.82), channel_id=1, source_target_pairs={{0,8},{1,9},{2,10},{3,11},{4,12},{5,13},{6,14},{7,15},{8,0},{9,1},... | collective-permute-start | bytes 2457608 | tf_op jit(solution)/shard_map/ppermute | solution.py:884
  62.5 14.4 %collective-permute-start.2 = (bf16[256,1024]{1,0:T(8,128)(2,1)S(1)}, bf16[256,1024]{1,0:T(8,128)(2,1)S(1)}, u32[]{:S(2)}, u32[]{:S(2)}) collective-permute-start(bf16[256,1024]{1,0:T(8,128)(2,1)S(1)} %collective-permute-done.1.t2), channel_id=1, source_target_pairs={{0,1},{1,0},{2,3},{3,2},{4,5},{5,4},{6,7},{7,6},{8,9},{9,8},{10,11... | collective-permute-start | bytes 1572872 | tf_op jit(solution)/shard_map/ppermute | solution.py:884
  62.5 27.1 %collective-permute-start.23 = (bf16[1600,256]{1,0:T(8,128)(2,1)S(1)}, bf16[1600,256]{1,0:T(8,128)(2,1)}, u32[]{:S(2)}, u32[]{:S(2)}) collective-permute-start(bf16[1600,256]{1,0:T(8,128)(2,1)S(1)} %collective-permute-done.8.s_other.refs_4_), channel_id=1, source_target_pairs={{8,10},{9,11},{10,8},{11,9},{12,14},{13,15},{14,12},{15,13},{16,18... | collective-permute-start | bytes 2457608 | tf_op jit(solution)/shard_map/ppermute | solution.py:884
  64.2 27.5 %collective-permute-start.31 = (bf16[1600,256]{1,0:T(8,128)(2,1)S(1)}, bf16[1600,256]{1,0:T(8,128)(2,1)S(1)}, u32[]{:S(2)}, u32[]{:S(2)}) collective-permute-start(bf16[1600,256]{1,0:T(8,128)(2,1)S(1)} %collective-permute-done.8.s_other.refs_4_), channel_id=1, source_target_pairs={{8,9},{9,8},{10,11},{11,10},{12,13},{13,12},{14,15},{15,14},{16,17... | collective-permute-start | bytes 2457608 | tf_op jit(solution)/shard_map/ppermute | solution.py:884
  74.4 20.7 %collective-permute-start.35 = (bf16[1600,256]{1,0:T(8,128)(2,1)}, bf16[1600,256]{1,0:T(8,128)(2,1)S(1)}, u32[]{:S(2)}, u32[]{:S(2)}) collective-permute-start(bf16[1600,256]{1,0:T(8,128)(2,1)} %collective-permute-done.19.refs_8_), channel_id=1, source_target_pairs={{8,9},{9,8},{10,11},{11,10},{12,13},{13,12},{14,15},{15,14},{16,17... | collective-permute-start | bytes 2457608 | tf_op jit(solution)/shard_map/ppermute | solution.py:884
  77.8 17.8 %collective-permute-start.11 = (bf16[1600,256]{1,0:T(8,128)(2,1)S(1)}, bf16[1600,256]{1,0:T(8,128)(2,1)S(1)}, u32[]{:S(2)}, u32[]{:S(2)}) collective-permute-start(bf16[1600,256]{1,0:T(8,128)(2,1)S(1)} %get-tuple-element.81.b_own.refs_1_), channel_id=1, source_target_pairs={{0,4},{1,5},{2,6},{3,7},{4,0},{5,1},{6,2},{7,3},{8,12},{9,13},{10,... | collective-permute-start | bytes 2457608 | tf_op jit(solution)/shard_map/ppermute | solution.py:884
  89.1 21.3 %collective-permute-start.21 = (bf16[1600,256]{1,0:T(8,128)(2,1)S(1)}, bf16[1600,256]{1,0:T(8,128)(2,1)}, u32[]{:S(2)}, u32[]{:S(2)}) collective-permute-start(bf16[1600,256]{1,0:T(8,128)(2,1)S(1)} %get-tuple-element.80.refs_2_), channel_id=1, source_target_pairs={{0,2},{1,3},{2,0},{3,1},{4,6},{5,7},{6,4},{7,5},{8,10},{9,11},{10,... | collective-permute-start | bytes 2457608 | tf_op jit(solution)/shard_map/ppermute | solution.py:884
  89.6 23.5 %collective-permute-start.17 = (bf16[1600,256]{1,0:T(8,128)(2,1)S(1)}, bf16[1600,256]{1,0:T(8,128)(2,1)S(1)}, u32[]{:S(2)}, u32[]{:S(2)}) collective-permute-start(bf16[1600,256]{1,0:T(8,128)(2,1)S(1)} %get-tuple-element.80.refs_2_), channel_id=1, source_target_pairs={{0,4},{1,5},{2,6},{3,7},{4,0},{5,1},{6,2},{7,3},{8,12},{9,13},{10,... | collective-permute-start | bytes 2457608 | tf_op jit(solution)/shard_map/ppermute | solution.py:884
  91.7 36.2 %collective-permute-start.20 = (bf16[1600,256]{1,0:T(8,128)(2,1)S(1)}, bf16[1600,256]{1,0:T(8,128)(2,1)S(1)}, u32[]{:S(2)}, u32[]{:S(2)}) collective-permute-start(bf16[1600,256]{1,0:T(8,128)(2,1)S(1)} %get-tuple-element.81.b_own.refs_1_), channel_id=1, source_target_pairs={{0,2},{1,3},{2,0},{3,1},{4,6},{5,7},{6,4},{7,5}} | collective-permute-start | bytes 2457608 | tf_op jit(solution)/shard_map/ppermute | solution.py:884
  95.1 32.8 %collective-permute-start.18 = (bf16[1600,256]{1,0:T(8,128)(2,1)}, bf16[1600,256]{1,0:T(8,128)(2,1)}, u32[]{:S(2)}, u32[]{:S(2)}) collective-permute-start(bf16[1600,256]{1,0:T(8,128)(2,1)} %collective-permute-done.16.refs_3_), channel_id=1, source_target_pairs={{0,4},{1,5},{2,6},{3,7},{4,0},{5,1},{6,2},{7,3},{8,12},{9,13},{10,... | collective-permute-start | bytes 2457608 | tf_op jit(solution)/shard_map/ppermute | solution.py:884
  95.5 33.8 %collective-permute-start.28 = (bf16[1600,256]{1,0:T(8,128)(2,1)S(1)}, bf16[1600,256]{1,0:T(8,128)(2,1)S(1)}, u32[]{:S(2)}, u32[]{:S(2)}) collective-permute-start(bf16[1600,256]{1,0:T(8,128)(2,1)S(1)} %get-tuple-element.81.b_own.refs_1_), channel_id=1, source_target_pairs={{0,1},{1,0},{2,3},{3,2},{4,5},{5,4},{6,7},{7,6}} | collective-permute-start | bytes 2457608 | tf_op jit(solution)/shard_map/ppermute | solution.py:884
  110.4 21.6 %collective-permute-start.29 = (bf16[1600,256]{1,0:T(8,128)(2,1)S(1)}, bf16[1600,256]{1,0:T(8,128)(2,1)S(1)}, u32[]{:S(2)}, u32[]{:S(2)}) collective-permute-start(bf16[1600,256]{1,0:T(8,128)(2,1)S(1)} %get-tuple-element.80.refs_2_), channel_id=1, source_target_pairs={{0,1},{1,0},{2,3},{3,2},{4,5},{5,4},{6,7},{7,6},{8,9},{9,8},{10,11... | collective-permute-start | bytes 2457608 | tf_op jit(solution)/shard_map/ppermute | solution.py:884
  113.1 49.6 %collective-permute-start.22 = (bf16[1600,256]{1,0:T(8,128)(2,1)}, bf16[1600,256]{1,0:T(8,128)(2,1)}, u32[]{:S(2)}, u32[]{:S(2)}) collective-permute-start(bf16[1600,256]{1,0:T(8,128)(2,1)} %collective-permute-done.16.refs_3_), channel_id=1, source_target_pairs={{0,2},{1,3},{2,0},{3,1},{4,6},{5,7},{6,4},{7,5},{8,10},{9,11},{10,... | collective-permute-start | bytes 2457608 | tf_op jit(solution)/shard_map/ppermute | solution.py:884
  127.8 34.9 %collective-permute-start.30 = (bf16[1600,256]{1,0:T(8,128)(2,1)}, bf16[1600,256]{1,0:T(8,128)(2,1)}, u32[]{:S(2)}, u32[]{:S(2)}) collective-permute-start(bf16[1600,256]{1,0:T(8,128)(2,1)} %collective-permute-done.16.refs_3_), channel_id=1, source_target_pairs={{0,1},{1,0},{2,3},{3,2},{4,5},{5,4},{6,7},{7,6},{8,9},{9,8},{10,11... | collective-permute-start | bytes 2457608 | tf_op jit(solution)/shard_map/ppermute | solution.py:884
  127.8 36.5 %collective-permute-start.39 = (bf16[1600,256]{1,0:T(8,128)(2,1)}, bf16[1600,256]{1,0:T(8,128)(2,1)}, u32[]{:S(2)}, u32[]{:S(2)}) collective-permute-start(bf16[1600,256]{1,0:T(8,128)(2,1)} %collective-permute-done.23.refs_12_), channel_id=1, source_target_pairs={{8,9},{9,8},{10,11},{11,10},{12,13},{13,12},{14,15},{15,14},{16,17... | collective-permute-start | bytes 2457608 | tf_op jit(solution)/shard_map/ppermute | solution.py:884
  129.4 43.9 %collective-permute-start.24 = (bf16[1600,256]{1,0:T(8,128)(2,1)S(1)}, bf16[1600,256]{1,0:T(8,128)(2,1)}, u32[]{:S(2)}, u32[]{:S(2)}) collective-permute-start(bf16[1600,256]{1,0:T(8,128)(2,1)S(1)} %collective-permute-done.11.b_other.refs_5_), channel_id=1, source_target_pairs={{0,2},{1,3},{2,0},{3,1},{4,6},{5,7},{6,4},{7,5}} | collective-permute-start | bytes 2457608 | tf_op jit(solution)/shard_map/ppermute | solution.py:884
  132.9 40.7 %collective-permute-start.25 = (bf16[1600,256]{1,0:T(8,128)(2,1)}, bf16[1600,256]{1,0:T(8,128)(2,1)}, u32[]{:S(2)}, u32[]{:S(2)}) collective-permute-start(bf16[1600,256]{1,0:T(8,128)(2,1)} %collective-permute-done.21.refs_10_), channel_id=1, source_target_pairs={{0,4},{1,5},{2,6},{3,7},{4,0},{5,1},{6,2},{7,3},{8,12},{9,13},{10,... | collective-permute-start | bytes 2457608 | tf_op jit(solution)/shard_map/ppermute | solution.py:884
  162.7 6.5 %collective-permute-start.13 = (bf16[256,256]{1,0:T(8,128)(2,1)S(1)}, bf16[256,256]{1,0:T(8,128)(2,1)}, u32[]{:S(2)}, u32[]{:S(2)}) collective-permute-start(bf16[256,256]{1,0:T(8,128)(2,1)S(1)} %get-tuple-element.43), channel_id=1, source_target_pairs={{0,2},{1,3},{2,0},{3,1},{4,6},{5,7},{6,4},{7,5},{8,10},{9,11},{10,... | collective-permute-start | bytes 393224 | tf_op jit(solution)/shard_map/ppermute | solution.py:884
  164.3 6.8 %collective-permute-start.14 = (bf16[256,256]{1,0:T(8,128)(2,1)S(1)}, bf16[256,256]{1,0:T(8,128)(2,1)}, u32[]{:S(2)}, u32[]{:S(2)}) collective-permute-start(bf16[256,256]{1,0:T(8,128)(2,1)S(1)} %get-tuple-element.44), channel_id=1, source_target_pairs={{0,3},{1,2},{2,1},{3,0},{4,7},{5,6},{6,5},{7,4},{8,11},{9,10},{10,... | collective-permute-start | bytes 393224 | tf_op jit(solution)/shard_map/ppermute | solution.py:884
  164.6 10.5 %collective-permute-start.32 = (bf16[1600,256]{1,0:T(8,128)(2,1)S(1)}, bf16[1600,256]{1,0:T(8,128)(2,1)S(1)}, u32[]{:S(2)}, u32[]{:S(2)}) collective-permute-start(bf16[1600,256]{1,0:T(8,128)(2,1)S(1)} %collective-permute-done.11.b_other.refs_5_), channel_id=1, source_target_pairs={{0,1},{1,0},{2,3},{3,2},{4,5},{5,4},{6,7},{7,6}} | collective-permute-start | bytes 2457608 | tf_op jit(solution)/shard_map/ppermute | solution.py:884
  169.2 5.9 %collective-permute-start.33 = (bf16[1600,256]{1,0:T(8,128)(2,1)S(1)}, bf16[1600,256]{1,0:T(8,128)(2,1)S(1)}, u32[]{:S(2)}, u32[]{:S(2)}) collective-permute-start(bf16[1600,256]{1,0:T(8,128)(2,1)S(1)} %copy-done.53), channel_id=1, source_target_pairs={{0,1},{1,0},{2,3},{3,2},{4,5},{5,4},{6,7},{7,6},{8,9},{9,8},{10,11... | collective-permute-start | bytes 2457608 | tf_op jit(solution)/shard_map/ppermute | solution.py:884
  171.1 4.5 collective-permute-start.36
  173.3 4.3 collective-permute-start.37
  173.6 20.8 %collective-permute-start.26 = (bf16[1600,256]{1,0:T(8,128)(2,1)}, bf16[1600,256]{1,0:T(8,128)(2,1)}, u32[]{:S(2)}, u32[]{:S(2)}) collective-permute-start(bf16[1600,256]{1,0:T(8,128)(2,1)} %collective-permute-done.18.refs_7_), channel_id=1, source_target_pairs={{0,2},{1,3},{2,0},{3,1},{4,6},{5,7},{6,4},{7,5},{8,10},{9,11},{10,... | collective-permute-start | bytes 2457608 | tf_op jit(solution)/shard_map/ppermute | solution.py:884
  175.1 20.7 %collective-permute-start.34 = (bf16[1600,256]{1,0:T(8,128)(2,1)}, bf16[1600,256]{1,0:T(8,128)(2,1)S(1)}, u32[]{:S(2)}, u32[]{:S(2)}) collective-permute-start(bf16[1600,256]{1,0:T(8,128)(2,1)} %collective-permute-done.18.refs_7_), channel_id=1, source_target_pairs={{0,1},{1,0},{2,3},{3,2},{4,5},{5,4},{6,7},{7,6},{8,9},{9,8},{10,11... | collective-permute-start | bytes 2457608 | tf_op jit(solution)/shard_map/ppermute | solution.py:884
  175.1 20.7 %collective-permute-start.38 = (bf16[1600,256]{1,0:T(8,128)(2,1)}, bf16[1600,256]{1,0:T(8,128)(2,1)}, u32[]{:S(2)}, u32[]{:S(2)}) collective-permute-start(bf16[1600,256]{1,0:T(8,128)(2,1)} %collective-permute-done.22.refs_11_), channel_id=1, source_target_pairs={{0,1},{1,0},{2,3},{3,2},{4,5},{5,4},{6,7},{7,6},{8,9},{9,8},{10,11... | collective-permute-start | bytes 2457608 | tf_op jit(solution)/shard_map/ppermute | solution.py:884
  175.6 20.2 %collective-permute-start.40 = (bf16[1600,256]{1,0:T(8,128)(2,1)}, bf16[1600,256]{1,0:T(8,128)(2,1)}, u32[]{:S(2)}, u32[]{:S(2)}) collective-permute-start(bf16[1600,256]{1,0:T(8,128)(2,1)} %collective-permute-done.24.refs_13_), channel_id=1, source_target_pairs={{0,1},{1,0},{2,3},{3,2},{4,5},{5,4},{6,7},{7,6}} | collective-permute-start | bytes 2457608 | tf_op jit(solution)/shard_map/ppermute | solution.py:884
  177.6 18.2 %collective-permute-start.41 = (bf16[1600,256]{1,0:T(8,128)(2,1)}, bf16[1600,256]{1,0:T(8,128)(2,1)}, u32[]{:S(2)}, u32[]{:S(2)}) collective-permute-start(bf16[1600,256]{1,0:T(8,128)(2,1)} %collective-permute-done.25.refs_14_), channel_id=1, source_target_pairs={{0,1},{1,0},{2,3},{3,2},{4,5},{5,4},{6,7},{7,6},{8,9},{9,8},{10,11... | collective-permute-start | bytes 2457608 | tf_op jit(solution)/shard_map/ppermute | solution.py:884
  244.6 32.9 %collective-permute-start.49 = (bf16[2,2,1600,256]{3,2,0,1:T(8,128)(2,1)}, bf16[2,2,1600,256]{3,2,0,1:T(8,128)(2,1)}, u32[]{:S(2)}, u32[]{:S(2)}) collective-permute-start(bf16[2,2,1600,256]{3,2,0,1:T(8,128)(2,1)} %copy.30), channel_id=1, source_target_pairs={{0,1},{1,0},{2,3},{3,2},{4,5},{5,4},{6,7},{7,6},{8,9},{9,8},{10,11... | collective-permute-start | bytes 9830408 | tf_op jit(solution)/shard_map/ppermute | solution.py:884
  244.7 38.3 %collective-permute-start.57 = (bf16[2,2,1600,256]{3,2,1,0:T(8,128)(2,1)}, bf16[2,2,1600,256]{3,2,1,0:T(8,128)(2,1)}, u32[]{:S(2)}, u32[]{:S(2)}) collective-permute-start(bf16[2,2,1600,256]{3,2,1,0:T(8,128)(2,1)} %get-tuple-element.67), channel_id=1, source_target_pairs={{0,1},{1,0},{2,3},{3,2},{4,5},{5,4},{6,7},{7,6},{8,9},{9,8},{10,11... | collective-permute-start | bytes 9830408 | tf_op jit(solution)/shard_map/ppermute | solution.py:884
  245.1 5.7 %collective-permute-start.43 = (bf16[256,256]{1,0:T(8,128)(2,1)S(1)}, bf16[256,256]{1,0:T(8,128)(2,1)S(1)}, u32[]{:S(2)}, u32[]{:S(2)}) collective-permute-start(bf16[256,256]{1,0:T(8,128)(2,1)S(1)} %copy-done.72), channel_id=1, source_target_pairs={{0,1},{1,0},{2,3},{3,2},{4,5},{5,4},{6,7},{7,6},{8,9},{9,8},{10,11... | collective-permute-start | bytes 393224 | tf_op jit(solution)/shard_map/ppermute | solution.py:884
  245.2 6.3 %collective-permute-start.44 = (bf16[256,256]{1,0:T(8,128)(2,1)S(1)}, bf16[256,256]{1,0:T(8,128)(2,1)S(1)}, u32[]{:S(2)}, u32[]{:S(2)}) collective-permute-start(bf16[256,256]{1,0:T(8,128)(2,1)S(1)} %copy-done.71), channel_id=1, source_target_pairs={{0,2},{1,3},{2,0},{3,1},{4,6},{5,7},{6,4},{7,5},{8,10},{9,11},{10,... | collective-permute-start | bytes 393224 | tf_op jit(solution)/shard_map/ppermute | solution.py:884
  246.7 6.5 %collective-permute-start.45 = (bf16[256,256]{1,0:T(8,128)(2,1)S(1)}, bf16[256,256]{1,0:T(8,128)(2,1)S(1)}, u32[]{:S(2)}, u32[]{:S(2)}) collective-permute-start(bf16[256,256]{1,0:T(8,128)(2,1)S(1)} %copy-done.70), channel_id=1, source_target_pairs={{0,3},{1,2},{2,1},{3,0},{4,7},{5,6},{6,5},{7,4},{8,11},{9,10},{10,... | collective-permute-start | bytes 393224 | tf_op jit(solution)/shard_map/ppermute | solution.py:884
  250.8 38.3 %collective-permute-start.54 = (bf16[2,2,1600,256]{3,2,0,1:T(8,128)(2,1)S(1)}, bf16[2,2,1600,256]{3,2,0,1:T(8,128)(2,1)S(1)}, u32[]{:S(2)}, u32[]{:S(2)}) collective-permute-start(bf16[2,2,1600,256]{3,2,0,1:T(8,128)(2,1)S(1)} %copy.32), channel_id=1, source_target_pairs={{0,1},{1,0},{2,3},{3,2},{4,5},{5,4},{6,7},{7,6},{8,9},{9,8},{10,11... | collective-permute-start | bytes 9830408 | tf_op jit(solution)/shard_map/ppermute | solution.py:884
  277.2 81.7 %collective-permute-start.48 = (bf16[1600,256]{1,0:T(8,128)(2,1)}, bf16[1600,256]{1,0:T(8,128)(2,1)}, u32[]{:S(2)}, u32[]{:S(2)}) collective-permute-start(bf16[1600,256]{1,0:T(8,128)(2,1)} %broadcast_select_fusion), channel_id=1, source_target_pairs={{0,4},{1,5},{2,6},{3,7},{4,0},{5,1},{6,2},{7,3},{8,12},{9,13},{10,... | collective-permute-start | bytes 2457608 | tf_op jit(solution)/shard_map/ppermute | solution.py:884
  281.7 38.9 %collective-permute-start.50 = (bf16[2,1600,256]{2,1,0:T(8,128)(2,1)}, bf16[2,1600,256]{2,1,0:T(8,128)(2,1)S(1)}, u32[]{:S(2)}, u32[]{:S(2)}) collective-permute-start(bf16[2,1600,256]{2,1,0:T(8,128)(2,1)} %slice_bitcast_fusion.4), channel_id=1, source_target_pairs={{0,2},{1,3},{2,0},{3,1},{4,6},{5,7},{6,4},{7,5},{8,10},{9,11},{10,... | collective-permute-start | bytes 4915208 | tf_op jit(solution)/shard_map/ppermute | solution.py:884
  287.2 46.4 %collective-permute-start.58 = (bf16[2,1600,256]{2,1,0:T(8,128)(2,1)}, bf16[2,1600,256]{2,1,0:T(8,128)(2,1)S(1)}, u32[]{:S(2)}, u32[]{:S(2)}) collective-permute-start(bf16[2,1600,256]{2,1,0:T(8,128)(2,1)} %slice_bitcast_fusion), channel_id=1, source_target_pairs={{0,4},{1,5},{2,6},{3,7},{4,0},{5,1},{6,2},{7,3},{8,12},{9,13},{10,... | collective-permute-start | bytes 4915208 | tf_op jit(solution)/shard_map/ppermute | solution.py:884
  290.2 65.5 %collective-permute-start.55 = (bf16[2,1600,256]{2,1,0:T(8,128)(2,1)S(1)}, bf16[2,1600,256]{2,1,0:T(8,128)(2,1)S(1)}, u32[]{:S(2)}, u32[]{:S(2)}) collective-permute-start(bf16[2,1600,256]{2,1,0:T(8,128)(2,1)S(1)} %slice_bitcast_fusion.2), channel_id=1, source_target_pairs={{0,2},{1,3},{2,0},{3,1},{4,6},{5,7},{6,4},{7,5},{8,10},{9,11},{10,... | collective-permute-start | bytes 4915208 | tf_op jit(solution)/shard_map/ppermute | solution.py:884
  321.0 37.9 %collective-permute-start.51 = (bf16[1600,256]{1,0:T(8,128)(2,1)S(1)}, bf16[1600,256]{1,0:T(8,128)(2,1)S(1)}, u32[]{:S(2)}, u32[]{:S(2)}) collective-permute-start(bf16[1600,256]{1,0:T(8,128)(2,1)S(1)} %slice_bitcast_fusion.10), channel_id=1, source_target_pairs={{0,4},{1,5},{2,6},{3,7},{4,0},{5,1},{6,2},{7,3},{8,12},{9,13},{10,... | collective-permute-start | bytes 2457608 | tf_op jit(solution)/shard_map/ppermute | solution.py:884
  334.1 38.3 %collective-permute-start.59 = (bf16[1600,256]{1,0:T(8,128)(2,1)S(1)}, bf16[1600,256]{1,0:T(8,128)(2,1)S(1)}, u32[]{:S(2)}, u32[]{:S(2)}) collective-permute-start(bf16[1600,256]{1,0:T(8,128)(2,1)S(1)} %slice_bitcast_fusion.6), channel_id=1, source_target_pairs={{0,2},{1,3},{2,0},{3,1},{4,6},{5,7},{6,4},{7,5},{8,10},{9,11},{10,... | collective-permute-start | bytes 2457608 | tf_op jit(solution)/shard_map/ppermute | solution.py:884
  356.1 18.8 %collective-permute-start.56 = (bf16[1600,256]{1,0:T(8,128)(2,1)S(1)}, bf16[1600,256]{1,0:T(8,128)(2,1)S(1)}, u32[]{:S(2)}, u32[]{:S(2)}) collective-permute-start(bf16[1600,256]{1,0:T(8,128)(2,1)S(1)} %slice_bitcast_fusion.8), channel_id=1, source_target_pairs={{0,4},{1,5},{2,6},{3,7},{4,0},{5,1},{6,2},{7,3},{8,12},{9,13},{10,... | collective-permute-start | bytes 2457608 | tf_op jit(solution)/shard_map/ppermute | solution.py:884
  362.1 25.9 %collective-permute-start.52 = (bf16[1600,256]{1,0:T(8,128)(2,1)}, bf16[1600,256]{1,0:T(8,128)(2,1)}, u32[]{:S(2)}, u32[]{:S(2)}) collective-permute-start(bf16[1600,256]{1,0:T(8,128)(2,1)} %get-tuple-element.78), channel_id=1, source_target_pairs={{0,8},{1,9},{2,10},{3,11},{4,12},{5,13},{6,14},{7,15},{8,0},{9,1},... | collective-permute-start | bytes 2457608 | tf_op jit(solution)/shard_map/ppermute | solution.py:884
  376.3 44.2 %collective-permute-start.60 = (bf16[1600,256]{1,0:T(8,128)(2,1)}, bf16[1600,256]{1,0:T(8,128)(2,1)}, u32[]{:S(2)}, u32[]{:S(2)}) collective-permute-start(bf16[1600,256]{1,0:T(8,128)(2,1)} %broadcast_select_fusion.1), channel_id=1, source_target_pairs={{0,8},{1,9},{2,10},{3,11},{4,12},{5,13},{6,14},{7,15},{8,0},{9,1},... | collective-permute-start | bytes 2457608 | tf_op jit(solution)/shard_map/ppermute | solution.py:884
  382.9 68.2 %collective-permute-start.46 = (bf16[2,256,1024]{2,1,0:T(8,128)(2,1)S(1)}, bf16[2,256,1024]{2,1,0:T(8,128)(2,1)S(1)}, u32[]{:S(2)}, u32[]{:S(2)}) collective-permute-start(bf16[2,256,1024]{2,1,0:T(8,128)(2,1)S(1)} %get-tuple-element.57), channel_id=1, source_target_pairs={{0,1},{1,0},{2,3},{3,2},{4,5},{5,4},{6,7},{7,6},{8,9},{9,8},{10,11... | collective-permute-start | bytes 3145736 | tf_op jit(solution)/shard_map/ppermute | solution.py:884
  384.2 42.7 %collective-permute-start.63 = (f32[4,32,256]{2,1,0:T(8,128)S(1)}, f32[4,32,256]{2,1,0:T(8,128)S(1)}, u32[]{:S(2)}, u32[]{:S(2)}) collective-permute-start(f32[4,32,256]{2,1,0:T(8,128)S(1)} %add.186), channel_id=1, source_target_pairs={{0,2},{1,3},{2,0},{3,1},{4,6},{5,7},{6,4},{7,5},{8,10},{9,11},{10,... | collective-permute-start | bytes 393224 | tf_op jit(solution)/shard_map/ppermute | solution.py:884
  390.5 62.2 %collective-permute-start.53 = (bf16[1600,256]{1,0:T(8,128)(2,1)S(1)}, bf16[1600,256]{1,0:T(8,128)(2,1)S(1)}, u32[]{:S(2)}, u32[]{:S(2)}) collective-permute-start(bf16[1600,256]{1,0:T(8,128)(2,1)S(1)} %fusion.7), channel_id=1, source_target_pairs={{8,24},{9,25},{10,26},{11,27},{12,28},{13,29},{14,30},{15,31},{16,... | collective-permute-start | bytes 2457608 | tf_op jit(solution)/shard_map/ppermute | solution.py:884
  422.6 30.1 %collective-permute-start.61 = (bf16[1600,256]{1,0:T(8,128)(2,1)S(1)}, bf16[1600,256]{1,0:T(8,128)(2,1)S(1)}, u32[]{:S(2)}, u32[]{:S(2)}) collective-permute-start(bf16[1600,256]{1,0:T(8,128)(2,1)S(1)} %fusion.8), channel_id=1, source_target_pairs={{0,16},{1,17},{2,18},{3,19},{4,20},{5,21},{6,22},{7,23},{24,8},{25... | collective-permute-start | bytes 2457608 | tf_op jit(solution)/shard_map/ppermute | solution.py:884
  427.0 5.0 %collective-permute-start.64 = (f32[4,32,256]{2,1,0:T(8,128)S(1)}, f32[4,32,256]{2,1,0:T(8,128)S(1)}, u32[]{:S(2)}, u32[]{:S(2)}) collective-permute-start(f32[4,32,256]{2,1,0:T(8,128)S(1)} %add.187), channel_id=1, source_target_pairs={{0,4},{1,5},{2,6},{3,7},{4,0},{5,1},{6,2},{7,3},{8,12},{9,13},{10,... | collective-permute-start | bytes 393224 | tf_op jit(solution)/shard_map/ppermute | solution.py:884
  432.1 13.1 %collective-permute-start.65 = (f32[4,32,256]{2,1,0:T(8,128)S(1)}, f32[4,32,256]{2,1,0:T(8,128)S(1)}, u32[]{:S(2)}, u32[]{:S(2)}) collective-permute-start(f32[4,32,256]{2,1,0:T(8,128)S(1)} %add.188), channel_id=1, source_target_pairs={{0,8},{1,9},{2,10},{3,11},{4,12},{5,13},{6,14},{7,15},{8,0},{9,1},... | collective-permute-start | bytes 393224 | tf_op jit(solution)/shard_map/ppermute | solution.py:884
  445.2 5.9 %collective-permute-start.66 = (f32[4,32,256]{2,1,0:T(8,128)S(1)}, f32[4,32,256]{2,1,0:T(8,128)S(1)}, u32[]{:S(2)}, u32[]{:S(2)}) collective-permute-start(f32[4,32,256]{2,1,0:T(8,128)S(1)} %add.189), channel_id=1, source_target_pairs={{0,16},{1,17},{2,18},{3,19},{4,20},{5,21},{6,22},{7,23},{8,24},{9,... | collective-permute-start | bytes 393224 | tf_op jit(solution)/shard_map/ppermute | solution.py:884
  452.2 19.9 %collective-permute-start.47 = (bf16[256,1024]{1,0:T(8,128)(2,1)}, bf16[256,1024]{1,0:T(8,128)(2,1)}, u32[]{:S(2)}, u32[]{:S(2)}) collective-permute-start(bf16[256,1024]{1,0:T(8,128)(2,1)} %fusion.10), channel_id=1, source_target_pairs={{0,2},{1,3},{2,0},{3,1},{4,6},{5,7},{6,4},{7,5},{8,10},{9,11},{10,... | collective-permute-start | bytes 1572872 | tf_op jit(solution)/shard_map/ppermute | solution.py:884
  465.8 4.2 collective-permute-start.70
  470.0 4.6 collective-permute-start.71
  (81 other events, 1457.1 us)

commit v2 on v1

--- a/solution.py
+++ b/solution.py
@@ -52,7 +52,17 @@
 
 
 SEGMENTS = [segments(shard) for shard in range(8)]
-SLOT = ((0, 3, 2, 1), (1, 0, 3, 2), (1, 3, 0, 2), (1, 2, 3, 0))
+SLOT = ((0, 1, 3, 2), (2, 0, 3, 1), (1, 3, 0, 2), (2, 3, 1, 0))
+
+
+def buffers(z):
+    x_a, y_b = 9, 11
+    over_x = [7, 8, x_a, 13]
+    both = [y_b if z == 2 else x_a, y_b, 12, 14]
+    return [0, 1, 2, 3, 4, 5, 6, 10, *over_x, *both]
+
+
+BUFFER = [buffers(z) for z in range(4)]
 
 
 def dot(left, right):
@@ -92,7 +102,7 @@
     return [(a, min(most, rows - a)) for a in range(0, rows, most)]
 
 
-def pack_kernel(place, flat, piece, rolled, rows):
+def pack_kernel(place, flat, tails, piece, rolled, rows):
     shard = place[0]
     rows[0:PAD, :] = jnp.zeros((PAD, 128), jnp.float32)
     rows[PAD + LANE_ROWS : PAD + LANE_ROWS + PAD, :] = jnp.zeros((PAD, 128), jnp.float32)
@@ -118,6 +128,9 @@
         @pl.when(shard == case)
         def _(case=case):
             for _, row_a, row_b, offset, step, first in SEGMENTS[case]:
+                if offset == TAIL:
+                    piece[TAIL:PIECE, :] = tails[...]
+                    continue
                 count = row_b - row_a
                 base = PAD + first + step * row_a - lane_start(case)
                 for t in range(step):
@@ -129,11 +142,11 @@
                         )
 
 
-def pack(place, flat):
+def pack(place, flat, tails):
     return pl.pallas_call(
         pack_kernel,
         out_shape=struct((PIECE, 256)),
-        in_specs=[SMEM, VMEM],
+        in_specs=[SMEM, VMEM, VMEM],
         out_specs=VMEM,
         scratch_shapes=[
             pltpu.VMEM((8 + LANE_ROWS, 128), jnp.float32),
@@ -141,28 +154,46 @@
         ],
         compiler_params=pltpu.CompilerParams(vmem_limit_bytes=24 << 20),
         name="pack",
-    )(place, flat)
-
-
-def unpack_kernel(place, piece, extra, flat, square, rows):
+    )(place, flat, tails)
+
+
+def unpack_kernel(place, inner, inner_last, outer, outer_last, flat, square, rows, left, right, sem):
     shard = place[0]
+    is_inner = (place[1] == 1) | (place[1] == 2)
+
+    def fetch(first, second):
+        copies = [
+            pltpu.make_async_copy(first, left, sem.at[0]),
+            pltpu.make_async_copy(second, right, sem.at[1]),
+        ]
+        for copy in copies:
+            copy.start()
+        for copy in copies:
+            copy.wait()
+
+    @pl.when(is_inner)
+    def _():
+        fetch(inner, inner_last)
+
+    @pl.when(jnp.logical_not(is_inner))
+    def _():
+        fetch(outer, outer_last)
+
     for case in range(8):
 
         @pl.when(shard == case)
         def _(case=case):
-            for name, row_a, row_b, offset, step, first in SEGMENTS[case]:
+            for _, row_a, row_b, offset, step, first in SEGMENTS[case]:
                 count = row_b - row_a
                 base = PAD + first + step * row_a - lane_start(case)
                 for t in range(step):
                     source = offset + t // 2 * count
                     lanes = slice(t % 2 * 128, t % 2 * 128 + 128)
                     for a, n in chunks(count):
-                        if name == "vec":
-                            value = extra[0:16, lanes]
-                        elif name == "o" and case == 1:
-                            value = extra[16:32, lanes]
-                        else:
-                            value = wide(piece[source + a : source + a + n, lanes])
+                        spot = slice(source + a, source + a + n)
+                        value = wide(left[spot, lanes]) + wide(right[spot, lanes])
+                        if offset == TAIL:
+                            value = jnp.zeros((n, 128), jnp.float32)
                         rows[pl.ds(base + t + step * a, n, stride=step), :] = value
 
     square[...] = jnp.zeros_like(square)
@@ -187,16 +218,51 @@
             square[...] = total
 
 
-def unpack(place, piece, extra):
+def unpack(place, *pieces):
     return pl.pallas_call(
         unpack_kernel,
         out_shape=(struct((LANE_ROWS, 128), jnp.float32), struct((8, 128), jnp.float32)),
-        in_specs=[SMEM, VMEM, VMEM],
+        in_specs=[SMEM] + [ANY] * 4,
         out_specs=(VMEM, VMEM),
-        scratch_shapes=[pltpu.VMEM((PAD + LANE_ROWS + PAD, 128), jnp.float32)],
-        compiler_params=pltpu.CompilerParams(vmem_limit_bytes=24 << 20),
+        scratch_shapes=[
+            pltpu.VMEM((PAD + LANE_ROWS + PAD, 128), jnp.float32),
+            pltpu.VMEM((PIECE, 256), jnp.bfloat16),
+            pltpu.VMEM((PIECE, 256), jnp.bfloat16),
+            pltpu.SemaphoreType.DMA((2,)),
+        ],
+        compiler_params=pltpu.CompilerParams(vmem_limit_bytes=60 << 20),
         name="unpack",
-    )(place, piece, extra)
+    )(place, *pieces)
+
+
+def combine_kernel(split, place, *refs):
+    kept, sent = refs[-2:]
+    first = sum(wide(ref[...]) for ref in refs[:split])
+    second = sum(wide(ref[...]) for ref in refs[split:-2])
+    even = place[1] % 2 == 0
+    kept[...] = low(jnp.where(even, first, second))
+    sent[...] = low(jnp.where(even, second, first))
+
+
+def combine(place, first, second):
+    blocks = 5
+    size = PIECE // blocks
+
+    def spec(piece):
+        if piece.ndim == 4:
+            return pl.BlockSpec((None, None, size, 256), lambda n: (0, 0, n, 0))
+        return pl.BlockSpec((size, 256), lambda n: (n, 0))
+
+    pieces = [*first, *second]
+    return pl.pallas_call(
+        partial(combine_kernel, len(first)),
+        grid=(blocks,),
+        out_shape=(struct((PIECE, 256)), struct((PIECE, 256))),
+        in_specs=[SMEM] + [spec(piece) for piece in pieces],
+        out_specs=(pl.BlockSpec((size, 256), lambda n: (n, 0)),) * 2,
+        compiler_params=pltpu.CompilerParams(vmem_limit_bytes=60 << 20),
+        name="combine",
+    )(place, *pieces)
 
 
 def column_sum(values):
@@ -210,10 +276,17 @@
 
 
 def attend_kernel(
-    place, t0, t1, t2, t3, embed, bias, s_own, s_other, b_own, b_other,
-    stream_out, weight_out, q_out, k_out, v_out, h0, h1, h2, h3, lse_out,
-    q_heads, k_heads, v_heads, o_heads, edge, sem,
+    place, embed, bias, t0, t1, t2, t3, p0, p1, p2, p3, p4, p5, p6, p7, p8,
+    stream_out, weight_out, q_out, k_out, v_out, h0, h1, h2, h3, lse_out, stack,
+    tokens, staged, q_heads, k_heads, v_heads, o_heads, edge, sem, sem_tokens, sem_in, sem_out,
 ):
+    fetches = [
+        pltpu.make_async_copy(ref, tokens.at[r], sem_tokens.at[r])
+        for r, ref in enumerate((t0, t1, t2, t3))
+    ]
+    for copy in fetches:
+        copy.start()
+
     def copies(first, second):
         return [
             pltpu.make_async_copy(first.at[0:1024, :], weight_out.at[0], sem.at[0]),
@@ -223,21 +296,30 @@
             pltpu.make_async_copy(second.at[512:1536, :], weight_out.at[2], sem.at[4]),
         ]
 
-    for bottom in range(2):
+    held = ((p0, p1), (p2, p3), (p4, p5))
+    for z in range(4):
         for y in range(2):
-            own, other = (s_own, s_other) if bottom else (b_own, b_other)
+            own, other = held[SLOT[z][0]]
             pair = (other, own) if y else (own, other)
 
-            @pl.when(((place[1] == 0) == bool(bottom)) & (place[2] == y))
+            @pl.when((place[1] == z) & (place[2] == y))
             def _(pair=pair):
                 for copy in copies(*pair):
                     copy.start()
 
-    for r, tokens in enumerate((t0, t1, t2, t3)):
-        stream_out[r] = low(wide(tokens[...]) + inside_column(place, r) * embed[...])
+    held_in = [
+        pltpu.make_async_copy(ref, staged.at[n], sem_in.at[n])
+        for n, ref in enumerate((p0, p2, p4, p6, p1, p3, p5, p7, p8))
+    ]
+    held_out = [pltpu.make_async_copy(staged.at[n], stack.at[n], sem_out.at[n]) for n in range(9)]
+    for copy in held_in:
+        copy.start()
+    for r, copy in enumerate(fetches):
+        copy.wait()
+        stream_out[r] = low(wide(tokens[r]) + inside_column(place, r) * embed[...])
     lanes = lax.broadcasted_iota(jnp.int32, (1024, 128), 1)
     v_heads[...] = jnp.broadcast_to((lanes >= 64).astype(jnp.bfloat16), (4, 1024, 128))
-    for copy in copies(s_own, s_other):
+    for copy in copies(p0, p1):
         copy.wait()
     weight_out[1, 512:528, :] = weight_out[1, 512:528, :] + edge[...]
     for r in range(4):
@@ -255,6 +337,9 @@
             k_heads[h, rows, :] = key[:, cols]
             v_heads[h, rows, 0:64] = value[:, cols]
     lse_out[...] = jnp.zeros_like(lse_out)
+    for before, copy in zip(held_in, held_out):
+        before.wait()
+        copy.start()
 
     def step(n, _):
         h, r = n // 4, n % 4
@@ -273,6 +358,8 @@
     for r, out in enumerate((h0, h1, h2, h3)):
         for h in range(4):
             out[:, h * 64 : h * 64 + 64] = o_heads[h, r * 256 : r * 256 + 256, :]
+    for copy in held_out:
+        copy.wait()
 
 
 def attend(place, tokens, embed, bias, pieces):
@@ -282,21 +369,29 @@
         attend_kernel,
         out_shape=(
             struct((4, 256, 1024)), struct((3, 1024, 256)), square, square, square,
-            block, block, block, block, struct((1024, 128), jnp.float32),
+            block, block, block, block, struct((1024, 128), jnp.float32), struct((9, PIECE, 256)),
         ),
-        in_specs=[SMEM] + [VMEM] * 6 + [ANY] * 4,
-        out_specs=(VMEM,) * 10,
+        in_specs=[SMEM] + [VMEM] * 2 + [ANY] * 13,
+        out_specs=(VMEM,) * 10 + (ANY,),
         scratch_shapes=[
+            pltpu.VMEM((4, 256, 1024), jnp.bfloat16),
+            pltpu.VMEM((9, PIECE, 256), jnp.bfloat16),
             pltpu.VMEM((4, 1024, 64), jnp.bfloat16),
             pltpu.VMEM((4, 1024, 64), jnp.bfloat16),
             pltpu.VMEM((4, 1024, 128), jnp.bfloat16),
             pltpu.VMEM((4, 1024, 64), jnp.bfloat16),
             pltpu.VMEM((16, 256), jnp.bfloat16),
             pltpu.SemaphoreType.DMA((5,)),
+            pltpu.SemaphoreType.DMA((4,)),
+            pltpu.SemaphoreType.DMA((9,)),
+            pltpu.SemaphoreType.DMA((9,)),
         ],
-        compiler_params=pltpu.CompilerParams(vmem_limit_bytes=40 << 20),
+        compiler_params=pltpu.CompilerParams(vmem_limit_bytes=48 << 20),
+        cost_estimate=pl.CostEstimate(
+            flops=16_000_000_000, bytes_accessed=24_000_000, transcendentals=4_194_304
+        ),
         name="attend",
-    )(place, *tokens, embed, bias, *pieces)
+    )(place, embed, bias, *tokens, *pieces)
 
 
 def attend_back_kernel(
@@ -367,6 +462,9 @@
         scratch_shapes=[pltpu.VMEM((4, 1024, 64), jnp.bfloat16)] * 5
         + [pltpu.VMEM((4, 64, 1024), jnp.float32)] * 2,
         compiler_params=pltpu.CompilerParams(vmem_limit_bytes=40 << 20),
+        cost_estimate=pl.CostEstimate(
+            flops=20_000_000_000, bytes_accessed=12_000_000, transcendentals=4_194_304
+        ),
         name="attend_back",
     )(place, query, key, value, lse, weight, *grads)
 
@@ -386,14 +484,20 @@
     return (scaled - row_mean(scaled) - xhat * row_mean(scaled * xhat)) * scale
 
 
+def target_piece(targets, k, ry, rx):
+    return targets[k - 1].at[ry, rx] if k == 1 else targets[k - 1].at[rx, ry]
+
+
 def layer_kernel(
     place, h0, h1, h2, h3, tokens, cotangent, embed, vectors, bias_up, out_head, *refs
 ):
-    pieces = refs[:32]
-    (block_out, resid_grad, g0, g1, g2, g3, sums, sums_up, head_grad) = refs[32:41]
-    grads_own, grads_other = refs[41:44], refs[44:47]
+    stack = refs[15]
+    pieces = (refs[:15], [stack.at[n] for n in range(9)] + list(refs[16:22]))
+    refs = refs[22:]
+    (block_out, resid_grad, g0, g1, g2, g3, sums, sums_up, head_grad) = refs[:9]
+    grads_own, grads_other = refs[9:12], refs[12:15]
     (w_out, w_up, w_down, edge_up, edge_down, hidden, slope, grad_up, grad_down,
-     grad_out, acc, sem, sem_out) = refs[47:]
+     grad_out, acc, sem, sem_out) = refs[15:]
 
     def fetch(z, y):
         made = {"out": [], "up": [], "down": []}
@@ -402,7 +506,7 @@
                 case = 2 * k + (y ^ ry)
                 for r in range(4):
                     rx, rc = r // 2, r % 2
-                    source = pieces[rc * 16 + rx * 8 + ry * 4 + SLOT[z][k]]
+                    source = pieces[rc][BUFFER[z][rx * 8 + ry * 4 + SLOT[z][k]]]
                     column = place[3] ^ r
                     for name, row_a, row_b, offset, step, _ in SEGMENTS[case]:
                         count = row_b - row_a
@@ -531,7 +635,7 @@
         targets = grads_other if rc else grads_own
         for case in range(2, 8):
             ry = place[2] ^ (case % 2)
-            piece = targets[case // 2 - 1].at[ry, rx]
+            piece = target_piece(targets, case // 2, ry, rx)
             for row_a, row_b, offset, count in send(case, "up", grad_up, column):
                 started.append(
                     (grad_up.at[pl.ds(column * 4, 4), row_a:row_b, :],
@@ -568,7 +672,7 @@
         rx, rc = r // 2, r % 2
         column = place[3] ^ r
         targets = grads_other if rc else grads_own
-        piece = targets[0].at[place[2], rx]
+        piece = target_piece(targets, 1, place[2], rx)
         last.append((grad_out.at[column], piece.at[0:1024, :]))
     for source, target in last:
         pltpu.make_async_copy(source, target, sem_out.at[1]).start()
@@ -588,7 +692,7 @@
             struct((8, D), jnp.float32), struct((16, 256), jnp.float32),
             struct((4, 16, 256), jnp.float32),
         ) + (grads,) * 6,
-        in_specs=[SMEM] + [VMEM] * 10 + [ANY] * 32,
+        in_specs=[SMEM] + [VMEM] * 10 + [ANY] * 22,
         out_specs=(VMEM,) * 9 + (ANY,) * 6,
         scratch_shapes=[
             pltpu.VMEM((4, 1024, 256), jnp.bfloat16),
@@ -606,6 +710,9 @@
             pltpu.SemaphoreType.DMA((2,)),
         ],
         compiler_params=pltpu.CompilerParams(vmem_limit_bytes=60 << 20),
+        cost_estimate=pl.CostEstimate(
+            flops=15_000_000_000, bytes_accessed=40_000_000, transcendentals=2_097_152
+        ),
         name="layer",
     )(place, *heads, tokens, cotangent, embed, vectors, bias_up, out_head, *pieces)
 
@@ -874,14 +981,15 @@
 AXES = ("dp", "fsdp")
 
 
-def send(values, route):
+def send(values, route, name="move"):
     pairs = []
     for n in range(32):
         there = route(n // 8, n // 4 % 2, n // 2 % 2, n % 2)
         if there is not None:
             z, y, x, c = there
             pairs.append((n, z * 8 + y * 4 + x * 2 + c))
-    return lax.ppermute(values, AXES, pairs)
+    with jax.named_scope(name):
+        return lax.ppermute(values, AXES, pairs)
 
 
 def to_core(z, y, x, c):
@@ -911,33 +1019,66 @@
 EVERY = (to_core, to_x, to_y, to_near, to_far)
 
 
-def total(values):
+def total(values, name):
     for route in EVERY:
-        values = values + send(values, route)
+        values = values + send(values, route, name)
     return values
 
 
-def gather_pieces(own, z):
+def after(values, *earlier):
+    return lax.optimization_barrier((values, *earlier))[0]
+
+
+PLANES = ((1, 2, 3), (0, 1, 3), (0, 2), (0, 1, 2, 3))
+
+
+def gather_pieces(own, z, y, tokens, run_attend):
+    def across(name, values, n):
+        return send(values, only(to_x, PLANES[n]), name)
+
     outer = (z == 0) | (z == 3)
-    got_1 = send(own, only(to_far, (0, 3)))
-    pass_1 = jnp.where(outer, own, got_1)
-    got_2 = send(pass_1, to_near)
-    got_3 = send(own, only(to_far, (1, 2)))
-    pass_2 = jnp.where(outer, got_3, own)
-    got_4 = send(pass_2, to_near)
-    slot_b = jnp.where(z == 2, got_1, got_2)
-    slot_v = jnp.where(z == 1, got_1, jnp.where(z == 2, got_2, got_3))
-    slots = [own, slot_b, slot_v, got_4]
-    planes = [(1, 2, 3), (0,), (0, 1, 2, 3), (0, 1, 2, 3)]
-    own_y = [send(piece, to_y) for piece in slots]
-    over_x = [send(piece, only(to_x, p)) for piece, p in zip(slots, planes)]
-    over_xy = [
-        send(over_x[n], only(to_y, planes[n])) if n == 2 else send(own_y[n], only(to_x, planes[n]))
-        for n in range(4)
+    first = send(own, lambda z, y, x, c: ((2, 0, 3, 1)[z], y, x, c), "first")
+    y0 = send(own, to_y, "y0")
+    x0 = across("x0", own, 0)
+    tokens_c = send(tokens, to_core, "tok_c")
+    second = send(jnp.where(outer, own, first), to_near, "second")
+    crossed = send(
+        after(own, first), lambda z, y, x, c: (3 - z, y, x, c) if z in (1, 2) else None, "crossed"
+    )
+    y1 = send(after(first, y0, x0), to_y, "y1")
+    x1 = across("x1", after(first, x0), 1)
+    tokens_x = send(after(tokens, first, x0), to_x, "tok_x")
+    third = send(after(crossed, second), only(to_near, (1, 2)), "third")
+    y2 = send(after(second, y1), to_y, "y2")
+    x_a = send(after(jnp.where(z % 2 == 0, second, y0), x1), to_x, "xa")
+    last = jnp.where(outer, third, crossed)
+    tokens_xc = send(after(tokens_x, third), to_core, "tok_xc")
+    y3 = send(after(last, y2), to_y, "y3")
+    y_b = send(after(jnp.where(z == 2, x0, x1), y2), to_y, "yb")
+    yx2 = across("yx2", after(y2, last), 2)
+    x3 = across("x3", after(last, y2), 3)
+    tail_0, tail_1, tail_2 = (
+        jnp.where(y == 1, mine[TAIL:], other[TAIL:])
+        for mine, other in ((own, y0), (first, y1), (second, y2))
+    )
+    attended = run_attend(
+        after(last, y2), (own, y0, first, y1, second, y2, last, x0, x1),
+        (tokens, tokens_c, tokens_x, tokens_xc),
+        jnp.where(z == 3, tail_0, jnp.where(z == 1, tail_1, tail_2)),
+        jnp.where(z == 0, tail_0, jnp.where(z == 2, tail_1, tail_2)),
+    )
+    attended = lax.optimization_barrier((*attended, x_a, y3, yx2))[: len(attended)]
+    stack = send(attended[-1], to_core, "stack")
+    yx3 = across("yx3", after(y3, attended[-1]), 3)
+    later = [
+        send(after(piece, attended[-1]), only(to_core, planes), name)
+        for piece, planes, name in (
+            (x_a, (0, 1, 2, 3), "cxa"), (y3, (0, 1, 2, 3), "cy3"), (y_b, (0, 1, 2, 3), "cyb"),
+            (yx2, PLANES[2], "cyx2"), (x3, (0, 1, 2, 3), "cx3"), (yx3, (0, 1, 2, 3), "cyx3"),
+        )
     ]
-    mine = slots + own_y + over_x + over_xy
-    core = [send(piece, only(to_core, planes[n % 4])) for n, piece in enumerate(mine)]
-    return slots, own_y, mine + core
+    mine = [own, first, second, last, y0, y1, y2, x0, x1, x_a, y3, y_b, yx2, x3, yx3]
+    return attended[:-1], [*mine, stack, *later]
 
 
 def add(left, right):
@@ -960,65 +1101,74 @@
     z, y = shard // 2, shard % 2
     place = jnp.stack([shard, z, y, j, block_start[0], block_length[0]]).astype(jnp.int32)
     flat = jnp.pad(master, (0, LANE_ROWS * 128 - SHARD)).reshape(LANE_ROWS, 128)
-    own = pack(place, flat)
-    tokens_c = send(tokens, to_core)
-    tokens_x = send(tokens, to_x)
-    tokens_xc = send(tokens_x, to_core)
-
-    tail = own[TAIL : TAIL + 16]
-    zero = jnp.zeros_like(tail)
-    shared = jnp.concatenate([jnp.where(shard == 7, tail, zero), jnp.where(shard == 1, tail, zero)])
+    vec_rows = jnp.pad(master[SHARD - 3584 :].reshape(14, 256), ((0, 2), (0, 0)))
+    head_rows = jnp.pad(master[SHARD - 896 :], (0, 3200)).reshape(16, 256)
+    tail = low(jnp.where(shard == 7, vec_rows, head_rows))
+    tail_x = send(tail, to_x, "tail_x")
+    tail_c = send(jnp.concatenate([tail, tail_x]), to_core, "tail_c")
+    own = pack(place, flat, jnp.concatenate([tail, tail_c[:16], tail_x, tail_c[16:]]))
     here = (jnp.arange(4) == j)[:, None, None]
-    shared = total(jnp.where(here, shared[None], jnp.zeros_like(shared)[None]))
-    vec = wide(shared[:, :16])
-    out_head = shared[:, 16:]
-    vec_own = lax.dynamic_index_in_dim(vec, j, 0, keepdims=False)
     time_frac = timestep[0].astype(jnp.float32) / 5000.0
-    full = vec.transpose(1, 0, 2).reshape(16, D)
-    embed = time_frac * full[12:13] + full[13:14]
-    vectors = jnp.concatenate([full[2:4], full[8:12], jnp.zeros((2, D), jnp.float32)])
-    bias_up = vec[:, 4:8].reshape(16, 256)
-
-    slots, slots_y, pieces = gather_pieces(own, z)
-
-    (stream, weight, query, key, value, h0, h1, h2, h3, lse) = attend(
-        place,
-        (tokens, tokens_c, tokens_x, tokens_xc),
-        embed,
-        vec_own[0:8],
-        (slots[0], slots_y[0], slots[1], slots_y[1]),
-    )
+    vectors = {}
+
+    def absolute(relative):
+        blocks = relative.reshape(4, 16, 256)
+        blocks = jnp.where(j % 2 == 1, jnp.concatenate([blocks[1:2], blocks[0:1], blocks[3:4], blocks[2:3]]), blocks)
+        return jnp.where(j // 2 == 1, jnp.concatenate([blocks[2:4], blocks[0:2]]), blocks)
+
+    def run_attend(ready, held, all_tokens, vec_tail, head_tail):
+        vec = wide(absolute(vec_tail))
+        full = vec.transpose(1, 0, 2).reshape(16, D)
+        vec_own = wide(vec_tail[:16])
+        vectors["embed"] = time_frac * full[12:13] + full[13:14]
+        vectors["rows"] = jnp.concatenate([full[2:4], full[8:12], jnp.zeros((2, D), jnp.float32)])
+        vectors["up"] = vec[:, 4:8].reshape(16, 256)
+        vectors["head"] = absolute(head_tail)
+        return attend(after(place, ready), all_tokens, vectors["embed"], vec_own[0:8], held)
+
+    attended, pieces = gather_pieces(own, z, y, tokens, run_attend)
+    stream, weight, query, key, value, h0, h1, h2, h3, lse = attended
 
     def to_relative(r):
         return lambda z, y, x, c: (z, y, x ^ (r // 2), c ^ (r % 2))
 
-    def exchange(blocks):
-        return [blocks[0]] + [send(blocks[r], to_relative(r)) for r in range(1, 4)]
+    def exchange(blocks, name):
+        return [blocks[0]] + [send(blocks[r], to_relative(r), name) for r in range(1, 4)]
 
     (block_out, resid_grad, g0, g1, g2, g3, sums, sums_up, head_grad, *grads) = layer(
-        place, exchange((h0, h1, h2, h3)), tokens, cotangent, embed, vectors, bias_up, out_head, pieces
+        place, exchange((h0, h1, h2, h3), "heads"), tokens, cotangent, vectors["embed"],
+        vectors["rows"], vectors["up"], vectors["head"], pieces,
     )
     grads_own, grads_other = grads[:3], grads[3:]
 
+    moved = {k: send(grads_other[k - 1], to_core, f"rc{k}") for k in (2, 1)}
+    moved[3] = send(after(grads_other[2], moved[2], moved[1]), to_core, "rc3")
+
+    def over_cores(k, a, b):
+        return add(grads_own[k - 1][a, b], moved[k][a, b])
+
+    grad_heads = exchange((g0, g1, g2, g3), "heads_grad")
+    starts = {
+        name: after(low(over_cores(k, 1, b)), *grad_heads)
+        for name, k, b in (("d1", 1, 1), ("d2", 2, 1), ("e1", 1, 0), ("e2", 2, 0))
+    }
+    d1 = send(starts["d1"], to_y, "d1")
+    d2 = send(starts["d2"], to_x, "d2")
+    e1 = send(starts["e1"], to_y, "e1")
+    e2 = send(starts["e2"], to_x, "e2")
+
     (q_grad, k_grad, v_grad, kept, sent, sums_qkv) = attend_back(
-        place, query, key, value, lse, weight, exchange((g0, g1, g2, g3))
-    )
-
-    part = {}
-    for k in (3, 2, 1):
-        both = low(add(grads_own[k - 1], send(grads_other[k - 1], to_core)))
-        if k == 1:
-            both = low(add(both[0], send(both[1], to_y)))
-            part[k] = low(add(both[0], send(both[1], to_x)))
-        else:
-            both = low(add(both[:, 0], send(both[:, 1], to_x)))
-            part[k] = low(add(both[0], send(both[1], to_y)))
-    even = z % 2 == 0
-    outer = (z == 0) | (z == 3)
-    inner_part = add(
-        jnp.where(even, part[2], part[1]), send(jnp.where(even, part[1], part[2]), to_near)
-    )
-    inner_sum = add(inner_part, send(low(inner_part), only(to_far, (0, 3))))
+        after(place, *starts.values()),
+        query, key, value, lse, weight, grad_heads,
+    )
+
+    q_grad, k_grad, v_grad, kept, sent, sums_qkv, d1, d2 = lax.optimization_barrier(
+        (q_grad, k_grad, v_grad, kept, sent, sums_qkv, d1, d2)
+    )
+    f1 = send(low(over_cores(1, 0, 1) + wide(d1)), to_x, "f1")
+    f2 = send(low(over_cores(2, 0, 1) + wide(d2)), to_y, "f2")
+    d3 = send(after(low(over_cores(3, 1, 1)), e1, e2), to_x, "d3")
+    e3 = send(after(low(over_cores(3, 1, 0)), f1), to_x, "e3")
 
     rows = stream.reshape(1024, D)
     w_grads = [low(product_inner(rows, grad)) for grad in (q_grad, k_grad, v_grad)]
@@ -1026,26 +1176,31 @@
     piece_0 = jnp.concatenate([w_grads[0], w_grads[1][:528], rest])
     piece_1 = jnp.concatenate([w_grads[1][512:], w_grads[2], rest, rest[:16]])
     low_row = y == 0
-    part[0] = low(
-        add(
-            jnp.where(low_row, piece_0, piece_1),
-            send(jnp.where(low_row, piece_1, piece_0), to_y),
-        )
-    )
-    outer_part = add(
-        jnp.where(even, part[0], part[3]), send(jnp.where(even, part[3], part[0]), to_near)
-    )
-    outer_sum = add(outer_part, send(low(outer_part), only(to_far, (1, 2))))
-
-    from_core = send(sent, to_core)
+    ry0 = send(after(jnp.where(low_row, piece_1, piece_0), e1), to_y, "ry0")
+    f3 = send(low(over_cores(3, 0, 1) + wide(after(d3, ry0))), to_y, "f3")
+
+    kept_1, sent_1 = combine(
+        place, (grads_own[1], moved[2], e2, f2), (grads_own[0], moved[1], e1, f1)
+    )
+    inner_part = low(add(kept_1, send(sent_1, to_near, "rz_inner1")))
+    inner_last = send(inner_part, only(to_far, (0, 3)), "rz_inner2")
+    kept_0, sent_0 = combine(
+        place, (jnp.where(low_row, piece_0, piece_1), ry0), (grads_own[2], moved[3], e3, f3)
+    )
+    outer_part = low(add(kept_0, send(sent_0, to_near, "rz_outer1")))
+    outer_last = send(outer_part, only(to_far, (1, 2)), "rz_outer2")
+
+    from_core = send(sent, to_core, "in_c")
+    in_x = send(after(low(kept[1] + wide(from_core[1])), e3), to_x, "in_x")
     input_grad = (
         resid_grad
         + kept[0]
         + wide(from_core[0])
-        + wide(send(low(kept[1] + wide(from_core[1])), to_x))
+        + wide(in_x)
     )
 
     time_grad = sums[6] + sums_qkv[0]
+    rows_of = [sums[0], sums[1]]
     vec_grad = jnp.concatenate(
         [
             jnp.where(here, sums_qkv[1:3, :256][None], 0.0),
@@ -1059,12 +1214,33 @@
         ],
         axis=1,
     )
-    extra = lax.dynamic_index_in_dim(total(vec_grad), j, 0, keepdims=False)
-    vector_grad = extra[:14].reshape(-1)
-
-    grad_flat, square = unpack(place, jnp.where(outer, outer_sum, inner_sum), extra)
-    grad_shard = grad_flat.reshape(-1)[:SHARD]
-    grad_norm = jnp.sqrt(jnp.sum(total(square)))
+    vec_grad = vec_grad.reshape(2, 2, 32, 256)
+    core_bit, x_bit = j % 2, j // 2
+    kept_c = jnp.where(core_bit == 1, vec_grad[:, 1], vec_grad[:, 0])
+    sent_c = jnp.where(core_bit == 1, vec_grad[:, 0], vec_grad[:, 1])
+    by_x = kept_c + send(sent_c, to_core, "vec_c")
+    kept_x = jnp.where(x_bit == 1, by_x[1], by_x[0])
+    mine = kept_x + send(jnp.where(x_bit == 1, by_x[0], by_x[1]), to_x, "vec_x")
+
+    grad_flat, square = unpack(after(place, input_grad), inner_part, inner_last, outer_part, outer_last)
+    mine = jnp.concatenate([mine, square.reshape(4, 256), jnp.zeros((4, 256), jnp.float32)])
+    for route in (to_y, to_near, to_far):
+        mine = mine + send(mine, route, "norm")
+    vec_sum, head_sum = mine[:14].reshape(-1), mine[16:20].reshape(-1)[:896]
+    vector_grad = vec_sum
+    square_sum = (jnp.sum(mine[32:36]) + jnp.sum(vec_sum * vec_sum) + jnp.sum(head_sum * head_sum))
+    square_sum = jnp.broadcast_to(square_sum, (8, 128))
+    for route in (to_x, to_core):
+        square_sum = square_sum + send(square_sum, route, "norm")
+    grad_norm = jnp.sqrt(square_sum[0, 0])
+    grad_flat = grad_flat.reshape(-1)
+    edge = grad_flat[SHARD - 3584 : SHARD]
+    edge = jnp.where(
+        shard == 7,
+        vec_sum,
+        jnp.where(shard == 1, jnp.concatenate([edge[: 3584 - 896], head_sum]), edge),
+    )
+    grad_shard = lax.dynamic_update_slice(grad_flat, edge, (SHARD - 3584,))[:SHARD]
     clip_limit = 4.0 * math.sqrt(PARAMS)
     clipped = grad_shard * (clip_limit / jnp.maximum(grad_norm, clip_limit))
     new_first = 0.9 * first_moment + 0.1 * clipped

time: 494 us -> 417 us (0.84); the launches traced: 484 us -> 415 us
  waiting for transfers between devices: 233 us -> 198 us
  starting transfers between devices: 96.1 us -> 64 us
  local copies, waits for them, and re-layouts: 28 us -> 11.9 us
  Pallas kernels: 80.6 us -> 96.5 us
    ppermute x72 -> x59, waiting for transfers between devices: 233 us -> 198 us  [send(): return lax.ppermute(values, AXES, pairs)]
    ppermute x72 -> x59, starting transfers between devices: 96.1 us -> 64 us  [send(): return lax.ppermute(values, AXES, pairs)]
    pallas_call x0 -> x2, Pallas kernels: none -> 10.9 us  [combine(): pl.pallas_call(partial(combine_kernel, len(first)), grid=(blocks,), out_s...]
    unnamed x146 -> x107, local copies, waits for them, and re-layouts: 14.6 us -> 5.13 us
    pallas_call x2 -> x0, local copies, waits for them, and re-layouts: 6.2 us -> none  [layer(): pl.pallas_call(layer_kernel, out_shape=(struct((256, D)), struct((256, D)...]
    select_n x8 -> x11, other arithmetic: 11.4 us -> 6.96 us  [the longest x1 1.54 us: gather_pieces(): y_b = send(after(jnp.where(z == 2, x0, x1), y2), to_y, 'yb')]
    convert_element_type x9 -> x10, other arithmetic: 13.5 us -> 15.1 us  [low(): return values.astype(jnp.bfloat16)]
  transfers between devices with their start and end apart: 72 -> 59, of which waited for: 36 -> 33; matrix products, arithmetic and copies ran while one was open for 8% -> 8% of each run, Pallas kernels for 7% -> 12%
where the time goes in v2:
time: 417 us; the launch traced here: 415 us
  waiting for transfers between devices  198 us (47%)
  Pallas kernels  96.5 us (23%)
  starting transfers between devices  64 us (15%)
  other arithmetic  35.4 us (8%)
  local copies, waits for them, and re-layouts  11.9 us (3%)
  between operations  7.41 us (2%)
    ppermute x59, waiting for transfers between devices, send(): return lax.ppermute(values, AXES, pairs)  198 us
    ppermute x59, starting transfers between devices, send(): return lax.ppermute(values, AXES, pairs)  64 us
    pallas_call x1, Pallas kernels, layer(): pl.pallas_call(layer_kernel, out_shape=(struct((256, D)), struct((256, D)...  43.5 us
    pallas_call x1, Pallas kernels, attend_back(): pl.pallas_call(attend_back_kernel, out_shape=(square, square, square, str...  20.4 us
    pallas_call x1, Pallas kernels, attend(): pl.pallas_call(attend_kernel, out_shape=(struct((4, 256, 1024)), struct((...  17.3 us
    convert_element_type x10, other arithmetic, low(): return values.astype(jnp.bfloat16)  15.1 us
    pallas_call x2, Pallas kernels, combine(): pl.pallas_call(partial(combine_kernel, len(first)), grid=(blocks,), out_s...  10.9 us
  transfers between devices with their start and end apart: 59, of which 33 were waited for; matrix products, arithmetic and copies ran while one was open for 8% of the time, Pallas kernels for 12%

profile of v2, /device:TPU:0, one launch (start us, length us, event | category | flops | bytes accessed | tf_op | source)
XLA Modules:
  0.0 415.2 jit_solution(14969818651477310092)
XLA Ops:
  2.3 3.0 collective-permute-start
  5.3 1.6 collective-permute-done
  6.9 1.5 pad_bitcast_fusion.flat
  10.7 3.4 collective-permute-start.2
  14.1 1.6 collective-permute-start.7
  15.7 1.9 collective-permute-start.6
  17.6 14.7 %collective-permute-done.2.p2.refs_1_ = bf16[1600,256]{1,0:T(8,128)(2,1)S(1)} collective-permute-done((bf16[1600,256]{1,0:T(8,128)(2,1)S(1)}, bf16[1600,256]{1,0:T(8,128)(2,1)S(1)}, u32[]{:S(2)}, u32[]{:S(2)}) %collective-permute-start.2) | collective-permute-done | bytes 819232 | tf_op jit(solution)/shard_map/first/ppermute | solution.py:992
  32.4 2.3 collective-permute-start.4
  34.7 1.6 collective-permute-start.3
  36.3 2.1 collective-permute-start.8
  38.4 3.4 collective-permute-start.13
  41.8 11.1 %collective-permute-done.4.p4.refs_2_ = bf16[1600,256]{1,0:T(8,128)(2,1)} collective-permute-done((bf16[1600,256]{1,0:T(8,128)(2,1)S(1)}, bf16[1600,256]{1,0:T(8,128)(2,1)}, u32[]{:S(2)}, u32[]{:S(2)}) %collective-permute-start.4) | collective-permute-done | bytes 819232 | tf_op jit(solution)/shard_map/second/ppermute | solution.py:992
  54.2 2.1 collective-permute-done.8.p3.refs_5_
  57.2 1.7 collective-permute-start.9
  59.6 1.6 collective-permute-start.11
  63.0 11.4 %collective-permute-done.11.t2 = bf16[256,1024]{1,0:T(8,128)(2,1)S(1)} collective-permute-done((bf16[256,1024]{1,0:T(8,128)(2,1)S(1)}, bf16[256,1024]{1,0:T(8,128)(2,1)S(1)}, u32[]{:S(2)}, u32[]{:S(2)}) %collective-permute-start.11) | collective-permute-done | bytes 524320 | tf_op jit(solution)/shard_map/tok_x/ppermute | solution.py:992
  78.7 1.5 collective-permute-start.15
  80.2 3.4 collective-permute-start.16
  83.7 17.3 %attend.1 = (bf16[4,256,1024]{2,1,0:T(8,128)(2,1)}, bf16[3,1024,256]{2,1,0:T(8,128)(2,1)}, bf16[1024,256]{1,0:T(8,128)(2,1)S(1)}, bf16[1024,256]{1,0:T(8,128)(2,...) custom-call(s32[6]{0:T(128)S(1)} %stack.19.place, ...), custom_call_target="tpu_custom_call" | custom-call | flops 16000000000 | bytes 24000000 | tf_op jit(solution)/shard_map/attend/pallas_call | solution.py:368
  101.1 8.1 %collective-permute-done.16.refs_12_ = bf16[1600,256]{1,0:T(8,128)(2,1)} collective-permute-done((bf16[1600,256]{1,0:T(8,128)(2,1)}, bf16[1600,256]{1,0:T(8,128)(2,1)}, u32[]{:S(2)}, u32[]{:S(2)}) %collective-permute-start.16) | collective-permute-done | bytes 819232 | tf_op jit(solution)/shard_map/yx2/ppermute | solution.py:992
  109.2 1.5 broadcast_select_fusion.2
  111.1 1.5 collective-permute-start.21
  113.1 1.9 collective-permute-start.27
  115.0 16.1 %collective-permute-done.20.refs_11_ = bf16[1600,256]{1,0:T(8,128)(2,1)S(1)} collective-permute-done((bf16[1600,256]{1,0:T(8,128)(2,1)S(1)}, bf16[1600,256]{1,0:T(8,128)(2,1)S(1)}, u32[]{:S(2)}, u32[]{:S(2)}) %collective-permute-start.20) | collective-permute-done | bytes 819232 | tf_op jit(solution)/shard_map/yb/ppermute | solution.py:992
  132.2 1.5 collective-permute-done.17.h1
  133.7 1.5 collective-permute-start.18
  135.2 14.6 %collective-permute-done.22.refs_14_ = bf16[1600,256]{1,0:T(8,128)(2,1)S(1)} collective-permute-done((bf16[1600,256]{1,0:T(8,128)(2,1)S(1)}, bf16[1600,256]{1,0:T(8,128)(2,1)S(1)}, u32[]{:S(2)}, u32[]{:S(2)}) %collective-permute-start.22) | collective-permute-done | bytes 819232 | tf_op jit(solution)/shard_map/yx3/ppermute | solution.py:992
  152.1 3.4 collective-permute-done.19.h3
  161.4 43.5 %layer.1 = (bf16[256,1024]{1,0:T(8,128)(2,1)}, f32[256,1024]{1,0:T(8,128)}, bf16[256,256]{1,0:T(8,128)(2,1)}, bf16[256,256]{1,0:T(8,128)(2,1)}, bf16[256,256]{1,...) custom-call(s32[6]{0:T(128)} %copy-done.1, ...), custom_call_target="tpu_custom_call" | custom-call | flops 15000000512 | bytes 40000000 | tf_op jit(solution)/shard_map/layer/pallas_call | solution.py:688
  207.4 7.0 %collective-permute-done.34.refs_1_ = bf16[2,2,1600,256]{3,2,1,0:T(8,128)(2,1)S(1)} collective-permute-done((bf16[2,2,1600,256]{3,2,1,0:T(8,128)(2,1)}, bf16[2,2,1600,256]{3,2,1,0:T(8,128)(2,1)S(1)}, u32[]{:S(2)}, u32[]{:S(2)}) %collective-permute-start.34) | collective-permute-done | bytes 3276832 | tf_op jit(solution)/shard_map/rc2/ppermute | solution.py:992
  214.4 3.0 fusion.8
  218.0 2.0 fusion.7
  220.7 1.9 collective-permute-start.35
  224.2 20.4 %attend_back.1 = (bf16[1024,256]{1,0:T(8,128)(2,1)S(1)}, bf16[1024,256]{1,0:T(8,128)(2,1)S(1)}, bf16[1024,256]{1,0:T(8,128)(2,1)S(1)}, f32[2,256,1024]{2,1,0:T(8...) custom-call(s32[6]{0:T(128)S(1)} %copy-done.2, bf16[1024,256]{1,0:T(8,128)(2,1)S(1)} %copy-done.7, ...), custom_call_target="tpu_custom_call" | custom-call | flops 20000000000 | bytes 12000000 | tf_op jit(solution)/shard_map/attend_back/pallas_call | solution.py:454
  248.4 10.0 %collective-permute-done.46.refs_6_ = bf16[1600,256]{1,0:T(8,128)(2,1)S(1)} collective-permute-done((bf16[1600,256]{1,0:T(8,128)(2,1)S(1)}, bf16[1600,256]{1,0:T(8,128)(2,1)S(1)}, u32[]{:S(2)}, u32[]{:S(2)}) %collective-permute-start.46) | collective-permute-done | bytes 819232 | tf_op jit(solution)/shard_map/e1/ppermute | solution.py:992
  258.4 1.7 collective-permute-start.49
  260.2 1.5 fusion.2
  261.7 1.5 collective-permute-start.39
  263.2 1.8 fusion.10
  265.6 2.6 fusion.1
  268.9 14.0 %collective-permute-done.39.refs_7_ = bf16[1600,256]{1,0:T(8,128)(2,1)S(1)} collective-permute-done((bf16[1600,256]{1,0:T(8,128)(2,1)S(1)}, bf16[1600,256]{1,0:T(8,128)(2,1)S(1)}, u32[]{:S(2)}, u32[]{:S(2)}) %collective-permute-start.39) | collective-permute-done | bytes 819232 | tf_op jit(solution)/shard_map/f1/ppermute | solution.py:992
  284.4 16.1 %collective-permute-done.50 = bf16[1600,256]{1,0:T(8,128)(2,1)S(1)} collective-permute-done((bf16[1600,256]{1,0:T(8,128)(2,1)S(1)}, bf16[1600,256]{1,0:T(8,128)(2,1)S(1)}, u32[]{:S(2)}, u32[]{:S(2)}) %collective-permute-start.50) | collective-permute-done | bytes 819232 | tf_op jit(solution)/shard_map/d3/ppermute | solution.py:992
  303.8 5.7 %combine.2 = (bf16[1600,256]{1,0:T(8,128)(2,1)}, bf16[1600,256]{1,0:T(8,128)(2,1)}) custom-call(s32[6]{0:T(128)} %copy-done.1, bf16[2,2,1600,256]{3,2,1,0:T(8,128)(2,1)} %get-tuple-element.138.refs_0_, bf16[2,2,1600,256]{3,2,1,0:T(8,128)(2,1)} %copy-done.19, bf16[1600,256]{1,0:T(8,128)(2,1)} %copy-done.32, ...), custom_call_target="tpu_custom_call" | custom-call | tf_op jit(solution)/shard_map/combine/pallas_call | solution.py:257
  309.7 6.1 %collective-permute-done.40.refs_4_ = bf16[1600,256]{1,0:T(8,128)(2,1)} collective-permute-done((bf16[1600,256]{1,0:T(8,128)(2,1)}, bf16[1600,256]{1,0:T(8,128)(2,1)}, u32[]{:S(2)}, u32[]{:S(2)}) %collective-permute-start.40) | collective-permute-done | bytes 819232 | tf_op jit(solution)/shard_map/e3/ppermute | solution.py:992
  315.8 1.8 collective-permute-done.51.refs_5_
  317.7 5.3 %combine.3 = (bf16[1600,256]{1,0:T(8,128)(2,1)}, bf16[1600,256]{1,0:T(8,128)(2,1)}) custom-call(s32[6]{0:T(128)} %copy-done.1, bf16[1600,256]{1,0:T(8,128)(2,1)} %get-tuple-element.197.refs_0_, bf16[1600,256]{1,0:T(8,128)(2,1)} %copy-done.26, bf16[2,2,1600,256]{3,2,1,0:T(8,128)(2,1)} %get-tuple-element.157.refs_2_, bf16[2,2,1600,256]{3,2,1,0:T(8,128)(2,1)} %copy-done.17, ...), custom_call_target="tpu_custom_call" | custom-call | tf_op jit(solution)/shard_map/combine/pallas_call | solution.py:257
  324.4 4.7 %collective-permute-done.47 = bf16[1600,256]{1,0:T(8,128)(2,1)} collective-permute-done((bf16[1600,256]{1,0:T(8,128)(2,1)}, bf16[1600,256]{1,0:T(8,128)(2,1)}, u32[]{:S(2)}, u32[]{:S(2)}) %collective-permute-start.47) | collective-permute-done | bytes 819232 | tf_op jit(solution)/shard_map/rz_inner1/ppermute | solution.py:992
  330.4 6.8 %collective-permute-start.48 = (bf16[1600,256]{1,0:T(8,128)(2,1)S(1)}, bf16[1600,256]{1,0:T(8,128)(2,1)S(1)}, u32[]{:S(2)}, u32[]{:S(2)}) collective-permute-start(bf16[1600,256]{1,0:T(8,128)(2,1)S(1)} %add_convert_fusion.2.inner), channel_id=1, source_target_pairs={{0,16},{1,17},{2,18},{3,19},{4,20},{5,21},{6,22},{7,23},{24,8},{25... | collective-permute-start | bytes 2457608 | tf_op jit(solution)/shard_map/rz_inner2/ppermute | solution.py:992
  337.2 1.5 collective-permute-start.41
  338.7 5.7 %collective-permute-done.52 = bf16[1600,256]{1,0:T(8,128)(2,1)S(1)} collective-permute-done((bf16[1600,256]{1,0:T(8,128)(2,1)}, bf16[1600,256]{1,0:T(8,128)(2,1)S(1)}, u32[]{:S(2)}, u32[]{:S(2)}) %collective-permute-start.52) | collective-permute-done | bytes 819232 | tf_op jit(solution)/shard_map/rz_outer1/ppermute | solution.py:992
  346.0 1.5 collective-permute-start.43
  347.5 2.4 collective-permute-done.43
  350.0 2.3 fusion.4
  352.3 6.0 %collective-permute-done.48.inner_last = bf16[1600,256]{1,0:T(8,128)(2,1)S(1)} collective-permute-done((bf16[1600,256]{1,0:T(8,128)(2,1)S(1)}, bf16[1600,256]{1,0:T(8,128)(2,1)S(1)}, u32[]{:S(2)}, u32[]{:S(2)}) %collective-permute-start.48) | collective-permute-done | bytes 819232 | tf_op jit(solution)/shard_map/rz_inner2/ppermute | solution.py:992
  359.2 20.8 %collective-permute-done.53.outer_last = bf16[1600,256]{1,0:T(8,128)(2,1)} collective-permute-done((bf16[1600,256]{1,0:T(8,128)(2,1)S(1)}, bf16[1600,256]{1,0:T(8,128)(2,1)}, u32[]{:S(2)}, u32[]{:S(2)}) %collective-permute-start.53) | collective-permute-done | bytes 819232 | tf_op jit(solution)/shard_map/rz_outer2/ppermute | solution.py:992
  380.0 3.6 unpack.1
  384.4 1.9 collective-permute-start.54
  386.2 2.1 collective-permute-done.54
  388.5 4.4 %collective-permute-done.55 = f32[40,256]{1,0:T(8,128)S(1)} collective-permute-done((f32[40,256]{1,0:T(8,128)S(1)}, f32[40,256]{1,0:T(8,128)S(1)}, u32[]{:S(2)}, u32[]{:S(2)}) %collective-permute-start.55) | collective-permute-done | bytes 40992 | tf_op jit(solution)/shard_map/norm/ppermute | solution.py:992
  392.9 4.9 %collective-permute-done.56 = f32[40,256]{1,0:T(8,128)S(1)} collective-permute-done((f32[40,256]{1,0:T(8,128)S(1)}, f32[40,256]{1,0:T(8,128)S(1)}, u32[]{:S(2)}, u32[]{:S(2)}) %collective-permute-start.56) | collective-permute-done | bytes 40992 | tf_op jit(solution)/shard_map/norm/ppermute | solution.py:992
  401.6 1.5 collective-permute-start.57
  403.8 1.4 collective-permute-done.57
  405.2 1.5 fusion.16
  408.1 6.0 %multiply_add_fusion = (f32[393664]{0:T(1024)}, f32[393664]{0:T(1024)}, f32[393664]{0:T(1024)}, f32[393664]{0:T(1024)}) fusion(f32[393664]{0:T(1024)S(1)} %copy-done.23, f32[393664]{0:T(1024)S(1)} %copy-done.20, f32[]{:T(128)S(6)} %div.48, f32[394240]{0:T(1024)} %fusion.16, f32[393664]{0:T(1024)} %param.13, f32[393664]{0:T(1024)} %param.12), kind=kLoop, calls=%fused_computation.17 | loop fusion | flops 7479616 | bytes 14171908 | tf_op jit(solution)/shard_map/add | solution.py:1251
  (258 shorter events, 45.8 us)
Async XLA Ops:
  2.3 4.6 %collective-permute-start = (bf16[16,256]{1,0:T(8,128)(2,1)S(1)}, bf16[16,256]{1,0:T(8,128)(2,1)S(1)}, u32[]{:S(2)}, u32[]{:S(2)}) collective-permute-start(bf16[16,256]{1,0:T(8,128)(2,1)S(1)} %select_convert_fusion), channel_id=1, source_target_pairs={{0,2},{1,3},{2,0},{3,1},{4,6},{5,7},{6,4},{7,5},{8,10},{9,11},{10,... | collective-permute-start | bytes 24584 | tf_op jit(solution)/shard_map/tail_x/ppermute | solution.py:992
  6.9 2.9 collective-permute-start.1
  9.8 73.9 %copy-start.1 = (s32[6]{0:T(128)}, s32[6]{0:T(128)S(1)}, u32[]{:S(2)}) copy-start(s32[6]{0:T(128)S(1)} %stack.19.place) | copy-start | bytes 76
  10.7 73.0 %copy-start = (bf16[1600,256]{1,0:T(8,128)(2,1)}, bf16[1600,256]{1,0:T(8,128)(2,1)S(1)}, u32[]{:S(2)}) copy-start(bf16[1600,256]{1,0:T(8,128)(2,1)S(1)} %pack.1.p0.refs_0_) | copy-start | bytes 2457604
  10.7 21.6 %collective-permute-start.2 = (bf16[1600,256]{1,0:T(8,128)(2,1)S(1)}, bf16[1600,256]{1,0:T(8,128)(2,1)S(1)}, u32[]{:S(2)}, u32[]{:S(2)}) collective-permute-start(bf16[1600,256]{1,0:T(8,128)(2,1)S(1)} %pack.1.p0.refs_0_), channel_id=1, source_target_pairs={{0,16},{1,17},{2,18},{3,19},{4,20},{5,21},{6,22},{7,23},{8,0},{9,1... | collective-permute-start | bytes 2457608 | tf_op jit(solution)/shard_map/first/ppermute | solution.py:992
  14.1 22.1 %collective-permute-start.7 = (bf16[1600,256]{1,0:T(8,128)(2,1)S(1)}, bf16[1600,256]{1,0:T(8,128)(2,1)}, u32[]{:S(2)}, u32[]{:S(2)}) collective-permute-start(bf16[1600,256]{1,0:T(8,128)(2,1)S(1)} %pack.1.p0.refs_0_), channel_id=1, source_target_pairs={{8,10},{9,11},{10,8},{11,9},{12,14},{13,15},{14,12},{15,13},{16,18... | collective-permute-start | bytes 2457608 | tf_op jit(solution)/shard_map/x0/ppermute | solution.py:992
  15.7 20.6 %collective-permute-start.6 = (bf16[1600,256]{1,0:T(8,128)(2,1)S(1)}, bf16[1600,256]{1,0:T(8,128)(2,1)}, u32[]{:S(2)}, u32[]{:S(2)}) collective-permute-start(bf16[1600,256]{1,0:T(8,128)(2,1)S(1)} %pack.1.p0.refs_0_), channel_id=1, source_target_pairs={{0,4},{1,5},{2,6},{3,7},{4,0},{5,1},{6,2},{7,3},{8,12},{9,13},{10,... | collective-permute-start | bytes 2457608 | tf_op jit(solution)/shard_map/y0/ppermute | solution.py:992
  32.4 20.5 %collective-permute-start.4 = (bf16[1600,256]{1,0:T(8,128)(2,1)S(1)}, bf16[1600,256]{1,0:T(8,128)(2,1)}, u32[]{:S(2)}, u32[]{:S(2)}) collective-permute-start(bf16[1600,256]{1,0:T(8,128)(2,1)S(1)} %broadcast_select_fusion.5), channel_id=1, source_target_pairs={{0,8},{1,9},{2,10},{3,11},{4,12},{5,13},{6,14},{7,15},{8,0},{9,1},... | collective-permute-start | bytes 2457608 | tf_op jit(solution)/shard_map/second/ppermute | solution.py:992
  34.7 18.2 %collective-permute-start.3 = (bf16[1600,256]{1,0:T(8,128)(2,1)S(1)}, bf16[1600,256]{1,0:T(8,128)(2,1)}, u32[]{:S(2)}, u32[]{:S(2)}) collective-permute-start(bf16[1600,256]{1,0:T(8,128)(2,1)S(1)} %pack.1.p0.refs_0_), channel_id=1, source_target_pairs={{8,16},{9,17},{10,18},{11,19},{12,20},{13,21},{14,22},{15,23},{16,... | collective-permute-start | bytes 2457608 | tf_op jit(solution)/shard_map/crossed/ppermute | solution.py:992
  36.3 20.0 %collective-permute-start.8 = (bf16[1600,256]{1,0:T(8,128)(2,1)S(1)}, bf16[1600,256]{1,0:T(8,128)(2,1)S(1)}, u32[]{:S(2)}, u32[]{:S(2)}) collective-permute-start(bf16[1600,256]{1,0:T(8,128)(2,1)S(1)} %collective-permute-done.2.p2.refs_1_), channel_id=1, source_target_pairs={{0,4},{1,5},{2,6},{3,7},{4,0},{5,1},{6,2},{7,3},{8,12},{9,13},{10,... | collective-permute-start | bytes 2457608 | tf_op jit(solution)/shard_map/y1/ppermute | solution.py:992
  38.4 23.9 %collective-permute-start.13 = (bf16[1600,256]{1,0:T(8,128)(2,1)S(1)}, bf16[1600,256]{1,0:T(8,128)(2,1)}, u32[]{:S(2)}, u32[]{:S(2)}) collective-permute-start(bf16[1600,256]{1,0:T(8,128)(2,1)S(1)} %collective-permute-done.2.p2.refs_1_), channel_id=1, source_target_pairs={{0,2},{1,3},{2,0},{3,1},{4,6},{5,7},{6,4},{7,5},{8,10},{9,11},{10,... | collective-permute-start | bytes 2457608 | tf_op jit(solution)/shard_map/x1/ppermute | solution.py:992
  52.9 22.8 %collective-permute-start.5 = (bf16[1600,256]{1,0:T(8,128)(2,1)}, bf16[1600,256]{1,0:T(8,128)(2,1)}, u32[]{:S(2)}, u32[]{:S(2)}) collective-permute-start(bf16[1600,256]{1,0:T(8,128)(2,1)} %collective-permute-done.3), channel_id=1, source_target_pairs={{8,0},{9,1},{10,2},{11,3},{12,4},{13,5},{14,6},{15,7},{16,24},{17,... | collective-permute-start | bytes 2457608 | tf_op jit(solution)/shard_map/third/ppermute | solution.py:992
  57.2 19.4 %collective-permute-start.9 = (bf16[1600,256]{1,0:T(8,128)(2,1)}, bf16[1600,256]{1,0:T(8,128)(2,1)}, u32[]{:S(2)}, u32[]{:S(2)}) collective-permute-start(bf16[1600,256]{1,0:T(8,128)(2,1)} %collective-permute-done.4.p4.refs_2_), channel_id=1, source_target_pairs={{0,4},{1,5},{2,6},{3,7},{4,0},{5,1},{6,2},{7,3},{8,12},{9,13},{10,... | collective-permute-start | bytes 2457608 | tf_op jit(solution)/shard_map/y2/ppermute | solution.py:992
  58.9 24.8 %collective-permute-start.10 = (bf16[256,1024]{1,0:T(8,128)(2,1)S(1)}, bf16[256,1024]{1,0:T(8,128)(2,1)S(1)}, u32[]{:S(2)}, u32[]{:S(2)}) collective-permute-start(bf16[256,1024]{1,0:T(8,128)(2,1)S(1)} %copy-done.4), channel_id=1, source_target_pairs={{0,1},{1,0},{2,3},{3,2},{4,5},{5,4},{6,7},{7,6},{8,9},{9,8},{10,11... | collective-permute-start | bytes 1572872 | tf_op jit(solution)/shard_map/tok_c/ppermute | solution.py:992
  59.6 14.8 %collective-permute-start.11 = (bf16[256,1024]{1,0:T(8,128)(2,1)S(1)}, bf16[256,1024]{1,0:T(8,128)(2,1)S(1)}, u32[]{:S(2)}, u32[]{:S(2)}) collective-permute-start(bf16[256,1024]{1,0:T(8,128)(2,1)S(1)} %copy-done.4), channel_id=1, source_target_pairs={{0,2},{1,3},{2,0},{3,1},{4,6},{5,7},{6,4},{7,5},{8,10},{9,11},{10,... | collective-permute-start | bytes 1572872 | tf_op jit(solution)/shard_map/tok_x/ppermute | solution.py:992
  62.4 38.7 %collective-permute-start.14 = (bf16[1600,256]{1,0:T(8,128)(2,1)S(1)}, bf16[1600,256]{1,0:T(8,128)(2,1)S(1)}, u32[]{:S(2)}, u32[]{:S(2)}) collective-permute-start(bf16[1600,256]{1,0:T(8,128)(2,1)S(1)} %broadcast_select_fusion.3), channel_id=1, source_target_pairs={{0,2},{1,3},{2,0},{3,1},{4,6},{5,7},{6,4},{7,5},{8,10},{9,11},{10,... | collective-permute-start | bytes 2457608 | tf_op jit(solution)/shard_map/xa/ppermute | solution.py:992
  75.7 7.9 %collective-permute-start.12 = (bf16[256,1024]{1,0:T(8,128)(2,1)S(1)}, bf16[256,1024]{1,0:T(8,128)(2,1)S(1)}, u32[]{:S(2)}, u32[]{:S(2)}) collective-permute-start(bf16[256,1024]{1,0:T(8,128)(2,1)S(1)} %collective-permute-done.11.t2), channel_id=1, source_target_pairs={{0,1},{1,0},{2,3},{3,2},{4,5},{5,4},{6,7},{7,6},{8,9},{9,8},{10,11... | collective-permute-start | bytes 1572872 | tf_op jit(solution)/shard_map/tok_xc/ppermute | solution.py:992
  78.7 30.5 %collective-permute-start.15 = (bf16[1600,256]{1,0:T(8,128)(2,1)S(1)}, bf16[1600,256]{1,0:T(8,128)(2,1)S(1)}, u32[]{:S(2)}, u32[]{:S(2)}) collective-permute-start(bf16[1600,256]{1,0:T(8,128)(2,1)S(1)} %broadcast_select_fusion.4.p6.refs_3_), channel_id=1, source_target_pairs={{0,4},{1,5},{2,6},{3,7},{4,0},{5,1},{6,2},{7,3},{8,12},{9,13},{10,... | collective-permute-start | bytes 2457608 | tf_op jit(solution)/shard_map/y3/ppermute | solution.py:992
  80.2 29.0 %collective-permute-start.16 = (bf16[1600,256]{1,0:T(8,128)(2,1)}, bf16[1600,256]{1,0:T(8,128)(2,1)}, u32[]{:S(2)}, u32[]{:S(2)}) collective-permute-start(bf16[1600,256]{1,0:T(8,128)(2,1)} %collective-permute-done.9.p5.refs_6_), channel_id=1, source_target_pairs={{0,2},{1,3},{2,0},{3,1},{4,6},{5,7},{6,4},{7,5},{16,18},{17,19},{1... | collective-permute-start | bytes 2457608 | tf_op jit(solution)/shard_map/yx2/ppermute | solution.py:992
  109.2 52.2 %copy-start.41 = (bf16[1600,256]{1,0:T(8,128)(2,1)}, bf16[1600,256]{1,0:T(8,128)(2,1)S(1)}, u32[]{:S(2)}) copy-start(bf16[1600,256]{1,0:T(8,128)(2,1)S(1)} %collective-permute-done.15.refs_10_) | copy-start | bytes 2457604
  109.2 52.1 %collective-permute-start.23 = (bf16[9,1600,256]{2,1,0:T(8,128)(2,1)}, bf16[9,1600,256]{2,1,0:T(8,128)(2,1)}, u32[]{:S(2)}, u32[]{:S(2)}) collective-permute-start(bf16[9,1600,256]{2,1,0:T(8,128)(2,1)} %get-tuple-element.122), channel_id=1, source_target_pairs={{0,1},{1,0},{2,3},{3,2},{4,5},{5,4},{6,7},{7,6},{8,9},{9,8},{10,11... | collective-permute-start | bytes 22118408 | tf_op jit(solution)/shard_map/stack/ppermute | solution.py:992
  110.7 20.4 %collective-permute-start.20 = (bf16[1600,256]{1,0:T(8,128)(2,1)S(1)}, bf16[1600,256]{1,0:T(8,128)(2,1)S(1)}, u32[]{:S(2)}, u32[]{:S(2)}) collective-permute-start(bf16[1600,256]{1,0:T(8,128)(2,1)S(1)} %broadcast_select_fusion.2), channel_id=1, source_target_pairs={{0,4},{1,5},{2,6},{3,7},{4,0},{5,1},{6,2},{7,3},{8,12},{9,13},{10,... | collective-permute-start | bytes 2457608 | tf_op jit(solution)/shard_map/yb/ppermute | solution.py:992
  111.1 21.1 %collective-permute-start.21 = (bf16[1600,256]{1,0:T(8,128)(2,1)S(1)}, bf16[1600,256]{1,0:T(8,128)(2,1)S(1)}, u32[]{:S(2)}, u32[]{:S(2)}) collective-permute-start(bf16[1600,256]{1,0:T(8,128)(2,1)S(1)} %copy-done.31), channel_id=1, source_target_pairs={{0,2},{1,3},{2,0},{3,1},{4,6},{5,7},{6,4},{7,5},{8,10},{9,11},{10,... | collective-permute-start | bytes 2457608 | tf_op jit(solution)/shard_map/x3/ppermute | solution.py:992
  112.6 37.2 %collective-permute-start.22 = (bf16[1600,256]{1,0:T(8,128)(2,1)S(1)}, bf16[1600,256]{1,0:T(8,128)(2,1)S(1)}, u32[]{:S(2)}, u32[]{:S(2)}) collective-permute-start(bf16[1600,256]{1,0:T(8,128)(2,1)S(1)} %collective-permute-done.15.refs_10_), channel_id=1, source_target_pairs={{0,2},{1,3},{2,0},{3,1},{4,6},{5,7},{6,4},{7,5},{8,10},{9,11},{10,... | collective-permute-start | bytes 2457608 | tf_op jit(solution)/shard_map/yx3/ppermute | solution.py:992
  113.1 42.5 %collective-permute-start.27 = (bf16[1600,256]{1,0:T(8,128)(2,1)}, bf16[1600,256]{1,0:T(8,128)(2,1)}, u32[]{:S(2)}, u32[]{:S(2)}) collective-permute-start(bf16[1600,256]{1,0:T(8,128)(2,1)} %collective-permute-done.16.refs_12_), channel_id=1, source_target_pairs={{0,1},{1,0},{2,3},{3,2},{4,5},{5,4},{6,7},{7,6},{16,17},{17,16},{1... | collective-permute-start | bytes 2457608 | tf_op jit(solution)/shard_map/cyx2/ppermute | solution.py:992
  131.2 24.9 %collective-permute-start.26 = (bf16[1600,256]{1,0:T(8,128)(2,1)S(1)}, bf16[1600,256]{1,0:T(8,128)(2,1)}, u32[]{:S(2)}, u32[]{:S(2)}) collective-permute-start(bf16[1600,256]{1,0:T(8,128)(2,1)S(1)} %collective-permute-done.20.refs_11_), channel_id=1, source_target_pairs={{0,1},{1,0},{2,3},{3,2},{4,5},{5,4},{6,7},{7,6},{8,9},{9,8},{10,11... | collective-permute-start | bytes 2457608 | tf_op jit(solution)/shard_map/cyb/ppermute | solution.py:992
  132.2 1.5 collective-permute-start.17
  133.7 17.9 %collective-permute-start.18 = (bf16[256,256]{1,0:T(8,128)(2,1)S(1)}, bf16[256,256]{1,0:T(8,128)(2,1)S(1)}, u32[]{:S(2)}, u32[]{:S(2)}) collective-permute-start(bf16[256,256]{1,0:T(8,128)(2,1)S(1)} %get-tuple-element.119), channel_id=1, source_target_pairs={{0,2},{1,3},{2,0},{3,1},{4,6},{5,7},{6,4},{7,5},{8,10},{9,11},{10,... | collective-permute-start | bytes 393224 | tf_op jit(solution)/shard_map/heads/ppermute | solution.py:992
  149.8 5.8 %collective-permute-start.19 = (bf16[256,256]{1,0:T(8,128)(2,1)S(1)}, bf16[256,256]{1,0:T(8,128)(2,1)S(1)}, u32[]{:S(2)}, u32[]{:S(2)}) collective-permute-start(bf16[256,256]{1,0:T(8,128)(2,1)S(1)} %get-tuple-element.120), channel_id=1, source_target_pairs={{0,3},{1,2},{2,1},{3,0},{4,7},{5,6},{6,5},{7,4},{8,11},{9,10},{10,... | collective-permute-start | bytes 393224 | tf_op jit(solution)/shard_map/heads/ppermute | solution.py:992
  151.6 7.6 %collective-permute-start.25 = (bf16[1600,256]{1,0:T(8,128)(2,1)S(1)}, bf16[1600,256]{1,0:T(8,128)(2,1)S(1)}, u32[]{:S(2)}, u32[]{:S(2)}) collective-permute-start(bf16[1600,256]{1,0:T(8,128)(2,1)S(1)} %collective-permute-done.15.refs_10_), channel_id=1, source_target_pairs={{0,1},{1,0},{2,3},{3,2},{4,5},{5,4},{6,7},{7,6},{8,9},{9,8},{10,11... | collective-permute-start | bytes 2457608 | tf_op jit(solution)/shard_map/cy3/ppermute | solution.py:992
  155.5 2.5 collective-permute-start.28
  155.6 3.6 collective-permute-start.24
  156.0 4.4 %collective-permute-start.29 = (bf16[1600,256]{1,0:T(8,128)(2,1)}, bf16[1600,256]{1,0:T(8,128)(2,1)S(1)}, u32[]{:S(2)}, u32[]{:S(2)}) collective-permute-start(bf16[1600,256]{1,0:T(8,128)(2,1)} %copy-done.44), channel_id=1, source_target_pairs={{0,1},{1,0},{2,3},{3,2},{4,5},{5,4},{6,7},{7,6},{8,9},{9,8},{10,11... | collective-permute-start | bytes 2457608 | tf_op jit(solution)/shard_map/cyx3/ppermute | solution.py:992
  204.9 9.5 %collective-permute-start.34 = (bf16[2,2,1600,256]{3,2,1,0:T(8,128)(2,1)}, bf16[2,2,1600,256]{3,2,1,0:T(8,128)(2,1)S(1)}, u32[]{:S(2)}, u32[]{:S(2)}) collective-permute-start(bf16[2,2,1600,256]{3,2,1,0:T(8,128)(2,1)} %get-tuple-element.139), channel_id=1, source_target_pairs={{0,1},{1,0},{2,3},{3,2},{4,5},{5,4},{6,7},{7,6},{8,9},{9,8},{10,11... | collective-permute-start | bytes 9830408 | tf_op jit(solution)/shard_map/rc2/ppermute | solution.py:992
  205.1 12.4 %collective-permute-start.30 = (bf16[2,2,1600,256]{3,2,1,0:T(8,128)(2,1)}, bf16[2,2,1600,256]{3,2,1,0:T(8,128)(2,1)}, u32[]{:S(2)}, u32[]{:S(2)}) collective-permute-start(bf16[2,2,1600,256]{3,2,1,0:T(8,128)(2,1)} %get-tuple-element.132), channel_id=1, source_target_pairs={{0,1},{1,0},{2,3},{3,2},{4,5},{5,4},{6,7},{7,6},{8,9},{9,8},{10,11... | collective-permute-start | bytes 9830408 | tf_op jit(solution)/shard_map/rc1/ppermute | solution.py:992
  205.5 11.9 %collective-permute-start.31 = (bf16[256,256]{1,0:T(8,128)(2,1)}, bf16[256,256]{1,0:T(8,128)(2,1)S(1)}, u32[]{:S(2)}, u32[]{:S(2)}) collective-permute-start(bf16[256,256]{1,0:T(8,128)(2,1)} %get-tuple-element.134), channel_id=1, source_target_pairs={{0,1},{1,0},{2,3},{3,2},{4,5},{5,4},{6,7},{7,6},{8,9},{9,8},{10,11... | collective-permute-start | bytes 393224 | tf_op jit(solution)/shard_map/heads_grad/ppermute | solution.py:992
  205.7 11.8 %collective-permute-start.32 = (bf16[256,256]{1,0:T(8,128)(2,1)}, bf16[256,256]{1,0:T(8,128)(2,1)S(1)}, u32[]{:S(2)}, u32[]{:S(2)}) collective-permute-start(bf16[256,256]{1,0:T(8,128)(2,1)} %get-tuple-element.135), channel_id=1, source_target_pairs={{0,2},{1,3},{2,0},{3,1},{4,6},{5,7},{6,4},{7,5},{8,10},{9,11},{10,... | collective-permute-start | bytes 393224 | tf_op jit(solution)/shard_map/heads_grad/ppermute | solution.py:992
  206.3 11.1 %collective-permute-start.33 = (bf16[256,256]{1,0:T(8,128)(2,1)}, bf16[256,256]{1,0:T(8,128)(2,1)S(1)}, u32[]{:S(2)}, u32[]{:S(2)}) collective-permute-start(bf16[256,256]{1,0:T(8,128)(2,1)} %get-tuple-element.136), channel_id=1, source_target_pairs={{0,3},{1,2},{2,1},{3,0},{4,7},{5,6},{6,5},{7,4},{8,11},{9,10},{10,... | collective-permute-start | bytes 393224 | tf_op jit(solution)/shard_map/heads_grad/ppermute | solution.py:992
  220.0 24.6 %collective-permute-start.36 = (bf16[1600,256]{1,0:T(8,128)(2,1)S(1)}, bf16[1600,256]{1,0:T(8,128)(2,1)S(1)}, u32[]{:S(2)}, u32[]{:S(2)}) collective-permute-start(bf16[1600,256]{1,0:T(8,128)(2,1)S(1)} %get-tuple-element.140), channel_id=1, source_target_pairs={{0,2},{1,3},{2,0},{3,1},{4,6},{5,7},{6,4},{7,5},{8,10},{9,11},{10,... | collective-permute-start | bytes 2457608 | tf_op jit(solution)/shard_map/d2/ppermute | solution.py:992
  220.7 23.9 %collective-permute-start.35 = (bf16[1600,256]{1,0:T(8,128)(2,1)S(1)}, bf16[1600,256]{1,0:T(8,128)(2,1)S(1)}, u32[]{:S(2)}, u32[]{:S(2)}) collective-permute-start(bf16[1600,256]{1,0:T(8,128)(2,1)S(1)} %get-tuple-element.137), channel_id=1, source_target_pairs={{0,4},{1,5},{2,6},{3,7},{4,0},{5,1},{6,2},{7,3},{8,12},{9,13},{10,... | collective-permute-start | bytes 2457608 | tf_op jit(solution)/shard_map/d1/ppermute | solution.py:992
  222.6 42.4 %collective-permute-start.44 = (bf16[1600,256]{1,0:T(8,128)(2,1)S(1)}, bf16[1600,256]{1,0:T(8,128)(2,1)S(1)}, u32[]{:S(2)}, u32[]{:S(2)}) collective-permute-start(bf16[1600,256]{1,0:T(8,128)(2,1)S(1)} %get-tuple-element.142), channel_id=1, source_target_pairs={{0,2},{1,3},{2,0},{3,1},{4,6},{5,7},{6,4},{7,5},{8,10},{9,11},{10,... | collective-permute-start | bytes 2457608 | tf_op jit(solution)/shard_map/e2/ppermute | solution.py:992
  224.0 34.4 %collective-permute-start.46 = (bf16[1600,256]{1,0:T(8,128)(2,1)S(1)}, bf16[1600,256]{1,0:T(8,128)(2,1)S(1)}, u32[]{:S(2)}, u32[]{:S(2)}) collective-permute-start(bf16[1600,256]{1,0:T(8,128)(2,1)S(1)} %get-tuple-element.141), channel_id=1, source_target_pairs={{0,4},{1,5},{2,6},{3,7},{4,0},{5,1},{6,2},{7,3},{8,12},{9,13},{10,... | collective-permute-start | bytes 2457608 | tf_op jit(solution)/shard_map/e1/ppermute | solution.py:992
  224.1 39.0 %collective-permute-start.38 = (bf16[2,2,1600,256]{3,2,1,0:T(8,128)(2,1)}, bf16[2,2,1600,256]{3,2,1,0:T(8,128)(2,1)S(1)}, u32[]{:S(2)}, u32[]{:S(2)}) collective-permute-start(bf16[2,2,1600,256]{3,2,1,0:T(8,128)(2,1)} %get-tuple-element.159), channel_id=1, source_target_pairs={{0,1},{1,0},{2,3},{3,2},{4,5},{5,4},{6,7},{7,6},{8,9},{9,8},{10,11... | collective-permute-start | bytes 9830408 | tf_op jit(solution)/shard_map/rc3/ppermute | solution.py:992
  258.4 25.9 %collective-permute-start.49 = (bf16[1600,256]{1,0:T(8,128)(2,1)S(1)}, bf16[1600,256]{1,0:T(8,128)(2,1)S(1)}, u32[]{:S(2)}, u32[]{:S(2)}) collective-permute-start(bf16[1600,256]{1,0:T(8,128)(2,1)S(1)} %get-tuple-element.175), channel_id=1, source_target_pairs={{0,4},{1,5},{2,6},{3,7},{4,0},{5,1},{6,2},{7,3},{8,12},{9,13},{10,... | collective-permute-start | bytes 2457608 | tf_op jit(solution)/shard_map/ry0/ppermute | solution.py:992
  261.7 21.2 %collective-permute-start.39 = (bf16[1600,256]{1,0:T(8,128)(2,1)S(1)}, bf16[1600,256]{1,0:T(8,128)(2,1)S(1)}, u32[]{:S(2)}, u32[]{:S(2)}) collective-permute-start(bf16[1600,256]{1,0:T(8,128)(2,1)S(1)} %fusion.2), channel_id=1, source_target_pairs={{0,2},{1,3},{2,0},{3,1},{4,6},{5,7},{6,4},{7,5},{8,10},{9,11},{10,... | collective-permute-start | bytes 2457608 | tf_op jit(solution)/shard_map/f1/ppermute | solution.py:992
  264.9 35.5 %collective-permute-start.50 = (bf16[1600,256]{1,0:T(8,128)(2,1)S(1)}, bf16[1600,256]{1,0:T(8,128)(2,1)S(1)}, u32[]{:S(2)}, u32[]{:S(2)}) collective-permute-start(bf16[1600,256]{1,0:T(8,128)(2,1)S(1)} %get-tuple-element.176), channel_id=1, source_target_pairs={{0,2},{1,3},{2,0},{3,1},{4,6},{5,7},{6,4},{7,5},{8,10},{9,11},{10,... | collective-permute-start | bytes 2457608 | tf_op jit(solution)/shard_map/d3/ppermute | solution.py:992
  268.2 35.6 %collective-permute-start.45 = (bf16[1600,256]{1,0:T(8,128)(2,1)}, bf16[1600,256]{1,0:T(8,128)(2,1)}, u32[]{:S(2)}, u32[]{:S(2)}) collective-permute-start(bf16[1600,256]{1,0:T(8,128)(2,1)} %fusion.1), channel_id=1, source_target_pairs={{0,4},{1,5},{2,6},{3,7},{4,0},{5,1},{6,2},{7,3},{8,12},{9,13},{10,... | collective-permute-start | bytes 2457608 | tf_op jit(solution)/shard_map/f2/ppermute | solution.py:992
  268.9 54.2 %collective-permute-start.37 = (bf16[2,256,1024]{2,1,0:T(8,128)(2,1)S(1)}, bf16[2,256,1024]{2,1,0:T(8,128)(2,1)}, u32[]{:S(2)}, u32[]{:S(2)}) collective-permute-start(bf16[2,256,1024]{2,1,0:T(8,128)(2,1)S(1)} %get-tuple-element.156), channel_id=1, source_target_pairs={{0,1},{1,0},{2,3},{3,2},{4,5},{5,4},{6,7},{7,6},{8,9},{9,8},{10,11... | collective-permute-start | bytes 3145736 | tf_op jit(solution)/shard_map/in_c/ppermute | solution.py:992
  282.9 32.9 %collective-permute-start.40 = (bf16[1600,256]{1,0:T(8,128)(2,1)}, bf16[1600,256]{1,0:T(8,128)(2,1)}, u32[]{:S(2)}, u32[]{:S(2)}) collective-permute-start(bf16[1600,256]{1,0:T(8,128)(2,1)} %get-tuple-element.161), channel_id=1, source_target_pairs={{0,2},{1,3},{2,0},{3,1},{4,6},{5,7},{6,4},{7,5},{8,10},{9,11},{10,... | collective-permute-start | bytes 2457608 | tf_op jit(solution)/shard_map/e3/ppermute | solution.py:992
  301.7 15.9 %collective-permute-start.51 = (bf16[1600,256]{1,0:T(8,128)(2,1)}, bf16[1600,256]{1,0:T(8,128)(2,1)}, u32[]{:S(2)}, u32[]{:S(2)}) collective-permute-start(bf16[1600,256]{1,0:T(8,128)(2,1)} %fusion), channel_id=1, source_target_pairs={{0,4},{1,5},{2,6},{3,7},{4,0},{5,1},{6,2},{7,3},{8,12},{9,13},{10,... | collective-permute-start | bytes 2457608 | tf_op jit(solution)/shard_map/f3/ppermute | solution.py:992
  309.5 19.5 %collective-permute-start.47 = (bf16[1600,256]{1,0:T(8,128)(2,1)}, bf16[1600,256]{1,0:T(8,128)(2,1)}, u32[]{:S(2)}, u32[]{:S(2)}) collective-permute-start(bf16[1600,256]{1,0:T(8,128)(2,1)} %get-tuple-element.170), channel_id=1, source_target_pairs={{0,8},{1,9},{2,10},{3,11},{4,12},{5,13},{6,14},{7,15},{8,0},{9,1},... | collective-permute-start | bytes 2457608 | tf_op jit(solution)/shard_map/rz_inner1/ppermute | solution.py:992
  322.9 21.5 %collective-permute-start.52 = (bf16[1600,256]{1,0:T(8,128)(2,1)}, bf16[1600,256]{1,0:T(8,128)(2,1)S(1)}, u32[]{:S(2)}, u32[]{:S(2)}) collective-permute-start(bf16[1600,256]{1,0:T(8,128)(2,1)} %get-tuple-element.179), channel_id=1, source_target_pairs={{0,8},{1,9},{2,10},{3,11},{4,12},{5,13},{6,14},{7,15},{8,0},{9,1},... | collective-permute-start | bytes 2457608 | tf_op jit(solution)/shard_map/rz_outer1/ppermute | solution.py:992
  323.0 22.9 %collective-permute-start.42 = (f32[2,32,256]{2,1,0:T(8,128)S(1)}, f32[2,32,256]{2,1,0:T(8,128)S(1)}, u32[]{:S(2)}, u32[]{:S(2)}) collective-permute-start(f32[2,32,256]{2,1,0:T(8,128)S(1)} %select_bitcast_fusion), channel_id=1, source_target_pairs={{0,1},{1,0},{2,3},{3,2},{4,5},{5,4},{6,7},{7,6},{8,9},{9,8},{10,11... | collective-permute-start | bytes 196616 | tf_op jit(solution)/shard_map/vec_c/ppermute | solution.py:992
  330.4 27.9 %collective-permute-start.48 = (bf16[1600,256]{1,0:T(8,128)(2,1)S(1)}, bf16[1600,256]{1,0:T(8,128)(2,1)S(1)}, u32[]{:S(2)}, u32[]{:S(2)}) collective-permute-start(bf16[1600,256]{1,0:T(8,128)(2,1)S(1)} %add_convert_fusion.2.inner), channel_id=1, source_target_pairs={{0,16},{1,17},{2,18},{3,19},{4,20},{5,21},{6,22},{7,23},{24,8},{25... | collective-permute-start | bytes 2457608 | tf_op jit(solution)/shard_map/rz_inner2/ppermute | solution.py:992
  337.2 12.8 %collective-permute-start.41 = (bf16[256,1024]{1,0:T(8,128)(2,1)S(1)}, bf16[256,1024]{1,0:T(8,128)(2,1)S(1)}, u32[]{:S(2)}, u32[]{:S(2)}) collective-permute-start(bf16[256,1024]{1,0:T(8,128)(2,1)S(1)} %fusion.11), channel_id=1, source_target_pairs={{0,2},{1,3},{2,0},{3,1},{4,6},{5,7},{6,4},{7,5},{8,10},{9,11},{10,... | collective-permute-start | bytes 1572872 | tf_op jit(solution)/shard_map/in_x/ppermute | solution.py:992
  344.6 35.4 %collective-permute-start.53 = (bf16[1600,256]{1,0:T(8,128)(2,1)S(1)}, bf16[1600,256]{1,0:T(8,128)(2,1)}, u32[]{:S(2)}, u32[]{:S(2)}) collective-permute-start(bf16[1600,256]{1,0:T(8,128)(2,1)S(1)} %add_convert_fusion.outer), channel_id=1, source_target_pairs={{8,24},{9,25},{10,26},{11,27},{12,28},{13,29},{14,30},{15,31},{16,... | collective-permute-start | bytes 2457608 | tf_op jit(solution)/shard_map/rz_outer2/ppermute | solution.py:992
  346.0 4.0 collective-permute-start.43
  352.3 55.7 %copy-start.20 = (f32[393664]{0:T(1024)S(1)}, f32[393664]{0:T(1024)}, u32[]{:S(2)}) copy-start(f32[393664]{0:T(1024)} %param.11) | copy-start | bytes 4723972
  359.2 48.8 %copy-start.23 = (f32[393664]{0:T(1024)S(1)}, f32[393664]{0:T(1024)}, u32[]{:S(2)}) copy-start(f32[393664]{0:T(1024)} %param.14) | copy-start | bytes 4723972
  384.4 4.0 collective-permute-start.54
  388.4 4.4 %collective-permute-start.55 = (f32[40,256]{1,0:T(8,128)S(1)}, f32[40,256]{1,0:T(8,128)S(1)}, u32[]{:S(2)}, u32[]{:S(2)}) collective-permute-start(f32[40,256]{1,0:T(8,128)S(1)} %fusion.17), channel_id=1, source_target_pairs={{0,8},{1,9},{2,10},{3,11},{4,12},{5,13},{6,14},{7,15},{8,0},{9,1},... | collective-permute-start | bytes 122888 | tf_op jit(solution)/shard_map/norm/ppermute | solution.py:992
  392.9 4.9 %collective-permute-start.56 = (f32[40,256]{1,0:T(8,128)S(1)}, f32[40,256]{1,0:T(8,128)S(1)}, u32[]{:S(2)}, u32[]{:S(2)}) collective-permute-start(f32[40,256]{1,0:T(8,128)S(1)} %add.191), channel_id=1, source_target_pairs={{0,16},{1,17},{2,18},{3,19},{4,20},{5,21},{6,22},{7,23},{8,24},{9,... | collective-permute-start | bytes 122888 | tf_op jit(solution)/shard_map/norm/ppermute | solution.py:992
  401.6 3.7 collective-permute-start.57
  405.2 1.6 collective-permute-start.58
  (48 other events, 803.6 us)

commit v3 on v2

--- a/solution.py
+++ b/solution.py
@@ -245,7 +245,7 @@
 
 
 def combine(place, first, second):
-    blocks = 5
+    blocks = 2
     size = PIECE // blocks
 
     def spec(piece):
@@ -278,7 +278,7 @@
 def attend_kernel(
     place, embed, bias, t0, t1, t2, t3, p0, p1, p2, p3, p4, p5, p6, p7, p8,
     stream_out, weight_out, q_out, k_out, v_out, h0, h1, h2, h3, lse_out, stack,
-    tokens, staged, q_heads, k_heads, v_heads, o_heads, edge, sem, sem_tokens, sem_in, sem_out,
+    tokens, staged, q_heads, k_t, v_heads, o_heads, edge, sem, sem_tokens, sem_in, sem_out,
 ):
     fetches = [
         pltpu.make_async_copy(ref, tokens.at[r], sem_tokens.at[r])
@@ -334,27 +334,28 @@
         for h in range(4):
             cols = slice(h * 64, h * 64 + 64)
             q_heads[h, rows, :] = query[:, cols] * 0.125
-            k_heads[h, rows, :] = key[:, cols]
             v_heads[h, rows, 0:64] = value[:, cols]
+        k_t[:, rows] = key.T
     lse_out[...] = jnp.zeros_like(lse_out)
     for before, copy in zip(held_in, held_out):
         before.wait()
         copy.start()
 
-    def step(n, _):
-        h, r = n // 4, n % 4
-        rows = pl.ds(pl.multiple_of(r * 256, 256), 256)
-        scores = dot_last(q_heads[h, rows, :], k_heads[h])
-        highest = jnp.max(scores, axis=1, keepdims=True)
-        weights = low(jnp.exp(scores - highest))
-        result = dot(weights, v_heads[h])
-        total = result[:, 64:65]
-        o_heads[h, rows, :] = low(result[:, 0:64] / total)
-        lane = lax.broadcasted_iota(jnp.int32, (256, 128), 1)
-        lse_out[rows, :] = jnp.where(lane == h, highest + jnp.log(total), lse_out[rows, :])
+    def head_step(h, _):
+        key_t = k_t[pl.ds(pl.multiple_of(h * 64, 64), 64), :]
+        for r in range(4):
+            rows = slice(r * 256, r * 256 + 256)
+            scores = dot(q_heads[h, rows, :], key_t)
+            highest = jnp.max(scores, axis=1, keepdims=True)
+            weights = low(jnp.exp(scores - highest))
+            result = dot(weights, v_heads[h])
+            total = result[:, 64:65]
+            o_heads[h, rows, :] = low(result[:, 0:64] / total)
+            lane = lax.broadcasted_iota(jnp.int32, (256, 128), 1)
+            lse_out[rows, :] = jnp.where(lane == h, highest + jnp.log(total), lse_out[rows, :])
         return 0
 
-    lax.fori_loop(0, 16, step, 0)
+    lax.fori_loop(0, 4, head_step, 0, unroll=4)
     for r, out in enumerate((h0, h1, h2, h3)):
         for h in range(4):
             out[:, h * 64 : h * 64 + 64] = o_heads[h, r * 256 : r * 256 + 256, :]
@@ -377,7 +378,7 @@
             pltpu.VMEM((4, 256, 1024), jnp.bfloat16),
             pltpu.VMEM((9, PIECE, 256), jnp.bfloat16),
             pltpu.VMEM((4, 1024, 64), jnp.bfloat16),
-            pltpu.VMEM((4, 1024, 64), jnp.bfloat16),
+            pltpu.VMEM((256, 1024), jnp.bfloat16),
             pltpu.VMEM((4, 1024, 128), jnp.bfloat16),
             pltpu.VMEM((4, 1024, 64), jnp.bfloat16),
             pltpu.VMEM((16, 256), jnp.bfloat16),
@@ -397,41 +398,46 @@
 def attend_back_kernel(
     place, q_in, k_in, v_in, lse, weight, g0, g1, g2, g3,
     q_grad, k_grad, v_grad, kept, sent, sums,
-    q_heads, k_heads, v_heads, g_heads, dq_heads, dk_heads, dv_heads,
+    q_heads, k_heads, g_heads, q_t, k_t, v_t, g_t, dq_heads, dk_t, dv_t,
 ):
     for r, grad in enumerate((g0, g1, g2, g3)):
         rows = slice(r * 256, r * 256 + 256)
+        g_t[:, rows] = grad[...].T
         for h in range(4):
             cols = slice(h * 64, h * 64 + 64)
             q_heads[h, rows, :] = q_in[rows, cols] * 0.125
             k_heads[h, rows, :] = k_in[rows, cols]
-            v_heads[h, rows, :] = v_in[rows, cols]
             g_heads[h, rows, :] = grad[:, cols]
-
-    def step(n, _):
-        h, r = n // 4, n % 4
-        rows = pl.ds(pl.multiple_of(r * 256, 256), 256)
-        query, grad = q_heads[h, rows, :], g_heads[h, rows, :]
-        scores = dot_last(query, k_heads[h])
-        lane = lax.broadcasted_iota(jnp.int32, (256, 128), 1)
-        logsum = jnp.sum(jnp.where(lane == h, lse[rows, :], 0.0), axis=1, keepdims=True)
-        probs = jnp.exp(scores - logsum)
-        weighted = probs * dot_last(grad, v_heads[h])
-        inner = jnp.sum(weighted, axis=1, keepdims=True)
-        score_grad = low(weighted - probs * inner)
-        dq_heads[h, rows, :] = low(dot(score_grad, k_heads[h]) * 0.125)
-        dk_heads[h] += dot_first(query, score_grad)
-        dv_heads[h] += dot_first(grad, low(probs))
+    q_t[...] = (q_in[...] * 0.125).T
+    k_t[...] = k_in[...].T
+    v_t[...] = v_in[...].T
+
+    def head_step(h, _):
+        mine = pl.ds(pl.multiple_of(h * 64, 64), 64)
+        key_t, value_t, key = k_t[mine, :], v_t[mine, :], k_heads[h]
+        key_sum = jnp.zeros((64, 1024), jnp.float32)
+        value_sum = jnp.zeros((64, 1024), jnp.float32)
+        for r in range(4):
+            rows = slice(r * 256, r * 256 + 256)
+            scores = dot(q_heads[h, rows, :], key_t)
+            lane = lax.broadcasted_iota(jnp.int32, (256, 128), 1)
+            logsum = jnp.sum(jnp.where(lane == h, lse[rows, :], 0.0), axis=1, keepdims=True)
+            probs = jnp.exp(scores - logsum)
+            weighted = probs * dot(g_heads[h, rows, :], value_t)
+            inner = jnp.sum(weighted, axis=1, keepdims=True)
+            score_grad = low(weighted - probs * inner)
+            dq_heads[h, rows, :] = low(dot(score_grad, key) * 0.125)
+            key_sum += dot(q_t[mine, rows], score_grad)
+            value_sum += dot(g_t[mine, rows], low(probs))
+        dk_t[mine, :] = low(key_sum)
+        dv_t[mine, :] = low(value_sum)
         return 0
 
-    dk_heads[...] = jnp.zeros_like(dk_heads)
-    dv_heads[...] = jnp.zeros_like(dv_heads)
-    lax.fori_loop(0, 16, step, 0)
+    lax.fori_loop(0, 4, head_step, 0, unroll=4)
     for h in range(4):
-        cols = slice(h * 64, h * 64 + 64)
-        q_grad[:, cols] = dq_heads[h]
-        k_grad[:, cols] = low(dk_heads[h].T)
-        v_grad[:, cols] = low(dv_heads[h].T)
+        q_grad[:, h * 64 : h * 64 + 64] = dq_heads[h]
+    k_grad[...] = dk_t[...].T
+    v_grad[...] = dv_t[...].T
     sums[...] = jnp.zeros_like(sums)
     sums[1:2, 0:256] = column_sum(wide(q_grad[...]))
     sums[2:3, 0:256] = column_sum(wide(v_grad[...]))
@@ -459,8 +465,10 @@
         ),
         in_specs=[SMEM] + [VMEM] * 9,
         out_specs=(VMEM,) * 6,
-        scratch_shapes=[pltpu.VMEM((4, 1024, 64), jnp.bfloat16)] * 5
-        + [pltpu.VMEM((4, 64, 1024), jnp.float32)] * 2,
+        scratch_shapes=[pltpu.VMEM((4, 1024, 64), jnp.bfloat16)] * 3
+        + [pltpu.VMEM((256, 1024), jnp.bfloat16)] * 4
+        + [pltpu.VMEM((4, 1024, 64), jnp.bfloat16)]
+        + [pltpu.VMEM((256, 1024), jnp.bfloat16)] * 2,
         compiler_params=pltpu.CompilerParams(vmem_limit_bytes=40 << 20),
         cost_estimate=pl.CostEstimate(
             flops=20_000_000_000, bytes_accessed=12_000_000, transcendentals=4_194_304
@@ -497,7 +505,7 @@
     (block_out, resid_grad, g0, g1, g2, g3, sums, sums_up, head_grad) = refs[:9]
     grads_own, grads_other = refs[9:12], refs[12:15]
     (w_out, w_up, w_down, edge_up, edge_down, hidden, slope, grad_up, grad_down,
-     grad_out, acc, sem, sem_out) = refs[15:]
+     grad_out, acc, acc_t, grad_t, sem, sem_out) = refs[15:]
 
     def fetch(z, y):
         made = {"out": [], "up": [], "down": []}
@@ -511,7 +519,9 @@
                     for name, row_a, row_b, offset, step, _ in SEGMENTS[case]:
                         count = row_b - row_a
                         if name == "o":
-                            made["out"].append((source.at[offset : offset + count, :], w_out.at[column]))
+                            made["out"].append(
+                                (source.at[offset : offset + count, :], w_out.at[:, pl.ds(column * 256, 256)])
+                            )
                         elif name == "up":
                             block = source.at[offset : offset + 4 * count, :].reshape(4, count, 256)
                             target = w_up.at[pl.ds(column * 4, 4)]
@@ -529,11 +539,11 @@
                             if row_a:
                                 skip = 16
                                 made["down"].append(
-                                    (source.at[offset : offset + 16, :], edge_down.at[case - 6, column])
+                                    (source.at[offset : offset + 16, :], edge_down.at[case - 6, :, pl.ds(column * 256, 256)])
                                 )
                             made["down"].append(
                                 (source.at[offset + skip : offset + count, :],
-                                 w_down.at[column, row_a + skip : row_b, :])
+                                 w_down.at[row_a + skip : row_b, pl.ds(column * 256, 256)])
                             )
         return made
 
@@ -555,14 +565,15 @@
     here = inside_column(place, 0)
     stream = wide(tokens[...]) + here * embed[...]
     arrived([w_out], 0)
-    w_out[:, 0:16, :] = w_out[:, 0:16, :] + out_head[...]
+    for n in range(4):
+        cols = slice(n * 256, n * 256 + 256)
+        w_out[0:16, cols] = w_out[0:16, cols] + out_head[n]
     heads = (h0, h1, h2, h3)
-    for n in range(4):
-        total = jnp.zeros((256, 256), jnp.float32)
-        for r in range(4):
-            rows = pl.ds(pl.multiple_of((place[3] ^ r) * 256, 256), 256)
-            total += dot(heads[r][...], w_out[n, rows, :])
-        acc[:, n * 256 : n * 256 + 256] = total
+
+    def head_rows(r):
+        return pl.ds(pl.multiple_of((place[3] ^ r) * 256, 256), 256)
+
+    acc[...] = sum(dot(heads[r][...], w_out[head_rows(r), :]) for r in range(4))
     bias_out, bias_down, gain_a, shift_a, gain_f, shift_f = (vectors[n : n + 1, :] for n in range(6))
     xhat_a, scale_a = normalise(stream + acc[...] + bias_out)
     normed = xhat_a * gain_a + shift_a
@@ -575,24 +586,16 @@
     def up(g, _):
         pre = dot(normed_low, w_up[g]) + bias_up[pl.ds(g, 1), :]
         inner = 0.5 * (1.0 + lax.erf(pre * (1.0 / math.sqrt(2.0))))
-        hidden[g] = low(pre * inner)
-        slope[g] = inner + pre * (jnp.exp(-0.5 * pre * pre) * (1.0 / math.sqrt(2.0 * math.pi)))
+        hidden[:, pl.ds(pl.multiple_of(g * 256, 256), 256)] = low(pre * inner)
+        bend = inner + pre * (jnp.exp(-0.5 * pre * pre) * (1.0 / math.sqrt(2.0 * math.pi)))
+        slope[pl.ds(pl.multiple_of(g * 256, 256), 256), :] = bend.T
         return 0
 
-    lax.fori_loop(0, 16, up, 0)
+    lax.fori_loop(0, 16, up, 0, unroll=8)
     arrived([w_down] + [edge_down], 2)
     for n, row in enumerate((1024, 2560)):
-        w_down[:, row : row + 16, :] = w_down[:, row : row + 16, :] + edge_down[n]
-    acc[...] = normed + bias_down
-
-    def down(g, _):
-        rows = pl.ds(pl.multiple_of(g * 256, 256), 256)
-        for n in range(4):
-            cols = slice(n * 256, n * 256 + 256)
-            acc[:, cols] += dot(hidden[g], w_down[n, rows, :])
-        return 0
-
-    lax.fori_loop(0, 16, down, 0)
+        w_down[row : row + 16, :] = w_down[row : row + 16, :] + edge_down[n]
+    acc[...] = normed + bias_down + dot(hidden[...], w_down[...])
     xhat_f, scale_f = normalise(acc[...])
     block_out[...] = low(xhat_f * gain_f + shift_f)
 
@@ -602,51 +605,67 @@
     acc[...] = normalise_back(out_grad, gain_f, xhat_f, scale_f)
     ffn_grad = low(acc[...])
     sums[1:2, :] = column_sum(wide(ffn_grad))
+    grad_t[...] = ffn_grad.T
     normed_t = normed_low.T
 
-    def back_step(g, _):
-        rows = pl.ds(pl.multiple_of(g * 256, 256), 256)
-        total = jnp.zeros((256, 256), jnp.float32)
+    def routes(case, name):
+        return [
+            (row_a, row_b, offset, row_b - row_a)
+            for seg, row_a, row_b, offset, _, _ in SEGMENTS[case]
+            if seg == name
+        ]
+
+    def outputs_up(case, column, targets, rx):
+        piece = target_piece(targets, case // 2, place[2] ^ (case % 2), rx)
+        return [
+            pltpu.make_async_copy(
+                grad_up.at[column * 4 : column * 4 + 4, row_a:row_b, :],
+                piece.at[offset : offset + 4 * count, :].reshape(4, count, 256),
+                sem_out.at[0],
+            )
+            for row_a, row_b, offset, count in routes(case, "up")
+        ]
+
+    def outputs(case):
+        made = []
+        for r in range(4):
+            rx, rc = r // 2, r % 2
+            column = place[3] ^ r
+            targets = grads_other if rc else grads_own
+            piece = target_piece(targets, case // 2, place[2] ^ (case % 2), rx)
+            for row_a, row_b, offset, count in routes(case, "down"):
+                source = grad_down.at[row_a:row_b, pl.ds(column * 256, 256)]
+                target = piece.at[offset : offset + count, :]
+                made.append(pltpu.make_async_copy(source, target, sem_out.at[0]))
+        return made
+
+    acc_t[...] = jnp.zeros_like(acc_t)
+
+    for chunk in range(4):
+        rows = slice(chunk * 1024, chunk * 1024 + 1024)
+        pre_grad_t = low(dot(w_down[rows, :], grad_t[...]) * slope[rows, :])
+        pre_grad = pre_grad_t.T
+        sums_up[chunk : chunk + 1, :] = column_sum(wide(pre_grad))
         for n in range(4):
-            total += dot_last(ffn_grad[:, n * 256 : n * 256 + 256], w_down[n, rows, :])
-        pre_grad = low(total * slope[g])
-        sums_up[pl.ds(g, 1), :] = column_sum(wide(pre_grad))
-        acc[...] += dot_last(pre_grad, w_up[g])
-        grad_up[g] = low(dot(normed_t, pre_grad))
-        part = low(dot_first(hidden[g], ffn_grad))
-        for n in range(4):
-            grad_down[n, rows, :] = part[:, n * 256 : n * 256 + 256]
-        return 0
-
-    lax.fori_loop(0, 16, back_step, 0)
-
-    def send(case, name, source, column):
-        made = []
-        for seg, row_a, row_b, offset, _, _ in SEGMENTS[case]:
-            count = row_b - row_a
-            if seg == name:
-                made.append((row_a, row_b, offset, count))
-        return made
-
-    started = []
-    for r in range(4):
-        rx, rc = r // 2, r % 2
-        column = place[3] ^ r
-        targets = grads_other if rc else grads_own
-        for case in range(2, 8):
-            ry = place[2] ^ (case % 2)
-            piece = target_piece(targets, case // 2, ry, rx)
-            for row_a, row_b, offset, count in send(case, "up", grad_up, column):
-                started.append(
-                    (grad_up.at[pl.ds(column * 4, 4), row_a:row_b, :],
-                     piece.at[offset : offset + 4 * count, :].reshape(4, count, 256))
-                )
-            for row_a, row_b, offset, count in send(case, "down", grad_down, column):
-                started.append(
-                    (grad_down.at[column, row_a:row_b, :], piece.at[offset : offset + count, :])
-                )
-    for source, target in started:
-        pltpu.make_async_copy(source, target, sem_out.at[0]).start()
+            g = chunk * 4 + n
+            acc_t[...] += dot(w_up[g], pre_grad_t[n * 256 : n * 256 + 256, :])
+            grad_up[g] = low(dot(normed_t, pre_grad[:, n * 256 : n * 256 + 256]))
+        grad_down[rows, :] = low(dot_first(hidden[:, rows], ffn_grad))
+        relative = place[3] ^ chunk
+        for side, targets in enumerate((grads_own, grads_other)):
+
+            @pl.when(relative % 2 == side)
+            def _(chunk=chunk, targets=targets, relative=relative):
+                for case in range(2, 6):
+                    for copy in outputs_up(case, chunk, targets, relative // 2):
+                        copy.start()
+
+        for case in {1: (5,), 2: (6,)}.get(chunk, ()):
+            for copy in outputs(case):
+                copy.start()
+    for copy in outputs(7):
+        copy.start()
+    acc[...] += acc_t[...].T
 
     normed_grad = acc[...]
     sums[2:3, :] = column_sum(normed_grad * xhat_a)
@@ -655,29 +674,30 @@
     resid_grad[...] = attn_wide
     sums[6:7, :] = column_sum(here * attn_wide)
     attn_grad = low(attn_wide)
+    grad_t[...] = attn_grad.T
     sums[0:1, :] = column_sum(wide(attn_grad))
     sums[7:8, :] = jnp.zeros((1, D), jnp.float32)
     for r, out in enumerate((g0, g1, g2, g3)):
-        rows = pl.ds(pl.multiple_of((place[3] ^ r) * 256, 256), 256)
-        total = jnp.zeros((256, 256), jnp.float32)
-        for n in range(4):
-            total += dot_last(attn_grad[:, n * 256 : n * 256 + 256], w_out[n, rows, :])
-        out[...] = low(total)
-        part = dot_first(heads[r][...], attn_grad)
-        for n in range(4):
-            grad_out[n, rows, :] = low(part[:, n * 256 : n * 256 + 256])
-    head_grad[...] = wide(grad_out[:, 0:16, :])
+        out[...] = low(dot(w_out[head_rows(r), :], grad_t[...]).T)
+        grad_out[head_rows(r), :] = low(dot_first(heads[r][...], attn_grad))
+    for n in range(4):
+        head_grad[n] = wide(grad_out[0:16, n * 256 : n * 256 + 256])
     last = []
     for r in range(4):
         rx, rc = r // 2, r % 2
         column = place[3] ^ r
         targets = grads_other if rc else grads_own
         piece = target_piece(targets, 1, place[2], rx)
-        last.append((grad_out.at[column], piece.at[0:1024, :]))
+        last.append((grad_out.at[:, pl.ds(column * 256, 256)], piece.at[0:1024, :]))
     for source, target in last:
         pltpu.make_async_copy(source, target, sem_out.at[1]).start()
-    for source, target in started:
-        pltpu.make_async_copy(source, target, sem_out.at[0]).wait()
+    for case in range(5, 8):
+        for copy in outputs(case):
+            copy.wait()
+    for column in range(4):
+        for case in range(2, 6):
+            for copy in outputs_up(case, column, grads_own, 0):
+                copy.wait()
     for source, target in last:
         pltpu.make_async_copy(source, target, sem_out.at[1]).wait()
 
@@ -689,23 +709,25 @@
         layer_kernel,
         out_shape=(
             struct((256, D)), struct((256, D), jnp.float32), block, block, block, block,
-            struct((8, D), jnp.float32), struct((16, 256), jnp.float32),
+            struct((8, D), jnp.float32), struct((4, 1024), jnp.float32),
             struct((4, 16, 256), jnp.float32),
         ) + (grads,) * 6,
         in_specs=[SMEM] + [VMEM] * 10 + [ANY] * 22,
         out_specs=(VMEM,) * 9 + (ANY,) * 6,
         scratch_shapes=[
-            pltpu.VMEM((4, 1024, 256), jnp.bfloat16),
+            pltpu.VMEM((D, D), jnp.bfloat16),
             pltpu.VMEM((16, 1024, 256), jnp.bfloat16),
-            pltpu.VMEM((4, 4096, 256), jnp.bfloat16),
+            pltpu.VMEM((FF, D), jnp.bfloat16),
             pltpu.VMEM((3, 16, 16, 256), jnp.bfloat16),
-            pltpu.VMEM((2, 4, 16, 256), jnp.bfloat16),
-            pltpu.VMEM((16, 256, 256), jnp.bfloat16),
-            pltpu.VMEM((16, 256, 256), jnp.float32),
+            pltpu.VMEM((2, 16, D), jnp.bfloat16),
+            pltpu.VMEM((256, FF), jnp.bfloat16),
+            pltpu.VMEM((FF, 256), jnp.float32),
             pltpu.VMEM((16, 1024, 256), jnp.bfloat16),
-            pltpu.VMEM((4, 4096, 256), jnp.bfloat16),
-            pltpu.VMEM((4, 1024, 256), jnp.bfloat16),
+            pltpu.VMEM((FF, D), jnp.bfloat16),
+            pltpu.VMEM((D, D), jnp.bfloat16),
             pltpu.VMEM((256, D), jnp.float32),
+            pltpu.VMEM((D, 256), jnp.float32),
+            pltpu.VMEM((D, 256), jnp.bfloat16),
             pltpu.SemaphoreType.DMA((3,)),
             pltpu.SemaphoreType.DMA((2,)),
         ],
@@ -1025,6 +1047,14 @@
     return values
 
 
+def to_relative(r):
+    return lambda z, y, x, c: (z, y, x ^ (r // 2), c ^ (r % 2))
+
+
+def exchange(blocks, name):
+    return [blocks[0]] + [send(blocks[r], to_relative(r), name) for r in range(1, 4)]
+
+
 def after(values, *earlier):
     return lax.optimization_barrier((values, *earlier))[0]
 
@@ -1039,18 +1069,18 @@
     outer = (z == 0) | (z == 3)
     first = send(own, lambda z, y, x, c: ((2, 0, 3, 1)[z], y, x, c), "first")
     y0 = send(own, to_y, "y0")
+    tokens_x = send(tokens, to_x, "tok_x")
     x0 = across("x0", own, 0)
     tokens_c = send(tokens, to_core, "tok_c")
-    second = send(jnp.where(outer, own, first), to_near, "second")
+    second = send(after(jnp.where(outer, own, first), tokens_x), to_near, "second")
     crossed = send(
         after(own, first), lambda z, y, x, c: (3 - z, y, x, c) if z in (1, 2) else None, "crossed"
     )
-    y1 = send(after(first, y0, x0), to_y, "y1")
+    y1 = send(after(first, y0), to_y, "y1")
     x1 = across("x1", after(first, x0), 1)
-    tokens_x = send(after(tokens, first, x0), to_x, "tok_x")
     third = send(after(crossed, second), only(to_near, (1, 2)), "third")
     y2 = send(after(second, y1), to_y, "y2")
-    x_a = send(after(jnp.where(z % 2 == 0, second, y0), x1), to_x, "xa")
+    x_a = send(jnp.where(z % 2 == 0, second, y0), to_x, "xa")
     last = jnp.where(outer, third, crossed)
     tokens_xc = send(after(tokens_x, third), to_core, "tok_xc")
     y3 = send(after(last, y2), to_y, "y3")
@@ -1067,9 +1097,10 @@
         jnp.where(z == 3, tail_0, jnp.where(z == 1, tail_1, tail_2)),
         jnp.where(z == 0, tail_0, jnp.where(z == 2, tail_1, tail_2)),
     )
-    attended = lax.optimization_barrier((*attended, x_a, y3, yx2))[: len(attended)]
+    attended = lax.optimization_barrier((*attended, x_a, y3, yx2, x3, y_b))[: len(attended)]
     stack = send(attended[-1], to_core, "stack")
-    yx3 = across("yx3", after(y3, attended[-1]), 3)
+    heads = exchange(attended[5:9], "heads")
+    yx3 = across("yx3", after(y3, x3, attended[-1]), 3)
     later = [
         send(after(piece, attended[-1]), only(to_core, planes), name)
         for piece, planes, name in (
@@ -1078,7 +1109,7 @@
         )
     ]
     mine = [own, first, second, last, y0, y1, y2, x0, x1, x_a, y3, y_b, yx2, x3, yx3]
-    return attended[:-1], [*mine, stack, *later]
+    return attended[:5], heads, attended[9], [*mine, stack, *later]
 
 
 def add(left, right):
@@ -1126,17 +1157,11 @@
         vectors["head"] = absolute(head_tail)
         return attend(after(place, ready), all_tokens, vectors["embed"], vec_own[0:8], held)
 
-    attended, pieces = gather_pieces(own, z, y, tokens, run_attend)
-    stream, weight, query, key, value, h0, h1, h2, h3, lse = attended
-
-    def to_relative(r):
-        return lambda z, y, x, c: (z, y, x ^ (r // 2), c ^ (r % 2))
-
-    def exchange(blocks, name):
-        return [blocks[0]] + [send(blocks[r], to_relative(r), name) for r in range(1, 4)]
+    attended, heads, lse, pieces = gather_pieces(own, z, y, tokens, run_attend)
+    stream, weight, query, key, value = attended
 
     (block_out, resid_grad, g0, g1, g2, g3, sums, sums_up, head_grad, *grads) = layer(
-        place, exchange((h0, h1, h2, h3), "heads"), tokens, cotangent, vectors["embed"],
+        place, heads, tokens, cotangent, vectors["embed"],
         vectors["rows"], vectors["up"], vectors["head"], pieces,
     )
     grads_own, grads_other = grads[:3], grads[3:]
@@ -1165,9 +1190,19 @@
     q_grad, k_grad, v_grad, kept, sent, sums_qkv, d1, d2 = lax.optimization_barrier(
         (q_grad, k_grad, v_grad, kept, sent, sums_qkv, d1, d2)
     )
-    f1 = send(low(over_cores(1, 0, 1) + wide(d1)), to_x, "f1")
-    f2 = send(low(over_cores(2, 0, 1) + wide(d2)), to_y, "f2")
-    d3 = send(after(low(over_cores(3, 1, 1)), e1, e2), to_x, "d3")
+    sum_1 = low(over_cores(1, 0, 1) + wide(d1))
+    sum_2 = low(over_cores(2, 0, 1) + wide(d2))
+    sum_3 = low(over_cores(3, 1, 1))
+    sum_1, sum_2, sum_3, e1, e2, sent = lax.optimization_barrier(
+        (sum_1, sum_2, sum_3, e1, e2, sent)
+    )
+    from_core = send(sent, to_core, "in_c")
+    f1 = send(sum_1, to_x, "f1")
+    f2 = send(sum_2, to_y, "f2")
+    q_grad, k_grad, v_grad, sum_3, from_core = lax.optimization_barrier(
+        (q_grad, k_grad, v_grad, sum_3, from_core)
+    )
+    d3 = send(sum_3, to_x, "d3")
     e3 = send(after(low(over_cores(3, 1, 0)), f1), to_x, "e3")
 
     rows = stream.reshape(1024, D)
@@ -1176,21 +1211,21 @@
     piece_0 = jnp.concatenate([w_grads[0], w_grads[1][:528], rest])
     piece_1 = jnp.concatenate([w_grads[1][512:], w_grads[2], rest, rest[:16]])
     low_row = y == 0
-    ry0 = send(after(jnp.where(low_row, piece_1, piece_0), e1), to_y, "ry0")
-    f3 = send(low(over_cores(3, 0, 1) + wide(after(d3, ry0))), to_y, "f3")
-
+    other_row = jnp.where(low_row, piece_1, piece_0)
+    ry0 = send(other_row, to_y, "ry0")
     kept_1, sent_1 = combine(
-        place, (grads_own[1], moved[2], e2, f2), (grads_own[0], moved[1], e1, f1)
-    )
-    inner_part = low(add(kept_1, send(sent_1, to_near, "rz_inner1")))
+        after(place, other_row, sum_3), (grads_own[1], moved[2], e2, f2), (grads_own[0], moved[1], e1, f1)
+    )
+    got_inner = send(sent_1, to_near, "rz_inner1")
+    inner_part = low(add(kept_1, got_inner))
     inner_last = send(inner_part, only(to_far, (0, 3)), "rz_inner2")
+    f3 = send(low(over_cores(3, 0, 1) + wide(after(d3, ry0, got_inner))), to_y, "f3")
     kept_0, sent_0 = combine(
         place, (jnp.where(low_row, piece_0, piece_1), ry0), (grads_own[2], moved[3], e3, f3)
     )
-    outer_part = low(add(kept_0, send(sent_0, to_near, "rz_outer1")))
+    outer_part = low(add(kept_0, send(after(sent_0, inner_last), to_near, "rz_outer1")))
     outer_last = send(outer_part, only(to_far, (1, 2)), "rz_outer2")
 
-    from_core = send(sent, to_core, "in_c")
     in_x = send(after(low(kept[1] + wide(from_core[1])), e3), to_x, "in_x")
     input_grad = (
         resid_grad

time: 417 us -> 377 us (0.904)
  Pallas kernels: 96.5 us -> 71.8 us
  waiting for transfers between devices: 198 us -> 180 us
  starting transfers between devices: 64 us -> 57.7 us
    ppermute x59, waiting for transfers between devices: 198 us -> 180 us  [send(): return lax.ppermute(values, AXES, pairs)]
    pallas_call x1, Pallas kernels: 43.5 us -> 28.7 us  [layer(): pl.pallas_call(layer_kernel, out_shape=(struct((256, D)), struct((256, D)...]
    ppermute x59, starting transfers between devices: 64 us -> 57.7 us  [send(): return lax.ppermute(values, AXES, pairs)]
    pallas_call x1, Pallas kernels: 20.4 us -> 16 us  [attend_back(): pl.pallas_call(attend_back_kernel, out_shape=(square, square, square, str...]
  transfers between devices with their start and end apart: 59 -> 59, of which waited for: 33 -> 38; matrix products, arithmetic and copies ran while one was open for 8% -> 10% of each run, Pallas kernels for 12% -> 9%
where the time goes in v3:
time: 377 us; the launch traced here: 372 us
  waiting for transfers between devices  180 us (48%)
  Pallas kernels  71.8 us (19%)
  starting transfers between devices  57.7 us (15%)
  other arithmetic  36.8 us (10%)
  local copies, waits for them, and re-layouts  14.1 us (4%)
  between operations  7.66 us (2%)
  matrix products  4.1 us (1%)
    ppermute x59, waiting for transfers between devices, send(): return lax.ppermute(values, AXES, pairs)  180 us
    ppermute x59, starting transfers between devices, send(): return lax.ppermute(values, AXES, pairs)  57.7 us
    pallas_call x1, Pallas kernels, layer(): pl.pallas_call(layer_kernel, out_shape=(struct((256, D)), struct((256, D)...  28.7 us
    convert_element_type x10, other arithmetic, low(): return values.astype(jnp.bfloat16)  16.8 us
    pallas_call x1, Pallas kernels, attend_back(): pl.pallas_call(attend_back_kernel, out_shape=(square, square, square, str...  16 us
    pallas_call x1, Pallas kernels, attend(): pl.pallas_call(attend_kernel, out_shape=(struct((4, 256, 1024)), struct((...  14.5 us
    pallas_call x2, Pallas kernels, combine(): pl.pallas_call(partial(combine_kernel, len(first)), grid=(blocks,), out_s...  7.78 us
  transfers between devices with their start and end apart: 59, of which 38 were waited for; matrix products, arithmetic and copies ran while one was open for 10% of the time, Pallas kernels for 9%

profile of v3, /device:TPU:0, one launch (start us, length us, event | category | flops | bytes accessed | tf_op | source)
XLA Modules:
  0.0 372.0 jit_solution(7833913941715925214)
XLA Ops:
  2.3 3.0 collective-permute-start
  5.3 1.6 collective-permute-done
  6.9 1.5 pad_bitcast_fusion.flat
  10.8 3.4 collective-permute-start.2
  14.2 1.9 collective-permute-start.7
  16.0 1.5 collective-permute-start.4
  18.2 14.1 %collective-permute-done.2.p2.refs_1_ = bf16[1600,256]{1,0:T(8,128)(2,1)S(1)} collective-permute-done((bf16[1600,256]{1,0:T(8,128)(2,1)S(1)}, bf16[1600,256]{1,0:T(8,128)(2,1)S(1)}, u32[]{:S(2)}, u32[]{:S(2)}) %collective-permute-start.2) | collective-permute-done | bytes 819232 | tf_op jit(solution)/shard_map/first/ppermute | solution.py:1014
  32.4 2.4 collective-permute-done.7.p1.refs_4_
  34.8 1.7 collective-permute-start.8
  37.7 1.6 collective-permute-start.3
  40.2 3.4 collective-permute-start.13
  44.4 10.2 %collective-permute-done.8.p3.refs_5_ = bf16[1600,256]{1,0:T(8,128)(2,1)} collective-permute-done((bf16[1600,256]{1,0:T(8,128)(2,1)S(1)}, bf16[1600,256]{1,0:T(8,128)(2,1)}, u32[]{:S(2)}, u32[]{:S(2)}) %collective-permute-start.8) | collective-permute-done | bytes 819232 | tf_op jit(solution)/shard_map/y1/ppermute | solution.py:1014
  54.6 2.5 collective-permute-done.5.p4.refs_2_
  57.5 1.3 collective-permute-start.6
  60.0 1.6 collective-permute-start.14
  62.1 1.3 broadcast_select_fusion.2
  63.4 14.9 %collective-permute-done.6 = bf16[1600,256]{1,0:T(8,128)(2,1)S(1)} collective-permute-done((bf16[1600,256]{1,0:T(8,128)(2,1)}, bf16[1600,256]{1,0:T(8,128)(2,1)S(1)}, u32[]{:S(2)}, u32[]{:S(2)}) %collective-permute-start.6) | collective-permute-done | bytes 819232 | tf_op jit(solution)/shard_map/third/ppermute | solution.py:1014
  79.5 1.5 collective-permute-start.17
  83.8 2.4 collective-permute-start.16
  86.3 14.5 %attend.1 = (bf16[4,256,1024]{2,1,0:T(8,128)(2,1)}, bf16[3,1024,256]{2,1,0:T(8,128)(2,1)}, bf16[1024,256]{1,0:T(8,128)(2,1)S(1)}, bf16[1024,256]{1,0:T(8,128)(2,...) custom-call(s32[6]{0:T(128)S(1)} %stack.19.place, ...), custom_call_target="tpu_custom_call" | custom-call | flops 16000000000 | bytes 24000000 | tf_op jit(solution)/shard_map/attend/pallas_call | solution.py:369
  104.7 8.8 %collective-permute-done.18.refs_11_ = bf16[1600,256]{1,0:T(8,128)(2,1)S(1)} collective-permute-done((bf16[1600,256]{1,0:T(8,128)(2,1)S(1)}, bf16[1600,256]{1,0:T(8,128)(2,1)S(1)}, u32[]{:S(2)}, u32[]{:S(2)}) %collective-permute-start.18) | collective-permute-done | bytes 819232 | tf_op jit(solution)/shard_map/yb/ppermute | solution.py:1014
  114.3 1.6 collective-permute-start.22
  116.0 2.2 collective-permute-start.27
  118.5 8.0 %collective-permute-done.19.h1 = bf16[256,256]{1,0:T(8,128)(2,1)S(1)} collective-permute-done((bf16[256,256]{1,0:T(8,128)(2,1)S(1)}, bf16[256,256]{1,0:T(8,128)(2,1)S(1)}, u32[]{:S(2)}, u32[]{:S(2)}) %collective-permute-start.19) | collective-permute-done | bytes 131104 | tf_op jit(solution)/shard_map/heads/ppermute | solution.py:1014
  127.0 8.4 %collective-permute-done.22.refs_14_ = bf16[1600,256]{1,0:T(8,128)(2,1)S(1)} collective-permute-done((bf16[1600,256]{1,0:T(8,128)(2,1)S(1)}, bf16[1600,256]{1,0:T(8,128)(2,1)S(1)}, u32[]{:S(2)}, u32[]{:S(2)}) %collective-permute-start.22) | collective-permute-done | bytes 819232 | tf_op jit(solution)/shard_map/yx3/ppermute | solution.py:1014
  136.4 1.3 collective-permute-done.20.h2
  137.8 3.4 collective-permute-done.21.h3
  143.7 2.3 collective-permute-done.24.refs_16_
  147.9 28.7 %layer.1 = (bf16[256,1024]{1,0:T(8,128)(2,1)}, f32[256,1024]{1,0:T(8,128)}, bf16[256,256]{1,0:T(8,128)(2,1)}, bf16[256,256]{1,0:T(8,128)(2,1)}, bf16[256,256]{1,...) custom-call(s32[6]{0:T(128)} %copy-done.1, ...), custom_call_target="tpu_custom_call" | custom-call | flops 15000000512 | bytes 40000000 | tf_op jit(solution)/shard_map/layer/pallas_call | solution.py:708
  179.0 3.7 collective-permute-done.34.refs_1_
  182.7 3.0 fusion.8
  185.7 1.8 collective-permute-done.31.g1
  187.8 1.3 fusion.7
  193.3 16.0 %attend_back.1 = (bf16[1024,256]{1,0:T(8,128)(2,1)S(1)}, bf16[1024,256]{1,0:T(8,128)(2,1)S(1)}, bf16[1024,256]{1,0:T(8,128)(2,1)S(1)}, f32[2,256,1024]{2,1,0:T(8...) custom-call(s32[6]{0:T(128)S(1)} %copy-done.2, bf16[1024,256]{1,0:T(8,128)(2,1)S(1)} %copy-done.12, ...), custom_call_target="tpu_custom_call" | custom-call | flops 20000000000 | bytes 12000000 | tf_op jit(solution)/shard_map/attend_back/pallas_call | solution.py:460
  211.5 2.6 fusion.1
  214.1 2.5 fusion.2
  216.6 1.9 fusion.10
  218.7 8.6 %collective-permute-done.39.refs_2_ = bf16[1600,256]{1,0:T(8,128)(2,1)} collective-permute-done((bf16[1600,256]{1,0:T(8,128)(2,1)S(1)}, bf16[1600,256]{1,0:T(8,128)(2,1)}, u32[]{:S(2)}, u32[]{:S(2)}) %collective-permute-start.39) | collective-permute-done | bytes 819232 | tf_op jit(solution)/shard_map/e2/ppermute | solution.py:1014
  230.9 2.6 convolution_convert_fusion.1
  235.4 1.6 broadcast_select_fusion
  236.9 12.3 %collective-permute-done.41.refs_7_ = bf16[1600,256]{1,0:T(8,128)(2,1)} collective-permute-done((bf16[1600,256]{1,0:T(8,128)(2,1)}, bf16[1600,256]{1,0:T(8,128)(2,1)}, u32[]{:S(2)}, u32[]{:S(2)}) %collective-permute-start.41) | collective-permute-done | bytes 819232 | tf_op jit(solution)/shard_map/f1/ppermute | solution.py:1014
  250.1 4.2 %combine.2 = (bf16[1600,256]{1,0:T(8,128)(2,1)}, bf16[1600,256]{1,0:T(8,128)(2,1)}) custom-call(s32[6]{0:T(128)} %copy-done.1, bf16[2,2,1600,256]{3,2,1,0:T(8,128)(2,1)} %get-tuple-element.149.refs_0_, bf16[2,2,1600,256]{3,2,1,0:T(8,128)(2,1)} %copy-done.24, bf16[1600,256]{1,0:T(8,128)(2,1)} %collective-permute-done.39.refs_2_, ...), custom_call_target="tpu_custom_call" | custom-call | tf_op jit(solution)/shard_map/combine/pallas_call | solution.py:257
  257.6 16.5 %collective-permute-done.47 = bf16[1600,256]{1,0:T(8,128)(2,1)S(1)} collective-permute-done((bf16[1600,256]{1,0:T(8,128)(2,1)}, bf16[1600,256]{1,0:T(8,128)(2,1)S(1)}, u32[]{:S(2)}, u32[]{:S(2)}) %collective-permute-start.47) | collective-permute-done | bytes 819232 | tf_op jit(solution)/shard_map/rz_inner1/ppermute | solution.py:1014
  274.2 2.5 collective-permute-done.50
  276.7 2.6 fusion
  280.5 5.2 %collective-permute-start.48 = (bf16[1600,256]{1,0:T(8,128)(2,1)S(1)}, bf16[1600,256]{1,0:T(8,128)(2,1)}, u32[]{:S(2)}, u32[]{:S(2)}) collective-permute-start(bf16[1600,256]{1,0:T(8,128)(2,1)S(1)} %add_convert_fusion.1.inner), channel_id=1, source_target_pairs={{0,16},{1,17},{2,18},{3,19},{4,20},{5,21},{6,22},{7,23},{24,8},{25... | collective-permute-start | bytes 2457608 | tf_op jit(solution)/shard_map/rz_inner2/ppermute | solution.py:1014
  287.0 5.5 %collective-permute-done.42.refs_4_ = bf16[1600,256]{1,0:T(8,128)(2,1)} collective-permute-done((bf16[1600,256]{1,0:T(8,128)(2,1)}, bf16[1600,256]{1,0:T(8,128)(2,1)}, u32[]{:S(2)}, u32[]{:S(2)}) %collective-permute-start.42) | collective-permute-done | bytes 819232 | tf_op jit(solution)/shard_map/e3/ppermute | solution.py:1014
  292.5 3.7 %collective-permute-done.51.refs_5_ = bf16[1600,256]{1,0:T(8,128)(2,1)} collective-permute-done((bf16[1600,256]{1,0:T(8,128)(2,1)}, bf16[1600,256]{1,0:T(8,128)(2,1)}, u32[]{:S(2)}, u32[]{:S(2)}) %collective-permute-start.51) | collective-permute-done | bytes 819232 | tf_op jit(solution)/shard_map/f3/ppermute | solution.py:1014
  296.2 3.6 combine.3
  301.6 1.2 fusion.11
  303.8 12.3 %collective-permute-done.52 = bf16[1600,256]{1,0:T(8,128)(2,1)} collective-permute-done((bf16[1600,256]{1,0:T(8,128)(2,1)}, bf16[1600,256]{1,0:T(8,128)(2,1)}, u32[]{:S(2)}, u32[]{:S(2)}) %collective-permute-start.52) | collective-permute-done | bytes 819232 | tf_op jit(solution)/shard_map/rz_outer1/ppermute | solution.py:1014
  316.2 1.4 add_convert_fusion.outer
  317.6 1.3 collective-permute-start.53
  319.9 3.0 collective-permute-done.45
  322.9 2.3 fusion.4
  325.2 11.3 %collective-permute-done.53.outer_last = bf16[1600,256]{1,0:T(8,128)(2,1)} collective-permute-done((bf16[1600,256]{1,0:T(8,128)(2,1)S(1)}, bf16[1600,256]{1,0:T(8,128)(2,1)}, u32[]{:S(2)}, u32[]{:S(2)}) %collective-permute-start.53) | collective-permute-done | bytes 819232 | tf_op jit(solution)/shard_map/rz_outer2/ppermute | solution.py:1014
  336.5 4.0 %unpack.1 = (f32[3080,128]{1,0:T(8,128)}, f32[8,128]{1,0:T(8,128)}) custom-call(s32[6]{0:T(128)} %copy-done.1, bf16[1600,256]{1,0:T(8,128)(2,1)} %copy-done.27, bf16[1600,256]{1,0:T(8,128)(2,1)} %collective-permute-done.48.inner_last, bf16[1600,256]{1,0:T(8,128)(2,1)} %copy-done.28, bf16[1600,256]{1,0:T(8,128)(2,1)} %collective-permute-done.53.outer_last), custom_call_target="tpu_custom_call" | custom-call | tf_op jit(solution)/shard_map/unpack/pallas_call | solution.py:222
  341.3 1.3 collective-permute-start.54
  342.6 2.7 collective-permute-done.54
  345.4 4.0 %collective-permute-done.55 = f32[40,256]{1,0:T(8,128)S(1)} collective-permute-done((f32[40,256]{1,0:T(8,128)S(1)}, f32[40,256]{1,0:T(8,128)S(1)}, u32[]{:S(2)}, u32[]{:S(2)}) %collective-permute-start.55) | collective-permute-done | bytes 40992 | tf_op jit(solution)/shard_map/norm/ppermute | solution.py:1014
  349.5 4.8 %collective-permute-done.56 = f32[40,256]{1,0:T(8,128)S(1)} collective-permute-done((f32[40,256]{1,0:T(8,128)S(1)}, f32[40,256]{1,0:T(8,128)S(1)}, u32[]{:S(2)}, u32[]{:S(2)}) %collective-permute-start.56) | collective-permute-done | bytes 40992 | tf_op jit(solution)/shard_map/norm/ppermute | solution.py:1014
  359.8 1.9 collective-permute-done.57
  361.7 1.6 fusion.16
  364.5 6.0 %multiply_add_fusion = (f32[393664]{0:T(1024)}, f32[393664]{0:T(1024)}, f32[393664]{0:T(1024)}, f32[393664]{0:T(1024)}) fusion(f32[393664]{0:T(1024)S(1)} %copy-done.29, f32[393664]{0:T(1024)S(1)} %copy-done.26, f32[]{:T(128)S(6)} %div.48, f32[394240]{0:T(1024)} %fusion.16, f32[393664]{0:T(1024)} %param.13, f32[393664]{0:T(1024)} %param.12), kind=kLoop, calls=%fused_computation.17 | loop fusion | flops 7479616 | bytes 14171908 | tf_op jit(solution)/shard_map/add | solution.py:1286
  (264 shorter events, 52.7 us)
Async XLA Ops:
  2.3 4.6 %collective-permute-start = (bf16[16,256]{1,0:T(8,128)(2,1)S(1)}, bf16[16,256]{1,0:T(8,128)(2,1)S(1)}, u32[]{:S(2)}, u32[]{:S(2)}) collective-permute-start(bf16[16,256]{1,0:T(8,128)(2,1)S(1)} %select_convert_fusion), channel_id=1, source_target_pairs={{0,2},{1,3},{2,0},{3,1},{4,6},{5,7},{6,4},{7,5},{8,10},{9,11},{10,... | collective-permute-start | bytes 24584 | tf_op jit(solution)/shard_map/tail_x/ppermute | solution.py:1014
  6.9 3.0 collective-permute-start.1
  9.9 76.4 %copy-start.1 = (s32[6]{0:T(128)}, s32[6]{0:T(128)S(1)}, u32[]{:S(2)}) copy-start(s32[6]{0:T(128)S(1)} %stack.19.place) | copy-start | bytes 76
  10.8 75.5 %copy-start = (bf16[1600,256]{1,0:T(8,128)(2,1)}, bf16[1600,256]{1,0:T(8,128)(2,1)S(1)}, u32[]{:S(2)}) copy-start(bf16[1600,256]{1,0:T(8,128)(2,1)S(1)} %pack.1.p0.refs_0_) | copy-start | bytes 2457604
  10.8 21.6 %collective-permute-start.2 = (bf16[1600,256]{1,0:T(8,128)(2,1)S(1)}, bf16[1600,256]{1,0:T(8,128)(2,1)S(1)}, u32[]{:S(2)}, u32[]{:S(2)}) collective-permute-start(bf16[1600,256]{1,0:T(8,128)(2,1)S(1)} %pack.1.p0.refs_0_), channel_id=1, source_target_pairs={{0,16},{1,17},{2,18},{3,19},{4,20},{5,21},{6,22},{7,23},{8,0},{9,1... | collective-permute-start | bytes 2457608 | tf_op jit(solution)/shard_map/first/ppermute | solution.py:1014
  14.2 20.6 %collective-permute-start.7 = (bf16[1600,256]{1,0:T(8,128)(2,1)S(1)}, bf16[1600,256]{1,0:T(8,128)(2,1)}, u32[]{:S(2)}, u32[]{:S(2)}) collective-permute-start(bf16[1600,256]{1,0:T(8,128)(2,1)S(1)} %pack.1.p0.refs_0_), channel_id=1, source_target_pairs={{0,4},{1,5},{2,6},{3,7},{4,0},{5,1},{6,2},{7,3},{8,12},{9,13},{10,... | collective-permute-start | bytes 2457608 | tf_op jit(solution)/shard_map/y0/ppermute | solution.py:1014
  16.0 21.5 %collective-permute-start.4 = (bf16[256,1024]{1,0:T(8,128)(2,1)S(1)}, bf16[256,1024]{1,0:T(8,128)(2,1)S(1)}, u32[]{:S(2)}, u32[]{:S(2)}) collective-permute-start(bf16[256,1024]{1,0:T(8,128)(2,1)S(1)} %copy-done.4), channel_id=1, source_target_pairs={{0,2},{1,3},{2,0},{3,1},{4,6},{5,7},{6,4},{7,5},{8,10},{9,11},{10,... | collective-permute-start | bytes 1572872 | tf_op jit(solution)/shard_map/tok_x/ppermute | solution.py:1014
  17.5 21.8 %collective-permute-start.12 = (bf16[1600,256]{1,0:T(8,128)(2,1)S(1)}, bf16[1600,256]{1,0:T(8,128)(2,1)S(1)}, u32[]{:S(2)}, u32[]{:S(2)}) collective-permute-start(bf16[1600,256]{1,0:T(8,128)(2,1)S(1)} %pack.1.p0.refs_0_), channel_id=1, source_target_pairs={{8,10},{9,11},{10,8},{11,9},{12,14},{13,15},{14,12},{15,13},{16,18... | collective-permute-start | bytes 2457608 | tf_op jit(solution)/shard_map/x0/ppermute | solution.py:1014
  32.3 48.6 %copy-start.31 = (bf16[1600,256]{1,0:T(8,128)(2,1)}, bf16[1600,256]{1,0:T(8,128)(2,1)S(1)}, u32[]{:S(2)}) copy-start(bf16[1600,256]{1,0:T(8,128)(2,1)S(1)} %collective-permute-done.2.p2.refs_1_) | copy-start | bytes 2457604
  34.8 19.8 %collective-permute-start.8 = (bf16[1600,256]{1,0:T(8,128)(2,1)S(1)}, bf16[1600,256]{1,0:T(8,128)(2,1)}, u32[]{:S(2)}, u32[]{:S(2)}) collective-permute-start(bf16[1600,256]{1,0:T(8,128)(2,1)S(1)} %collective-permute-done.2.p2.refs_1_), channel_id=1, source_target_pairs={{0,4},{1,5},{2,6},{3,7},{4,0},{5,1},{6,2},{7,3},{8,12},{9,13},{10,... | collective-permute-start | bytes 2457608 | tf_op jit(solution)/shard_map/y1/ppermute | solution.py:1014
  37.5 19.6 %collective-permute-start.5 = (bf16[1600,256]{1,0:T(8,128)(2,1)}, bf16[1600,256]{1,0:T(8,128)(2,1)}, u32[]{:S(2)}, u32[]{:S(2)}) collective-permute-start(bf16[1600,256]{1,0:T(8,128)(2,1)} %broadcast_select_fusion.5), channel_id=1, source_target_pairs={{0,8},{1,9},{2,10},{3,11},{4,12},{5,13},{6,14},{7,15},{8,0},{9,1},... | collective-permute-start | bytes 2457608 | tf_op jit(solution)/shard_map/second/ppermute | solution.py:1014
  37.7 19.8 %collective-permute-start.3 = (bf16[1600,256]{1,0:T(8,128)(2,1)S(1)}, bf16[1600,256]{1,0:T(8,128)(2,1)}, u32[]{:S(2)}, u32[]{:S(2)}) collective-permute-start(bf16[1600,256]{1,0:T(8,128)(2,1)S(1)} %pack.1.p0.refs_0_), channel_id=1, source_target_pairs={{8,16},{9,17},{10,18},{11,19},{12,20},{13,21},{14,22},{15,23},{16,... | collective-permute-start | bytes 2457608 | tf_op jit(solution)/shard_map/crossed/ppermute | solution.py:1014
  40.2 21.9 %collective-permute-start.13 = (bf16[1600,256]{1,0:T(8,128)(2,1)S(1)}, bf16[1600,256]{1,0:T(8,128)(2,1)}, u32[]{:S(2)}, u32[]{:S(2)}) collective-permute-start(bf16[1600,256]{1,0:T(8,128)(2,1)S(1)} %collective-permute-done.2.p2.refs_1_), channel_id=1, source_target_pairs={{0,2},{1,3},{2,0},{3,1},{4,6},{5,7},{6,4},{7,5},{8,10},{9,11},{10,... | collective-permute-start | bytes 2457608 | tf_op jit(solution)/shard_map/x1/ppermute | solution.py:1014
  43.6 38.4 %collective-permute-start.10 = (bf16[256,1024]{1,0:T(8,128)(2,1)S(1)}, bf16[256,1024]{1,0:T(8,128)(2,1)S(1)}, u32[]{:S(2)}, u32[]{:S(2)}) collective-permute-start(bf16[256,1024]{1,0:T(8,128)(2,1)S(1)} %copy-done.4), channel_id=1, source_target_pairs={{0,1},{1,0},{2,3},{3,2},{4,5},{5,4},{6,7},{7,6},{8,9},{9,8},{10,11... | collective-permute-start | bytes 1572872 | tf_op jit(solution)/shard_map/tok_c/ppermute | solution.py:1014
  57.1 21.4 %collective-permute-start.9 = (bf16[1600,256]{1,0:T(8,128)(2,1)}, bf16[1600,256]{1,0:T(8,128)(2,1)S(1)}, u32[]{:S(2)}, u32[]{:S(2)}) collective-permute-start(bf16[1600,256]{1,0:T(8,128)(2,1)} %collective-permute-done.5.p4.refs_2_), channel_id=1, source_target_pairs={{0,4},{1,5},{2,6},{3,7},{4,0},{5,1},{6,2},{7,3},{8,12},{9,13},{10,... | collective-permute-start | bytes 2457608 | tf_op jit(solution)/shard_map/y2/ppermute | solution.py:1014
  57.5 20.8 %collective-permute-start.6 = (bf16[1600,256]{1,0:T(8,128)(2,1)}, bf16[1600,256]{1,0:T(8,128)(2,1)S(1)}, u32[]{:S(2)}, u32[]{:S(2)}) collective-permute-start(bf16[1600,256]{1,0:T(8,128)(2,1)} %collective-permute-done.3), channel_id=1, source_target_pairs={{8,0},{9,1},{10,2},{11,3},{12,4},{13,5},{14,6},{15,7},{16,24},{17,... | collective-permute-start | bytes 2457608 | tf_op jit(solution)/shard_map/third/ppermute | solution.py:1014
  60.0 44.7 %collective-permute-start.14 = (bf16[1600,256]{1,0:T(8,128)(2,1)S(1)}, bf16[1600,256]{1,0:T(8,128)(2,1)S(1)}, u32[]{:S(2)}, u32[]{:S(2)}) collective-permute-start(bf16[1600,256]{1,0:T(8,128)(2,1)S(1)} %broadcast_select_fusion.3), channel_id=1, source_target_pairs={{0,2},{1,3},{2,0},{3,1},{4,6},{5,7},{6,4},{7,5},{8,10},{9,11},{10,... | collective-permute-start | bytes 2457608 | tf_op jit(solution)/shard_map/xa/ppermute | solution.py:1014
  78.5 35.7 %collective-permute-start.15 = (bf16[1600,256]{1,0:T(8,128)(2,1)S(1)}, bf16[1600,256]{1,0:T(8,128)(2,1)S(1)}, u32[]{:S(2)}, u32[]{:S(2)}) collective-permute-start(bf16[1600,256]{1,0:T(8,128)(2,1)S(1)} %broadcast_select_fusion.4.p6.refs_3_), channel_id=1, source_target_pairs={{0,4},{1,5},{2,6},{3,7},{4,0},{5,1},{6,2},{7,3},{8,12},{9,13},{10,... | collective-permute-start | bytes 2457608 | tf_op jit(solution)/shard_map/y3/ppermute | solution.py:1014
  79.5 34.7 %collective-permute-start.17 = (bf16[1600,256]{1,0:T(8,128)(2,1)S(1)}, bf16[1600,256]{1,0:T(8,128)(2,1)}, u32[]{:S(2)}, u32[]{:S(2)}) collective-permute-start(bf16[1600,256]{1,0:T(8,128)(2,1)S(1)} %broadcast_select_fusion.4.p6.refs_3_), channel_id=1, source_target_pairs={{0,2},{1,3},{2,0},{3,1},{4,6},{5,7},{6,4},{7,5},{8,10},{9,11},{10,... | collective-permute-start | bytes 2457608 | tf_op jit(solution)/shard_map/x3/ppermute | solution.py:1014
  81.8 2.0 collective-permute-start.11
  82.0 31.5 %collective-permute-start.18 = (bf16[1600,256]{1,0:T(8,128)(2,1)S(1)}, bf16[1600,256]{1,0:T(8,128)(2,1)S(1)}, u32[]{:S(2)}, u32[]{:S(2)}) collective-permute-start(bf16[1600,256]{1,0:T(8,128)(2,1)S(1)} %broadcast_select_fusion.2), channel_id=1, source_target_pairs={{0,4},{1,5},{2,6},{3,7},{4,0},{5,1},{6,2},{7,3},{8,12},{9,13},{10,... | collective-permute-start | bytes 2457608 | tf_op jit(solution)/shard_map/yb/ppermute | solution.py:1014
  83.8 30.4 %collective-permute-start.16 = (bf16[1600,256]{1,0:T(8,128)(2,1)S(1)}, bf16[1600,256]{1,0:T(8,128)(2,1)}, u32[]{:S(2)}, u32[]{:S(2)}) collective-permute-start(bf16[1600,256]{1,0:T(8,128)(2,1)S(1)} %collective-permute-done.9.p5.refs_6_), channel_id=1, source_target_pairs={{0,2},{1,3},{2,0},{3,1},{4,6},{5,7},{6,4},{7,5},{16,18},{17,19},{1... | collective-permute-start | bytes 2457608 | tf_op jit(solution)/shard_map/yx2/ppermute | solution.py:1014
  104.7 31.1 %copy-start.43 = (bf16[1600,256]{1,0:T(8,128)(2,1)}, bf16[1600,256]{1,0:T(8,128)(2,1)S(1)}, u32[]{:S(2)}) copy-start(bf16[1600,256]{1,0:T(8,128)(2,1)S(1)} %collective-permute-done.14.refs_9_) | copy-start | bytes 2457604
  114.2 33.6 %collective-permute-start.23 = (bf16[9,1600,256]{2,1,0:T(8,128)(2,1)}, bf16[9,1600,256]{2,1,0:T(8,128)(2,1)}, u32[]{:S(2)}, u32[]{:S(2)}) collective-permute-start(bf16[9,1600,256]{2,1,0:T(8,128)(2,1)} %get-tuple-element.132), channel_id=1, source_target_pairs={{0,1},{1,0},{2,3},{3,2},{4,5},{5,4},{6,7},{7,6},{8,9},{9,8},{10,11... | collective-permute-start | bytes 22118408 | tf_op jit(solution)/shard_map/stack/ppermute | solution.py:1014
  114.3 21.1 %collective-permute-start.22 = (bf16[1600,256]{1,0:T(8,128)(2,1)S(1)}, bf16[1600,256]{1,0:T(8,128)(2,1)S(1)}, u32[]{:S(2)}, u32[]{:S(2)}) collective-permute-start(bf16[1600,256]{1,0:T(8,128)(2,1)S(1)} %collective-permute-done.15.refs_10_), channel_id=1, source_target_pairs={{0,2},{1,3},{2,0},{3,1},{4,6},{5,7},{6,4},{7,5},{8,10},{9,11},{10,... | collective-permute-start | bytes 2457608 | tf_op jit(solution)/shard_map/yx3/ppermute | solution.py:1014
  115.8 25.4 %collective-permute-start.28 = (bf16[1600,256]{1,0:T(8,128)(2,1)}, bf16[1600,256]{1,0:T(8,128)(2,1)S(1)}, u32[]{:S(2)}, u32[]{:S(2)}) collective-permute-start(bf16[1600,256]{1,0:T(8,128)(2,1)} %collective-permute-done.17.refs_13_), channel_id=1, source_target_pairs={{0,1},{1,0},{2,3},{3,2},{4,5},{5,4},{6,7},{7,6},{8,9},{9,8},{10,11... | collective-permute-start | bytes 2457608 | tf_op jit(solution)/shard_map/cx3/ppermute | solution.py:1014
  116.0 25.7 %collective-permute-start.27 = (bf16[1600,256]{1,0:T(8,128)(2,1)}, bf16[1600,256]{1,0:T(8,128)(2,1)}, u32[]{:S(2)}, u32[]{:S(2)}) collective-permute-start(bf16[1600,256]{1,0:T(8,128)(2,1)} %collective-permute-done.16.refs_12_), channel_id=1, source_target_pairs={{0,1},{1,0},{2,3},{3,2},{4,5},{5,4},{6,7},{7,6},{16,17},{17,16},{1... | collective-permute-start | bytes 2457608 | tf_op jit(solution)/shard_map/cyx2/ppermute | solution.py:1014
  118.3 8.3 %collective-permute-start.19 = (bf16[256,256]{1,0:T(8,128)(2,1)S(1)}, bf16[256,256]{1,0:T(8,128)(2,1)S(1)}, u32[]{:S(2)}, u32[]{:S(2)}) collective-permute-start(bf16[256,256]{1,0:T(8,128)(2,1)S(1)} %get-tuple-element.129), channel_id=1, source_target_pairs={{0,1},{1,0},{2,3},{3,2},{4,5},{5,4},{6,7},{7,6},{8,9},{9,8},{10,11... | collective-permute-start | bytes 393224 | tf_op jit(solution)/shard_map/heads/ppermute | solution.py:1014
  126.5 11.2 %collective-permute-start.20 = (bf16[256,256]{1,0:T(8,128)(2,1)S(1)}, bf16[256,256]{1,0:T(8,128)(2,1)S(1)}, u32[]{:S(2)}, u32[]{:S(2)}) collective-permute-start(bf16[256,256]{1,0:T(8,128)(2,1)S(1)} %get-tuple-element.130), channel_id=1, source_target_pairs={{0,2},{1,3},{2,0},{3,1},{4,6},{5,7},{6,4},{7,5},{8,10},{9,11},{10,... | collective-permute-start | bytes 393224 | tf_op jit(solution)/shard_map/heads/ppermute | solution.py:1014
  135.4 5.8 %collective-permute-start.21 = (bf16[256,256]{1,0:T(8,128)(2,1)S(1)}, bf16[256,256]{1,0:T(8,128)(2,1)S(1)}, u32[]{:S(2)}, u32[]{:S(2)}) collective-permute-start(bf16[256,256]{1,0:T(8,128)(2,1)S(1)} %get-tuple-element.131), channel_id=1, source_target_pairs={{0,3},{1,2},{2,1},{3,0},{4,7},{5,6},{6,5},{7,4},{8,11},{9,10},{10,... | collective-permute-start | bytes 393224 | tf_op jit(solution)/shard_map/heads/ppermute | solution.py:1014
  137.8 5.3 %collective-permute-start.26 = (bf16[1600,256]{1,0:T(8,128)(2,1)}, bf16[1600,256]{1,0:T(8,128)(2,1)S(1)}, u32[]{:S(2)}, u32[]{:S(2)}) collective-permute-start(bf16[1600,256]{1,0:T(8,128)(2,1)} %copy-done.45), channel_id=1, source_target_pairs={{0,1},{1,0},{2,3},{3,2},{4,5},{5,4},{6,7},{7,6},{8,9},{9,8},{10,11... | collective-permute-start | bytes 2457608 | tf_op jit(solution)/shard_map/cyb/ppermute | solution.py:1014
  141.2 2.5 collective-permute-start.25
  141.3 4.8 %collective-permute-start.24 = (bf16[1600,256]{1,0:T(8,128)(2,1)}, bf16[1600,256]{1,0:T(8,128)(2,1)S(1)}, u32[]{:S(2)}, u32[]{:S(2)}) collective-permute-start(bf16[1600,256]{1,0:T(8,128)(2,1)} %copy-done.43), channel_id=1, source_target_pairs={{0,1},{1,0},{2,3},{3,2},{4,5},{5,4},{6,7},{7,6},{8,9},{9,8},{10,11... | collective-permute-start | bytes 2457608 | tf_op jit(solution)/shard_map/cxa/ppermute | solution.py:1014
  141.7 4.4 %collective-permute-start.29 = (bf16[1600,256]{1,0:T(8,128)(2,1)S(1)}, bf16[1600,256]{1,0:T(8,128)(2,1)S(1)}, u32[]{:S(2)}, u32[]{:S(2)}) collective-permute-start(bf16[1600,256]{1,0:T(8,128)(2,1)S(1)} %collective-permute-done.22.refs_14_), channel_id=1, source_target_pairs={{0,1},{1,0},{2,3},{3,2},{4,5},{5,4},{6,7},{7,6},{8,9},{9,8},{10,11... | collective-permute-start | bytes 2457608 | tf_op jit(solution)/shard_map/cyx3/ppermute | solution.py:1014
  176.6 6.1 %collective-permute-start.34 = (bf16[2,2,1600,256]{3,2,1,0:T(8,128)(2,1)}, bf16[2,2,1600,256]{3,2,1,0:T(8,128)(2,1)S(1)}, u32[]{:S(2)}, u32[]{:S(2)}) collective-permute-start(bf16[2,2,1600,256]{3,2,1,0:T(8,128)(2,1)} %get-tuple-element.150), channel_id=1, source_target_pairs={{0,1},{1,0},{2,3},{3,2},{4,5},{5,4},{6,7},{7,6},{8,9},{9,8},{10,11... | collective-permute-start | bytes 9830408 | tf_op jit(solution)/shard_map/rc2/ppermute | solution.py:1014
  176.7 10.9 %collective-permute-start.30 = (bf16[2,2,1600,256]{3,2,1,0:T(8,128)(2,1)}, bf16[2,2,1600,256]{3,2,1,0:T(8,128)(2,1)S(1)}, u32[]{:S(2)}, u32[]{:S(2)}) collective-permute-start(bf16[2,2,1600,256]{3,2,1,0:T(8,128)(2,1)} %get-tuple-element.143), channel_id=1, source_target_pairs={{0,1},{1,0},{2,3},{3,2},{4,5},{5,4},{6,7},{7,6},{8,9},{9,8},{10,11... | collective-permute-start | bytes 9830408 | tf_op jit(solution)/shard_map/rc1/ppermute | solution.py:1014
  177.1 10.4 %collective-permute-start.31 = (bf16[256,256]{1,0:T(8,128)(2,1)}, bf16[256,256]{1,0:T(8,128)(2,1)S(1)}, u32[]{:S(2)}, u32[]{:S(2)}) collective-permute-start(bf16[256,256]{1,0:T(8,128)(2,1)} %get-tuple-element.145), channel_id=1, source_target_pairs={{0,1},{1,0},{2,3},{3,2},{4,5},{5,4},{6,7},{7,6},{8,9},{9,8},{10,11... | collective-permute-start | bytes 393224 | tf_op jit(solution)/shard_map/heads_grad/ppermute | solution.py:1014
  177.2 10.3 %collective-permute-start.32 = (bf16[256,256]{1,0:T(8,128)(2,1)}, bf16[256,256]{1,0:T(8,128)(2,1)S(1)}, u32[]{:S(2)}, u32[]{:S(2)}) collective-permute-start(bf16[256,256]{1,0:T(8,128)(2,1)} %get-tuple-element.146), channel_id=1, source_target_pairs={{0,2},{1,3},{2,0},{3,1},{4,6},{5,7},{6,4},{7,5},{8,10},{9,11},{10,... | collective-permute-start | bytes 393224 | tf_op jit(solution)/shard_map/heads_grad/ppermute | solution.py:1014
  178.1 9.4 %collective-permute-start.33 = (bf16[256,256]{1,0:T(8,128)(2,1)}, bf16[256,256]{1,0:T(8,128)(2,1)S(1)}, u32[]{:S(2)}, u32[]{:S(2)}) collective-permute-start(bf16[256,256]{1,0:T(8,128)(2,1)} %get-tuple-element.147), channel_id=1, source_target_pairs={{0,3},{1,2},{2,1},{3,0},{4,7},{5,6},{6,5},{7,4},{8,11},{9,10},{10,... | collective-permute-start | bytes 393224 | tf_op jit(solution)/shard_map/heads_grad/ppermute | solution.py:1014
  187.6 29.0 %collective-permute-start.37 = (bf16[2,2,1600,256]{3,2,1,0:T(8,128)(2,1)}, bf16[2,2,1600,256]{3,2,1,0:T(8,128)(2,1)S(1)}, u32[]{:S(2)}, u32[]{:S(2)}) collective-permute-start(bf16[2,2,1600,256]{3,2,1,0:T(8,128)(2,1)} %get-tuple-element.174), channel_id=1, source_target_pairs={{0,1},{1,0},{2,3},{3,2},{4,5},{5,4},{6,7},{7,6},{8,9},{9,8},{10,11... | collective-permute-start | bytes 9830408 | tf_op jit(solution)/shard_map/rc3/ppermute | solution.py:1014
  189.2 21.2 %collective-permute-start.36 = (bf16[1600,256]{1,0:T(8,128)(2,1)S(1)}, bf16[1600,256]{1,0:T(8,128)(2,1)}, u32[]{:S(2)}, u32[]{:S(2)}) collective-permute-start(bf16[1600,256]{1,0:T(8,128)(2,1)S(1)} %get-tuple-element.151), channel_id=1, source_target_pairs={{0,2},{1,3},{2,0},{3,1},{4,6},{5,7},{6,4},{7,5},{8,10},{9,11},{10,... | collective-permute-start | bytes 2457608 | tf_op jit(solution)/shard_map/d2/ppermute | solution.py:1014
  190.0 21.4 %collective-permute-start.35 = (bf16[1600,256]{1,0:T(8,128)(2,1)}, bf16[1600,256]{1,0:T(8,128)(2,1)}, u32[]{:S(2)}, u32[]{:S(2)}) collective-permute-start(bf16[1600,256]{1,0:T(8,128)(2,1)} %get-tuple-element.148), channel_id=1, source_target_pairs={{0,4},{1,5},{2,6},{3,7},{4,0},{5,1},{6,2},{7,3},{8,12},{9,13},{10,... | collective-permute-start | bytes 2457608 | tf_op jit(solution)/shard_map/d1/ppermute | solution.py:1014
  191.3 36.1 %collective-permute-start.39 = (bf16[1600,256]{1,0:T(8,128)(2,1)S(1)}, bf16[1600,256]{1,0:T(8,128)(2,1)}, u32[]{:S(2)}, u32[]{:S(2)}) collective-permute-start(bf16[1600,256]{1,0:T(8,128)(2,1)S(1)} %get-tuple-element.153), channel_id=1, source_target_pairs={{0,2},{1,3},{2,0},{3,1},{4,6},{5,7},{6,4},{7,5},{8,10},{9,11},{10,... | collective-permute-start | bytes 2457608 | tf_op jit(solution)/shard_map/e2/ppermute | solution.py:1014
  192.4 35.8 %collective-permute-start.38 = (bf16[1600,256]{1,0:T(8,128)(2,1)S(1)}, bf16[1600,256]{1,0:T(8,128)(2,1)}, u32[]{:S(2)}, u32[]{:S(2)}) collective-permute-start(bf16[1600,256]{1,0:T(8,128)(2,1)S(1)} %get-tuple-element.152), channel_id=1, source_target_pairs={{0,4},{1,5},{2,6},{3,7},{4,0},{5,1},{6,2},{7,3},{8,12},{9,13},{10,... | collective-permute-start | bytes 2457608 | tf_op jit(solution)/shard_map/e1/ppermute | solution.py:1014
  228.1 2.8 collective-permute-start.40
  228.2 21.0 %collective-permute-start.41 = (bf16[1600,256]{1,0:T(8,128)(2,1)}, bf16[1600,256]{1,0:T(8,128)(2,1)}, u32[]{:S(2)}, u32[]{:S(2)}) collective-permute-start(bf16[1600,256]{1,0:T(8,128)(2,1)} %fusion.2), channel_id=1, source_target_pairs={{0,2},{1,3},{2,0},{3,1},{4,6},{5,7},{6,4},{7,5},{8,10},{9,11},{10,... | collective-permute-start | bytes 2457608 | tf_op jit(solution)/shard_map/f1/ppermute | solution.py:1014
  229.4 20.7 %collective-permute-start.46 = (bf16[1600,256]{1,0:T(8,128)(2,1)}, bf16[1600,256]{1,0:T(8,128)(2,1)}, u32[]{:S(2)}, u32[]{:S(2)}) collective-permute-start(bf16[1600,256]{1,0:T(8,128)(2,1)} %fusion.1), channel_id=1, source_target_pairs={{0,4},{1,5},{2,6},{3,7},{4,0},{5,1},{6,2},{7,3},{8,12},{9,13},{10,... | collective-permute-start | bytes 2457608 | tf_op jit(solution)/shard_map/f2/ppermute | solution.py:1014
  254.2 19.8 %collective-permute-start.47 = (bf16[1600,256]{1,0:T(8,128)(2,1)}, bf16[1600,256]{1,0:T(8,128)(2,1)S(1)}, u32[]{:S(2)}, u32[]{:S(2)}) collective-permute-start(bf16[1600,256]{1,0:T(8,128)(2,1)} %get-tuple-element.197), channel_id=1, source_target_pairs={{0,8},{1,9},{2,10},{3,11},{4,12},{5,13},{6,14},{7,15},{8,0},{9,1},... | collective-permute-start | bytes 2457608 | tf_op jit(solution)/shard_map/rz_inner1/ppermute | solution.py:1014
  254.4 19.8 %collective-permute-start.49 = (bf16[1600,256]{1,0:T(8,128)(2,1)}, bf16[1600,256]{1,0:T(8,128)(2,1)}, u32[]{:S(2)}, u32[]{:S(2)}) collective-permute-start(bf16[1600,256]{1,0:T(8,128)(2,1)} %get-tuple-element.219), channel_id=1, source_target_pairs={{0,4},{1,5},{2,6},{3,7},{4,0},{5,1},{6,2},{7,3},{8,12},{9,13},{10,... | collective-permute-start | bytes 2457608 | tf_op jit(solution)/shard_map/ry0/ppermute | solution.py:1014
  255.5 21.2 %collective-permute-start.50 = (bf16[1600,256]{1,0:T(8,128)(2,1)S(1)}, bf16[1600,256]{1,0:T(8,128)(2,1)S(1)}, u32[]{:S(2)}, u32[]{:S(2)}) collective-permute-start(bf16[1600,256]{1,0:T(8,128)(2,1)S(1)} %copy-done.32), channel_id=1, source_target_pairs={{0,2},{1,3},{2,0},{3,1},{4,6},{5,7},{6,4},{7,5},{8,10},{9,11},{10,... | collective-permute-start | bytes 2457608 | tf_op jit(solution)/shard_map/d3/ppermute | solution.py:1014
  256.5 36.0 %collective-permute-start.42 = (bf16[1600,256]{1,0:T(8,128)(2,1)}, bf16[1600,256]{1,0:T(8,128)(2,1)}, u32[]{:S(2)}, u32[]{:S(2)}) collective-permute-start(bf16[1600,256]{1,0:T(8,128)(2,1)} %get-tuple-element.180), channel_id=1, source_target_pairs={{0,2},{1,3},{2,0},{3,1},{4,6},{5,7},{6,4},{7,5},{8,10},{9,11},{10,... | collective-permute-start | bytes 2457608 | tf_op jit(solution)/shard_map/e3/ppermute | solution.py:1014
  279.3 16.9 %collective-permute-start.51 = (bf16[1600,256]{1,0:T(8,128)(2,1)}, bf16[1600,256]{1,0:T(8,128)(2,1)}, u32[]{:S(2)}, u32[]{:S(2)}) collective-permute-start(bf16[1600,256]{1,0:T(8,128)(2,1)} %fusion), channel_id=1, source_target_pairs={{0,4},{1,5},{2,6},{3,7},{4,0},{5,1},{6,2},{7,3},{8,12},{9,13},{10,... | collective-permute-start | bytes 2457608 | tf_op jit(solution)/shard_map/f3/ppermute | solution.py:1014
  280.5 19.9 %collective-permute-start.48 = (bf16[1600,256]{1,0:T(8,128)(2,1)S(1)}, bf16[1600,256]{1,0:T(8,128)(2,1)}, u32[]{:S(2)}, u32[]{:S(2)}) collective-permute-start(bf16[1600,256]{1,0:T(8,128)(2,1)S(1)} %add_convert_fusion.1.inner), channel_id=1, source_target_pairs={{0,16},{1,17},{2,18},{3,19},{4,20},{5,21},{6,22},{7,23},{24,8},{25... | collective-permute-start | bytes 2457608 | tf_op jit(solution)/shard_map/rz_inner2/ppermute | solution.py:1014
  300.4 15.8 %collective-permute-start.52 = (bf16[1600,256]{1,0:T(8,128)(2,1)}, bf16[1600,256]{1,0:T(8,128)(2,1)}, u32[]{:S(2)}, u32[]{:S(2)}) collective-permute-start(bf16[1600,256]{1,0:T(8,128)(2,1)} %get-tuple-element.201), channel_id=1, source_target_pairs={{0,8},{1,9},{2,10},{3,11},{4,12},{5,13},{6,14},{7,15},{8,0},{9,1},... | collective-permute-start | bytes 2457608 | tf_op jit(solution)/shard_map/rz_outer1/ppermute | solution.py:1014
  301.6 17.3 %collective-permute-start.44 = (f32[2,32,256]{2,1,0:T(8,128)S(1)}, f32[2,32,256]{2,1,0:T(8,128)S(1)}, u32[]{:S(2)}, u32[]{:S(2)}) collective-permute-start(f32[2,32,256]{2,1,0:T(8,128)S(1)} %select_bitcast_fusion), channel_id=1, source_target_pairs={{0,1},{1,0},{2,3},{3,2},{4,5},{5,4},{6,7},{7,6},{8,9},{9,8},{10,11... | collective-permute-start | bytes 196616 | tf_op jit(solution)/shard_map/vec_c/ppermute | solution.py:1014
  302.9 20.0 %collective-permute-start.43 = (bf16[256,1024]{1,0:T(8,128)(2,1)S(1)}, bf16[256,1024]{1,0:T(8,128)(2,1)S(1)}, u32[]{:S(2)}, u32[]{:S(2)}) collective-permute-start(bf16[256,1024]{1,0:T(8,128)(2,1)S(1)} %fusion.11), channel_id=1, source_target_pairs={{0,2},{1,3},{2,0},{3,1},{4,6},{5,7},{6,4},{7,5},{8,10},{9,11},{10,... | collective-permute-start | bytes 1572872 | tf_op jit(solution)/shard_map/in_x/ppermute | solution.py:1014
  317.6 18.9 %collective-permute-start.53 = (bf16[1600,256]{1,0:T(8,128)(2,1)S(1)}, bf16[1600,256]{1,0:T(8,128)(2,1)}, u32[]{:S(2)}, u32[]{:S(2)}) collective-permute-start(bf16[1600,256]{1,0:T(8,128)(2,1)S(1)} %add_convert_fusion.outer), channel_id=1, source_target_pairs={{8,24},{9,25},{10,26},{11,27},{12,28},{13,29},{14,30},{15,31},{16,... | collective-permute-start | bytes 2457608 | tf_op jit(solution)/shard_map/rz_outer2/ppermute | solution.py:1014
  318.9 4.0 %collective-permute-start.45 = (f32[32,256]{1,0:T(8,128)S(1)}, f32[32,256]{1,0:T(8,128)S(1)}, u32[]{:S(2)}, u32[]{:S(2)}) collective-permute-start(f32[32,256]{1,0:T(8,128)S(1)} %select_bitcast_fusion.1), channel_id=1, source_target_pairs={{0,2},{1,3},{2,0},{3,1},{4,6},{5,7},{6,4},{7,5},{8,10},{9,11},{10,... | collective-permute-start | bytes 98312 | tf_op jit(solution)/shard_map/vec_x/ppermute | solution.py:1014
  325.2 39.3 %copy-start.26 = (f32[393664]{0:T(1024)S(1)}, f32[393664]{0:T(1024)}, u32[]{:S(2)}) copy-start(f32[393664]{0:T(1024)} %param.11) | copy-start | bytes 4723972
  341.3 4.0 %collective-permute-start.54 = (f32[40,256]{1,0:T(8,128)S(1)}, f32[40,256]{1,0:T(8,128)S(1)}, u32[]{:S(2)}, u32[]{:S(2)}) collective-permute-start(f32[40,256]{1,0:T(8,128)S(1)} %maximum_maximum_fusion.1), channel_id=1, source_target_pairs={{0,4},{1,5},{2,6},{3,7},{4,0},{5,1},{6,2},{7,3},{8,12},{9,13},{10,... | collective-permute-start | bytes 122888 | tf_op jit(solution)/shard_map/norm/ppermute | solution.py:1014
  345.3 4.0 %collective-permute-start.55 = (f32[40,256]{1,0:T(8,128)S(1)}, f32[40,256]{1,0:T(8,128)S(1)}, u32[]{:S(2)}, u32[]{:S(2)}) collective-permute-start(f32[40,256]{1,0:T(8,128)S(1)} %fusion.17), channel_id=1, source_target_pairs={{0,8},{1,9},{2,10},{3,11},{4,12},{5,13},{6,14},{7,15},{8,0},{9,1},... | collective-permute-start | bytes 122888 | tf_op jit(solution)/shard_map/norm/ppermute | solution.py:1014
  349.3 4.9 %collective-permute-start.56 = (f32[40,256]{1,0:T(8,128)S(1)}, f32[40,256]{1,0:T(8,128)S(1)}, u32[]{:S(2)}, u32[]{:S(2)}) collective-permute-start(f32[40,256]{1,0:T(8,128)S(1)} %add.191), channel_id=1, source_target_pairs={{0,16},{1,17},{2,18},{3,19},{4,20},{5,21},{6,22},{7,23},{8,24},{9,... | collective-permute-start | bytes 122888 | tf_op jit(solution)/shard_map/norm/ppermute | solution.py:1014
  358.0 3.7 collective-permute-start.57
  361.7 1.6 collective-permute-start.58
  (51 other events, 459.2 us)

commit v4 on v3

--- a/solution.py
+++ b/solution.py
@@ -215,13 +215,13 @@
                     value = jnp.where(row * 128 + lane < SHARD, value, 0.0)
                 flat[a : a + n, :] = value
                 total += jnp.sum((value * value).reshape(n // 8, 8, 128), axis=0)
-            square[...] = total
+            square[:, 0:128] = total
 
 
 def unpack(place, *pieces):
     return pl.pallas_call(
         unpack_kernel,
-        out_shape=(struct((LANE_ROWS, 128), jnp.float32), struct((8, 128), jnp.float32)),
+        out_shape=(struct((LANE_ROWS, 128), jnp.float32), struct((8, 256), jnp.float32)),
         in_specs=[SMEM] + [ANY] * 4,
         out_specs=(VMEM, VMEM),
         scratch_shapes=[
@@ -1135,7 +1135,7 @@
     vec_rows = jnp.pad(master[SHARD - 3584 :].reshape(14, 256), ((0, 2), (0, 0)))
     head_rows = jnp.pad(master[SHARD - 896 :], (0, 3200)).reshape(16, 256)
     tail = low(jnp.where(shard == 7, vec_rows, head_rows))
-    tail_x = send(tail, to_x, "tail_x")
+    tail_x = after(send(tail, to_x, "tail_x"), flat)
     tail_c = send(jnp.concatenate([tail, tail_x]), to_core, "tail_c")
     own = pack(place, flat, jnp.concatenate([tail, tail_c[:16], tail_x, tail_c[16:]]))
     here = (jnp.arange(4) == j)[:, None, None]
@@ -1219,9 +1219,9 @@
     got_inner = send(sent_1, to_near, "rz_inner1")
     inner_part = low(add(kept_1, got_inner))
     inner_last = send(inner_part, only(to_far, (0, 3)), "rz_inner2")
-    f3 = send(low(over_cores(3, 0, 1) + wide(after(d3, ry0, got_inner))), to_y, "f3")
+    f3 = send(low(over_cores(3, 0, 1) + wide(after(d3, ry0))), to_y, "f3")
     kept_0, sent_0 = combine(
-        place, (jnp.where(low_row, piece_0, piece_1), ry0), (grads_own[2], moved[3], e3, f3)
+        after(place, inner_part), (jnp.where(low_row, piece_0, piece_1), ry0), (grads_own[2], moved[3], e3, f3)
     )
     outer_part = low(add(kept_0, send(after(sent_0, inner_last), to_near, "rz_outer1")))
     outer_last = send(outer_part, only(to_far, (1, 2)), "rz_outer2")
@@ -1245,7 +1245,7 @@
             (time_frac * time_grad).reshape(4, 1, 256),
             time_grad.reshape(4, 1, 256),
             jnp.zeros((4, 2, 256), jnp.float32),
-            head_grad,
+            jnp.where(jnp.arange(4096).reshape(1, 16, 256) < 896, head_grad, 0.0),
         ],
         axis=1,
     )
@@ -1258,12 +1258,13 @@
     mine = kept_x + send(jnp.where(x_bit == 1, by_x[0], by_x[1]), to_x, "vec_x")
 
     grad_flat, square = unpack(after(place, input_grad), inner_part, inner_last, outer_part, outer_last)
-    mine = jnp.concatenate([mine, square.reshape(4, 256), jnp.zeros((4, 256), jnp.float32)])
+    mine = jnp.concatenate([mine, square])
     for route in (to_y, to_near, to_far):
         mine = mine + send(mine, route, "norm")
     vec_sum, head_sum = mine[:14].reshape(-1), mine[16:20].reshape(-1)[:896]
     vector_grad = vec_sum
-    square_sum = (jnp.sum(mine[32:36]) + jnp.sum(vec_sum * vec_sum) + jnp.sum(head_sum * head_sum))
+    is_sum = jnp.arange(40)[:, None] >= 32
+    square_sum = jnp.sum(jnp.where(is_sum, mine, mine * mine))
     square_sum = jnp.broadcast_to(square_sum, (8, 128))
     for route in (to_x, to_core):
         square_sum = square_sum + send(square_sum, route, "norm")

time: 377 us -> 374 us (level)
  waiting for transfers between devices: 180 us -> 175 us
    ppermute x59, waiting for transfers between devices: 180 us -> 175 us  [send(): return lax.ppermute(values, AXES, pairs)]
  transfers between devices with their start and end apart: 59 -> 59, of which waited for: 38 -> 37; matrix products, arithmetic and copies ran while one was open for 10% -> 10% of each run, Pallas kernels for 9% -> 10%
where the time goes in v4:
time: 374 us; the launch traced here: 369 us
  waiting for transfers between devices  175 us (47%)
  Pallas kernels  71.7 us (19%)
  starting transfers between devices  59.1 us (16%)
  other arithmetic  38.9 us (10%)
  local copies, waits for them, and re-layouts  14.1 us (4%)
  between operations  5.74 us (2%)
  matrix products  4.1 us (1%)
    ppermute x59, waiting for transfers between devices, send(): return lax.ppermute(values, AXES, pairs)  175 us
    ppermute x59, starting transfers between devices, send(): return lax.ppermute(values, AXES, pairs)  59.1 us
    pallas_call x1, Pallas kernels, layer(): pl.pallas_call(layer_kernel, out_shape=(struct((256, D)), struct((256, D)...  28.6 us
    convert_element_type x10, other arithmetic, low(): return values.astype(jnp.bfloat16)  17.4 us
    pallas_call x1, Pallas kernels, attend_back(): pl.pallas_call(attend_back_kernel, out_shape=(square, square, square, str...  16 us
    pallas_call x1, Pallas kernels, attend(): pl.pallas_call(attend_kernel, out_shape=(struct((4, 256, 1024)), struct((...  14.5 us
    pallas_call x2, Pallas kernels, combine(): pl.pallas_call(partial(combine_kernel, len(first)), grid=(blocks,), out_s...  7.81 us
  transfers between devices with their start and end apart: 59, of which 37 were waited for; matrix products, arithmetic and copies ran while one was open for 10% of the time, Pallas kernels for 10%

profile of v4, /device:TPU:0, one launch (start us, length us, event | category | flops | bytes accessed | tf_op | source)
XLA Modules:
  0.0 368.9 jit_solution(1843534843463034770)
XLA Ops:
  2.3 3.0 collective-permute-start
  5.3 1.5 pad_bitcast_fusion.flat
  9.2 3.4 collective-permute-start.2
  12.6 1.9 collective-permute-start.7
  14.4 1.5 collective-permute-start.4
  16.6 14.1 %collective-permute-done.2.p2.refs_1_ = bf16[1600,256]{1,0:T(8,128)(2,1)S(1)} collective-permute-done((bf16[1600,256]{1,0:T(8,128)(2,1)S(1)}, bf16[1600,256]{1,0:T(8,128)(2,1)S(1)}, u32[]{:S(2)}, u32[]{:S(2)}) %collective-permute-start.2) | collective-permute-done | bytes 819232 | tf_op jit(solution)/shard_map/first/ppermute | solution.py:1014
  30.8 2.4 collective-permute-done.7.p1.refs_4_
  33.2 1.7 collective-permute-start.8
  36.1 1.6 collective-permute-start.3
  38.7 3.4 collective-permute-start.13
  42.8 10.1 %collective-permute-done.8.p3.refs_5_ = bf16[1600,256]{1,0:T(8,128)(2,1)} collective-permute-done((bf16[1600,256]{1,0:T(8,128)(2,1)S(1)}, bf16[1600,256]{1,0:T(8,128)(2,1)}, u32[]{:S(2)}, u32[]{:S(2)}) %collective-permute-start.8) | collective-permute-done | bytes 819232 | tf_op jit(solution)/shard_map/y1/ppermute | solution.py:1014
  53.0 2.5 collective-permute-done.5.p4.refs_2_
  55.9 1.3 collective-permute-start.6
  58.4 1.6 collective-permute-start.14
  61.9 14.9 %collective-permute-done.6 = bf16[1600,256]{1,0:T(8,128)(2,1)S(1)} collective-permute-done((bf16[1600,256]{1,0:T(8,128)(2,1)}, bf16[1600,256]{1,0:T(8,128)(2,1)S(1)}, u32[]{:S(2)}, u32[]{:S(2)}) %collective-permute-start.6) | collective-permute-done | bytes 819232 | tf_op jit(solution)/shard_map/third/ppermute | solution.py:1014
  77.9 1.5 collective-permute-start.17
  82.2 2.4 collective-permute-start.16
  84.7 14.5 %attend.1 = (bf16[4,256,1024]{2,1,0:T(8,128)(2,1)}, bf16[3,1024,256]{2,1,0:T(8,128)(2,1)}, bf16[1024,256]{1,0:T(8,128)(2,1)S(1)}, bf16[1024,256]{1,0:T(8,128)(2,...) custom-call(s32[6]{0:T(128)S(1)} %stack.19.place, ...), custom_call_target="tpu_custom_call" | custom-call | flops 16000000000 | bytes 24000000 | tf_op jit(solution)/shard_map/attend/pallas_call | solution.py:369
  103.1 8.9 %collective-permute-done.18.refs_11_ = bf16[1600,256]{1,0:T(8,128)(2,1)S(1)} collective-permute-done((bf16[1600,256]{1,0:T(8,128)(2,1)S(1)}, bf16[1600,256]{1,0:T(8,128)(2,1)S(1)}, u32[]{:S(2)}, u32[]{:S(2)}) %collective-permute-start.18) | collective-permute-done | bytes 819232 | tf_op jit(solution)/shard_map/yb/ppermute | solution.py:1014
  112.7 1.6 collective-permute-start.22
  114.4 2.2 collective-permute-start.27
  116.9 8.0 %collective-permute-done.19.h1 = bf16[256,256]{1,0:T(8,128)(2,1)S(1)} collective-permute-done((bf16[256,256]{1,0:T(8,128)(2,1)S(1)}, bf16[256,256]{1,0:T(8,128)(2,1)S(1)}, u32[]{:S(2)}, u32[]{:S(2)}) %collective-permute-start.19) | collective-permute-done | bytes 131104 | tf_op jit(solution)/shard_map/heads/ppermute | solution.py:1014
  125.5 8.4 %collective-permute-done.22.refs_14_ = bf16[1600,256]{1,0:T(8,128)(2,1)S(1)} collective-permute-done((bf16[1600,256]{1,0:T(8,128)(2,1)S(1)}, bf16[1600,256]{1,0:T(8,128)(2,1)S(1)}, u32[]{:S(2)}, u32[]{:S(2)}) %collective-permute-start.22) | collective-permute-done | bytes 819232 | tf_op jit(solution)/shard_map/yx3/ppermute | solution.py:1014
  134.9 1.3 collective-permute-done.20.h2
  136.2 3.4 collective-permute-done.21.h3
  142.1 2.3 collective-permute-done.24.refs_16_
  146.4 28.6 %layer.1 = (bf16[256,1024]{1,0:T(8,128)(2,1)}, f32[256,1024]{1,0:T(8,128)}, bf16[256,256]{1,0:T(8,128)(2,1)}, bf16[256,256]{1,0:T(8,128)(2,1)}, bf16[256,256]{1,...) custom-call(s32[6]{0:T(128)} %copy-done.1, ...), custom_call_target="tpu_custom_call" | custom-call | flops 15000000512 | bytes 40000000 | tf_op jit(solution)/shard_map/layer/pallas_call | solution.py:708
  177.4 3.7 collective-permute-done.34.refs_1_
  181.1 3.0 fusion.8
  184.2 1.8 collective-permute-done.31.g1
  186.3 1.3 fusion.7
  188.5 1.3 collective-permute-start.35
  191.7 16.0 %attend_back.1 = (bf16[1024,256]{1,0:T(8,128)(2,1)S(1)}, bf16[1024,256]{1,0:T(8,128)(2,1)S(1)}, bf16[1024,256]{1,0:T(8,128)(2,1)S(1)}, f32[2,256,1024]{2,1,0:T(8...) custom-call(s32[6]{0:T(128)S(1)} %copy-done.2, bf16[1024,256]{1,0:T(8,128)(2,1)S(1)} %copy-done.12, ...), custom_call_target="tpu_custom_call" | custom-call | flops 20000000000 | bytes 12000000 | tf_op jit(solution)/shard_map/attend_back/pallas_call | solution.py:460
  209.9 2.6 fusion.1
  212.5 2.5 fusion.2
  215.0 2.0 fusion.10
  217.4 8.4 %collective-permute-done.39.refs_2_ = bf16[1600,256]{1,0:T(8,128)(2,1)} collective-permute-done((bf16[1600,256]{1,0:T(8,128)(2,1)S(1)}, bf16[1600,256]{1,0:T(8,128)(2,1)}, u32[]{:S(2)}, u32[]{:S(2)}) %collective-permute-start.39) | collective-permute-done | bytes 819232 | tf_op jit(solution)/shard_map/e2/ppermute | solution.py:1014
  227.8 1.3 collective-permute-start.46
  229.4 2.6 convolution_convert_fusion.2
  233.9 1.6 broadcast_select_fusion
  237.8 10.2 %collective-permute-done.41.refs_7_ = bf16[1600,256]{1,0:T(8,128)(2,1)} collective-permute-done((bf16[1600,256]{1,0:T(8,128)(2,1)}, bf16[1600,256]{1,0:T(8,128)(2,1)}, u32[]{:S(2)}, u32[]{:S(2)}) %collective-permute-start.41) | collective-permute-done | bytes 819232 | tf_op jit(solution)/shard_map/f1/ppermute | solution.py:1014
  249.2 4.2 %combine.2 = (bf16[1600,256]{1,0:T(8,128)(2,1)}, bf16[1600,256]{1,0:T(8,128)(2,1)}) custom-call(s32[6]{0:T(128)} %copy-done.1, bf16[2,2,1600,256]{3,2,1,0:T(8,128)(2,1)} %get-tuple-element.152.refs_0_, bf16[2,2,1600,256]{3,2,1,0:T(8,128)(2,1)} %copy-done.24, bf16[1600,256]{1,0:T(8,128)(2,1)} %collective-permute-done.39.refs_2_, ...), custom_call_target="tpu_custom_call" | custom-call | tf_op jit(solution)/shard_map/combine/pallas_call | solution.py:257
  254.4 11.5 %collective-permute-done.49.refs_1_ = bf16[1600,256]{1,0:T(8,128)(2,1)S(1)} collective-permute-done((bf16[1600,256]{1,0:T(8,128)(2,1)}, bf16[1600,256]{1,0:T(8,128)(2,1)S(1)}, u32[]{:S(2)}, u32[]{:S(2)}) %collective-permute-start.49) | collective-permute-done | bytes 819232 | tf_op jit(solution)/shard_map/ry0/ppermute | solution.py:1014
  265.9 3.2 fusion
  269.1 1.3 collective-permute-start.51
  270.4 2.1 collective-permute-done.47
  272.7 5.2 %collective-permute-start.48 = (bf16[1600,256]{1,0:T(8,128)(2,1)S(1)}, bf16[1600,256]{1,0:T(8,128)(2,1)}, u32[]{:S(2)}, u32[]{:S(2)}) collective-permute-start(bf16[1600,256]{1,0:T(8,128)(2,1)S(1)} %add_convert_fusion.1.inner), channel_id=1, source_target_pairs={{0,16},{1,17},{2,18},{3,19},{4,20},{5,21},{6,22},{7,23},{24,8},{25... | collective-permute-start | bytes 2457608 | tf_op jit(solution)/shard_map/rz_inner2/ppermute | solution.py:1014
  279.3 3.5 collective-permute-done.42.refs_4_
  282.8 6.3 %collective-permute-done.51.refs_5_ = bf16[1600,256]{1,0:T(8,128)(2,1)} collective-permute-done((bf16[1600,256]{1,0:T(8,128)(2,1)}, bf16[1600,256]{1,0:T(8,128)(2,1)}, u32[]{:S(2)}, u32[]{:S(2)}) %collective-permute-start.51) | collective-permute-done | bytes 819232 | tf_op jit(solution)/shard_map/f3/ppermute | solution.py:1014
  289.1 3.6 combine.3
  296.6 15.3 %collective-permute-done.52 = bf16[1600,256]{1,0:T(8,128)(2,1)} collective-permute-done((bf16[1600,256]{1,0:T(8,128)(2,1)}, bf16[1600,256]{1,0:T(8,128)(2,1)}, u32[]{:S(2)}, u32[]{:S(2)}) %collective-permute-start.52) | collective-permute-done | bytes 819232 | tf_op jit(solution)/shard_map/rz_outer1/ppermute | solution.py:1014
  311.9 1.4 add_convert_fusion.outer
  313.3 1.3 collective-permute-start.53
  315.6 3.0 collective-permute-done.45
  318.6 2.3 fusion.4
  321.0 12.9 %collective-permute-done.53.outer_last = bf16[1600,256]{1,0:T(8,128)(2,1)} collective-permute-done((bf16[1600,256]{1,0:T(8,128)(2,1)S(1)}, bf16[1600,256]{1,0:T(8,128)(2,1)}, u32[]{:S(2)}, u32[]{:S(2)}) %collective-permute-start.53) | collective-permute-done | bytes 819232 | tf_op jit(solution)/shard_map/rz_outer2/ppermute | solution.py:1014
  333.9 4.0 %unpack.1 = (f32[3080,128]{1,0:T(8,128)}, f32[8,256]{1,0:T(8,128)}) custom-call(s32[6]{0:T(128)} %copy-done.1, bf16[1600,256]{1,0:T(8,128)(2,1)} %copy-done.27, bf16[1600,256]{1,0:T(8,128)(2,1)} %collective-permute-done.48.inner_last, bf16[1600,256]{1,0:T(8,128)(2,1)} %copy-done.28, bf16[1600,256]{1,0:T(8,128)(2,1)} %collective-permute-done.53.outer_last), custom_call_target="tpu_custom_call" | custom-call | tf_op jit(solution)/shard_map/unpack/pallas_call | solution.py:222
  338.6 2.1 collective-permute-start.54
  340.7 2.0 collective-permute-done.54
  343.3 4.0 %collective-permute-done.55 = f32[40,256]{1,0:T(8,128)S(1)} collective-permute-done((f32[40,256]{1,0:T(8,128)S(1)}, f32[40,256]{1,0:T(8,128)S(1)}, u32[]{:S(2)}, u32[]{:S(2)}) %collective-permute-start.55) | collective-permute-done | bytes 40992 | tf_op jit(solution)/shard_map/norm/ppermute | solution.py:1014
  348.2 4.1 %collective-permute-done.56 = f32[40,256]{1,0:T(8,128)S(1)} collective-permute-done((f32[40,256]{1,0:T(8,128)S(1)}, f32[40,256]{1,0:T(8,128)S(1)}, u32[]{:S(2)}, u32[]{:S(2)}) %collective-permute-start.56) | collective-permute-done | bytes 40992 | tf_op jit(solution)/shard_map/norm/ppermute | solution.py:1014
  354.6 2.7 collective-permute-done.57
  358.0 1.6 fusion.17
  361.5 6.0 %multiply_add_fusion = (f32[393664]{0:T(1024)}, f32[393664]{0:T(1024)}, f32[393664]{0:T(1024)}, f32[393664]{0:T(1024)}) fusion(f32[393664]{0:T(1024)S(1)} %copy-done.29, f32[393664]{0:T(1024)S(1)} %copy-done.26, f32[]{:T(128)S(6)} %div.48, f32[394240]{0:T(1024)} %fusion.17, f32[393664]{0:T(1024)} %param.13, f32[393664]{0:T(1024)} %param.12), kind=kLoop, calls=%fused_computation.17 | loop fusion | flops 7479616 | bytes 14171908 | tf_op jit(solution)/shard_map/add | solution.py:1287
  (263 shorter events, 53.5 us)
Async XLA Ops:
  2.3 4.6 %collective-permute-start = (bf16[16,256]{1,0:T(8,128)(2,1)S(1)}, bf16[16,256]{1,0:T(8,128)(2,1)S(1)}, u32[]{:S(2)}, u32[]{:S(2)}) collective-permute-start(bf16[16,256]{1,0:T(8,128)(2,1)S(1)} %select_convert_fusion), channel_id=1, source_target_pairs={{0,2},{1,3},{2,0},{3,1},{4,6},{5,7},{6,4},{7,5},{8,10},{9,11},{10,... | collective-permute-start | bytes 24584 | tf_op jit(solution)/shard_map/tail_x/ppermute | solution.py:1014
  6.9 1.4 collective-permute-start.1
  8.3 76.3 %copy-start.1 = (s32[6]{0:T(128)}, s32[6]{0:T(128)S(1)}, u32[]{:S(2)}) copy-start(s32[6]{0:T(128)S(1)} %stack.19.place) | copy-start | bytes 76
  9.2 75.5 %copy-start = (bf16[1600,256]{1,0:T(8,128)(2,1)}, bf16[1600,256]{1,0:T(8,128)(2,1)S(1)}, u32[]{:S(2)}) copy-start(bf16[1600,256]{1,0:T(8,128)(2,1)S(1)} %pack.1.p0.refs_0_) | copy-start | bytes 2457604
  9.2 21.5 %collective-permute-start.2 = (bf16[1600,256]{1,0:T(8,128)(2,1)S(1)}, bf16[1600,256]{1,0:T(8,128)(2,1)S(1)}, u32[]{:S(2)}, u32[]{:S(2)}) collective-permute-start(bf16[1600,256]{1,0:T(8,128)(2,1)S(1)} %pack.1.p0.refs_0_), channel_id=1, source_target_pairs={{0,16},{1,17},{2,18},{3,19},{4,20},{5,21},{6,22},{7,23},{8,0},{9,1... | collective-permute-start | bytes 2457608 | tf_op jit(solution)/shard_map/first/ppermute | solution.py:1014
  12.6 20.6 %collective-permute-start.7 = (bf16[1600,256]{1,0:T(8,128)(2,1)S(1)}, bf16[1600,256]{1,0:T(8,128)(2,1)}, u32[]{:S(2)}, u32[]{:S(2)}) collective-permute-start(bf16[1600,256]{1,0:T(8,128)(2,1)S(1)} %pack.1.p0.refs_0_), channel_id=1, source_target_pairs={{0,4},{1,5},{2,6},{3,7},{4,0},{5,1},{6,2},{7,3},{8,12},{9,13},{10,... | collective-permute-start | bytes 2457608 | tf_op jit(solution)/shard_map/y0/ppermute | solution.py:1014
  14.4 21.5 %collective-permute-start.4 = (bf16[256,1024]{1,0:T(8,128)(2,1)S(1)}, bf16[256,1024]{1,0:T(8,128)(2,1)S(1)}, u32[]{:S(2)}, u32[]{:S(2)}) collective-permute-start(bf16[256,1024]{1,0:T(8,128)(2,1)S(1)} %copy-done.4), channel_id=1, source_target_pairs={{0,2},{1,3},{2,0},{3,1},{4,6},{5,7},{6,4},{7,5},{8,10},{9,11},{10,... | collective-permute-start | bytes 1572872 | tf_op jit(solution)/shard_map/tok_x/ppermute | solution.py:1014
  15.9 21.8 %collective-permute-start.12 = (bf16[1600,256]{1,0:T(8,128)(2,1)S(1)}, bf16[1600,256]{1,0:T(8,128)(2,1)S(1)}, u32[]{:S(2)}, u32[]{:S(2)}) collective-permute-start(bf16[1600,256]{1,0:T(8,128)(2,1)S(1)} %pack.1.p0.refs_0_), channel_id=1, source_target_pairs={{8,10},{9,11},{10,8},{11,9},{12,14},{13,15},{14,12},{15,13},{16,18... | collective-permute-start | bytes 2457608 | tf_op jit(solution)/shard_map/x0/ppermute | solution.py:1014
  30.8 48.6 %copy-start.31 = (bf16[1600,256]{1,0:T(8,128)(2,1)}, bf16[1600,256]{1,0:T(8,128)(2,1)S(1)}, u32[]{:S(2)}) copy-start(bf16[1600,256]{1,0:T(8,128)(2,1)S(1)} %collective-permute-done.2.p2.refs_1_) | copy-start | bytes 2457604
  33.2 19.8 %collective-permute-start.8 = (bf16[1600,256]{1,0:T(8,128)(2,1)S(1)}, bf16[1600,256]{1,0:T(8,128)(2,1)}, u32[]{:S(2)}, u32[]{:S(2)}) collective-permute-start(bf16[1600,256]{1,0:T(8,128)(2,1)S(1)} %collective-permute-done.2.p2.refs_1_), channel_id=1, source_target_pairs={{0,4},{1,5},{2,6},{3,7},{4,0},{5,1},{6,2},{7,3},{8,12},{9,13},{10,... | collective-permute-start | bytes 2457608 | tf_op jit(solution)/shard_map/y1/ppermute | solution.py:1014
  35.9 19.6 %collective-permute-start.5 = (bf16[1600,256]{1,0:T(8,128)(2,1)}, bf16[1600,256]{1,0:T(8,128)(2,1)}, u32[]{:S(2)}, u32[]{:S(2)}) collective-permute-start(bf16[1600,256]{1,0:T(8,128)(2,1)} %broadcast_select_fusion.5), channel_id=1, source_target_pairs={{0,8},{1,9},{2,10},{3,11},{4,12},{5,13},{6,14},{7,15},{8,0},{9,1},... | collective-permute-start | bytes 2457608 | tf_op jit(solution)/shard_map/second/ppermute | solution.py:1014
  36.1 19.8 %collective-permute-start.3 = (bf16[1600,256]{1,0:T(8,128)(2,1)S(1)}, bf16[1600,256]{1,0:T(8,128)(2,1)}, u32[]{:S(2)}, u32[]{:S(2)}) collective-permute-start(bf16[1600,256]{1,0:T(8,128)(2,1)S(1)} %pack.1.p0.refs_0_), channel_id=1, source_target_pairs={{8,16},{9,17},{10,18},{11,19},{12,20},{13,21},{14,22},{15,23},{16,... | collective-permute-start | bytes 2457608 | tf_op jit(solution)/shard_map/crossed/ppermute | solution.py:1014
  38.7 21.9 %collective-permute-start.13 = (bf16[1600,256]{1,0:T(8,128)(2,1)S(1)}, bf16[1600,256]{1,0:T(8,128)(2,1)}, u32[]{:S(2)}, u32[]{:S(2)}) collective-permute-start(bf16[1600,256]{1,0:T(8,128)(2,1)S(1)} %collective-permute-done.2.p2.refs_1_), channel_id=1, source_target_pairs={{0,2},{1,3},{2,0},{3,1},{4,6},{5,7},{6,4},{7,5},{8,10},{9,11},{10,... | collective-permute-start | bytes 2457608 | tf_op jit(solution)/shard_map/x1/ppermute | solution.py:1014
  42.1 38.3 %collective-permute-start.10 = (bf16[256,1024]{1,0:T(8,128)(2,1)S(1)}, bf16[256,1024]{1,0:T(8,128)(2,1)S(1)}, u32[]{:S(2)}, u32[]{:S(2)}) collective-permute-start(bf16[256,1024]{1,0:T(8,128)(2,1)S(1)} %copy-done.4), channel_id=1, source_target_pairs={{0,1},{1,0},{2,3},{3,2},{4,5},{5,4},{6,7},{7,6},{8,9},{9,8},{10,11... | collective-permute-start | bytes 1572872 | tf_op jit(solution)/shard_map/tok_c/ppermute | solution.py:1014
  55.5 21.4 %collective-permute-start.9 = (bf16[1600,256]{1,0:T(8,128)(2,1)}, bf16[1600,256]{1,0:T(8,128)(2,1)S(1)}, u32[]{:S(2)}, u32[]{:S(2)}) collective-permute-start(bf16[1600,256]{1,0:T(8,128)(2,1)} %collective-permute-done.5.p4.refs_2_), channel_id=1, source_target_pairs={{0,4},{1,5},{2,6},{3,7},{4,0},{5,1},{6,2},{7,3},{8,12},{9,13},{10,... | collective-permute-start | bytes 2457608 | tf_op jit(solution)/shard_map/y2/ppermute | solution.py:1014
  55.9 20.8 %collective-permute-start.6 = (bf16[1600,256]{1,0:T(8,128)(2,1)}, bf16[1600,256]{1,0:T(8,128)(2,1)S(1)}, u32[]{:S(2)}, u32[]{:S(2)}) collective-permute-start(bf16[1600,256]{1,0:T(8,128)(2,1)} %collective-permute-done.3), channel_id=1, source_target_pairs={{8,0},{9,1},{10,2},{11,3},{12,4},{13,5},{14,6},{15,7},{16,24},{17,... | collective-permute-start | bytes 2457608 | tf_op jit(solution)/shard_map/third/ppermute | solution.py:1014
  58.4 44.6 %collective-permute-start.14 = (bf16[1600,256]{1,0:T(8,128)(2,1)S(1)}, bf16[1600,256]{1,0:T(8,128)(2,1)S(1)}, u32[]{:S(2)}, u32[]{:S(2)}) collective-permute-start(bf16[1600,256]{1,0:T(8,128)(2,1)S(1)} %broadcast_select_fusion.3), channel_id=1, source_target_pairs={{0,2},{1,3},{2,0},{3,1},{4,6},{5,7},{6,4},{7,5},{8,10},{9,11},{10,... | collective-permute-start | bytes 2457608 | tf_op jit(solution)/shard_map/xa/ppermute | solution.py:1014
  76.9 35.8 %collective-permute-start.15 = (bf16[1600,256]{1,0:T(8,128)(2,1)S(1)}, bf16[1600,256]{1,0:T(8,128)(2,1)S(1)}, u32[]{:S(2)}, u32[]{:S(2)}) collective-permute-start(bf16[1600,256]{1,0:T(8,128)(2,1)S(1)} %broadcast_select_fusion.4.p6.refs_3_), channel_id=1, source_target_pairs={{0,4},{1,5},{2,6},{3,7},{4,0},{5,1},{6,2},{7,3},{8,12},{9,13},{10,... | collective-permute-start | bytes 2457608 | tf_op jit(solution)/shard_map/y3/ppermute | solution.py:1014
  77.9 34.7 %collective-permute-start.17 = (bf16[1600,256]{1,0:T(8,128)(2,1)S(1)}, bf16[1600,256]{1,0:T(8,128)(2,1)}, u32[]{:S(2)}, u32[]{:S(2)}) collective-permute-start(bf16[1600,256]{1,0:T(8,128)(2,1)S(1)} %broadcast_select_fusion.4.p6.refs_3_), channel_id=1, source_target_pairs={{0,2},{1,3},{2,0},{3,1},{4,6},{5,7},{6,4},{7,5},{8,10},{9,11},{10,... | collective-permute-start | bytes 2457608 | tf_op jit(solution)/shard_map/x3/ppermute | solution.py:1014
  80.2 2.0 collective-permute-start.11
  80.4 31.5 %collective-permute-start.18 = (bf16[1600,256]{1,0:T(8,128)(2,1)S(1)}, bf16[1600,256]{1,0:T(8,128)(2,1)S(1)}, u32[]{:S(2)}, u32[]{:S(2)}) collective-permute-start(bf16[1600,256]{1,0:T(8,128)(2,1)S(1)} %broadcast_select_fusion.2), channel_id=1, source_target_pairs={{0,4},{1,5},{2,6},{3,7},{4,0},{5,1},{6,2},{7,3},{8,12},{9,13},{10,... | collective-permute-start | bytes 2457608 | tf_op jit(solution)/shard_map/yb/ppermute | solution.py:1014
  82.2 30.4 %collective-permute-start.16 = (bf16[1600,256]{1,0:T(8,128)(2,1)S(1)}, bf16[1600,256]{1,0:T(8,128)(2,1)}, u32[]{:S(2)}, u32[]{:S(2)}) collective-permute-start(bf16[1600,256]{1,0:T(8,128)(2,1)S(1)} %collective-permute-done.9.p5.refs_6_), channel_id=1, source_target_pairs={{0,2},{1,3},{2,0},{3,1},{4,6},{5,7},{6,4},{7,5},{16,18},{17,19},{1... | collective-permute-start | bytes 2457608 | tf_op jit(solution)/shard_map/yx2/ppermute | solution.py:1014
  103.1 31.2 %copy-start.43 = (bf16[1600,256]{1,0:T(8,128)(2,1)}, bf16[1600,256]{1,0:T(8,128)(2,1)S(1)}, u32[]{:S(2)}) copy-start(bf16[1600,256]{1,0:T(8,128)(2,1)S(1)} %collective-permute-done.14.refs_9_) | copy-start | bytes 2457604
  112.6 33.7 %collective-permute-start.23 = (bf16[9,1600,256]{2,1,0:T(8,128)(2,1)}, bf16[9,1600,256]{2,1,0:T(8,128)(2,1)}, u32[]{:S(2)}, u32[]{:S(2)}) collective-permute-start(bf16[9,1600,256]{2,1,0:T(8,128)(2,1)} %get-tuple-element.135), channel_id=1, source_target_pairs={{0,1},{1,0},{2,3},{3,2},{4,5},{5,4},{6,7},{7,6},{8,9},{9,8},{10,11... | collective-permute-start | bytes 22118408 | tf_op jit(solution)/shard_map/stack/ppermute | solution.py:1014
  112.7 21.1 %collective-permute-start.22 = (bf16[1600,256]{1,0:T(8,128)(2,1)S(1)}, bf16[1600,256]{1,0:T(8,128)(2,1)S(1)}, u32[]{:S(2)}, u32[]{:S(2)}) collective-permute-start(bf16[1600,256]{1,0:T(8,128)(2,1)S(1)} %collective-permute-done.15.refs_10_), channel_id=1, source_target_pairs={{0,2},{1,3},{2,0},{3,1},{4,6},{5,7},{6,4},{7,5},{8,10},{9,11},{10,... | collective-permute-start | bytes 2457608 | tf_op jit(solution)/shard_map/yx3/ppermute | solution.py:1014
  114.3 25.4 %collective-permute-start.28 = (bf16[1600,256]{1,0:T(8,128)(2,1)}, bf16[1600,256]{1,0:T(8,128)(2,1)S(1)}, u32[]{:S(2)}, u32[]{:S(2)}) collective-permute-start(bf16[1600,256]{1,0:T(8,128)(2,1)} %collective-permute-done.17.refs_13_), channel_id=1, source_target_pairs={{0,1},{1,0},{2,3},{3,2},{4,5},{5,4},{6,7},{7,6},{8,9},{9,8},{10,11... | collective-permute-start | bytes 2457608 | tf_op jit(solution)/shard_map/cx3/ppermute | solution.py:1014
  114.4 25.7 %collective-permute-start.27 = (bf16[1600,256]{1,0:T(8,128)(2,1)}, bf16[1600,256]{1,0:T(8,128)(2,1)}, u32[]{:S(2)}, u32[]{:S(2)}) collective-permute-start(bf16[1600,256]{1,0:T(8,128)(2,1)} %collective-permute-done.16.refs_12_), channel_id=1, source_target_pairs={{0,1},{1,0},{2,3},{3,2},{4,5},{5,4},{6,7},{7,6},{16,17},{17,16},{1... | collective-permute-start | bytes 2457608 | tf_op jit(solution)/shard_map/cyx2/ppermute | solution.py:1014
  116.7 8.3 %collective-permute-start.19 = (bf16[256,256]{1,0:T(8,128)(2,1)S(1)}, bf16[256,256]{1,0:T(8,128)(2,1)S(1)}, u32[]{:S(2)}, u32[]{:S(2)}) collective-permute-start(bf16[256,256]{1,0:T(8,128)(2,1)S(1)} %get-tuple-element.132), channel_id=1, source_target_pairs={{0,1},{1,0},{2,3},{3,2},{4,5},{5,4},{6,7},{7,6},{8,9},{9,8},{10,11... | collective-permute-start | bytes 393224 | tf_op jit(solution)/shard_map/heads/ppermute | solution.py:1014
  125.0 11.2 %collective-permute-start.20 = (bf16[256,256]{1,0:T(8,128)(2,1)S(1)}, bf16[256,256]{1,0:T(8,128)(2,1)S(1)}, u32[]{:S(2)}, u32[]{:S(2)}) collective-permute-start(bf16[256,256]{1,0:T(8,128)(2,1)S(1)} %get-tuple-element.133), channel_id=1, source_target_pairs={{0,2},{1,3},{2,0},{3,1},{4,6},{5,7},{6,4},{7,5},{8,10},{9,11},{10,... | collective-permute-start | bytes 393224 | tf_op jit(solution)/shard_map/heads/ppermute | solution.py:1014
  133.8 5.8 %collective-permute-start.21 = (bf16[256,256]{1,0:T(8,128)(2,1)S(1)}, bf16[256,256]{1,0:T(8,128)(2,1)S(1)}, u32[]{:S(2)}, u32[]{:S(2)}) collective-permute-start(bf16[256,256]{1,0:T(8,128)(2,1)S(1)} %get-tuple-element.134), channel_id=1, source_target_pairs={{0,3},{1,2},{2,1},{3,0},{4,7},{5,6},{6,5},{7,4},{8,11},{9,10},{10,... | collective-permute-start | bytes 393224 | tf_op jit(solution)/shard_map/heads/ppermute | solution.py:1014
  136.2 5.4 %collective-permute-start.26 = (bf16[1600,256]{1,0:T(8,128)(2,1)}, bf16[1600,256]{1,0:T(8,128)(2,1)S(1)}, u32[]{:S(2)}, u32[]{:S(2)}) collective-permute-start(bf16[1600,256]{1,0:T(8,128)(2,1)} %copy-done.45), channel_id=1, source_target_pairs={{0,1},{1,0},{2,3},{3,2},{4,5},{5,4},{6,7},{7,6},{8,9},{9,8},{10,11... | collective-permute-start | bytes 2457608 | tf_op jit(solution)/shard_map/cyb/ppermute | solution.py:1014
  139.6 2.5 collective-permute-start.25
  139.7 4.8 %collective-permute-start.24 = (bf16[1600,256]{1,0:T(8,128)(2,1)}, bf16[1600,256]{1,0:T(8,128)(2,1)S(1)}, u32[]{:S(2)}, u32[]{:S(2)}) collective-permute-start(bf16[1600,256]{1,0:T(8,128)(2,1)} %copy-done.43), channel_id=1, source_target_pairs={{0,1},{1,0},{2,3},{3,2},{4,5},{5,4},{6,7},{7,6},{8,9},{9,8},{10,11... | collective-permute-start | bytes 2457608 | tf_op jit(solution)/shard_map/cxa/ppermute | solution.py:1014
  140.1 4.4 %collective-permute-start.29 = (bf16[1600,256]{1,0:T(8,128)(2,1)S(1)}, bf16[1600,256]{1,0:T(8,128)(2,1)S(1)}, u32[]{:S(2)}, u32[]{:S(2)}) collective-permute-start(bf16[1600,256]{1,0:T(8,128)(2,1)S(1)} %collective-permute-done.22.refs_14_), channel_id=1, source_target_pairs={{0,1},{1,0},{2,3},{3,2},{4,5},{5,4},{6,7},{7,6},{8,9},{9,8},{10,11... | collective-permute-start | bytes 2457608 | tf_op jit(solution)/shard_map/cyx3/ppermute | solution.py:1014
  175.0 6.1 %collective-permute-start.34 = (bf16[2,2,1600,256]{3,2,1,0:T(8,128)(2,1)}, bf16[2,2,1600,256]{3,2,1,0:T(8,128)(2,1)S(1)}, u32[]{:S(2)}, u32[]{:S(2)}) collective-permute-start(bf16[2,2,1600,256]{3,2,1,0:T(8,128)(2,1)} %get-tuple-element.153), channel_id=1, source_target_pairs={{0,1},{1,0},{2,3},{3,2},{4,5},{5,4},{6,7},{7,6},{8,9},{9,8},{10,11... | collective-permute-start | bytes 9830408 | tf_op jit(solution)/shard_map/rc2/ppermute | solution.py:1014
  175.2 10.8 %collective-permute-start.30 = (bf16[2,2,1600,256]{3,2,1,0:T(8,128)(2,1)}, bf16[2,2,1600,256]{3,2,1,0:T(8,128)(2,1)S(1)}, u32[]{:S(2)}, u32[]{:S(2)}) collective-permute-start(bf16[2,2,1600,256]{3,2,1,0:T(8,128)(2,1)} %get-tuple-element.146), channel_id=1, source_target_pairs={{0,1},{1,0},{2,3},{3,2},{4,5},{5,4},{6,7},{7,6},{8,9},{9,8},{10,11... | collective-permute-start | bytes 9830408 | tf_op jit(solution)/shard_map/rc1/ppermute | solution.py:1014
  175.6 10.4 %collective-permute-start.31 = (bf16[256,256]{1,0:T(8,128)(2,1)}, bf16[256,256]{1,0:T(8,128)(2,1)S(1)}, u32[]{:S(2)}, u32[]{:S(2)}) collective-permute-start(bf16[256,256]{1,0:T(8,128)(2,1)} %get-tuple-element.148), channel_id=1, source_target_pairs={{0,1},{1,0},{2,3},{3,2},{4,5},{5,4},{6,7},{7,6},{8,9},{9,8},{10,11... | collective-permute-start | bytes 393224 | tf_op jit(solution)/shard_map/heads_grad/ppermute | solution.py:1014
  175.7 10.3 %collective-permute-start.32 = (bf16[256,256]{1,0:T(8,128)(2,1)}, bf16[256,256]{1,0:T(8,128)(2,1)S(1)}, u32[]{:S(2)}, u32[]{:S(2)}) collective-permute-start(bf16[256,256]{1,0:T(8,128)(2,1)} %get-tuple-element.149), channel_id=1, source_target_pairs={{0,2},{1,3},{2,0},{3,1},{4,6},{5,7},{6,4},{7,5},{8,10},{9,11},{10,... | collective-permute-start | bytes 393224 | tf_op jit(solution)/shard_map/heads_grad/ppermute | solution.py:1014
  176.6 9.4 %collective-permute-start.33 = (bf16[256,256]{1,0:T(8,128)(2,1)}, bf16[256,256]{1,0:T(8,128)(2,1)S(1)}, u32[]{:S(2)}, u32[]{:S(2)}) collective-permute-start(bf16[256,256]{1,0:T(8,128)(2,1)} %get-tuple-element.150), channel_id=1, source_target_pairs={{0,3},{1,2},{2,1},{3,0},{4,7},{5,6},{6,5},{7,4},{8,11},{9,10},{10,... | collective-permute-start | bytes 393224 | tf_op jit(solution)/shard_map/heads_grad/ppermute | solution.py:1014
  186.0 29.0 %collective-permute-start.37 = (bf16[2,2,1600,256]{3,2,1,0:T(8,128)(2,1)}, bf16[2,2,1600,256]{3,2,1,0:T(8,128)(2,1)S(1)}, u32[]{:S(2)}, u32[]{:S(2)}) collective-permute-start(bf16[2,2,1600,256]{3,2,1,0:T(8,128)(2,1)} %get-tuple-element.177), channel_id=1, source_target_pairs={{0,1},{1,0},{2,3},{3,2},{4,5},{5,4},{6,7},{7,6},{8,9},{9,8},{10,11... | collective-permute-start | bytes 9830408 | tf_op jit(solution)/shard_map/rc3/ppermute | solution.py:1014
  187.6 21.2 %collective-permute-start.36 = (bf16[1600,256]{1,0:T(8,128)(2,1)S(1)}, bf16[1600,256]{1,0:T(8,128)(2,1)}, u32[]{:S(2)}, u32[]{:S(2)}) collective-permute-start(bf16[1600,256]{1,0:T(8,128)(2,1)S(1)} %get-tuple-element.154), channel_id=1, source_target_pairs={{0,2},{1,3},{2,0},{3,1},{4,6},{5,7},{6,4},{7,5},{8,10},{9,11},{10,... | collective-permute-start | bytes 2457608 | tf_op jit(solution)/shard_map/d2/ppermute | solution.py:1014
  188.5 21.4 %collective-permute-start.35 = (bf16[1600,256]{1,0:T(8,128)(2,1)}, bf16[1600,256]{1,0:T(8,128)(2,1)}, u32[]{:S(2)}, u32[]{:S(2)}) collective-permute-start(bf16[1600,256]{1,0:T(8,128)(2,1)} %get-tuple-element.151), channel_id=1, source_target_pairs={{0,4},{1,5},{2,6},{3,7},{4,0},{5,1},{6,2},{7,3},{8,12},{9,13},{10,... | collective-permute-start | bytes 2457608 | tf_op jit(solution)/shard_map/d1/ppermute | solution.py:1014
  189.8 36.0 %collective-permute-start.39 = (bf16[1600,256]{1,0:T(8,128)(2,1)S(1)}, bf16[1600,256]{1,0:T(8,128)(2,1)}, u32[]{:S(2)}, u32[]{:S(2)}) collective-permute-start(bf16[1600,256]{1,0:T(8,128)(2,1)S(1)} %get-tuple-element.156), channel_id=1, source_target_pairs={{0,2},{1,3},{2,0},{3,1},{4,6},{5,7},{6,4},{7,5},{8,10},{9,11},{10,... | collective-permute-start | bytes 2457608 | tf_op jit(solution)/shard_map/e2/ppermute | solution.py:1014
  190.9 35.7 %collective-permute-start.38 = (bf16[1600,256]{1,0:T(8,128)(2,1)S(1)}, bf16[1600,256]{1,0:T(8,128)(2,1)}, u32[]{:S(2)}, u32[]{:S(2)}) collective-permute-start(bf16[1600,256]{1,0:T(8,128)(2,1)S(1)} %get-tuple-element.155), channel_id=1, source_target_pairs={{0,4},{1,5},{2,6},{3,7},{4,0},{5,1},{6,2},{7,3},{8,12},{9,13},{10,... | collective-permute-start | bytes 2457608 | tf_op jit(solution)/shard_map/e1/ppermute | solution.py:1014
  226.6 2.8 collective-permute-start.40
  226.7 21.4 %collective-permute-start.41 = (bf16[1600,256]{1,0:T(8,128)(2,1)}, bf16[1600,256]{1,0:T(8,128)(2,1)}, u32[]{:S(2)}, u32[]{:S(2)}) collective-permute-start(bf16[1600,256]{1,0:T(8,128)(2,1)} %fusion.2), channel_id=1, source_target_pairs={{0,2},{1,3},{2,0},{3,1},{4,6},{5,7},{6,4},{7,5},{8,10},{9,11},{10,... | collective-permute-start | bytes 2457608 | tf_op jit(solution)/shard_map/f1/ppermute | solution.py:1014
  227.8 21.4 %collective-permute-start.46 = (bf16[1600,256]{1,0:T(8,128)(2,1)}, bf16[1600,256]{1,0:T(8,128)(2,1)}, u32[]{:S(2)}, u32[]{:S(2)}) collective-permute-start(bf16[1600,256]{1,0:T(8,128)(2,1)} %fusion.1), channel_id=1, source_target_pairs={{0,4},{1,5},{2,6},{3,7},{4,0},{5,1},{6,2},{7,3},{8,12},{9,13},{10,... | collective-permute-start | bytes 2457608 | tf_op jit(solution)/shard_map/f2/ppermute | solution.py:1014
  235.4 30.5 %collective-permute-start.49 = (bf16[1600,256]{1,0:T(8,128)(2,1)}, bf16[1600,256]{1,0:T(8,128)(2,1)S(1)}, u32[]{:S(2)}, u32[]{:S(2)}) collective-permute-start(bf16[1600,256]{1,0:T(8,128)(2,1)} %get-tuple-element.225), channel_id=1, source_target_pairs={{0,4},{1,5},{2,6},{3,7},{4,0},{5,1},{6,2},{7,3},{8,12},{9,13},{10,... | collective-permute-start | bytes 2457608 | tf_op jit(solution)/shard_map/ry0/ppermute | solution.py:1014
  236.7 29.2 %collective-permute-start.50 = (bf16[1600,256]{1,0:T(8,128)(2,1)}, bf16[1600,256]{1,0:T(8,128)(2,1)}, u32[]{:S(2)}, u32[]{:S(2)}) collective-permute-start(bf16[1600,256]{1,0:T(8,128)(2,1)} %get-tuple-element.194), channel_id=1, source_target_pairs={{0,2},{1,3},{2,0},{3,1},{4,6},{5,7},{6,4},{7,5},{8,10},{9,11},{10,... | collective-permute-start | bytes 2457608 | tf_op jit(solution)/shard_map/d3/ppermute | solution.py:1014
  253.4 19.1 %collective-permute-start.47 = (bf16[1600,256]{1,0:T(8,128)(2,1)}, bf16[1600,256]{1,0:T(8,128)(2,1)S(1)}, u32[]{:S(2)}, u32[]{:S(2)}) collective-permute-start(bf16[1600,256]{1,0:T(8,128)(2,1)} %get-tuple-element.200), channel_id=1, source_target_pairs={{0,8},{1,9},{2,10},{3,11},{4,12},{5,13},{6,14},{7,15},{8,0},{9,1},... | collective-permute-start | bytes 2457608 | tf_op jit(solution)/shard_map/rz_inner1/ppermute | solution.py:1014
  253.5 29.2 %collective-permute-start.42 = (bf16[1600,256]{1,0:T(8,128)(2,1)}, bf16[1600,256]{1,0:T(8,128)(2,1)}, u32[]{:S(2)}, u32[]{:S(2)}) collective-permute-start(bf16[1600,256]{1,0:T(8,128)(2,1)} %get-tuple-element.183), channel_id=1, source_target_pairs={{0,2},{1,3},{2,0},{3,1},{4,6},{5,7},{6,4},{7,5},{8,10},{9,11},{10,... | collective-permute-start | bytes 2457608 | tf_op jit(solution)/shard_map/e3/ppermute | solution.py:1014
  269.1 20.0 %collective-permute-start.51 = (bf16[1600,256]{1,0:T(8,128)(2,1)}, bf16[1600,256]{1,0:T(8,128)(2,1)}, u32[]{:S(2)}, u32[]{:S(2)}) collective-permute-start(bf16[1600,256]{1,0:T(8,128)(2,1)} %fusion), channel_id=1, source_target_pairs={{0,4},{1,5},{2,6},{3,7},{4,0},{5,1},{6,2},{7,3},{8,12},{9,13},{10,... | collective-permute-start | bytes 2457608 | tf_op jit(solution)/shard_map/f3/ppermute | solution.py:1014
  272.7 20.2 %collective-permute-start.48 = (bf16[1600,256]{1,0:T(8,128)(2,1)S(1)}, bf16[1600,256]{1,0:T(8,128)(2,1)}, u32[]{:S(2)}, u32[]{:S(2)}) collective-permute-start(bf16[1600,256]{1,0:T(8,128)(2,1)S(1)} %add_convert_fusion.1.inner), channel_id=1, source_target_pairs={{0,16},{1,17},{2,18},{3,19},{4,20},{5,21},{6,22},{7,23},{24,8},{25... | collective-permute-start | bytes 2457608 | tf_op jit(solution)/shard_map/rz_inner2/ppermute | solution.py:1014
  292.9 18.9 %collective-permute-start.52 = (bf16[1600,256]{1,0:T(8,128)(2,1)}, bf16[1600,256]{1,0:T(8,128)(2,1)}, u32[]{:S(2)}, u32[]{:S(2)}) collective-permute-start(bf16[1600,256]{1,0:T(8,128)(2,1)} %get-tuple-element.205), channel_id=1, source_target_pairs={{0,8},{1,9},{2,10},{3,11},{4,12},{5,13},{6,14},{7,15},{8,0},{9,1},... | collective-permute-start | bytes 2457608 | tf_op jit(solution)/shard_map/rz_outer1/ppermute | solution.py:1014
  294.3 20.3 %collective-permute-start.44 = (f32[2,32,256]{2,1,0:T(8,128)S(1)}, f32[2,32,256]{2,1,0:T(8,128)S(1)}, u32[]{:S(2)}, u32[]{:S(2)}) collective-permute-start(f32[2,32,256]{2,1,0:T(8,128)S(1)} %select_bitcast_fusion), channel_id=1, source_target_pairs={{0,1},{1,0},{2,3},{3,2},{4,5},{5,4},{6,7},{7,6},{8,9},{9,8},{10,11... | collective-permute-start | bytes 196616 | tf_op jit(solution)/shard_map/vec_c/ppermute | solution.py:1014
  295.6 23.0 %collective-permute-start.43 = (bf16[256,1024]{1,0:T(8,128)(2,1)S(1)}, bf16[256,1024]{1,0:T(8,128)(2,1)S(1)}, u32[]{:S(2)}, u32[]{:S(2)}) collective-permute-start(bf16[256,1024]{1,0:T(8,128)(2,1)S(1)} %fusion.11), channel_id=1, source_target_pairs={{0,2},{1,3},{2,0},{3,1},{4,6},{5,7},{6,4},{7,5},{8,10},{9,11},{10,... | collective-permute-start | bytes 1572872 | tf_op jit(solution)/shard_map/in_x/ppermute | solution.py:1014
  313.3 20.6 %collective-permute-start.53 = (bf16[1600,256]{1,0:T(8,128)(2,1)S(1)}, bf16[1600,256]{1,0:T(8,128)(2,1)}, u32[]{:S(2)}, u32[]{:S(2)}) collective-permute-start(bf16[1600,256]{1,0:T(8,128)(2,1)S(1)} %add_convert_fusion.outer), channel_id=1, source_target_pairs={{8,24},{9,25},{10,26},{11,27},{12,28},{13,29},{14,30},{15,31},{16,... | collective-permute-start | bytes 2457608 | tf_op jit(solution)/shard_map/rz_outer2/ppermute | solution.py:1014
  314.6 4.0 %collective-permute-start.45 = (f32[32,256]{1,0:T(8,128)S(1)}, f32[32,256]{1,0:T(8,128)S(1)}, u32[]{:S(2)}, u32[]{:S(2)}) collective-permute-start(f32[32,256]{1,0:T(8,128)S(1)} %select_bitcast_fusion.1), channel_id=1, source_target_pairs={{0,2},{1,3},{2,0},{3,1},{4,6},{5,7},{6,4},{7,5},{8,10},{9,11},{10,... | collective-permute-start | bytes 98312 | tf_op jit(solution)/shard_map/vec_x/ppermute | solution.py:1014
  321.0 40.5 %copy-start.26 = (f32[393664]{0:T(1024)S(1)}, f32[393664]{0:T(1024)}, u32[]{:S(2)}) copy-start(f32[393664]{0:T(1024)} %param.11) | copy-start | bytes 4723972
  338.6 4.1 %collective-permute-start.54 = (f32[40,256]{1,0:T(8,128)S(1)}, f32[40,256]{1,0:T(8,128)S(1)}, u32[]{:S(2)}, u32[]{:S(2)}) collective-permute-start(f32[40,256]{1,0:T(8,128)S(1)} %pad_maximum_fusion.1), channel_id=1, source_target_pairs={{0,4},{1,5},{2,6},{3,7},{4,0},{5,1},{6,2},{7,3},{8,12},{9,13},{10,... | collective-permute-start | bytes 122888 | tf_op jit(solution)/shard_map/norm/ppermute | solution.py:1014
  343.3 4.0 %collective-permute-start.55 = (f32[40,256]{1,0:T(8,128)S(1)}, f32[40,256]{1,0:T(8,128)S(1)}, u32[]{:S(2)}, u32[]{:S(2)}) collective-permute-start(f32[40,256]{1,0:T(8,128)S(1)} %fusion.18), channel_id=1, source_target_pairs={{0,8},{1,9},{2,10},{3,11},{4,12},{5,13},{6,14},{7,15},{8,0},{9,1},... | collective-permute-start | bytes 122888 | tf_op jit(solution)/shard_map/norm/ppermute | solution.py:1014
  347.3 4.9 %collective-permute-start.56 = (f32[40,256]{1,0:T(8,128)S(1)}, f32[40,256]{1,0:T(8,128)S(1)}, u32[]{:S(2)}, u32[]{:S(2)}) collective-permute-start(f32[40,256]{1,0:T(8,128)S(1)} %add.191), channel_id=1, source_target_pairs={{0,16},{1,17},{2,18},{3,19},{4,20},{5,21},{6,22},{7,23},{8,24},{9,... | collective-permute-start | bytes 122888 | tf_op jit(solution)/shard_map/norm/ppermute | solution.py:1014
  353.6 3.7 collective-permute-start.57
  357.9 1.6 collective-permute-start.58
  (51 other events, 460.0 us)

commit v5 on v4

--- a/solution.py
+++ b/solution.py
@@ -1038,13 +1038,8 @@
     return lambda z, y, x, c: route(z, y, x, c) if z in planes else None
 
 
-EVERY = (to_core, to_x, to_y, to_near, to_far)
-
-
-def total(values, name):
-    for route in EVERY:
-        values = values + send(values, route, name)
-    return values
+def to_opposite(z, y, x, c):
+    return 3 - z, y, x, c
 
 
 def to_relative(r):
@@ -1057,6 +1052,11 @@
 
 def after(values, *earlier):
     return lax.optimization_barrier((values, *earlier))[0]
+
+
+def together(values, routes, *beside):
+    near, far, both = (send(values, route, "norm") for route in routes)
+    return (values + near) + (far + after(both, *beside))
 
 
 PLANES = ((1, 2, 3), (0, 1, 3), (0, 2), (0, 1, 2, 3))
@@ -1259,16 +1259,13 @@
 
     grad_flat, square = unpack(after(place, input_grad), inner_part, inner_last, outer_part, outer_last)
     mine = jnp.concatenate([mine, square])
-    for route in (to_y, to_near, to_far):
-        mine = mine + send(mine, route, "norm")
+    mine = mine + send(mine, to_y, "norm")
+    mine = together(mine, (to_near, to_far, to_opposite))
     vec_sum, head_sum = mine[:14].reshape(-1), mine[16:20].reshape(-1)[:896]
     vector_grad = vec_sum
     is_sum = jnp.arange(40)[:, None] >= 32
     square_sum = jnp.sum(jnp.where(is_sum, mine, mine * mine))
     square_sum = jnp.broadcast_to(square_sum, (8, 128))
-    for route in (to_x, to_core):
-        square_sum = square_sum + send(square_sum, route, "norm")
-    grad_norm = jnp.sqrt(square_sum[0, 0])
     grad_flat = grad_flat.reshape(-1)
     edge = grad_flat[SHARD - 3584 : SHARD]
     edge = jnp.where(
@@ -1276,7 +1273,10 @@
         vec_sum,
         jnp.where(shard == 1, jnp.concatenate([edge[: 3584 - 896], head_sum]), edge),
     )
-    grad_shard = lax.dynamic_update_slice(grad_flat, edge, (SHARD - 3584,))[:SHARD]
+    grad_shard = lax.dynamic_update_slice(grad_flat, edge, (SHARD - 3584,))
+    square_sum = together(square_sum, (to_core, to_x, to_relative(3)), grad_shard)
+    grad_shard = grad_shard[:SHARD]
+    grad_norm = jnp.sqrt(square_sum[0, 0])
     clip_limit = 4.0 * math.sqrt(PARAMS)
     clipped = grad_shard * (clip_limit / jnp.maximum(grad_norm, clip_limit))
     new_first = 0.9 * first_moment + 0.1 * clipped

time: 374 us -> 372 us (level)
  waiting for transfers between devices: 175 us -> 167 us
  starting transfers between devices: 59.1 us -> 65.1 us
    ppermute x59 -> x61, waiting for transfers between devices: 175 us -> 167 us  [send(): return lax.ppermute(values, AXES, pairs)]
    ppermute x59 -> x61, starting transfers between devices: 59.1 us -> 65.1 us  [send(): return lax.ppermute(values, AXES, pairs)]
  transfers between devices with their start and end apart: 59 -> 61, of which waited for: 37 -> 36; matrix products, arithmetic and copies ran while one was open for 10% -> 10% of each run, Pallas kernels for 10% -> 10%
where the time goes in v5:
time: 372 us; the launch traced here: 366 us
  waiting for transfers between devices  167 us (45%)
  Pallas kernels  71.8 us (19%)
  starting transfers between devices  65.1 us (17%)
  other arithmetic  38.2 us (10%)
  local copies, waits for them, and re-layouts  14 us (4%)
  between operations  5.71 us (2%)
  matrix products  4.09 us (1%)
    ppermute x61, waiting for transfers between devices, send(): return lax.ppermute(values, AXES, pairs)  167 us
    ppermute x61, starting transfers between devices, send(): return lax.ppermute(values, AXES, pairs)  65.1 us
    pallas_call x1, Pallas kernels, layer(): pl.pallas_call(layer_kernel, out_shape=(struct((256, D)), struct((256, D)...  28.6 us
    convert_element_type x10, other arithmetic, low(): return values.astype(jnp.bfloat16)  17.4 us
    pallas_call x1, Pallas kernels, attend_back(): pl.pallas_call(attend_back_kernel, out_shape=(square, square, square, str...  16 us
    pallas_call x1, Pallas kernels, attend(): pl.pallas_call(attend_kernel, out_shape=(struct((4, 256, 1024)), struct((...  14.5 us
    pallas_call x2, Pallas kernels, combine(): pl.pallas_call(partial(combine_kernel, len(first)), grid=(blocks,), out_s...  7.82 us
  transfers between devices with their start and end apart: 61, of which 36 were waited for; matrix products, arithmetic and copies ran while one was open for 10% of the time, Pallas kernels for 10%

profile of v5, /device:TPU:0, one launch (start us, length us, event | category | flops | bytes accessed | tf_op | source)
XLA Modules:
  0.0 366.4 jit_solution(13008779139737522425)
XLA Ops:
  2.3 3.0 collective-permute-start
  5.3 1.5 pad_bitcast_fusion.flat
  9.2 3.4 collective-permute-start.2
  12.6 1.9 collective-permute-start.7
  14.4 1.5 collective-permute-start.4
  16.6 14.1 %collective-permute-done.2.p2.refs_1_ = bf16[1600,256]{1,0:T(8,128)(2,1)S(1)} collective-permute-done((bf16[1600,256]{1,0:T(8,128)(2,1)S(1)}, bf16[1600,256]{1,0:T(8,128)(2,1)S(1)}, u32[]{:S(2)}, u32[]{:S(2)}) %collective-permute-start.2) | collective-permute-done | bytes 819232 | tf_op jit(solution)/shard_map/first/ppermute | solution.py:1014
  30.8 2.4 collective-permute-done.7.p1.refs_4_
  33.2 1.7 collective-permute-start.8
  36.1 1.6 collective-permute-start.3
  38.6 3.4 collective-permute-start.13
  42.8 10.2 %collective-permute-done.8.p3.refs_5_ = bf16[1600,256]{1,0:T(8,128)(2,1)} collective-permute-done((bf16[1600,256]{1,0:T(8,128)(2,1)S(1)}, bf16[1600,256]{1,0:T(8,128)(2,1)}, u32[]{:S(2)}, u32[]{:S(2)}) %collective-permute-start.8) | collective-permute-done | bytes 819232 | tf_op jit(solution)/shard_map/y1/ppermute | solution.py:1014
  53.0 2.5 collective-permute-done.5.p4.refs_2_
  58.4 1.6 collective-permute-start.14
  61.8 14.9 %collective-permute-done.6 = bf16[1600,256]{1,0:T(8,128)(2,1)S(1)} collective-permute-done((bf16[1600,256]{1,0:T(8,128)(2,1)}, bf16[1600,256]{1,0:T(8,128)(2,1)S(1)}, u32[]{:S(2)}, u32[]{:S(2)}) %collective-permute-start.6) | collective-permute-done | bytes 819232 | tf_op jit(solution)/shard_map/third/ppermute | solution.py:1014
  77.9 1.5 collective-permute-start.17
  82.2 2.4 collective-permute-start.16
  84.7 14.5 %attend.1 = (bf16[4,256,1024]{2,1,0:T(8,128)(2,1)}, bf16[3,1024,256]{2,1,0:T(8,128)(2,1)}, bf16[1024,256]{1,0:T(8,128)(2,1)S(1)}, bf16[1024,256]{1,0:T(8,128)(2,...) custom-call(s32[6]{0:T(128)S(1)} %stack.19.place, ...), custom_call_target="tpu_custom_call" | custom-call | flops 16000000000 | bytes 24000000 | tf_op jit(solution)/shard_map/attend/pallas_call | solution.py:369
  103.1 8.8 %collective-permute-done.18.refs_11_ = bf16[1600,256]{1,0:T(8,128)(2,1)S(1)} collective-permute-done((bf16[1600,256]{1,0:T(8,128)(2,1)S(1)}, bf16[1600,256]{1,0:T(8,128)(2,1)S(1)}, u32[]{:S(2)}, u32[]{:S(2)}) %collective-permute-start.18) | collective-permute-done | bytes 819232 | tf_op jit(solution)/shard_map/yb/ppermute | solution.py:1014
  112.7 1.6 collective-permute-start.22
  114.4 2.2 collective-permute-start.27
  116.9 8.0 %collective-permute-done.19.h1 = bf16[256,256]{1,0:T(8,128)(2,1)S(1)} collective-permute-done((bf16[256,256]{1,0:T(8,128)(2,1)S(1)}, bf16[256,256]{1,0:T(8,128)(2,1)S(1)}, u32[]{:S(2)}, u32[]{:S(2)}) %collective-permute-start.19) | collective-permute-done | bytes 131104 | tf_op jit(solution)/shard_map/heads/ppermute | solution.py:1014
  125.4 8.4 %collective-permute-done.22.refs_14_ = bf16[1600,256]{1,0:T(8,128)(2,1)S(1)} collective-permute-done((bf16[1600,256]{1,0:T(8,128)(2,1)S(1)}, bf16[1600,256]{1,0:T(8,128)(2,1)S(1)}, u32[]{:S(2)}, u32[]{:S(2)}) %collective-permute-start.22) | collective-permute-done | bytes 819232 | tf_op jit(solution)/shard_map/yx3/ppermute | solution.py:1014
  134.9 1.3 collective-permute-done.20.h2
  136.2 3.4 collective-permute-done.21.h3
  142.1 2.3 collective-permute-done.24.refs_16_
  146.3 28.6 %layer.1 = (bf16[256,1024]{1,0:T(8,128)(2,1)}, f32[256,1024]{1,0:T(8,128)}, bf16[256,256]{1,0:T(8,128)(2,1)}, bf16[256,256]{1,0:T(8,128)(2,1)}, bf16[256,256]{1,...) custom-call(s32[6]{0:T(128)} %copy-done.1, ...), custom_call_target="tpu_custom_call" | custom-call | flops 15000000512 | bytes 40000000 | tf_op jit(solution)/shard_map/layer/pallas_call | solution.py:708
  177.4 3.7 collective-permute-done.34.refs_1_
  181.1 3.0 fusion.8
  184.1 1.8 collective-permute-done.31.g1
  186.2 1.3 fusion.7
  188.4 1.4 collective-permute-start.35
  191.6 16.0 %attend_back.1 = (bf16[1024,256]{1,0:T(8,128)(2,1)S(1)}, bf16[1024,256]{1,0:T(8,128)(2,1)S(1)}, bf16[1024,256]{1,0:T(8,128)(2,1)S(1)}, f32[2,256,1024]{2,1,0:T(8...) custom-call(s32[6]{0:T(128)S(1)} %copy-done.2, bf16[1024,256]{1,0:T(8,128)(2,1)S(1)} %copy-done.12, ...), custom_call_target="tpu_custom_call" | custom-call | flops 20000000000 | bytes 12000000 | tf_op jit(solution)/shard_map/attend_back/pallas_call | solution.py:460
  209.8 2.6 fusion.1
  212.4 2.5 fusion.2
  214.9 2.0 fusion.10
  217.3 8.4 %collective-permute-done.39.refs_2_ = bf16[1600,256]{1,0:T(8,128)(2,1)} collective-permute-done((bf16[1600,256]{1,0:T(8,128)(2,1)S(1)}, bf16[1600,256]{1,0:T(8,128)(2,1)}, u32[]{:S(2)}, u32[]{:S(2)}) %collective-permute-start.39) | collective-permute-done | bytes 819232 | tf_op jit(solution)/shard_map/e2/ppermute | solution.py:1014
  227.7 1.4 collective-permute-start.46
  229.3 2.6 convolution_convert_fusion.2
  233.8 1.6 broadcast_select_fusion
  235.3 1.4 collective-permute-start.49
  237.9 10.1 %collective-permute-done.41.refs_7_ = bf16[1600,256]{1,0:T(8,128)(2,1)} collective-permute-done((bf16[1600,256]{1,0:T(8,128)(2,1)}, bf16[1600,256]{1,0:T(8,128)(2,1)}, u32[]{:S(2)}, u32[]{:S(2)}) %collective-permute-start.41) | collective-permute-done | bytes 819232 | tf_op jit(solution)/shard_map/f1/ppermute | solution.py:1014
  249.1 4.2 %combine.2 = (bf16[1600,256]{1,0:T(8,128)(2,1)}, bf16[1600,256]{1,0:T(8,128)(2,1)}) custom-call(s32[6]{0:T(128)} %copy-done.1, bf16[2,2,1600,256]{3,2,1,0:T(8,128)(2,1)} %get-tuple-element.153.refs_0_, bf16[2,2,1600,256]{3,2,1,0:T(8,128)(2,1)} %copy-done.24, bf16[1600,256]{1,0:T(8,128)(2,1)} %collective-permute-done.39.refs_2_, ...), custom_call_target="tpu_custom_call" | custom-call | tf_op jit(solution)/shard_map/combine/pallas_call | solution.py:257
  254.4 11.5 %collective-permute-done.49.refs_1_ = bf16[1600,256]{1,0:T(8,128)(2,1)S(1)} collective-permute-done((bf16[1600,256]{1,0:T(8,128)(2,1)}, bf16[1600,256]{1,0:T(8,128)(2,1)S(1)}, u32[]{:S(2)}, u32[]{:S(2)}) %collective-permute-start.49) | collective-permute-done | bytes 819232 | tf_op jit(solution)/shard_map/ry0/ppermute | solution.py:1014
  265.9 3.2 fusion
  269.1 1.4 collective-permute-start.51
  270.4 2.0 collective-permute-done.47
  272.6 5.3 %collective-permute-start.48 = (bf16[1600,256]{1,0:T(8,128)(2,1)S(1)}, bf16[1600,256]{1,0:T(8,128)(2,1)}, u32[]{:S(2)}, u32[]{:S(2)}) collective-permute-start(bf16[1600,256]{1,0:T(8,128)(2,1)S(1)} %add_convert_fusion.1.inner), channel_id=1, source_target_pairs={{0,16},{1,17},{2,18},{3,19},{4,20},{5,21},{6,22},{7,23},{24,8},{25... | collective-permute-start | bytes 2457608 | tf_op jit(solution)/shard_map/rz_inner2/ppermute | solution.py:1014
  279.3 3.4 collective-permute-done.42.refs_4_
  282.7 6.4 %collective-permute-done.51.refs_5_ = bf16[1600,256]{1,0:T(8,128)(2,1)} collective-permute-done((bf16[1600,256]{1,0:T(8,128)(2,1)}, bf16[1600,256]{1,0:T(8,128)(2,1)}, u32[]{:S(2)}, u32[]{:S(2)}) %collective-permute-start.51) | collective-permute-done | bytes 819232 | tf_op jit(solution)/shard_map/f3/ppermute | solution.py:1014
  289.1 3.6 combine.3
  296.5 15.4 %collective-permute-done.52 = bf16[1600,256]{1,0:T(8,128)(2,1)} collective-permute-done((bf16[1600,256]{1,0:T(8,128)(2,1)}, bf16[1600,256]{1,0:T(8,128)(2,1)}, u32[]{:S(2)}, u32[]{:S(2)}) %collective-permute-start.52) | collective-permute-done | bytes 819232 | tf_op jit(solution)/shard_map/rz_outer1/ppermute | solution.py:1014
  311.8 1.4 add_convert_fusion.outer
  313.2 1.3 collective-permute-start.53
  315.5 3.0 collective-permute-done.45
  318.6 2.3 fusion.4
  320.9 12.9 %collective-permute-done.53.outer_last = bf16[1600,256]{1,0:T(8,128)(2,1)} collective-permute-done((bf16[1600,256]{1,0:T(8,128)(2,1)S(1)}, bf16[1600,256]{1,0:T(8,128)(2,1)}, u32[]{:S(2)}, u32[]{:S(2)}) %collective-permute-start.53) | collective-permute-done | bytes 819232 | tf_op jit(solution)/shard_map/rz_outer2/ppermute | solution.py:1014
  333.8 4.0 %unpack.1 = (f32[3080,128]{1,0:T(8,128)}, f32[8,256]{1,0:T(8,128)}) custom-call(s32[6]{0:T(128)} %copy-done.1, bf16[1600,256]{1,0:T(8,128)(2,1)} %copy-done.27, bf16[1600,256]{1,0:T(8,128)(2,1)} %collective-permute-done.48.inner_last, bf16[1600,256]{1,0:T(8,128)(2,1)} %copy-done.28, bf16[1600,256]{1,0:T(8,128)(2,1)} %collective-permute-done.53.outer_last), custom_call_target="tpu_custom_call" | custom-call | tf_op jit(solution)/shard_map/unpack/pallas_call | solution.py:222
  338.5 2.2 collective-permute-start.54
  340.7 2.0 collective-permute-done.54
  343.4 1.8 collective-permute-start.56
  345.2 2.6 collective-permute-start.57
  348.6 2.4 collective-permute-done.57
  354.5 1.5 fusion.17
  358.9 6.0 %multiply_add_fusion = (f32[393664]{0:T(1024)}, f32[393664]{0:T(1024)}, f32[393664]{0:T(1024)}, f32[393664]{0:T(1024)}) fusion(f32[393664]{0:T(1024)S(1)} %copy-done.29, f32[393664]{0:T(1024)S(1)} %copy-done.26, f32[]{:T(128)S(6)} %div.48, f32[394240]{0:T(1024)} %fusion.17, f32[393664]{0:T(1024)} %param.13, f32[393664]{0:T(1024)} %param.12), kind=kLoop, calls=%fused_computation.17 | loop fusion | flops 7479616 | bytes 14171908 | tf_op jit(solution)/shard_map/add | solution.py:1287
  (265 shorter events, 54.6 us)
Async XLA Ops:
  2.3 4.6 %collective-permute-start = (bf16[16,256]{1,0:T(8,128)(2,1)S(1)}, bf16[16,256]{1,0:T(8,128)(2,1)S(1)}, u32[]{:S(2)}, u32[]{:S(2)}) collective-permute-start(bf16[16,256]{1,0:T(8,128)(2,1)S(1)} %select_convert_fusion), channel_id=1, source_target_pairs={{0,2},{1,3},{2,0},{3,1},{4,6},{5,7},{6,4},{7,5},{8,10},{9,11},{10,... | collective-permute-start | bytes 24584 | tf_op jit(solution)/shard_map/tail_x/ppermute | solution.py:1014
  6.9 1.4 collective-permute-start.1
  8.3 76.3 %copy-start.1 = (s32[6]{0:T(128)}, s32[6]{0:T(128)S(1)}, u32[]{:S(2)}) copy-start(s32[6]{0:T(128)S(1)} %stack.19.place) | copy-start | bytes 76
  9.2 75.5 %copy-start = (bf16[1600,256]{1,0:T(8,128)(2,1)}, bf16[1600,256]{1,0:T(8,128)(2,1)S(1)}, u32[]{:S(2)}) copy-start(bf16[1600,256]{1,0:T(8,128)(2,1)S(1)} %pack.1.p0.refs_0_) | copy-start | bytes 2457604
  9.2 21.5 %collective-permute-start.2 = (bf16[1600,256]{1,0:T(8,128)(2,1)S(1)}, bf16[1600,256]{1,0:T(8,128)(2,1)S(1)}, u32[]{:S(2)}, u32[]{:S(2)}) collective-permute-start(bf16[1600,256]{1,0:T(8,128)(2,1)S(1)} %pack.1.p0.refs_0_), channel_id=1, source_target_pairs={{0,16},{1,17},{2,18},{3,19},{4,20},{5,21},{6,22},{7,23},{8,0},{9,1... | collective-permute-start | bytes 2457608 | tf_op jit(solution)/shard_map/first/ppermute | solution.py:1014
  12.6 20.6 %collective-permute-start.7 = (bf16[1600,256]{1,0:T(8,128)(2,1)S(1)}, bf16[1600,256]{1,0:T(8,128)(2,1)}, u32[]{:S(2)}, u32[]{:S(2)}) collective-permute-start(bf16[1600,256]{1,0:T(8,128)(2,1)S(1)} %pack.1.p0.refs_0_), channel_id=1, source_target_pairs={{0,4},{1,5},{2,6},{3,7},{4,0},{5,1},{6,2},{7,3},{8,12},{9,13},{10,... | collective-permute-start | bytes 2457608 | tf_op jit(solution)/shard_map/y0/ppermute | solution.py:1014
  14.4 21.5 %collective-permute-start.4 = (bf16[256,1024]{1,0:T(8,128)(2,1)S(1)}, bf16[256,1024]{1,0:T(8,128)(2,1)S(1)}, u32[]{:S(2)}, u32[]{:S(2)}) collective-permute-start(bf16[256,1024]{1,0:T(8,128)(2,1)S(1)} %copy-done.4), channel_id=1, source_target_pairs={{0,2},{1,3},{2,0},{3,1},{4,6},{5,7},{6,4},{7,5},{8,10},{9,11},{10,... | collective-permute-start | bytes 1572872 | tf_op jit(solution)/shard_map/tok_x/ppermute | solution.py:1014
  15.9 21.8 %collective-permute-start.12 = (bf16[1600,256]{1,0:T(8,128)(2,1)S(1)}, bf16[1600,256]{1,0:T(8,128)(2,1)S(1)}, u32[]{:S(2)}, u32[]{:S(2)}) collective-permute-start(bf16[1600,256]{1,0:T(8,128)(2,1)S(1)} %pack.1.p0.refs_0_), channel_id=1, source_target_pairs={{8,10},{9,11},{10,8},{11,9},{12,14},{13,15},{14,12},{15,13},{16,18... | collective-permute-start | bytes 2457608 | tf_op jit(solution)/shard_map/x0/ppermute | solution.py:1014
  30.8 48.6 %copy-start.31 = (bf16[1600,256]{1,0:T(8,128)(2,1)}, bf16[1600,256]{1,0:T(8,128)(2,1)S(1)}, u32[]{:S(2)}) copy-start(bf16[1600,256]{1,0:T(8,128)(2,1)S(1)} %collective-permute-done.2.p2.refs_1_) | copy-start | bytes 2457604
  33.2 19.8 %collective-permute-start.8 = (bf16[1600,256]{1,0:T(8,128)(2,1)S(1)}, bf16[1600,256]{1,0:T(8,128)(2,1)}, u32[]{:S(2)}, u32[]{:S(2)}) collective-permute-start(bf16[1600,256]{1,0:T(8,128)(2,1)S(1)} %collective-permute-done.2.p2.refs_1_), channel_id=1, source_target_pairs={{0,4},{1,5},{2,6},{3,7},{4,0},{5,1},{6,2},{7,3},{8,12},{9,13},{10,... | collective-permute-start | bytes 2457608 | tf_op jit(solution)/shard_map/y1/ppermute | solution.py:1014
  35.9 19.6 %collective-permute-start.5 = (bf16[1600,256]{1,0:T(8,128)(2,1)}, bf16[1600,256]{1,0:T(8,128)(2,1)}, u32[]{:S(2)}, u32[]{:S(2)}) collective-permute-start(bf16[1600,256]{1,0:T(8,128)(2,1)} %broadcast_select_fusion.5), channel_id=1, source_target_pairs={{0,8},{1,9},{2,10},{3,11},{4,12},{5,13},{6,14},{7,15},{8,0},{9,1},... | collective-permute-start | bytes 2457608 | tf_op jit(solution)/shard_map/second/ppermute | solution.py:1014
  36.1 19.8 %collective-permute-start.3 = (bf16[1600,256]{1,0:T(8,128)(2,1)S(1)}, bf16[1600,256]{1,0:T(8,128)(2,1)}, u32[]{:S(2)}, u32[]{:S(2)}) collective-permute-start(bf16[1600,256]{1,0:T(8,128)(2,1)S(1)} %pack.1.p0.refs_0_), channel_id=1, source_target_pairs={{8,16},{9,17},{10,18},{11,19},{12,20},{13,21},{14,22},{15,23},{16,... | collective-permute-start | bytes 2457608 | tf_op jit(solution)/shard_map/crossed/ppermute | solution.py:1014
  38.6 21.9 %collective-permute-start.13 = (bf16[1600,256]{1,0:T(8,128)(2,1)S(1)}, bf16[1600,256]{1,0:T(8,128)(2,1)}, u32[]{:S(2)}, u32[]{:S(2)}) collective-permute-start(bf16[1600,256]{1,0:T(8,128)(2,1)S(1)} %collective-permute-done.2.p2.refs_1_), channel_id=1, source_target_pairs={{0,2},{1,3},{2,0},{3,1},{4,6},{5,7},{6,4},{7,5},{8,10},{9,11},{10,... | collective-permute-start | bytes 2457608 | tf_op jit(solution)/shard_map/x1/ppermute | solution.py:1014
  42.0 38.4 %collective-permute-start.10 = (bf16[256,1024]{1,0:T(8,128)(2,1)S(1)}, bf16[256,1024]{1,0:T(8,128)(2,1)S(1)}, u32[]{:S(2)}, u32[]{:S(2)}) collective-permute-start(bf16[256,1024]{1,0:T(8,128)(2,1)S(1)} %copy-done.4), channel_id=1, source_target_pairs={{0,1},{1,0},{2,3},{3,2},{4,5},{5,4},{6,7},{7,6},{8,9},{9,8},{10,11... | collective-permute-start | bytes 1572872 | tf_op jit(solution)/shard_map/tok_c/ppermute | solution.py:1014
  55.5 21.4 %collective-permute-start.9 = (bf16[1600,256]{1,0:T(8,128)(2,1)}, bf16[1600,256]{1,0:T(8,128)(2,1)S(1)}, u32[]{:S(2)}, u32[]{:S(2)}) collective-permute-start(bf16[1600,256]{1,0:T(8,128)(2,1)} %collective-permute-done.5.p4.refs_2_), channel_id=1, source_target_pairs={{0,4},{1,5},{2,6},{3,7},{4,0},{5,1},{6,2},{7,3},{8,12},{9,13},{10,... | collective-permute-start | bytes 2457608 | tf_op jit(solution)/shard_map/y2/ppermute | solution.py:1014
  55.9 20.8 %collective-permute-start.6 = (bf16[1600,256]{1,0:T(8,128)(2,1)}, bf16[1600,256]{1,0:T(8,128)(2,1)S(1)}, u32[]{:S(2)}, u32[]{:S(2)}) collective-permute-start(bf16[1600,256]{1,0:T(8,128)(2,1)} %collective-permute-done.3), channel_id=1, source_target_pairs={{8,0},{9,1},{10,2},{11,3},{12,4},{13,5},{14,6},{15,7},{16,24},{17,... | collective-permute-start | bytes 2457608 | tf_op jit(solution)/shard_map/third/ppermute | solution.py:1014
  58.4 44.6 %collective-permute-start.14 = (bf16[1600,256]{1,0:T(8,128)(2,1)S(1)}, bf16[1600,256]{1,0:T(8,128)(2,1)S(1)}, u32[]{:S(2)}, u32[]{:S(2)}) collective-permute-start(bf16[1600,256]{1,0:T(8,128)(2,1)S(1)} %broadcast_select_fusion.3), channel_id=1, source_target_pairs={{0,2},{1,3},{2,0},{3,1},{4,6},{5,7},{6,4},{7,5},{8,10},{9,11},{10,... | collective-permute-start | bytes 2457608 | tf_op jit(solution)/shard_map/xa/ppermute | solution.py:1014
  76.9 35.7 %collective-permute-start.15 = (bf16[1600,256]{1,0:T(8,128)(2,1)S(1)}, bf16[1600,256]{1,0:T(8,128)(2,1)S(1)}, u32[]{:S(2)}, u32[]{:S(2)}) collective-permute-start(bf16[1600,256]{1,0:T(8,128)(2,1)S(1)} %broadcast_select_fusion.4.p6.refs_3_), channel_id=1, source_target_pairs={{0,4},{1,5},{2,6},{3,7},{4,0},{5,1},{6,2},{7,3},{8,12},{9,13},{10,... | collective-permute-start | bytes 2457608 | tf_op jit(solution)/shard_map/y3/ppermute | solution.py:1014
  77.9 34.7 %collective-permute-start.17 = (bf16[1600,256]{1,0:T(8,128)(2,1)S(1)}, bf16[1600,256]{1,0:T(8,128)(2,1)}, u32[]{:S(2)}, u32[]{:S(2)}) collective-permute-start(bf16[1600,256]{1,0:T(8,128)(2,1)S(1)} %broadcast_select_fusion.4.p6.refs_3_), channel_id=1, source_target_pairs={{0,2},{1,3},{2,0},{3,1},{4,6},{5,7},{6,4},{7,5},{8,10},{9,11},{10,... | collective-permute-start | bytes 2457608 | tf_op jit(solution)/shard_map/x3/ppermute | solution.py:1014
  80.2 2.0 collective-permute-start.11
  80.4 31.5 %collective-permute-start.18 = (bf16[1600,256]{1,0:T(8,128)(2,1)S(1)}, bf16[1600,256]{1,0:T(8,128)(2,1)S(1)}, u32[]{:S(2)}, u32[]{:S(2)}) collective-permute-start(bf16[1600,256]{1,0:T(8,128)(2,1)S(1)} %broadcast_select_fusion.2), channel_id=1, source_target_pairs={{0,4},{1,5},{2,6},{3,7},{4,0},{5,1},{6,2},{7,3},{8,12},{9,13},{10,... | collective-permute-start | bytes 2457608 | tf_op jit(solution)/shard_map/yb/ppermute | solution.py:1014
  82.2 30.4 %collective-permute-start.16 = (bf16[1600,256]{1,0:T(8,128)(2,1)S(1)}, bf16[1600,256]{1,0:T(8,128)(2,1)}, u32[]{:S(2)}, u32[]{:S(2)}) collective-permute-start(bf16[1600,256]{1,0:T(8,128)(2,1)S(1)} %collective-permute-done.9.p5.refs_6_), channel_id=1, source_target_pairs={{0,2},{1,3},{2,0},{3,1},{4,6},{5,7},{6,4},{7,5},{16,18},{17,19},{1... | collective-permute-start | bytes 2457608 | tf_op jit(solution)/shard_map/yx2/ppermute | solution.py:1014
  112.6 33.6 %collective-permute-start.23 = (bf16[9,1600,256]{2,1,0:T(8,128)(2,1)}, bf16[9,1600,256]{2,1,0:T(8,128)(2,1)}, u32[]{:S(2)}, u32[]{:S(2)}) collective-permute-start(bf16[9,1600,256]{2,1,0:T(8,128)(2,1)} %get-tuple-element.136), channel_id=1, source_target_pairs={{0,1},{1,0},{2,3},{3,2},{4,5},{5,4},{6,7},{7,6},{8,9},{9,8},{10,11... | collective-permute-start | bytes 22118408 | tf_op jit(solution)/shard_map/stack/ppermute | solution.py:1014
  112.7 21.1 %collective-permute-start.22 = (bf16[1600,256]{1,0:T(8,128)(2,1)S(1)}, bf16[1600,256]{1,0:T(8,128)(2,1)S(1)}, u32[]{:S(2)}, u32[]{:S(2)}) collective-permute-start(bf16[1600,256]{1,0:T(8,128)(2,1)S(1)} %collective-permute-done.15.refs_10_), channel_id=1, source_target_pairs={{0,2},{1,3},{2,0},{3,1},{4,6},{5,7},{6,4},{7,5},{8,10},{9,11},{10,... | collective-permute-start | bytes 2457608 | tf_op jit(solution)/shard_map/yx3/ppermute | solution.py:1014
  114.2 25.4 %collective-permute-start.28 = (bf16[1600,256]{1,0:T(8,128)(2,1)}, bf16[1600,256]{1,0:T(8,128)(2,1)S(1)}, u32[]{:S(2)}, u32[]{:S(2)}) collective-permute-start(bf16[1600,256]{1,0:T(8,128)(2,1)} %collective-permute-done.17.refs_13_), channel_id=1, source_target_pairs={{0,1},{1,0},{2,3},{3,2},{4,5},{5,4},{6,7},{7,6},{8,9},{9,8},{10,11... | collective-permute-start | bytes 2457608 | tf_op jit(solution)/shard_map/cx3/ppermute | solution.py:1014
  114.4 25.7 %collective-permute-start.27 = (bf16[1600,256]{1,0:T(8,128)(2,1)}, bf16[1600,256]{1,0:T(8,128)(2,1)}, u32[]{:S(2)}, u32[]{:S(2)}) collective-permute-start(bf16[1600,256]{1,0:T(8,128)(2,1)} %collective-permute-done.16.refs_12_), channel_id=1, source_target_pairs={{0,1},{1,0},{2,3},{3,2},{4,5},{5,4},{6,7},{7,6},{16,17},{17,16},{1... | collective-permute-start | bytes 2457608 | tf_op jit(solution)/shard_map/cyx2/ppermute | solution.py:1014
  116.7 8.3 %collective-permute-start.19 = (bf16[256,256]{1,0:T(8,128)(2,1)S(1)}, bf16[256,256]{1,0:T(8,128)(2,1)S(1)}, u32[]{:S(2)}, u32[]{:S(2)}) collective-permute-start(bf16[256,256]{1,0:T(8,128)(2,1)S(1)} %get-tuple-element.133), channel_id=1, source_target_pairs={{0,1},{1,0},{2,3},{3,2},{4,5},{5,4},{6,7},{7,6},{8,9},{9,8},{10,11... | collective-permute-start | bytes 393224 | tf_op jit(solution)/shard_map/heads/ppermute | solution.py:1014
  124.9 11.2 %collective-permute-start.20 = (bf16[256,256]{1,0:T(8,128)(2,1)S(1)}, bf16[256,256]{1,0:T(8,128)(2,1)S(1)}, u32[]{:S(2)}, u32[]{:S(2)}) collective-permute-start(bf16[256,256]{1,0:T(8,128)(2,1)S(1)} %get-tuple-element.134), channel_id=1, source_target_pairs={{0,2},{1,3},{2,0},{3,1},{4,6},{5,7},{6,4},{7,5},{8,10},{9,11},{10,... | collective-permute-start | bytes 393224 | tf_op jit(solution)/shard_map/heads/ppermute | solution.py:1014
  133.8 5.8 %collective-permute-start.21 = (bf16[256,256]{1,0:T(8,128)(2,1)S(1)}, bf16[256,256]{1,0:T(8,128)(2,1)S(1)}, u32[]{:S(2)}, u32[]{:S(2)}) collective-permute-start(bf16[256,256]{1,0:T(8,128)(2,1)S(1)} %get-tuple-element.135), channel_id=1, source_target_pairs={{0,3},{1,2},{2,1},{3,0},{4,7},{5,6},{6,5},{7,4},{8,11},{9,10},{10,... | collective-permute-start | bytes 393224 | tf_op jit(solution)/shard_map/heads/ppermute | solution.py:1014
  136.2 5.4 %collective-permute-start.26 = (bf16[1600,256]{1,0:T(8,128)(2,1)}, bf16[1600,256]{1,0:T(8,128)(2,1)S(1)}, u32[]{:S(2)}, u32[]{:S(2)}) collective-permute-start(bf16[1600,256]{1,0:T(8,128)(2,1)} %copy-done.45), channel_id=1, source_target_pairs={{0,1},{1,0},{2,3},{3,2},{4,5},{5,4},{6,7},{7,6},{8,9},{9,8},{10,11... | collective-permute-start | bytes 2457608 | tf_op jit(solution)/shard_map/cyb/ppermute | solution.py:1014
  139.6 2.5 collective-permute-start.25
  139.7 4.8 %collective-permute-start.24 = (bf16[1600,256]{1,0:T(8,128)(2,1)}, bf16[1600,256]{1,0:T(8,128)(2,1)S(1)}, u32[]{:S(2)}, u32[]{:S(2)}) collective-permute-start(bf16[1600,256]{1,0:T(8,128)(2,1)} %copy-done.43), channel_id=1, source_target_pairs={{0,1},{1,0},{2,3},{3,2},{4,5},{5,4},{6,7},{7,6},{8,9},{9,8},{10,11... | collective-permute-start | bytes 2457608 | tf_op jit(solution)/shard_map/cxa/ppermute | solution.py:1014
  140.1 4.4 %collective-permute-start.29 = (bf16[1600,256]{1,0:T(8,128)(2,1)S(1)}, bf16[1600,256]{1,0:T(8,128)(2,1)S(1)}, u32[]{:S(2)}, u32[]{:S(2)}) collective-permute-start(bf16[1600,256]{1,0:T(8,128)(2,1)S(1)} %collective-permute-done.22.refs_14_), channel_id=1, source_target_pairs={{0,1},{1,0},{2,3},{3,2},{4,5},{5,4},{6,7},{7,6},{8,9},{9,8},{10,11... | collective-permute-start | bytes 2457608 | tf_op jit(solution)/shard_map/cyx3/ppermute | solution.py:1014
  174.9 6.1 %collective-permute-start.34 = (bf16[2,2,1600,256]{3,2,1,0:T(8,128)(2,1)}, bf16[2,2,1600,256]{3,2,1,0:T(8,128)(2,1)S(1)}, u32[]{:S(2)}, u32[]{:S(2)}) collective-permute-start(bf16[2,2,1600,256]{3,2,1,0:T(8,128)(2,1)} %get-tuple-element.154), channel_id=1, source_target_pairs={{0,1},{1,0},{2,3},{3,2},{4,5},{5,4},{6,7},{7,6},{8,9},{9,8},{10,11... | collective-permute-start | bytes 9830408 | tf_op jit(solution)/shard_map/rc2/ppermute | solution.py:1014
  175.1 10.8 %collective-permute-start.30 = (bf16[2,2,1600,256]{3,2,1,0:T(8,128)(2,1)}, bf16[2,2,1600,256]{3,2,1,0:T(8,128)(2,1)S(1)}, u32[]{:S(2)}, u32[]{:S(2)}) collective-permute-start(bf16[2,2,1600,256]{3,2,1,0:T(8,128)(2,1)} %get-tuple-element.147), channel_id=1, source_target_pairs={{0,1},{1,0},{2,3},{3,2},{4,5},{5,4},{6,7},{7,6},{8,9},{9,8},{10,11... | collective-permute-start | bytes 9830408 | tf_op jit(solution)/shard_map/rc1/ppermute | solution.py:1014
  175.5 10.4 %collective-permute-start.31 = (bf16[256,256]{1,0:T(8,128)(2,1)}, bf16[256,256]{1,0:T(8,128)(2,1)S(1)}, u32[]{:S(2)}, u32[]{:S(2)}) collective-permute-start(bf16[256,256]{1,0:T(8,128)(2,1)} %get-tuple-element.149), channel_id=1, source_target_pairs={{0,1},{1,0},{2,3},{3,2},{4,5},{5,4},{6,7},{7,6},{8,9},{9,8},{10,11... | collective-permute-start | bytes 393224 | tf_op jit(solution)/shard_map/heads_grad/ppermute | solution.py:1014
  175.6 10.3 %collective-permute-start.32 = (bf16[256,256]{1,0:T(8,128)(2,1)}, bf16[256,256]{1,0:T(8,128)(2,1)S(1)}, u32[]{:S(2)}, u32[]{:S(2)}) collective-permute-start(bf16[256,256]{1,0:T(8,128)(2,1)} %get-tuple-element.150), channel_id=1, source_target_pairs={{0,2},{1,3},{2,0},{3,1},{4,6},{5,7},{6,4},{7,5},{8,10},{9,11},{10,... | collective-permute-start | bytes 393224 | tf_op jit(solution)/shard_map/heads_grad/ppermute | solution.py:1014
  176.5 9.4 %collective-permute-start.33 = (bf16[256,256]{1,0:T(8,128)(2,1)}, bf16[256,256]{1,0:T(8,128)(2,1)S(1)}, u32[]{:S(2)}, u32[]{:S(2)}) collective-permute-start(bf16[256,256]{1,0:T(8,128)(2,1)} %get-tuple-element.151), channel_id=1, source_target_pairs={{0,3},{1,2},{2,1},{3,0},{4,7},{5,6},{6,5},{7,4},{8,11},{9,10},{10,... | collective-permute-start | bytes 393224 | tf_op jit(solution)/shard_map/heads_grad/ppermute | solution.py:1014
  185.9 29.0 %collective-permute-start.37 = (bf16[2,2,1600,256]{3,2,1,0:T(8,128)(2,1)}, bf16[2,2,1600,256]{3,2,1,0:T(8,128)(2,1)S(1)}, u32[]{:S(2)}, u32[]{:S(2)}) collective-permute-start(bf16[2,2,1600,256]{3,2,1,0:T(8,128)(2,1)} %get-tuple-element.178), channel_id=1, source_target_pairs={{0,1},{1,0},{2,3},{3,2},{4,5},{5,4},{6,7},{7,6},{8,9},{9,8},{10,11... | collective-permute-start | bytes 9830408 | tf_op jit(solution)/shard_map/rc3/ppermute | solution.py:1014
  187.5 21.2 %collective-permute-start.36 = (bf16[1600,256]{1,0:T(8,128)(2,1)S(1)}, bf16[1600,256]{1,0:T(8,128)(2,1)}, u32[]{:S(2)}, u32[]{:S(2)}) collective-permute-start(bf16[1600,256]{1,0:T(8,128)(2,1)S(1)} %get-tuple-element.155), channel_id=1, source_target_pairs={{0,2},{1,3},{2,0},{3,1},{4,6},{5,7},{6,4},{7,5},{8,10},{9,11},{10,... | collective-permute-start | bytes 2457608 | tf_op jit(solution)/shard_map/d2/ppermute | solution.py:1014
  188.4 21.4 %collective-permute-start.35 = (bf16[1600,256]{1,0:T(8,128)(2,1)}, bf16[1600,256]{1,0:T(8,128)(2,1)}, u32[]{:S(2)}, u32[]{:S(2)}) collective-permute-start(bf16[1600,256]{1,0:T(8,128)(2,1)} %get-tuple-element.152), channel_id=1, source_target_pairs={{0,4},{1,5},{2,6},{3,7},{4,0},{5,1},{6,2},{7,3},{8,12},{9,13},{10,... | collective-permute-start | bytes 2457608 | tf_op jit(solution)/shard_map/d1/ppermute | solution.py:1014
  189.8 35.9 %collective-permute-start.39 = (bf16[1600,256]{1,0:T(8,128)(2,1)S(1)}, bf16[1600,256]{1,0:T(8,128)(2,1)}, u32[]{:S(2)}, u32[]{:S(2)}) collective-permute-start(bf16[1600,256]{1,0:T(8,128)(2,1)S(1)} %get-tuple-element.157), channel_id=1, source_target_pairs={{0,2},{1,3},{2,0},{3,1},{4,6},{5,7},{6,4},{7,5},{8,10},{9,11},{10,... | collective-permute-start | bytes 2457608 | tf_op jit(solution)/shard_map/e2/ppermute | solution.py:1014
  190.9 35.6 %collective-permute-start.38 = (bf16[1600,256]{1,0:T(8,128)(2,1)S(1)}, bf16[1600,256]{1,0:T(8,128)(2,1)}, u32[]{:S(2)}, u32[]{:S(2)}) collective-permute-start(bf16[1600,256]{1,0:T(8,128)(2,1)S(1)} %get-tuple-element.156), channel_id=1, source_target_pairs={{0,4},{1,5},{2,6},{3,7},{4,0},{5,1},{6,2},{7,3},{8,12},{9,13},{10,... | collective-permute-start | bytes 2457608 | tf_op jit(solution)/shard_map/e1/ppermute | solution.py:1014
  226.5 2.8 collective-permute-start.40
  226.6 21.4 %collective-permute-start.41 = (bf16[1600,256]{1,0:T(8,128)(2,1)}, bf16[1600,256]{1,0:T(8,128)(2,1)}, u32[]{:S(2)}, u32[]{:S(2)}) collective-permute-start(bf16[1600,256]{1,0:T(8,128)(2,1)} %fusion.2), channel_id=1, source_target_pairs={{0,2},{1,3},{2,0},{3,1},{4,6},{5,7},{6,4},{7,5},{8,10},{9,11},{10,... | collective-permute-start | bytes 2457608 | tf_op jit(solution)/shard_map/f1/ppermute | solution.py:1014
  227.7 21.4 %collective-permute-start.46 = (bf16[1600,256]{1,0:T(8,128)(2,1)}, bf16[1600,256]{1,0:T(8,128)(2,1)}, u32[]{:S(2)}, u32[]{:S(2)}) collective-permute-start(bf16[1600,256]{1,0:T(8,128)(2,1)} %fusion.1), channel_id=1, source_target_pairs={{0,4},{1,5},{2,6},{3,7},{4,0},{5,1},{6,2},{7,3},{8,12},{9,13},{10,... | collective-permute-start | bytes 2457608 | tf_op jit(solution)/shard_map/f2/ppermute | solution.py:1014
  235.3 30.5 %collective-permute-start.49 = (bf16[1600,256]{1,0:T(8,128)(2,1)}, bf16[1600,256]{1,0:T(8,128)(2,1)S(1)}, u32[]{:S(2)}, u32[]{:S(2)}) collective-permute-start(bf16[1600,256]{1,0:T(8,128)(2,1)} %get-tuple-element.227), channel_id=1, source_target_pairs={{0,4},{1,5},{2,6},{3,7},{4,0},{5,1},{6,2},{7,3},{8,12},{9,13},{10,... | collective-permute-start | bytes 2457608 | tf_op jit(solution)/shard_map/ry0/ppermute | solution.py:1014
  236.7 29.2 %collective-permute-start.50 = (bf16[1600,256]{1,0:T(8,128)(2,1)}, bf16[1600,256]{1,0:T(8,128)(2,1)}, u32[]{:S(2)}, u32[]{:S(2)}) collective-permute-start(bf16[1600,256]{1,0:T(8,128)(2,1)} %get-tuple-element.195), channel_id=1, source_target_pairs={{0,2},{1,3},{2,0},{3,1},{4,6},{5,7},{6,4},{7,5},{8,10},{9,11},{10,... | collective-permute-start | bytes 2457608 | tf_op jit(solution)/shard_map/d3/ppermute | solution.py:1014
  253.3 19.1 %collective-permute-start.47 = (bf16[1600,256]{1,0:T(8,128)(2,1)}, bf16[1600,256]{1,0:T(8,128)(2,1)S(1)}, u32[]{:S(2)}, u32[]{:S(2)}) collective-permute-start(bf16[1600,256]{1,0:T(8,128)(2,1)} %get-tuple-element.201), channel_id=1, source_target_pairs={{0,8},{1,9},{2,10},{3,11},{4,12},{5,13},{6,14},{7,15},{8,0},{9,1},... | collective-permute-start | bytes 2457608 | tf_op jit(solution)/shard_map/rz_inner1/ppermute | solution.py:1014
  253.5 29.2 %collective-permute-start.42 = (bf16[1600,256]{1,0:T(8,128)(2,1)}, bf16[1600,256]{1,0:T(8,128)(2,1)}, u32[]{:S(2)}, u32[]{:S(2)}) collective-permute-start(bf16[1600,256]{1,0:T(8,128)(2,1)} %get-tuple-element.184), channel_id=1, source_target_pairs={{0,2},{1,3},{2,0},{3,1},{4,6},{5,7},{6,4},{7,5},{8,10},{9,11},{10,... | collective-permute-start | bytes 2457608 | tf_op jit(solution)/shard_map/e3/ppermute | solution.py:1014
  269.1 20.0 %collective-permute-start.51 = (bf16[1600,256]{1,0:T(8,128)(2,1)}, bf16[1600,256]{1,0:T(8,128)(2,1)}, u32[]{:S(2)}, u32[]{:S(2)}) collective-permute-start(bf16[1600,256]{1,0:T(8,128)(2,1)} %fusion), channel_id=1, source_target_pairs={{0,4},{1,5},{2,6},{3,7},{4,0},{5,1},{6,2},{7,3},{8,12},{9,13},{10,... | collective-permute-start | bytes 2457608 | tf_op jit(solution)/shard_map/f3/ppermute | solution.py:1014
  272.6 20.3 %collective-permute-start.48 = (bf16[1600,256]{1,0:T(8,128)(2,1)S(1)}, bf16[1600,256]{1,0:T(8,128)(2,1)}, u32[]{:S(2)}, u32[]{:S(2)}) collective-permute-start(bf16[1600,256]{1,0:T(8,128)(2,1)S(1)} %add_convert_fusion.1.inner), channel_id=1, source_target_pairs={{0,16},{1,17},{2,18},{3,19},{4,20},{5,21},{6,22},{7,23},{24,8},{25... | collective-permute-start | bytes 2457608 | tf_op jit(solution)/shard_map/rz_inner2/ppermute | solution.py:1014
  292.9 18.9 %collective-permute-start.52 = (bf16[1600,256]{1,0:T(8,128)(2,1)}, bf16[1600,256]{1,0:T(8,128)(2,1)}, u32[]{:S(2)}, u32[]{:S(2)}) collective-permute-start(bf16[1600,256]{1,0:T(8,128)(2,1)} %get-tuple-element.206), channel_id=1, source_target_pairs={{0,8},{1,9},{2,10},{3,11},{4,12},{5,13},{6,14},{7,15},{8,0},{9,1},... | collective-permute-start | bytes 2457608 | tf_op jit(solution)/shard_map/rz_outer1/ppermute | solution.py:1014
  294.2 20.4 %collective-permute-start.44 = (f32[2,32,256]{2,1,0:T(8,128)S(1)}, f32[2,32,256]{2,1,0:T(8,128)S(1)}, u32[]{:S(2)}, u32[]{:S(2)}) collective-permute-start(f32[2,32,256]{2,1,0:T(8,128)S(1)} %select_bitcast_fusion), channel_id=1, source_target_pairs={{0,1},{1,0},{2,3},{3,2},{4,5},{5,4},{6,7},{7,6},{8,9},{9,8},{10,11... | collective-permute-start | bytes 196616 | tf_op jit(solution)/shard_map/vec_c/ppermute | solution.py:1014
  295.5 23.1 %collective-permute-start.43 = (bf16[256,1024]{1,0:T(8,128)(2,1)S(1)}, bf16[256,1024]{1,0:T(8,128)(2,1)S(1)}, u32[]{:S(2)}, u32[]{:S(2)}) collective-permute-start(bf16[256,1024]{1,0:T(8,128)(2,1)S(1)} %fusion.11), channel_id=1, source_target_pairs={{0,2},{1,3},{2,0},{3,1},{4,6},{5,7},{6,4},{7,5},{8,10},{9,11},{10,... | collective-permute-start | bytes 1572872 | tf_op jit(solution)/shard_map/in_x/ppermute | solution.py:1014
  313.2 20.6 %collective-permute-start.53 = (bf16[1600,256]{1,0:T(8,128)(2,1)S(1)}, bf16[1600,256]{1,0:T(8,128)(2,1)}, u32[]{:S(2)}, u32[]{:S(2)}) collective-permute-start(bf16[1600,256]{1,0:T(8,128)(2,1)S(1)} %add_convert_fusion.outer), channel_id=1, source_target_pairs={{8,24},{9,25},{10,26},{11,27},{12,28},{13,29},{14,30},{15,31},{16,... | collective-permute-start | bytes 2457608 | tf_op jit(solution)/shard_map/rz_outer2/ppermute | solution.py:1014
  314.6 4.0 %collective-permute-start.45 = (f32[32,256]{1,0:T(8,128)S(1)}, f32[32,256]{1,0:T(8,128)S(1)}, u32[]{:S(2)}, u32[]{:S(2)}) collective-permute-start(f32[32,256]{1,0:T(8,128)S(1)} %select_bitcast_fusion.1), channel_id=1, source_target_pairs={{0,2},{1,3},{2,0},{3,1},{4,6},{5,7},{6,4},{7,5},{8,10},{9,11},{10,... | collective-permute-start | bytes 98312 | tf_op jit(solution)/shard_map/vec_x/ppermute | solution.py:1014
  338.5 4.2 %collective-permute-start.54 = (f32[40,256]{1,0:T(8,128)S(1)}, f32[40,256]{1,0:T(8,128)S(1)}, u32[]{:S(2)}, u32[]{:S(2)}) collective-permute-start(f32[40,256]{1,0:T(8,128)S(1)} %pad_maximum_fusion.1), channel_id=1, source_target_pairs={{0,4},{1,5},{2,6},{3,7},{4,0},{5,1},{6,2},{7,3},{8,12},{9,13},{10,... | collective-permute-start | bytes 122888 | tf_op jit(solution)/shard_map/norm/ppermute | solution.py:1014
  343.4 7.6 %collective-permute-start.55 = (f32[40,256]{1,0:T(8,128)S(1)}, f32[40,256]{1,0:T(8,128)S(1)}, u32[]{:S(2)}, u32[]{:S(2)}) collective-permute-start(f32[40,256]{1,0:T(8,128)S(1)} %fusion.18), channel_id=1, source_target_pairs={{0,8},{1,9},{2,10},{3,11},{4,12},{5,13},{6,14},{7,15},{8,0},{9,1},... | collective-permute-start | bytes 122888 | tf_op jit(solution)/shard_map/norm/ppermute | solution.py:1014
  343.4 7.6 %collective-permute-start.56 = (f32[40,256]{1,0:T(8,128)S(1)}, f32[40,256]{1,0:T(8,128)S(1)}, u32[]{:S(2)}, u32[]{:S(2)}) collective-permute-start(f32[40,256]{1,0:T(8,128)S(1)} %fusion.18), channel_id=1, source_target_pairs={{0,16},{1,17},{2,18},{3,19},{4,20},{5,21},{6,22},{7,23},{8,24},{9,... | collective-permute-start | bytes 122888 | tf_op jit(solution)/shard_map/norm/ppermute | solution.py:1014
  345.2 5.8 %collective-permute-start.57 = (f32[40,256]{1,0:T(8,128)S(1)}, f32[40,256]{1,0:T(8,128)S(1)}, u32[]{:S(2)}, u32[]{:S(2)}) collective-permute-start(f32[40,256]{1,0:T(8,128)S(1)} %fusion.18), channel_id=1, source_target_pairs={{0,24},{1,25},{2,26},{3,27},{4,28},{5,29},{6,30},{7,31},{8,16},{9,... | collective-permute-start | bytes 122888 | tf_op jit(solution)/shard_map/norm/ppermute | solution.py:1014
  352.3 3.8 %collective-permute-start.60 = (f32[8,128]{1,0:T(8,128)S(1)}, f32[8,128]{1,0:T(8,128)S(1)}, u32[]{:S(2)}, u32[]{:S(2)}) collective-permute-start(f32[8,128]{1,0:T(8,128)S(1)} %broadcast_in_dim.61), channel_id=1, source_target_pairs={{0,3},{1,2},{2,1},{3,0},{4,7},{5,6},{6,5},{7,4},{8,11},{9,10},{10,... | collective-permute-start | bytes 12296 | tf_op jit(solution)/shard_map/norm/ppermute | solution.py:1014
  352.4 3.7 %collective-permute-start.58 = (f32[8,128]{1,0:T(8,128)S(1)}, f32[8,128]{1,0:T(8,128)S(1)}, u32[]{:S(2)}, u32[]{:S(2)}) collective-permute-start(f32[8,128]{1,0:T(8,128)S(1)} %broadcast_in_dim.61), channel_id=1, source_target_pairs={{0,1},{1,0},{2,3},{3,2},{4,5},{5,4},{6,7},{7,6},{8,9},{9,8},{10,11... | collective-permute-start | bytes 12296 | tf_op jit(solution)/shard_map/norm/ppermute | solution.py:1014
  353.4 3.6 collective-permute-start.59
  (53 other events, 523.8 us)

commit v6 on v5

--- a/solution.py
+++ b/solution.py
@@ -591,7 +591,7 @@
         slope[pl.ds(pl.multiple_of(g * 256, 256), 256), :] = bend.T
         return 0
 
-    lax.fori_loop(0, 16, up, 0, unroll=8)
+    lax.fori_loop(0, 16, up, 0, unroll=16)
     arrived([w_down] + [edge_down], 2)
     for n, row in enumerate((1024, 2560)):
         w_down[row : row + 16, :] = w_down[row : row + 16, :] + edge_down[n]

time: 372 us -> 371 us (level)
  no operation moved by 1% of the time
where the time goes in v6:
time: 371 us; the launch traced here: 366 us
  waiting for transfers between devices  167 us (45%)
  Pallas kernels  70.8 us (19%)
  starting transfers between devices  65.1 us (18%)
  other arithmetic  38.5 us (10%)
  local copies, waits for them, and re-layouts  14 us (4%)
  between operations  5.88 us (2%)
  matrix products  4.1 us (1%)
    ppermute x61, waiting for transfers between devices, send(): return lax.ppermute(values, AXES, pairs)  167 us
    ppermute x61, starting transfers between devices, send(): return lax.ppermute(values, AXES, pairs)  65.1 us
    pallas_call x1, Pallas kernels, layer(): pl.pallas_call(layer_kernel, out_shape=(struct((256, D)), struct((256, D)...  28 us
    convert_element_type x10, other arithmetic, low(): return values.astype(jnp.bfloat16)  17.4 us
    pallas_call x1, Pallas kernels, attend_back(): pl.pallas_call(attend_back_kernel, out_shape=(square, square, square, str...  15.9 us
    pallas_call x1, Pallas kernels, attend(): pl.pallas_call(attend_kernel, out_shape=(struct((4, 256, 1024)), struct((...  14.6 us
    pallas_call x2, Pallas kernels, combine(): pl.pallas_call(partial(combine_kernel, len(first)), grid=(blocks,), out_s...  7.82 us
  transfers between devices with their start and end apart: 61, of which 36 were waited for; matrix products, arithmetic and copies ran while one was open for 10% of the time, Pallas kernels for 10%

profile of v6, /device:TPU:0, one launch (start us, length us, event | category | flops | bytes accessed | tf_op | source)
XLA Modules:
  0.0 365.6 jit_solution(10659439713061395924)
XLA Ops:
  2.3 3.0 collective-permute-start
  5.3 1.5 pad_bitcast_fusion.flat
  9.2 3.4 collective-permute-start.2
  12.6 1.9 collective-permute-start.7
  14.4 1.5 collective-permute-start.4
  16.6 14.1 %collective-permute-done.2.p2.refs_1_ = bf16[1600,256]{1,0:T(8,128)(2,1)S(1)} collective-permute-done((bf16[1600,256]{1,0:T(8,128)(2,1)S(1)}, bf16[1600,256]{1,0:T(8,128)(2,1)S(1)}, u32[]{:S(2)}, u32[]{:S(2)}) %collective-permute-start.2) | collective-permute-done | bytes 819232 | tf_op jit(solution)/shard_map/first/ppermute | solution.py:1014
  30.8 2.4 collective-permute-done.7.p1.refs_4_
  33.2 1.7 collective-permute-start.8
  36.1 1.6 collective-permute-start.3
  38.6 3.4 collective-permute-start.13
  42.8 10.2 %collective-permute-done.8.p3.refs_5_ = bf16[1600,256]{1,0:T(8,128)(2,1)} collective-permute-done((bf16[1600,256]{1,0:T(8,128)(2,1)S(1)}, bf16[1600,256]{1,0:T(8,128)(2,1)}, u32[]{:S(2)}, u32[]{:S(2)}) %collective-permute-start.8) | collective-permute-done | bytes 819232 | tf_op jit(solution)/shard_map/y1/ppermute | solution.py:1014
  53.0 2.5 collective-permute-done.5.p4.refs_2_
  58.4 1.6 collective-permute-start.14
  61.8 14.9 %collective-permute-done.6 = bf16[1600,256]{1,0:T(8,128)(2,1)S(1)} collective-permute-done((bf16[1600,256]{1,0:T(8,128)(2,1)}, bf16[1600,256]{1,0:T(8,128)(2,1)S(1)}, u32[]{:S(2)}, u32[]{:S(2)}) %collective-permute-start.6) | collective-permute-done | bytes 819232 | tf_op jit(solution)/shard_map/third/ppermute | solution.py:1014
  77.9 1.5 collective-permute-start.17
  82.2 2.4 collective-permute-start.16
  84.7 14.6 %attend.1 = (bf16[4,256,1024]{2,1,0:T(8,128)(2,1)}, bf16[3,1024,256]{2,1,0:T(8,128)(2,1)}, bf16[1024,256]{1,0:T(8,128)(2,1)S(1)}, bf16[1024,256]{1,0:T(8,128)(2,...) custom-call(s32[6]{0:T(128)S(1)} %stack.19.place, ...), custom_call_target="tpu_custom_call" | custom-call | flops 16000000000 | bytes 24000000 | tf_op jit(solution)/shard_map/attend/pallas_call | solution.py:369
  103.1 8.8 %collective-permute-done.18.refs_11_ = bf16[1600,256]{1,0:T(8,128)(2,1)S(1)} collective-permute-done((bf16[1600,256]{1,0:T(8,128)(2,1)S(1)}, bf16[1600,256]{1,0:T(8,128)(2,1)S(1)}, u32[]{:S(2)}, u32[]{:S(2)}) %collective-permute-start.18) | collective-permute-done | bytes 819232 | tf_op jit(solution)/shard_map/yb/ppermute | solution.py:1014
  112.7 1.6 collective-permute-start.22
  114.4 2.2 collective-permute-start.27
  116.9 8.0 %collective-permute-done.19.h1 = bf16[256,256]{1,0:T(8,128)(2,1)S(1)} collective-permute-done((bf16[256,256]{1,0:T(8,128)(2,1)S(1)}, bf16[256,256]{1,0:T(8,128)(2,1)S(1)}, u32[]{:S(2)}, u32[]{:S(2)}) %collective-permute-start.19) | collective-permute-done | bytes 131104 | tf_op jit(solution)/shard_map/heads/ppermute | solution.py:1014
  125.4 8.4 %collective-permute-done.22.refs_14_ = bf16[1600,256]{1,0:T(8,128)(2,1)S(1)} collective-permute-done((bf16[1600,256]{1,0:T(8,128)(2,1)S(1)}, bf16[1600,256]{1,0:T(8,128)(2,1)S(1)}, u32[]{:S(2)}, u32[]{:S(2)}) %collective-permute-start.22) | collective-permute-done | bytes 819232 | tf_op jit(solution)/shard_map/yx3/ppermute | solution.py:1014
  134.9 1.3 collective-permute-done.20.h2
  136.2 3.4 collective-permute-done.21.h3
  142.1 2.3 collective-permute-done.24.refs_16_
  146.3 28.0 %layer.1 = (bf16[256,1024]{1,0:T(8,128)(2,1)}, f32[256,1024]{1,0:T(8,128)}, bf16[256,256]{1,0:T(8,128)(2,1)}, bf16[256,256]{1,0:T(8,128)(2,1)}, bf16[256,256]{1,...) custom-call(s32[6]{0:T(128)} %copy-done.1, ...), custom_call_target="tpu_custom_call" | custom-call | flops 15000000512 | bytes 40000000 | tf_op jit(solution)/shard_map/layer/pallas_call | solution.py:708
  176.7 3.7 %collective-permute-done.34.refs_1_ = bf16[2,2,1600,256]{3,2,1,0:T(8,128)(2,1)S(1)} collective-permute-done((bf16[2,2,1600,256]{3,2,1,0:T(8,128)(2,1)}, bf16[2,2,1600,256]{3,2,1,0:T(8,128)(2,1)S(1)}, u32[]{:S(2)}, u32[]{:S(2)}) %collective-permute-start.34) | collective-permute-done | bytes 3276832 | tf_op jit(solution)/shard_map/rc2/ppermute | solution.py:1014
  180.4 3.0 fusion.8
  183.4 1.8 collective-permute-done.31.g1
  185.5 1.3 fusion.7
  187.7 1.4 collective-permute-start.35
  191.0 15.9 %attend_back.1 = (bf16[1024,256]{1,0:T(8,128)(2,1)S(1)}, bf16[1024,256]{1,0:T(8,128)(2,1)S(1)}, bf16[1024,256]{1,0:T(8,128)(2,1)S(1)}, f32[2,256,1024]{2,1,0:T(8...) custom-call(s32[6]{0:T(128)S(1)} %copy-done.2, bf16[1024,256]{1,0:T(8,128)(2,1)S(1)} %copy-done.12, ...), custom_call_target="tpu_custom_call" | custom-call | flops 20000000000 | bytes 12000000 | tf_op jit(solution)/shard_map/attend_back/pallas_call | solution.py:460
  209.2 2.6 fusion.1
  211.8 2.5 fusion.2
  214.3 2.0 fusion.10
  216.6 8.4 %collective-permute-done.39.refs_2_ = bf16[1600,256]{1,0:T(8,128)(2,1)} collective-permute-done((bf16[1600,256]{1,0:T(8,128)(2,1)S(1)}, bf16[1600,256]{1,0:T(8,128)(2,1)}, u32[]{:S(2)}, u32[]{:S(2)}) %collective-permute-start.39) | collective-permute-done | bytes 819232 | tf_op jit(solution)/shard_map/e2/ppermute | solution.py:1014
  227.1 1.4 collective-permute-start.46
  228.6 2.6 convolution_convert_fusion.2
  233.1 1.8 broadcast_select_fusion
  234.9 1.4 collective-permute-start.49
  237.4 9.8 %collective-permute-done.41.refs_7_ = bf16[1600,256]{1,0:T(8,128)(2,1)} collective-permute-done((bf16[1600,256]{1,0:T(8,128)(2,1)}, bf16[1600,256]{1,0:T(8,128)(2,1)}, u32[]{:S(2)}, u32[]{:S(2)}) %collective-permute-start.41) | collective-permute-done | bytes 819232 | tf_op jit(solution)/shard_map/f1/ppermute | solution.py:1014
  248.5 4.2 %combine.2 = (bf16[1600,256]{1,0:T(8,128)(2,1)}, bf16[1600,256]{1,0:T(8,128)(2,1)}) custom-call(s32[6]{0:T(128)} %copy-done.1, bf16[2,2,1600,256]{3,2,1,0:T(8,128)(2,1)} %get-tuple-element.153.refs_0_, bf16[2,2,1600,256]{3,2,1,0:T(8,128)(2,1)} %copy-done.24, bf16[1600,256]{1,0:T(8,128)(2,1)} %collective-permute-done.39.refs_2_, ...), custom_call_target="tpu_custom_call" | custom-call | tf_op jit(solution)/shard_map/combine/pallas_call | solution.py:257
  253.7 11.5 %collective-permute-done.49.refs_1_ = bf16[1600,256]{1,0:T(8,128)(2,1)S(1)} collective-permute-done((bf16[1600,256]{1,0:T(8,128)(2,1)}, bf16[1600,256]{1,0:T(8,128)(2,1)S(1)}, u32[]{:S(2)}, u32[]{:S(2)}) %collective-permute-start.49) | collective-permute-done | bytes 819232 | tf_op jit(solution)/shard_map/ry0/ppermute | solution.py:1014
  265.2 3.2 fusion
  268.4 1.4 collective-permute-start.51
  269.8 1.9 collective-permute-done.47
  272.0 5.3 %collective-permute-start.48 = (bf16[1600,256]{1,0:T(8,128)(2,1)S(1)}, bf16[1600,256]{1,0:T(8,128)(2,1)}, u32[]{:S(2)}, u32[]{:S(2)}) collective-permute-start(bf16[1600,256]{1,0:T(8,128)(2,1)S(1)} %add_convert_fusion.1.inner), channel_id=1, source_target_pairs={{0,16},{1,17},{2,18},{3,19},{4,20},{5,21},{6,22},{7,23},{24,8},{25... | collective-permute-start | bytes 2457608 | tf_op jit(solution)/shard_map/rz_inner2/ppermute | solution.py:1014
  278.6 3.4 collective-permute-done.42.refs_4_
  282.0 6.4 %collective-permute-done.51.refs_5_ = bf16[1600,256]{1,0:T(8,128)(2,1)} collective-permute-done((bf16[1600,256]{1,0:T(8,128)(2,1)}, bf16[1600,256]{1,0:T(8,128)(2,1)}, u32[]{:S(2)}, u32[]{:S(2)}) %collective-permute-start.51) | collective-permute-done | bytes 819232 | tf_op jit(solution)/shard_map/f3/ppermute | solution.py:1014
  288.4 3.6 combine.3
  295.8 15.4 %collective-permute-done.52 = bf16[1600,256]{1,0:T(8,128)(2,1)} collective-permute-done((bf16[1600,256]{1,0:T(8,128)(2,1)}, bf16[1600,256]{1,0:T(8,128)(2,1)}, u32[]{:S(2)}, u32[]{:S(2)}) %collective-permute-start.52) | collective-permute-done | bytes 819232 | tf_op jit(solution)/shard_map/rz_outer1/ppermute | solution.py:1014
  311.2 1.4 add_convert_fusion.outer
  312.6 1.3 collective-permute-start.53
  314.9 3.0 collective-permute-done.45
  317.9 2.3 fusion.4
  320.3 12.9 %collective-permute-done.53.outer_last = bf16[1600,256]{1,0:T(8,128)(2,1)} collective-permute-done((bf16[1600,256]{1,0:T(8,128)(2,1)S(1)}, bf16[1600,256]{1,0:T(8,128)(2,1)}, u32[]{:S(2)}, u32[]{:S(2)}) %collective-permute-start.53) | collective-permute-done | bytes 819232 | tf_op jit(solution)/shard_map/rz_outer2/ppermute | solution.py:1014
  333.2 3.7 %unpack.1 = (f32[3080,128]{1,0:T(8,128)}, f32[8,256]{1,0:T(8,128)}) custom-call(s32[6]{0:T(128)} %copy-done.1, bf16[1600,256]{1,0:T(8,128)(2,1)} %copy-done.27, bf16[1600,256]{1,0:T(8,128)(2,1)} %collective-permute-done.48.inner_last, bf16[1600,256]{1,0:T(8,128)(2,1)} %copy-done.28, bf16[1600,256]{1,0:T(8,128)(2,1)} %collective-permute-done.53.outer_last), custom_call_target="tpu_custom_call" | custom-call | tf_op jit(solution)/shard_map/unpack/pallas_call | solution.py:222
  337.6 2.2 collective-permute-start.54
  339.8 2.0 collective-permute-done.54
  342.5 1.7 collective-permute-start.56
  344.3 2.6 collective-permute-start.57
  347.7 2.4 collective-permute-done.57
  353.6 1.5 fusion.17
  358.0 6.0 %multiply_add_fusion = (f32[393664]{0:T(1024)}, f32[393664]{0:T(1024)}, f32[393664]{0:T(1024)}, f32[393664]{0:T(1024)}) fusion(f32[393664]{0:T(1024)S(1)} %copy-done.29, f32[393664]{0:T(1024)S(1)} %copy-done.26, f32[]{:T(128)S(6)} %div.48, f32[394240]{0:T(1024)} %fusion.17, f32[393664]{0:T(1024)} %param.13, f32[393664]{0:T(1024)} %param.12), kind=kLoop, calls=%fused_computation.17 | loop fusion | flops 7479616 | bytes 14171908 | tf_op jit(solution)/shard_map/add | solution.py:1287
  (265 shorter events, 54.6 us)
Async XLA Ops:
  2.3 4.6 %collective-permute-start = (bf16[16,256]{1,0:T(8,128)(2,1)S(1)}, bf16[16,256]{1,0:T(8,128)(2,1)S(1)}, u32[]{:S(2)}, u32[]{:S(2)}) collective-permute-start(bf16[16,256]{1,0:T(8,128)(2,1)S(1)} %select_convert_fusion), channel_id=1, source_target_pairs={{0,2},{1,3},{2,0},{3,1},{4,6},{5,7},{6,4},{7,5},{8,10},{9,11},{10,... | collective-permute-start | bytes 24584 | tf_op jit(solution)/shard_map/tail_x/ppermute | solution.py:1014
  6.9 1.4 collective-permute-start.1
  8.3 76.3 %copy-start.1 = (s32[6]{0:T(128)}, s32[6]{0:T(128)S(1)}, u32[]{:S(2)}) copy-start(s32[6]{0:T(128)S(1)} %stack.19.place) | copy-start | bytes 76
  9.2 75.5 %copy-start = (bf16[1600,256]{1,0:T(8,128)(2,1)}, bf16[1600,256]{1,0:T(8,128)(2,1)S(1)}, u32[]{:S(2)}) copy-start(bf16[1600,256]{1,0:T(8,128)(2,1)S(1)} %pack.1.p0.refs_0_) | copy-start | bytes 2457604
  9.2 21.5 %collective-permute-start.2 = (bf16[1600,256]{1,0:T(8,128)(2,1)S(1)}, bf16[1600,256]{1,0:T(8,128)(2,1)S(1)}, u32[]{:S(2)}, u32[]{:S(2)}) collective-permute-start(bf16[1600,256]{1,0:T(8,128)(2,1)S(1)} %pack.1.p0.refs_0_), channel_id=1, source_target_pairs={{0,16},{1,17},{2,18},{3,19},{4,20},{5,21},{6,22},{7,23},{8,0},{9,1... | collective-permute-start | bytes 2457608 | tf_op jit(solution)/shard_map/first/ppermute | solution.py:1014
  12.6 20.6 %collective-permute-start.7 = (bf16[1600,256]{1,0:T(8,128)(2,1)S(1)}, bf16[1600,256]{1,0:T(8,128)(2,1)}, u32[]{:S(2)}, u32[]{:S(2)}) collective-permute-start(bf16[1600,256]{1,0:T(8,128)(2,1)S(1)} %pack.1.p0.refs_0_), channel_id=1, source_target_pairs={{0,4},{1,5},{2,6},{3,7},{4,0},{5,1},{6,2},{7,3},{8,12},{9,13},{10,... | collective-permute-start | bytes 2457608 | tf_op jit(solution)/shard_map/y0/ppermute | solution.py:1014
  14.4 21.5 %collective-permute-start.4 = (bf16[256,1024]{1,0:T(8,128)(2,1)S(1)}, bf16[256,1024]{1,0:T(8,128)(2,1)S(1)}, u32[]{:S(2)}, u32[]{:S(2)}) collective-permute-start(bf16[256,1024]{1,0:T(8,128)(2,1)S(1)} %copy-done.4), channel_id=1, source_target_pairs={{0,2},{1,3},{2,0},{3,1},{4,6},{5,7},{6,4},{7,5},{8,10},{9,11},{10,... | collective-permute-start | bytes 1572872 | tf_op jit(solution)/shard_map/tok_x/ppermute | solution.py:1014
  15.9 21.8 %collective-permute-start.12 = (bf16[1600,256]{1,0:T(8,128)(2,1)S(1)}, bf16[1600,256]{1,0:T(8,128)(2,1)S(1)}, u32[]{:S(2)}, u32[]{:S(2)}) collective-permute-start(bf16[1600,256]{1,0:T(8,128)(2,1)S(1)} %pack.1.p0.refs_0_), channel_id=1, source_target_pairs={{8,10},{9,11},{10,8},{11,9},{12,14},{13,15},{14,12},{15,13},{16,18... | collective-permute-start | bytes 2457608 | tf_op jit(solution)/shard_map/x0/ppermute | solution.py:1014
  30.8 48.6 %copy-start.31 = (bf16[1600,256]{1,0:T(8,128)(2,1)}, bf16[1600,256]{1,0:T(8,128)(2,1)S(1)}, u32[]{:S(2)}) copy-start(bf16[1600,256]{1,0:T(8,128)(2,1)S(1)} %collective-permute-done.2.p2.refs_1_) | copy-start | bytes 2457604
  33.2 19.8 %collective-permute-start.8 = (bf16[1600,256]{1,0:T(8,128)(2,1)S(1)}, bf16[1600,256]{1,0:T(8,128)(2,1)}, u32[]{:S(2)}, u32[]{:S(2)}) collective-permute-start(bf16[1600,256]{1,0:T(8,128)(2,1)S(1)} %collective-permute-done.2.p2.refs_1_), channel_id=1, source_target_pairs={{0,4},{1,5},{2,6},{3,7},{4,0},{5,1},{6,2},{7,3},{8,12},{9,13},{10,... | collective-permute-start | bytes 2457608 | tf_op jit(solution)/shard_map/y1/ppermute | solution.py:1014
  35.9 19.6 %collective-permute-start.5 = (bf16[1600,256]{1,0:T(8,128)(2,1)}, bf16[1600,256]{1,0:T(8,128)(2,1)}, u32[]{:S(2)}, u32[]{:S(2)}) collective-permute-start(bf16[1600,256]{1,0:T(8,128)(2,1)} %broadcast_select_fusion.5), channel_id=1, source_target_pairs={{0,8},{1,9},{2,10},{3,11},{4,12},{5,13},{6,14},{7,15},{8,0},{9,1},... | collective-permute-start | bytes 2457608 | tf_op jit(solution)/shard_map/second/ppermute | solution.py:1014
  36.1 19.8 %collective-permute-start.3 = (bf16[1600,256]{1,0:T(8,128)(2,1)S(1)}, bf16[1600,256]{1,0:T(8,128)(2,1)}, u32[]{:S(2)}, u32[]{:S(2)}) collective-permute-start(bf16[1600,256]{1,0:T(8,128)(2,1)S(1)} %pack.1.p0.refs_0_), channel_id=1, source_target_pairs={{8,16},{9,17},{10,18},{11,19},{12,20},{13,21},{14,22},{15,23},{16,... | collective-permute-start | bytes 2457608 | tf_op jit(solution)/shard_map/crossed/ppermute | solution.py:1014
  38.6 21.9 %collective-permute-start.13 = (bf16[1600,256]{1,0:T(8,128)(2,1)S(1)}, bf16[1600,256]{1,0:T(8,128)(2,1)}, u32[]{:S(2)}, u32[]{:S(2)}) collective-permute-start(bf16[1600,256]{1,0:T(8,128)(2,1)S(1)} %collective-permute-done.2.p2.refs_1_), channel_id=1, source_target_pairs={{0,2},{1,3},{2,0},{3,1},{4,6},{5,7},{6,4},{7,5},{8,10},{9,11},{10,... | collective-permute-start | bytes 2457608 | tf_op jit(solution)/shard_map/x1/ppermute | solution.py:1014
  42.0 38.4 %collective-permute-start.10 = (bf16[256,1024]{1,0:T(8,128)(2,1)S(1)}, bf16[256,1024]{1,0:T(8,128)(2,1)S(1)}, u32[]{:S(2)}, u32[]{:S(2)}) collective-permute-start(bf16[256,1024]{1,0:T(8,128)(2,1)S(1)} %copy-done.4), channel_id=1, source_target_pairs={{0,1},{1,0},{2,3},{3,2},{4,5},{5,4},{6,7},{7,6},{8,9},{9,8},{10,11... | collective-permute-start | bytes 1572872 | tf_op jit(solution)/shard_map/tok_c/ppermute | solution.py:1014
  55.5 21.4 %collective-permute-start.9 = (bf16[1600,256]{1,0:T(8,128)(2,1)}, bf16[1600,256]{1,0:T(8,128)(2,1)S(1)}, u32[]{:S(2)}, u32[]{:S(2)}) collective-permute-start(bf16[1600,256]{1,0:T(8,128)(2,1)} %collective-permute-done.5.p4.refs_2_), channel_id=1, source_target_pairs={{0,4},{1,5},{2,6},{3,7},{4,0},{5,1},{6,2},{7,3},{8,12},{9,13},{10,... | collective-permute-start | bytes 2457608 | tf_op jit(solution)/shard_map/y2/ppermute | solution.py:1014
  55.9 20.8 %collective-permute-start.6 = (bf16[1600,256]{1,0:T(8,128)(2,1)}, bf16[1600,256]{1,0:T(8,128)(2,1)S(1)}, u32[]{:S(2)}, u32[]{:S(2)}) collective-permute-start(bf16[1600,256]{1,0:T(8,128)(2,1)} %collective-permute-done.3), channel_id=1, source_target_pairs={{8,0},{9,1},{10,2},{11,3},{12,4},{13,5},{14,6},{15,7},{16,24},{17,... | collective-permute-start | bytes 2457608 | tf_op jit(solution)/shard_map/third/ppermute | solution.py:1014
  58.4 44.7 %collective-permute-start.14 = (bf16[1600,256]{1,0:T(8,128)(2,1)S(1)}, bf16[1600,256]{1,0:T(8,128)(2,1)S(1)}, u32[]{:S(2)}, u32[]{:S(2)}) collective-permute-start(bf16[1600,256]{1,0:T(8,128)(2,1)S(1)} %broadcast_select_fusion.3), channel_id=1, source_target_pairs={{0,2},{1,3},{2,0},{3,1},{4,6},{5,7},{6,4},{7,5},{8,10},{9,11},{10,... | collective-permute-start | bytes 2457608 | tf_op jit(solution)/shard_map/xa/ppermute | solution.py:1014
  76.9 35.7 %collective-permute-start.15 = (bf16[1600,256]{1,0:T(8,128)(2,1)S(1)}, bf16[1600,256]{1,0:T(8,128)(2,1)S(1)}, u32[]{:S(2)}, u32[]{:S(2)}) collective-permute-start(bf16[1600,256]{1,0:T(8,128)(2,1)S(1)} %broadcast_select_fusion.4.p6.refs_3_), channel_id=1, source_target_pairs={{0,4},{1,5},{2,6},{3,7},{4,0},{5,1},{6,2},{7,3},{8,12},{9,13},{10,... | collective-permute-start | bytes 2457608 | tf_op jit(solution)/shard_map/y3/ppermute | solution.py:1014
  77.9 34.7 %collective-permute-start.17 = (bf16[1600,256]{1,0:T(8,128)(2,1)S(1)}, bf16[1600,256]{1,0:T(8,128)(2,1)}, u32[]{:S(2)}, u32[]{:S(2)}) collective-permute-start(bf16[1600,256]{1,0:T(8,128)(2,1)S(1)} %broadcast_select_fusion.4.p6.refs_3_), channel_id=1, source_target_pairs={{0,2},{1,3},{2,0},{3,1},{4,6},{5,7},{6,4},{7,5},{8,10},{9,11},{10,... | collective-permute-start | bytes 2457608 | tf_op jit(solution)/shard_map/x3/ppermute | solution.py:1014
  80.2 2.0 collective-permute-start.11
  80.4 31.5 %collective-permute-start.18 = (bf16[1600,256]{1,0:T(8,128)(2,1)S(1)}, bf16[1600,256]{1,0:T(8,128)(2,1)S(1)}, u32[]{:S(2)}, u32[]{:S(2)}) collective-permute-start(bf16[1600,256]{1,0:T(8,128)(2,1)S(1)} %broadcast_select_fusion.2), channel_id=1, source_target_pairs={{0,4},{1,5},{2,6},{3,7},{4,0},{5,1},{6,2},{7,3},{8,12},{9,13},{10,... | collective-permute-start | bytes 2457608 | tf_op jit(solution)/shard_map/yb/ppermute | solution.py:1014
  82.2 30.4 %collective-permute-start.16 = (bf16[1600,256]{1,0:T(8,128)(2,1)S(1)}, bf16[1600,256]{1,0:T(8,128)(2,1)}, u32[]{:S(2)}, u32[]{:S(2)}) collective-permute-start(bf16[1600,256]{1,0:T(8,128)(2,1)S(1)} %collective-permute-done.9.p5.refs_6_), channel_id=1, source_target_pairs={{0,2},{1,3},{2,0},{3,1},{4,6},{5,7},{6,4},{7,5},{16,18},{17,19},{1... | collective-permute-start | bytes 2457608 | tf_op jit(solution)/shard_map/yx2/ppermute | solution.py:1014
  112.6 33.6 %collective-permute-start.23 = (bf16[9,1600,256]{2,1,0:T(8,128)(2,1)}, bf16[9,1600,256]{2,1,0:T(8,128)(2,1)}, u32[]{:S(2)}, u32[]{:S(2)}) collective-permute-start(bf16[9,1600,256]{2,1,0:T(8,128)(2,1)} %get-tuple-element.136), channel_id=1, source_target_pairs={{0,1},{1,0},{2,3},{3,2},{4,5},{5,4},{6,7},{7,6},{8,9},{9,8},{10,11... | collective-permute-start | bytes 22118408 | tf_op jit(solution)/shard_map/stack/ppermute | solution.py:1014
  112.7 21.1 %collective-permute-start.22 = (bf16[1600,256]{1,0:T(8,128)(2,1)S(1)}, bf16[1600,256]{1,0:T(8,128)(2,1)S(1)}, u32[]{:S(2)}, u32[]{:S(2)}) collective-permute-start(bf16[1600,256]{1,0:T(8,128)(2,1)S(1)} %collective-permute-done.15.refs_10_), channel_id=1, source_target_pairs={{0,2},{1,3},{2,0},{3,1},{4,6},{5,7},{6,4},{7,5},{8,10},{9,11},{10,... | collective-permute-start | bytes 2457608 | tf_op jit(solution)/shard_map/yx3/ppermute | solution.py:1014
  114.2 25.4 %collective-permute-start.28 = (bf16[1600,256]{1,0:T(8,128)(2,1)}, bf16[1600,256]{1,0:T(8,128)(2,1)S(1)}, u32[]{:S(2)}, u32[]{:S(2)}) collective-permute-start(bf16[1600,256]{1,0:T(8,128)(2,1)} %collective-permute-done.17.refs_13_), channel_id=1, source_target_pairs={{0,1},{1,0},{2,3},{3,2},{4,5},{5,4},{6,7},{7,6},{8,9},{9,8},{10,11... | collective-permute-start | bytes 2457608 | tf_op jit(solution)/shard_map/cx3/ppermute | solution.py:1014
  114.4 25.7 %collective-permute-start.27 = (bf16[1600,256]{1,0:T(8,128)(2,1)}, bf16[1600,256]{1,0:T(8,128)(2,1)}, u32[]{:S(2)}, u32[]{:S(2)}) collective-permute-start(bf16[1600,256]{1,0:T(8,128)(2,1)} %collective-permute-done.16.refs_12_), channel_id=1, source_target_pairs={{0,1},{1,0},{2,3},{3,2},{4,5},{5,4},{6,7},{7,6},{16,17},{17,16},{1... | collective-permute-start | bytes 2457608 | tf_op jit(solution)/shard_map/cyx2/ppermute | solution.py:1014
  116.7 8.3 %collective-permute-start.19 = (bf16[256,256]{1,0:T(8,128)(2,1)S(1)}, bf16[256,256]{1,0:T(8,128)(2,1)S(1)}, u32[]{:S(2)}, u32[]{:S(2)}) collective-permute-start(bf16[256,256]{1,0:T(8,128)(2,1)S(1)} %get-tuple-element.133), channel_id=1, source_target_pairs={{0,1},{1,0},{2,3},{3,2},{4,5},{5,4},{6,7},{7,6},{8,9},{9,8},{10,11... | collective-permute-start | bytes 393224 | tf_op jit(solution)/shard_map/heads/ppermute | solution.py:1014
  124.9 11.2 %collective-permute-start.20 = (bf16[256,256]{1,0:T(8,128)(2,1)S(1)}, bf16[256,256]{1,0:T(8,128)(2,1)S(1)}, u32[]{:S(2)}, u32[]{:S(2)}) collective-permute-start(bf16[256,256]{1,0:T(8,128)(2,1)S(1)} %get-tuple-element.134), channel_id=1, source_target_pairs={{0,2},{1,3},{2,0},{3,1},{4,6},{5,7},{6,4},{7,5},{8,10},{9,11},{10,... | collective-permute-start | bytes 393224 | tf_op jit(solution)/shard_map/heads/ppermute | solution.py:1014
  133.8 5.8 %collective-permute-start.21 = (bf16[256,256]{1,0:T(8,128)(2,1)S(1)}, bf16[256,256]{1,0:T(8,128)(2,1)S(1)}, u32[]{:S(2)}, u32[]{:S(2)}) collective-permute-start(bf16[256,256]{1,0:T(8,128)(2,1)S(1)} %get-tuple-element.135), channel_id=1, source_target_pairs={{0,3},{1,2},{2,1},{3,0},{4,7},{5,6},{6,5},{7,4},{8,11},{9,10},{10,... | collective-permute-start | bytes 393224 | tf_op jit(solution)/shard_map/heads/ppermute | solution.py:1014
  136.2 5.4 %collective-permute-start.26 = (bf16[1600,256]{1,0:T(8,128)(2,1)}, bf16[1600,256]{1,0:T(8,128)(2,1)S(1)}, u32[]{:S(2)}, u32[]{:S(2)}) collective-permute-start(bf16[1600,256]{1,0:T(8,128)(2,1)} %copy-done.45), channel_id=1, source_target_pairs={{0,1},{1,0},{2,3},{3,2},{4,5},{5,4},{6,7},{7,6},{8,9},{9,8},{10,11... | collective-permute-start | bytes 2457608 | tf_op jit(solution)/shard_map/cyb/ppermute | solution.py:1014
  139.6 2.5 collective-permute-start.25
  139.7 4.8 %collective-permute-start.24 = (bf16[1600,256]{1,0:T(8,128)(2,1)}, bf16[1600,256]{1,0:T(8,128)(2,1)S(1)}, u32[]{:S(2)}, u32[]{:S(2)}) collective-permute-start(bf16[1600,256]{1,0:T(8,128)(2,1)} %copy-done.43), channel_id=1, source_target_pairs={{0,1},{1,0},{2,3},{3,2},{4,5},{5,4},{6,7},{7,6},{8,9},{9,8},{10,11... | collective-permute-start | bytes 2457608 | tf_op jit(solution)/shard_map/cxa/ppermute | solution.py:1014
  140.1 4.4 %collective-permute-start.29 = (bf16[1600,256]{1,0:T(8,128)(2,1)S(1)}, bf16[1600,256]{1,0:T(8,128)(2,1)S(1)}, u32[]{:S(2)}, u32[]{:S(2)}) collective-permute-start(bf16[1600,256]{1,0:T(8,128)(2,1)S(1)} %collective-permute-done.22.refs_14_), channel_id=1, source_target_pairs={{0,1},{1,0},{2,3},{3,2},{4,5},{5,4},{6,7},{7,6},{8,9},{9,8},{10,11... | collective-permute-start | bytes 2457608 | tf_op jit(solution)/shard_map/cyx3/ppermute | solution.py:1014
  174.3 6.1 %collective-permute-start.34 = (bf16[2,2,1600,256]{3,2,1,0:T(8,128)(2,1)}, bf16[2,2,1600,256]{3,2,1,0:T(8,128)(2,1)S(1)}, u32[]{:S(2)}, u32[]{:S(2)}) collective-permute-start(bf16[2,2,1600,256]{3,2,1,0:T(8,128)(2,1)} %get-tuple-element.154), channel_id=1, source_target_pairs={{0,1},{1,0},{2,3},{3,2},{4,5},{5,4},{6,7},{7,6},{8,9},{9,8},{10,11... | collective-permute-start | bytes 9830408 | tf_op jit(solution)/shard_map/rc2/ppermute | solution.py:1014
  174.4 10.8 %collective-permute-start.30 = (bf16[2,2,1600,256]{3,2,1,0:T(8,128)(2,1)}, bf16[2,2,1600,256]{3,2,1,0:T(8,128)(2,1)S(1)}, u32[]{:S(2)}, u32[]{:S(2)}) collective-permute-start(bf16[2,2,1600,256]{3,2,1,0:T(8,128)(2,1)} %get-tuple-element.147), channel_id=1, source_target_pairs={{0,1},{1,0},{2,3},{3,2},{4,5},{5,4},{6,7},{7,6},{8,9},{9,8},{10,11... | collective-permute-start | bytes 9830408 | tf_op jit(solution)/shard_map/rc1/ppermute | solution.py:1014
  174.8 10.4 %collective-permute-start.31 = (bf16[256,256]{1,0:T(8,128)(2,1)}, bf16[256,256]{1,0:T(8,128)(2,1)S(1)}, u32[]{:S(2)}, u32[]{:S(2)}) collective-permute-start(bf16[256,256]{1,0:T(8,128)(2,1)} %get-tuple-element.149), channel_id=1, source_target_pairs={{0,1},{1,0},{2,3},{3,2},{4,5},{5,4},{6,7},{7,6},{8,9},{9,8},{10,11... | collective-permute-start | bytes 393224 | tf_op jit(solution)/shard_map/heads_grad/ppermute | solution.py:1014
  174.9 10.3 %collective-permute-start.32 = (bf16[256,256]{1,0:T(8,128)(2,1)}, bf16[256,256]{1,0:T(8,128)(2,1)S(1)}, u32[]{:S(2)}, u32[]{:S(2)}) collective-permute-start(bf16[256,256]{1,0:T(8,128)(2,1)} %get-tuple-element.150), channel_id=1, source_target_pairs={{0,2},{1,3},{2,0},{3,1},{4,6},{5,7},{6,4},{7,5},{8,10},{9,11},{10,... | collective-permute-start | bytes 393224 | tf_op jit(solution)/shard_map/heads_grad/ppermute | solution.py:1014
  175.9 9.4 %collective-permute-start.33 = (bf16[256,256]{1,0:T(8,128)(2,1)}, bf16[256,256]{1,0:T(8,128)(2,1)S(1)}, u32[]{:S(2)}, u32[]{:S(2)}) collective-permute-start(bf16[256,256]{1,0:T(8,128)(2,1)} %get-tuple-element.151), channel_id=1, source_target_pairs={{0,3},{1,2},{2,1},{3,0},{4,7},{5,6},{6,5},{7,4},{8,11},{9,10},{10,... | collective-permute-start | bytes 393224 | tf_op jit(solution)/shard_map/heads_grad/ppermute | solution.py:1014
  185.3 29.0 %collective-permute-start.37 = (bf16[2,2,1600,256]{3,2,1,0:T(8,128)(2,1)}, bf16[2,2,1600,256]{3,2,1,0:T(8,128)(2,1)S(1)}, u32[]{:S(2)}, u32[]{:S(2)}) collective-permute-start(bf16[2,2,1600,256]{3,2,1,0:T(8,128)(2,1)} %get-tuple-element.178), channel_id=1, source_target_pairs={{0,1},{1,0},{2,3},{3,2},{4,5},{5,4},{6,7},{7,6},{8,9},{9,8},{10,11... | collective-permute-start | bytes 9830408 | tf_op jit(solution)/shard_map/rc3/ppermute | solution.py:1014
  186.8 21.2 %collective-permute-start.36 = (bf16[1600,256]{1,0:T(8,128)(2,1)S(1)}, bf16[1600,256]{1,0:T(8,128)(2,1)}, u32[]{:S(2)}, u32[]{:S(2)}) collective-permute-start(bf16[1600,256]{1,0:T(8,128)(2,1)S(1)} %get-tuple-element.155), channel_id=1, source_target_pairs={{0,2},{1,3},{2,0},{3,1},{4,6},{5,7},{6,4},{7,5},{8,10},{9,11},{10,... | collective-permute-start | bytes 2457608 | tf_op jit(solution)/shard_map/d2/ppermute | solution.py:1014
  187.7 21.4 %collective-permute-start.35 = (bf16[1600,256]{1,0:T(8,128)(2,1)}, bf16[1600,256]{1,0:T(8,128)(2,1)}, u32[]{:S(2)}, u32[]{:S(2)}) collective-permute-start(bf16[1600,256]{1,0:T(8,128)(2,1)} %get-tuple-element.152), channel_id=1, source_target_pairs={{0,4},{1,5},{2,6},{3,7},{4,0},{5,1},{6,2},{7,3},{8,12},{9,13},{10,... | collective-permute-start | bytes 2457608 | tf_op jit(solution)/shard_map/d1/ppermute | solution.py:1014
  189.1 35.9 %collective-permute-start.39 = (bf16[1600,256]{1,0:T(8,128)(2,1)S(1)}, bf16[1600,256]{1,0:T(8,128)(2,1)}, u32[]{:S(2)}, u32[]{:S(2)}) collective-permute-start(bf16[1600,256]{1,0:T(8,128)(2,1)S(1)} %get-tuple-element.157), channel_id=1, source_target_pairs={{0,2},{1,3},{2,0},{3,1},{4,6},{5,7},{6,4},{7,5},{8,10},{9,11},{10,... | collective-permute-start | bytes 2457608 | tf_op jit(solution)/shard_map/e2/ppermute | solution.py:1014
  190.3 35.6 %collective-permute-start.38 = (bf16[1600,256]{1,0:T(8,128)(2,1)S(1)}, bf16[1600,256]{1,0:T(8,128)(2,1)}, u32[]{:S(2)}, u32[]{:S(2)}) collective-permute-start(bf16[1600,256]{1,0:T(8,128)(2,1)S(1)} %get-tuple-element.156), channel_id=1, source_target_pairs={{0,4},{1,5},{2,6},{3,7},{4,0},{5,1},{6,2},{7,3},{8,12},{9,13},{10,... | collective-permute-start | bytes 2457608 | tf_op jit(solution)/shard_map/e1/ppermute | solution.py:1014
  225.8 2.8 collective-permute-start.40
  225.9 21.4 %collective-permute-start.41 = (bf16[1600,256]{1,0:T(8,128)(2,1)}, bf16[1600,256]{1,0:T(8,128)(2,1)}, u32[]{:S(2)}, u32[]{:S(2)}) collective-permute-start(bf16[1600,256]{1,0:T(8,128)(2,1)} %fusion.2), channel_id=1, source_target_pairs={{0,2},{1,3},{2,0},{3,1},{4,6},{5,7},{6,4},{7,5},{8,10},{9,11},{10,... | collective-permute-start | bytes 2457608 | tf_op jit(solution)/shard_map/f1/ppermute | solution.py:1014
  227.1 21.4 %collective-permute-start.46 = (bf16[1600,256]{1,0:T(8,128)(2,1)}, bf16[1600,256]{1,0:T(8,128)(2,1)}, u32[]{:S(2)}, u32[]{:S(2)}) collective-permute-start(bf16[1600,256]{1,0:T(8,128)(2,1)} %fusion.1), channel_id=1, source_target_pairs={{0,4},{1,5},{2,6},{3,7},{4,0},{5,1},{6,2},{7,3},{8,12},{9,13},{10,... | collective-permute-start | bytes 2457608 | tf_op jit(solution)/shard_map/f2/ppermute | solution.py:1014
  234.9 30.3 %collective-permute-start.49 = (bf16[1600,256]{1,0:T(8,128)(2,1)}, bf16[1600,256]{1,0:T(8,128)(2,1)S(1)}, u32[]{:S(2)}, u32[]{:S(2)}) collective-permute-start(bf16[1600,256]{1,0:T(8,128)(2,1)} %get-tuple-element.227), channel_id=1, source_target_pairs={{0,4},{1,5},{2,6},{3,7},{4,0},{5,1},{6,2},{7,3},{8,12},{9,13},{10,... | collective-permute-start | bytes 2457608 | tf_op jit(solution)/shard_map/ry0/ppermute | solution.py:1014
  236.3 28.9 %collective-permute-start.50 = (bf16[1600,256]{1,0:T(8,128)(2,1)}, bf16[1600,256]{1,0:T(8,128)(2,1)}, u32[]{:S(2)}, u32[]{:S(2)}) collective-permute-start(bf16[1600,256]{1,0:T(8,128)(2,1)} %get-tuple-element.195), channel_id=1, source_target_pairs={{0,2},{1,3},{2,0},{3,1},{4,6},{5,7},{6,4},{7,5},{8,10},{9,11},{10,... | collective-permute-start | bytes 2457608 | tf_op jit(solution)/shard_map/d3/ppermute | solution.py:1014
  252.6 19.1 %collective-permute-start.47 = (bf16[1600,256]{1,0:T(8,128)(2,1)}, bf16[1600,256]{1,0:T(8,128)(2,1)S(1)}, u32[]{:S(2)}, u32[]{:S(2)}) collective-permute-start(bf16[1600,256]{1,0:T(8,128)(2,1)} %get-tuple-element.201), channel_id=1, source_target_pairs={{0,8},{1,9},{2,10},{3,11},{4,12},{5,13},{6,14},{7,15},{8,0},{9,1},... | collective-permute-start | bytes 2457608 | tf_op jit(solution)/shard_map/rz_inner1/ppermute | solution.py:1014
  252.8 29.2 %collective-permute-start.42 = (bf16[1600,256]{1,0:T(8,128)(2,1)}, bf16[1600,256]{1,0:T(8,128)(2,1)}, u32[]{:S(2)}, u32[]{:S(2)}) collective-permute-start(bf16[1600,256]{1,0:T(8,128)(2,1)} %get-tuple-element.184), channel_id=1, source_target_pairs={{0,2},{1,3},{2,0},{3,1},{4,6},{5,7},{6,4},{7,5},{8,10},{9,11},{10,... | collective-permute-start | bytes 2457608 | tf_op jit(solution)/shard_map/e3/ppermute | solution.py:1014
  268.4 20.0 %collective-permute-start.51 = (bf16[1600,256]{1,0:T(8,128)(2,1)}, bf16[1600,256]{1,0:T(8,128)(2,1)}, u32[]{:S(2)}, u32[]{:S(2)}) collective-permute-start(bf16[1600,256]{1,0:T(8,128)(2,1)} %fusion), channel_id=1, source_target_pairs={{0,4},{1,5},{2,6},{3,7},{4,0},{5,1},{6,2},{7,3},{8,12},{9,13},{10,... | collective-permute-start | bytes 2457608 | tf_op jit(solution)/shard_map/f3/ppermute | solution.py:1014
  272.0 20.3 %collective-permute-start.48 = (bf16[1600,256]{1,0:T(8,128)(2,1)S(1)}, bf16[1600,256]{1,0:T(8,128)(2,1)}, u32[]{:S(2)}, u32[]{:S(2)}) collective-permute-start(bf16[1600,256]{1,0:T(8,128)(2,1)S(1)} %add_convert_fusion.1.inner), channel_id=1, source_target_pairs={{0,16},{1,17},{2,18},{3,19},{4,20},{5,21},{6,22},{7,23},{24,8},{25... | collective-permute-start | bytes 2457608 | tf_op jit(solution)/shard_map/rz_inner2/ppermute | solution.py:1014
  292.3 18.9 %collective-permute-start.52 = (bf16[1600,256]{1,0:T(8,128)(2,1)}, bf16[1600,256]{1,0:T(8,128)(2,1)}, u32[]{:S(2)}, u32[]{:S(2)}) collective-permute-start(bf16[1600,256]{1,0:T(8,128)(2,1)} %get-tuple-element.206), channel_id=1, source_target_pairs={{0,8},{1,9},{2,10},{3,11},{4,12},{5,13},{6,14},{7,15},{8,0},{9,1},... | collective-permute-start | bytes 2457608 | tf_op jit(solution)/shard_map/rz_outer1/ppermute | solution.py:1014
  293.5 20.4 %collective-permute-start.44 = (f32[2,32,256]{2,1,0:T(8,128)S(1)}, f32[2,32,256]{2,1,0:T(8,128)S(1)}, u32[]{:S(2)}, u32[]{:S(2)}) collective-permute-start(f32[2,32,256]{2,1,0:T(8,128)S(1)} %select_bitcast_fusion), channel_id=1, source_target_pairs={{0,1},{1,0},{2,3},{3,2},{4,5},{5,4},{6,7},{7,6},{8,9},{9,8},{10,11... | collective-permute-start | bytes 196616 | tf_op jit(solution)/shard_map/vec_c/ppermute | solution.py:1014
  294.9 23.1 %collective-permute-start.43 = (bf16[256,1024]{1,0:T(8,128)(2,1)S(1)}, bf16[256,1024]{1,0:T(8,128)(2,1)S(1)}, u32[]{:S(2)}, u32[]{:S(2)}) collective-permute-start(bf16[256,1024]{1,0:T(8,128)(2,1)S(1)} %fusion.11), channel_id=1, source_target_pairs={{0,2},{1,3},{2,0},{3,1},{4,6},{5,7},{6,4},{7,5},{8,10},{9,11},{10,... | collective-permute-start | bytes 1572872 | tf_op jit(solution)/shard_map/in_x/ppermute | solution.py:1014
  312.6 20.6 %collective-permute-start.53 = (bf16[1600,256]{1,0:T(8,128)(2,1)S(1)}, bf16[1600,256]{1,0:T(8,128)(2,1)}, u32[]{:S(2)}, u32[]{:S(2)}) collective-permute-start(bf16[1600,256]{1,0:T(8,128)(2,1)S(1)} %add_convert_fusion.outer), channel_id=1, source_target_pairs={{8,24},{9,25},{10,26},{11,27},{12,28},{13,29},{14,30},{15,31},{16,... | collective-permute-start | bytes 2457608 | tf_op jit(solution)/shard_map/rz_outer2/ppermute | solution.py:1014
  313.9 4.0 %collective-permute-start.45 = (f32[32,256]{1,0:T(8,128)S(1)}, f32[32,256]{1,0:T(8,128)S(1)}, u32[]{:S(2)}, u32[]{:S(2)}) collective-permute-start(f32[32,256]{1,0:T(8,128)S(1)} %select_bitcast_fusion.1), channel_id=1, source_target_pairs={{0,2},{1,3},{2,0},{3,1},{4,6},{5,7},{6,4},{7,5},{8,10},{9,11},{10,... | collective-permute-start | bytes 98312 | tf_op jit(solution)/shard_map/vec_x/ppermute | solution.py:1014
  337.6 4.2 %collective-permute-start.54 = (f32[40,256]{1,0:T(8,128)S(1)}, f32[40,256]{1,0:T(8,128)S(1)}, u32[]{:S(2)}, u32[]{:S(2)}) collective-permute-start(f32[40,256]{1,0:T(8,128)S(1)} %pad_maximum_fusion.1), channel_id=1, source_target_pairs={{0,4},{1,5},{2,6},{3,7},{4,0},{5,1},{6,2},{7,3},{8,12},{9,13},{10,... | collective-permute-start | bytes 122888 | tf_op jit(solution)/shard_map/norm/ppermute | solution.py:1014
  342.5 7.5 %collective-permute-start.55 = (f32[40,256]{1,0:T(8,128)S(1)}, f32[40,256]{1,0:T(8,128)S(1)}, u32[]{:S(2)}, u32[]{:S(2)}) collective-permute-start(f32[40,256]{1,0:T(8,128)S(1)} %fusion.18), channel_id=1, source_target_pairs={{0,8},{1,9},{2,10},{3,11},{4,12},{5,13},{6,14},{7,15},{8,0},{9,1},... | collective-permute-start | bytes 122888 | tf_op jit(solution)/shard_map/norm/ppermute | solution.py:1014
  342.5 7.5 %collective-permute-start.56 = (f32[40,256]{1,0:T(8,128)S(1)}, f32[40,256]{1,0:T(8,128)S(1)}, u32[]{:S(2)}, u32[]{:S(2)}) collective-permute-start(f32[40,256]{1,0:T(8,128)S(1)} %fusion.18), channel_id=1, source_target_pairs={{0,16},{1,17},{2,18},{3,19},{4,20},{5,21},{6,22},{7,23},{8,24},{9,... | collective-permute-start | bytes 122888 | tf_op jit(solution)/shard_map/norm/ppermute | solution.py:1014
  344.3 5.8 %collective-permute-start.57 = (f32[40,256]{1,0:T(8,128)S(1)}, f32[40,256]{1,0:T(8,128)S(1)}, u32[]{:S(2)}, u32[]{:S(2)}) collective-permute-start(f32[40,256]{1,0:T(8,128)S(1)} %fusion.18), channel_id=1, source_target_pairs={{0,24},{1,25},{2,26},{3,27},{4,28},{5,29},{6,30},{7,31},{8,16},{9,... | collective-permute-start | bytes 122888 | tf_op jit(solution)/shard_map/norm/ppermute | solution.py:1014
  351.4 3.8 %collective-permute-start.60 = (f32[8,128]{1,0:T(8,128)S(1)}, f32[8,128]{1,0:T(8,128)S(1)}, u32[]{:S(2)}, u32[]{:S(2)}) collective-permute-start(f32[8,128]{1,0:T(8,128)S(1)} %broadcast_in_dim.61), channel_id=1, source_target_pairs={{0,3},{1,2},{2,1},{3,0},{4,7},{5,6},{6,5},{7,4},{8,11},{9,10},{10,... | collective-permute-start | bytes 12296 | tf_op jit(solution)/shard_map/norm/ppermute | solution.py:1014
  351.5 3.7 %collective-permute-start.58 = (f32[8,128]{1,0:T(8,128)S(1)}, f32[8,128]{1,0:T(8,128)S(1)}, u32[]{:S(2)}, u32[]{:S(2)}) collective-permute-start(f32[8,128]{1,0:T(8,128)S(1)} %broadcast_in_dim.61), channel_id=1, source_target_pairs={{0,1},{1,0},{2,3},{3,2},{4,5},{5,4},{6,7},{7,6},{8,9},{9,8},{10,11... | collective-permute-start | bytes 12296 | tf_op jit(solution)/shard_map/norm/ppermute | solution.py:1014
  352.5 3.6 collective-permute-start.59
  (53 other events, 523.5 us)
